TPU v7x, 128 devices: a whole 4x4x4 slice. The times are simulated.
128 devices in a mesh: blk: 16 (over x_lo, z, core), rep: 8 (over x_hi, y).
Axes of the slice: x: 4 (x_hi: 2, x_lo: 2; x = x_hi * 2 + x_lo), y: 4, z: 4, core: 2. Of those that a mesh axis runs over, the one named last changes fastest.
Arguments:
- features: bfloat16 [32768, 512], P(('blk', 'rep')), may hold values from -6 to 6
- weight: bfloat16 [512, 512], replicated, may hold values from -0.25 to 0.25
- layer_bias: float32 [512], replicated, may hold values from -4 to 4
- tile_values: bfloat16 [16, 8, 32, 8, 128, 128], P('blk', 'rep'), may hold values from -0.21875 to 0.21875
- tile_target: int32 [16, 8, 32, 8], P('blk', 'rep'), may hold values from 0 to 15, as said below
- tile_counts: int32 [16, 8, 32], P('blk', 'rep'), may hold values from 1 to 8, as said below
- cotangent: bfloat16 [32768, 512], P(('blk', 'rep')), may hold values from -6 to 6
Outputs:
- output: bfloat16 [32768, 512], P(('blk', 'rep'))
- grad_features: bfloat16 [32768, 512], P(('blk', 'rep'))
- grad_weight: float32 [512, 512], replicated
- grad_bias: float32 [512], replicated
Inputs may be any that keep to these rules, and one draw needn't show every extreme that they name: `tile_target`: within one source row tile of one list the 8 targets are distinct row tiles of the destination block. `tile_counts`: slots at or past the count are empty; every device's list has a source row tile with all 8 slots used.
All inputs are finite; a program needn't handle non-finite values.
Results may differ from a plain program's by a relative error of at most 0.008.
Values may be sent and summed in bfloat16 or wider, within the bound.
No kernel may reach another device: no remote copies, remote signals or barrier semaphores. Data moves between devices by JAX's collectives and lax.ppermute only.
A program may use at most 128 MiB of HBM per device.

v0:
```python
import math

import jax
import jax.numpy as jnp
from jax import lax
from jax.sharding import PartitionSpec as P


def swish_parts(summed, layer_bias, cotangent):
    shifted = summed + layer_bias[None, :]
    logistic = jax.nn.sigmoid(shifted)
    output = (shifted * logistic).astype(jnp.bfloat16)
    derivative = logistic * (1.0 + shifted * (1.0 - logistic))
    grad_summed = (cotangent.astype(jnp.float32) * derivative).astype(jnp.bfloat16)
    return (output, grad_summed)


def body(features, weight, layer_bias, tile_values, tile_target, tile_counts, cotangent):
    local_rows, feature_width = features.shape
    values = tile_values[0, 0]
    targets = tile_target[0, 0]
    counts = tile_counts[0, 0]
    tile_size = values.shape[-1]
    groups, slot_total = targets.shape
    dest_tiles = lax.axis_size("rep") * local_rows // tile_size
    active = lax.broadcasted_iota(jnp.int32, (groups, slot_total), 1) < counts[:, None]
    masked = jnp.where(active[:, :, None, None], values, jnp.zeros((), values.dtype))
    projected = jnp.dot(features, weight, preferred_element_type=jnp.float32).astype(jnp.bfloat16)

    def apply_group(running, group_id, sources):
        products = jnp.einsum(
            "sij,jf->sif", masked[group_id], sources, preferred_element_type=jnp.float32
        )
        return running.at[targets[group_id]].add(products)

    empty = jnp.zeros((dest_tiles, tile_size, feature_width), jnp.float32)
    running = empty
    incoming = lax.all_gather(projected, "blk", axis=0, tiled=True)
    number = incoming.shape[0] // tile_size
    blocks = incoming.reshape(number, tile_size, feature_width)

    def fold_group_step(current, offset):
        return (apply_group(current, offset, blocks[offset]), None)

    running, unused = lax.scan(fold_group_step, running, jnp.arange(number, dtype=jnp.int32))
    partial_value = running
    partial_value = partial_value.reshape(dest_tiles * tile_size, feature_width)
    summed = lax.psum_scatter(partial_value, "rep", scatter_dimension=0, tiled=True)
    output, grad_summed = swish_parts(summed, layer_bias, cotangent)
    grad_block = lax.all_gather(grad_summed, "rep", axis=0, tiled=True)
    grad_tiles = grad_block.reshape(dest_tiles, tile_size, feature_width)

    def back_group(group_id):
        gathered = grad_tiles[targets[group_id]]
        return jnp.einsum(
            "sij,sif->jf", masked[group_id], gathered, preferred_element_type=jnp.float32
        )

    row_count = lax.axis_size("blk") * local_rows
    number = row_count // tile_size

    def source_group_step(current, offset):
        return (current, back_group(offset))

    unused, terms = lax.scan(
        source_group_step, jnp.zeros((), jnp.float32), jnp.arange(number, dtype=jnp.int32)
    )
    grad_rows = lax.psum_scatter(
        terms.reshape(row_count, feature_width), "blk", scatter_dimension=0, tiled=True
    )
    grad_projected = grad_rows.astype(jnp.bfloat16)
    grad_features = lax.dot_general(
        grad_projected, weight, (((1,), (1,)), ((), ())), preferred_element_type=jnp.float32
    ).astype(jnp.bfloat16)
    weight_part = lax.dot_general(
        features, grad_projected, (((0,), (0,)), ((), ())), preferred_element_type=jnp.float32
    )
    bias_part = jnp.sum(grad_summed.astype(jnp.float32), axis=0)
    weight_total, bias_total = lax.psum((weight_part, bias_part), ("blk", "rep"))
    node_total = local_rows * lax.axis_size("blk") * lax.axis_size("rep")
    norm_scale = 1.0 / math.sqrt(node_total)
    return (output, grad_features, weight_total * norm_scale, bias_total * norm_scale)


def solution(mesh):
    placed = (
        P(("blk", "rep"), None),
        P(),
        P(),
        P("blk", "rep", None, None, None, None),
        P("blk", "rep", None, None),
        P("blk", "rep", None),
        P(("blk", "rep"), None),
    )
    return jax.shard_map(
        body,
        mesh=mesh,
        in_specs=placed,
        out_specs=(P(("blk", "rep"), None), P(("blk", "rep"), None), P(), P()),
        check_vma=False,
    )
```

profile of v0, /device:TPU:0, one launch (start us, length us, event | category | flops | bytes accessed | tf_op | source)
XLA Modules:
  0.0 910.9 jit_solution(14258984917883684823)
XLA Ops:
  10.3 11.9 %copy.12 = bf16[1,1,32,8,128,128]{4,5,3,2,1,0:T(8,128)(2,1)} copy(bf16[1,1,32,8,128,128]{5,4,3,2,1,0:T(8,128)(2,1)} %param.14) | data formatting | bytes 16777216 | tf_op args[3]
  22.4 7.3 bitcast_select_fusion
  29.6 20.6 %all-gather.3.cloned.1.call-done = bf16[4096,512]{1,0:T(8,128)(2,1)} async-done(((bf16[256,512]{1,0:T(8,128)(2,1)}), bf16[4096,512]{1,0:T(8,128)(2,1)}) %all-gather.3.cloned.1.call-update) | async-done | bytes 4194320 | tf_op jit(solution)/shard_map/all_gather | solution.py:38
  52.7 268.3 %while.20 = (s32[]{:T(128)}, f32[16,128,512]{2,1,0:T(8,128)}, s32[32]{0:T(128)S(1)}, s32[32,8]{1,0:T(8,128)S(1)}, bf16[32,8,128,128]{2,3,1,0:T(8,128)(2,1)}, /*i...) while((s32[]{:T(128)}, f32[16,128,512]{2,1,0:T(8,128)}, s32[32]{0:T(128)S(1)}, ...), condition=%wide.region_2.3_spmd, body=%wide.region_0.2_spmd.sunk | while | flops 134742048 | bytes 8783087 | solution.py:45
  65.1 4.5 scatter_fusion
  81.9 4.4 scatter_fusion
  132.2 4.5 scatter_fusion
  140.6 4.4 scatter_fusion
  157.4 4.4 scatter_fusion
  165.8 4.4 scatter_fusion
  174.2 4.4 scatter_fusion
  190.9 4.4 scatter_fusion
  207.7 4.4 scatter_fusion
  224.5 4.4 scatter_fusion
  241.2 4.4 scatter_fusion
  274.7 4.4 scatter_fusion
  291.5 4.4 scatter_fusion
  308.2 4.4 scatter_fusion
  321.1 84.7 %reduce-scatter.3.cloned.1.call-done = f32[256,512]{1,0:T(8,128)} async-done(((f32[2048,512]{1,0:T(8,128)}), f32[256,512]{1,0:T(8,128)}) %reduce-scatter.3.cloned.1.call-update) | async-done | bytes 524304 | tf_op jit(solution)/shard_map/reduce_scatter | solution.py:48
  408.0 53.8 %all-gather.5.cloned.1.call-done = bf16[2048,512]{1,0:T(8,128)(2,1)} async-done(((bf16[256,512]{1,0:T(8,128)(2,1)}), bf16[2048,512]{1,0:T(8,128)(2,1)}) %all-gather.5.cloned.1.call-update) | async-done | bytes 2097168 | tf_op jit(solution)/shard_map/all_gather | solution.py:50
  461.8 215.8 %while.21 = (s32[]{:T(128)}, f32[32,128,512]{2,1,0:T(8,128)}, s32[32]{0:T(128)S(1)}, bf16[32,8,128,128]{2,3,1,0:T(8,128)(2,1)}, s32[32,8]{1,0:T(8,128)S(1)}, /*i...) while((s32[]{:T(128)}, f32[32,128,512]{2,1,0:T(8,128)}, s32[32]{0:T(128)S(1)}, ...), condition=%wide.region_5.6_spmd, body=%wide.region_4.5_spmd.sunk | while | flops 134218784 | bytes 3674899 | solution.py:65
  677.7 73.0 %reduce-scatter.5.cloned.1.call-done = f32[256,512]{1,0:T(8,128)} async-done(((f32[4096,512]{1,0:T(8,128)}), f32[256,512]{1,0:T(8,128)}) %reduce-scatter.5.cloned.1.call-update) | async-done | bytes 524304 | tf_op jit(solution)/shard_map/reduce_scatter | solution.py:68
  753.1 64.4 %psum.15 = f32[512]{0:T(512)S(1)} all-reduce(f32[512]{0:T(512)S(1)} %get-tuple-element.104), channel_id=1, replica_groups=mesh['blk'=16,'rep'=8] {'blk','rep'}, use_global_device_ids=true, to_apply=%region_9.10 | all-reduce | flops 512 | bytes 4096 | tf_op jit(solution)/shard_map/psum | solution.py:79
  820.1 81.6 %all-reduce.2.cloned.1.call-done = f32[512,512]{0,1:T(8,128)} async-done(((f32[512,512]{0,1:T(8,128)}), f32[512,512]{0,1:T(8,128)}) %all-reduce.2.cloned.1.call-update) | async-done | bytes 1048592 | tf_op jit(solution)/shard_map/psum | solution.py:79
  (309 shorter events, 312.3 us)
Async XLA Ops:
  7.2 1.0 copy-start
  7.2 43.1 %all-gather.3.cloned.1.call-start = ((), (), s32[]{:S(2)}) async-start(), calls=%async_computation.2 | async-start | bytes 4456448 | tf_op jit(solution)/shard_map/all_gather | solution.py:38
  10.2 12.0 %copy-start.3 = (s32[1,1,32,8]{2,3,1,0:T(8,128)S(1)}, s32[1,1,32,8]{2,3,1,0:T(8,128)}, u32[]{:S(2)}) copy-start(s32[1,1,32,8]{2,3,1,0:T(8,128)} %param.15) | copy-start | bytes 3076
  10.2 12.1 %copy-start.5 = (s32[1,1,32]{2,1,0:T(1,128)S(1)}, s32[1,1,32]{2,1,0:T(1,128)}, u32[]{:S(2)}) copy-start(s32[1,1,32]{2,1,0:T(1,128)} %param.16) | copy-start | bytes 388
  10.2 395.6 %reduce-scatter.3.cloned.1.call-start = ((), (), s32[]{:S(2)}) async-start(), calls=%async_computation.3 | async-start | bytes 4718592 | tf_op jit(solution)/shard_map/reduce_scatter | solution.py:48
  321.0 84.8 %copy-start.2 = (bf16[256,512]{1,0:T(8,128)(2,1)S(1)}, bf16[256,512]{1,0:T(8,128)(2,1)}, u32[]{:S(2)}) copy-start(bf16[256,512]{1,0:T(8,128)(2,1)} %param.17) | copy-start | bytes 786436
  321.0 84.8 %copy-start.4 = (f32[512]{0:T(512)S(1)}, f32[512]{0:T(512)}, u32[]{:S(2)}) copy-start(f32[512]{0:T(512)} %param.13) | copy-start | bytes 6148
  321.1 140.7 %all-gather.5.cloned.1.call-start = ((), (), s32[]{:S(2)}) async-start(), calls=%async_computation.4 | async-start | bytes 2359296 | tf_op jit(solution)/shard_map/all_gather | solution.py:50
  407.9 342.8 %reduce-scatter.5.cloned.1.call-start = ((), (), s32[]{:S(2)}) async-start(), calls=%async_computation.5 | async-start | bytes 8912896 | tf_op jit(solution)/shard_map/reduce_scatter | solution.py:68
  677.6 73.1 %copy-start.1 = (bf16[256,512]{1,0:T(8,128)(2,1)S(1)}, bf16[256,512]{1,0:T(8,128)(2,1)}, u32[]{:S(2)}) copy-start(bf16[256,512]{1,0:T(8,128)(2,1)} %param.11) | copy-start | bytes 786436
  677.6 224.1 %all-reduce.2.cloned.1.call-start = ((), (), s32[]{:S(2)}) async-start(), calls=%async_computation.6 | async-start | bytes 2097152 | tf_op jit(solution)/shard_map/psum | solution.py:79
Sparse Core Ops, SparseCore 0:
  10.3 39.8 all-gather.2
  321.2 84.5 reduce-scatter.2
  409.0 52.6 all-gather.4
  677.7 72.8 reduce-scatter.4
  756.6 145.0 all-reduce.1
where the time goes:
time: 918 us; the launch traced here: 911 us
  waiting for transfers between devices  314 us (34%)
  other arithmetic  153 us (17%)
  loops' own time  126 us (14%)
  local copies, waits for them, and re-layouts  125 us (14%)
  matrix products  116 us (13%)
  blocking collectives  64.4 us (7%)
  between operations  13.8 us (2%)
    scatter-add x32, other arithmetic, apply_group(): return running.at[targets[group_id]].add(products)  141 us
    reduce_scatter x1, waiting for transfers between devices, body(): lax.psum_scatter(partial_value, 'rep', scatter_dimension=0, tiled=True)  84.7 us
    psum x1, waiting for transfers between devices, body(): lax.psum((weight_part, bias_part), ('blk', 'rep'))  81.6 us
    reduce_scatter x1, waiting for transfers between devices, body(): lax.psum_scatter(terms.reshape(row_count, feature_width), 'blk', scatter_...  73 us
    gather x32, local copies, waits for them, and re-layouts, back_group(): gathered = grad_tiles[targets[group_id]]  70.6 us
    psum x1, blocking collectives, body(): lax.psum((weight_part, bias_part), ('blk', 'rep'))  64.4 us
    dot_general x32, matrix products, back_group(): jnp.einsum('sij,sif->jf', masked[group_id], gathered, preferred_element_t...  63.1 us
    another operation x1, loops' own time, body(): lax.scan(source_group_step, jnp.zeros((), jnp.float32), jnp.arange(number...  63 us
  transfers between devices with their start and end apart: 5, of which 5 were waited for; matrix products, arithmetic and copies ran while one was open for 2% of the time, Pallas kernels for 0%

commit v1 on v0

v1 whole, which is shorter than its diff:
```python
import itertools
import math

import jax
import jax.numpy as jnp
import numpy as np
from jax import lax
from jax.experimental import pallas as pl
from jax.experimental.pallas import tpu as pltpu
from jax.sharding import Mesh, PartitionSpec as P

SIZES = {"xl": 2, "z": 4, "core": 2, "xh": 2, "y": 4}
BLK = ("xl", "z", "core")
REP = ("xh", "y")
CHIP = ("xl", "z")
ALL = BLK + REP
VMEM = 60 << 20


def send_by(value, axes, offsets):
    sizes = [SIZES[a] for a in axes]
    pairs = []
    for at in itertools.product(*[range(n) for n in sizes]):
        to = [(i + o) % n for i, o, n in zip(at, offsets, sizes)]
        pairs.append((int(np.ravel_multi_index(at, sizes)), int(np.ravel_multi_index(to, sizes))))
    return lax.ppermute(value, axes, pairs)


def all_offsets(axes):
    return list(itertools.product(*[range(SIZES[a]) for a in axes]))


def neighbours(axes, sign):
    found = []
    for offsets in all_offsets(axes):
        flat = jnp.int32(0)
        for axis, offset in zip(axes, offsets):
            n = SIZES[axis]
            flat = flat * n + (lax.axis_index(axis) + (n + sign * offset)) % n
        found.append(flat)
    return jnp.stack(found).astype(jnp.int32)


def forward_kernel(source_ref, slot_ref, count_ref, place_ref, x_ref, v_ref, out_ref, acc_ref):
    step = pl.program_id(0)
    tile = v_ref.shape[-1]
    slots = v_ref.shape[1]

    @pl.when(step == 0)
    def _():
        acc_ref[...] = jnp.zeros_like(acc_ref)

    for t in range(2):
        group = source_ref[step] * 2 + t
        count = count_ref[group]
        for s in range(0, slots, 2):

            @pl.when(s < count)
            def _():
                rows = x_ref[0, pl.ds(t * tile, tile), :]
                tiles = v_ref[t, pl.ds(s, 2)].reshape(2 * tile, tile)
                product = jnp.dot(tiles, rows, preferred_element_type=jnp.float32)
                for k in range(2):
                    acc_ref[slot_ref[group * slots + s + k]] += product[k * tile : (k + 1) * tile]

    @pl.when(step == pl.num_programs(0) - 1)
    def _():
        for i in range(out_ref.shape[0]):
            for t in range(2):
                out_ref[i, pl.ds(t * tile, tile), :] = acc_ref[place_ref[i] * 2 + t].astype(out_ref.dtype)


def aggregate(sources, slots, counts, places, gathered, values):
    steps, rows, width = gathered.shape
    groups, slot_total, tile, _ = values.shape
    parts = places.shape[0]
    return pl.pallas_call(
        forward_kernel,
        out_shape=jax.ShapeDtypeStruct((parts, rows, width), jnp.bfloat16),
        grid_spec=pltpu.PrefetchScalarGridSpec(
            num_scalar_prefetch=4,
            grid=(steps,),
            in_specs=[
                pl.BlockSpec((1, rows, width), lambda i, *_: (i, 0, 0)),
                pl.BlockSpec((2, slot_total, tile, tile), lambda i, source, *_: (source[i], 0, 0, 0)),
            ],
            out_specs=pl.BlockSpec((parts, rows, width), lambda i, *_: (0, 0, 0)),
            scratch_shapes=[pltpu.VMEM((parts * 2 + 1, tile, width), jnp.float32)],
        ),
        compiler_params=pltpu.CompilerParams(vmem_limit_bytes=VMEM),
    )(sources, slots, counts, places, gathered, values)


def backward_kernel(source_ref, slot_ref, count_ref, g_ref, v_ref, out_ref, acc_ref, table_ref):
    step = pl.program_id(0)
    tile = v_ref.shape[-1]
    slots = v_ref.shape[1]

    @pl.when(step == 0)
    def _():
        last = table_ref.shape[0] - 1
        table_ref[last] = jnp.zeros_like(table_ref[last])
        for i in range(last):
            table_ref[i] = g_ref[i]

    for t in range(2):
        group = source_ref[step] * 2 + t
        count = count_ref[group]
        for s in range(0, slots, 2):

            @pl.when(s < count)
            def _():
                tiles = v_ref[t, pl.ds(s, 2)].reshape(2 * tile, tile)
                rows = jnp.concatenate(
                    [table_ref[slot_ref[group * slots + s]], table_ref[slot_ref[group * slots + s + 1]]], axis=0
                )
                product = lax.dot_general(
                    tiles, rows, (((0,), (0,)), ((), ())), preferred_element_type=jnp.float32
                )
                if s == 0:
                    acc_ref[...] = product
                else:
                    acc_ref[...] += product

        out_ref[0, pl.ds(t * tile, tile), :] = acc_ref[...].astype(out_ref.dtype)


def spread(sources, slots, counts, tiles, values):
    total, tile, width = tiles.shape
    steps = sources.shape[0]
    slot_total = values.shape[1]
    return pl.pallas_call(
        backward_kernel,
        out_shape=jax.ShapeDtypeStruct((steps, 2 * tile, width), jnp.bfloat16),
        grid_spec=pltpu.PrefetchScalarGridSpec(
            num_scalar_prefetch=3,
            grid=(steps,),
            in_specs=[
                pl.BlockSpec((total, tile, width), lambda i, *_: (0, 0, 0)),
                pl.BlockSpec((2, slot_total, tile, tile), lambda i, source, *_: (source[i], 0, 0, 0)),
            ],
            out_specs=pl.BlockSpec((1, 2 * tile, width), lambda i, *_: (i, 0, 0)),
            scratch_shapes=[
                pltpu.VMEM((tile, width), jnp.float32),
                pltpu.VMEM((total + 1, tile, width), jnp.bfloat16),
            ],
        ),
        compiler_params=pltpu.CompilerParams(vmem_limit_bytes=VMEM),
    )(sources, slots, counts, tiles, values)


def middle_kernel(*refs):
    parts = refs[:-8]
    weight_ref, bias_ref, cotangent_ref, out_ref, back_ref, weight_part_ref, bias_part_ref, _ = refs[-8:]
    f32 = jnp.float32
    total = parts[0][...].astype(f32)
    for part in parts[1:]:
        total += part[...].astype(f32)
    rows = total.astype(jnp.bfloat16)
    shifted = jnp.dot(rows, weight_ref[...], preferred_element_type=f32) + bias_ref[...]
    logistic = jax.nn.sigmoid(shifted)
    out_ref[...] = (shifted * logistic).astype(jnp.bfloat16)
    derivative = logistic * (1.0 + shifted * (1.0 - logistic))
    grad = (cotangent_ref[...].astype(f32) * derivative).astype(jnp.bfloat16)
    back_ref[...] = lax.dot_general(
        grad, weight_ref[...], (((1,), (1,)), ((), ())), preferred_element_type=f32
    ).astype(jnp.bfloat16)
    weight_part_ref[...] = lax.dot_general(rows, grad, (((0,), (0,)), ((), ())), preferred_element_type=f32)
    bias_part_ref[...] = jnp.sum(grad.astype(f32), axis=0, keepdims=True)


def middle(parts, weight, layer_bias, cotangent):
    rows, width = cotangent.shape
    return pl.pallas_call(
        middle_kernel,
        out_shape=(
            jax.ShapeDtypeStruct((rows, width), jnp.bfloat16),
            jax.ShapeDtypeStruct((rows, width), jnp.bfloat16),
            jax.ShapeDtypeStruct((width, width), jnp.float32),
            jax.ShapeDtypeStruct((1, width), jnp.float32),
        ),
        scratch_shapes=[pltpu.VMEM((8, 128), jnp.float32)],
        compiler_params=pltpu.CompilerParams(vmem_limit_bytes=VMEM),
    )(*parts, weight, layer_bias[None, :], cotangent)


def body(features, weight, layer_bias, tile_values, tile_target, tile_counts, cotangent):
    local_rows, width = features.shape
    values = tile_values[0, 0]
    targets = tile_target[0, 0]
    counts = tile_counts[0, 0]
    groups, slot_total = targets.shape
    rep_total = math.prod(SIZES[a] for a in REP)
    tile = values.shape[-1]
    assert local_rows == 2 * tile
    dest_tiles = 2 * rep_total

    active = lax.broadcasted_iota(jnp.int32, targets.shape, 1) < counts[:, None]
    slots = jnp.where(active, targets, dest_tiles).reshape(-1)
    owner = targets // 2
    xh, y = SIZES["xh"], SIZES["y"]
    from_part = ((lax.axis_index("xh") + xh - owner // y) % xh) * y + (lax.axis_index("y") + y - owner % y) % y
    back_slots = jnp.where(active, from_part * 2 + targets % 2, dest_tiles).reshape(-1)

    chips = all_offsets(CHIP)
    parts = all_offsets(REP)

    own = jnp.stack([features] + [send_by(features, CHIP, o) for o in chips[1:]])
    gathered = jnp.concatenate([own, send_by(own, ("core",), (1,))])
    chip_at = neighbours(CHIP, -1)
    core = lax.axis_index("core")
    arrived = jnp.concatenate([chip_at * 2 + core, chip_at * 2 + 1 - core])
    partial = aggregate(arrived, slots, counts, neighbours(REP, 1), gathered, values)

    received = [partial[0]] + [send_by(partial[i], REP, o) for i, o in enumerate(parts) if i]
    output, back, weight_part, bias_part = middle(received, weight, layer_bias, cotangent)

    blocks = jnp.stack([back] + [send_by(back, REP, o) for o in parts[1:]])
    chip_to = neighbours(CHIP, 1)
    leaving = jnp.concatenate([chip_to * 2 + 1 - core, chip_to * 2 + core])
    terms = spread(leaving, back_slots, counts, blocks.reshape(dest_tiles, tile, width), values)
    terms = terms.reshape(2, len(chips), local_rows, width)
    crossed = send_by(terms[0], ("core",), (1,))
    merged = (terms[1].astype(jnp.float32) + crossed.astype(jnp.float32)).astype(jnp.bfloat16)
    total = merged[0].astype(jnp.float32)
    for i, o in enumerate(chips):
        if i:
            total += send_by(merged[i], CHIP, o).astype(jnp.float32)
    grad_features = total.astype(jnp.bfloat16)

    device_total = math.prod(SIZES.values())
    flat = jnp.concatenate([weight_part, jnp.pad(bias_part, ((0, device_total - 1), (0, 0)))])
    pieces = lax.all_to_all(flat.reshape(device_total, -1, width), ALL, 0, 0, tiled=True)
    piece = jnp.sum(pieces, axis=0)
    whole = lax.all_to_all(
        jnp.broadcast_to(piece[None], (device_total, *piece.shape)), ALL, 0, 0, tiled=True
    ).reshape(flat.shape)
    norm_scale = 1.0 / math.sqrt(local_rows * device_total)
    whole = whole * norm_scale
    return (output, grad_features, whole[:width], whole[width])


def solution(mesh):
    fine = Mesh(np.asarray(mesh.devices).reshape(tuple(SIZES.values())), tuple(SIZES))
    placed = (
        P(ALL, None),
        P(),
        P(),
        P(BLK, REP, None, None, None, None),
        P(BLK, REP, None, None),
        P(BLK, REP, None),
        P(ALL, None),
    )
    return jax.shard_map(
        body,
        mesh=fine,
        in_specs=placed,
        out_specs=(P(ALL, None), P(ALL, None), P(), P()),
        check_vma=False,
    )
```

time: 918 us -> 276 us (0.30)
  waiting for transfers between devices: 314 us -> 82.1 us
  other arithmetic: 153 us -> 10.5 us
  loops' own time: 126 us -> 0 us
  matrix products: 116 us -> 0 us
  local copies, waits for them, and re-layouts: 125 us -> 27.3 us
  starting transfers between devices: 0.21 us -> 71.2 us
  Pallas kernels: 0 us -> 36.9 us
  blocking collectives: 64.4 us -> 46.8 us
  between operations: 13.8 us -> 0.88 us
    reduce_scatter x2 -> x0, waiting for transfers between devices: 158 us -> none  [the longest x1 84.7 us: body(): lax.psum_scatter(partial_value, 'rep', scatter_dimension=0, tiled=True)]
    scatter-add x32 -> x0, other arithmetic: 141 us -> none  [apply_group(): return running.at[targets[group_id]].add(products)]
    another operation x2 -> x0, loops' own time: 126 us -> none  [the longest x1 63 us: body(): lax.scan(source_group_step, jnp.zeros((), jnp.float32), jnp.arange(number...]
    dot_general x67 -> x0, matrix products: 116 us -> none  [the longest x32 63.1 us: back_group(): jnp.einsum('sij,sif->jf', masked[group_id], gathered, preferred_element_t...]
    ppermute x0 -> x30, waiting for transfers between devices: none -> 82.1 us  [send_by(): return lax.ppermute(value, axes, pairs)]
    psum x1 -> x0, waiting for transfers between devices: 81.6 us -> none  [body(): lax.psum((weight_part, bias_part), ('blk', 'rep'))]
    all_gather x2 -> x0, waiting for transfers between devices: 74.4 us -> none  [the longest x1 53.8 us: body(): grad_block = lax.all_gather(grad_summed, 'rep', axis=0, tiled=True)]
    gather x32 -> x0, local copies, waits for them, and re-layouts: 70.6 us -> none  [back_group(): gathered = grad_tiles[targets[group_id]]]
  transfers between devices with their start and end apart: 5 -> 31, of which waited for: 5 -> 15; matrix products, arithmetic and copies ran while one was open for 2% -> 9% of each run, Pallas kernels for 0% -> 0%
where the time goes in v1:
time: 276 us
  waiting for transfers between devices  82.1 us (30%)
  starting transfers between devices  71.2 us (26%)
  blocking collectives  46.8 us (17%)
  Pallas kernels  36.9 us (13%)
  local copies, waits for them, and re-layouts  27.3 us (10%)
  other arithmetic  10.5 us (4%)
    ppermute x30, waiting for transfers between devices, send_by(): return lax.ppermute(value, axes, pairs)  82.1 us
    ppermute x30, starting transfers between devices, send_by(): return lax.ppermute(value, axes, pairs)  64.5 us
    all_to_all x1, blocking collectives, body(): lax.all_to_all(flat.reshape(device_total, -1, width), ALL, 0, 0, tiled=True)  46.8 us
    pallas_call x1, Pallas kernels, aggregate(): pl.pallas_call(forward_kernel, out_shape=jax.ShapeDtypeStruct((parts, row...  16.8 us
    pallas_call x1, Pallas kernels, spread(): pl.pallas_call(backward_kernel, out_shape=jax.ShapeDtypeStruct((steps, 2...  16.5 us
    unnamed x47, local copies, waits for them, and re-layouts  10.8 us
    all_to_all x1, starting transfers between devices, body(): lax.all_to_all(jnp.broadcast_to(piece[None], (device_total, *piece.shape)...  6.71 us
  transfers between devices with their start and end apart: 31, of which 15 were waited for; matrix products, arithmetic and copies ran while one was open for 9% of the time, Pallas kernels for 0%

profile of v1, /device:TPU:0, one launch (start us, length us, event | category | flops | bytes accessed | tf_op | source)
XLA Modules:
  0.0 275.7 jit_solution(12757799658528636526)
XLA Ops:
  2.7 3.6 %collective-permute-start.1 = (bf16[256,512]{1,0:T(8,128)(2,1)}, bf16[256,512]{1,0:T(8,128)(2,1)S(1)}, u32[]{:S(2)}, u32[]{:S(2)}) collective-permute-start(bf16[256,512]{1,0:T(8,128)(2,1)} %param.7), channel_id=1, source_target_pairs={{0,32},{16,48},{32,0},{48,16},{64,96},{80,112},{96,64},{112,80},{1... | collective-permute-start | bytes 786440 | tf_op jit(solution)/shard_map/ppermute | solution.py:26
  11.6 16.3 %collective-permute-start.5 = (bf16[256,512]{1,0:T(8,128)(2,1)}, bf16[256,512]{1,0:T(8,128)(2,1)S(1)}, u32[]{:S(2)}, u32[]{:S(2)}) collective-permute-start(bf16[256,512]{1,0:T(8,128)(2,1)} %param.7), channel_id=1, source_target_pairs={{0,96},{16,112},{32,64},{48,80},{64,32},{80,48},{96,0},{112,16},{1... | collective-permute-start | bytes 786440 | tf_op jit(solution)/shard_map/ppermute | solution.py:26
  43.0 16.8 %shard_map.102 = bf16[8,256,512]{2,1,0:T(8,128)(2,1)} custom-call(s32[16]{0:T(128)} %pad_add_fusion.source_ref, s32[256]{0:T(256)} %get-tuple-element.44.slot_ref, s32[32]{0:T(128)} %bitcast.108, s32[8]{0:T(128)} %stack.150.place_ref, bf16[16,256,512]{2,1,0:T(8,128)(2,1)} %constant_dynamic-update-slice_fusion.x_ref, bf16[32,8,128,128]{3,2,1,0:T(8,128)(2,1)} %bitcast.105), custom_call_target="tpu_custom_call" | custom-call | tf_op jit(solution)/shard_map/pallas_call | solution.py:77
  62.1 7.8 %collective-permute-start.10 = (bf16[256,512]{1,0:T(8,128)(2,1)S(1)}, bf16[256,512]{1,0:T(8,128)(2,1)S(1)}, u32[]{:S(2)}, u32[]{:S(2)}) collective-permute-start(bf16[256,512]{1,0:T(8,128)(2,1)S(1)} %get-tuple-element.23), channel_id=1, source_target_pairs={{0,3},{1,0},{2,1},{3,2},{4,7},{5,4},{6,5},{7,6},{8,11},{9,8},{10,9... | collective-permute-start | bytes 786440 | tf_op jit(solution)/shard_map/ppermute | solution.py:26
  69.9 2.5 collective-permute-start.12
  74.5 5.0 %collective-permute-start.14 = (bf16[256,512]{1,0:T(8,128)(2,1)S(1)}, bf16[256,512]{1,0:T(8,128)(2,1)S(1)}, u32[]{:S(2)}, u32[]{:S(2)}) collective-permute-start(bf16[256,512]{1,0:T(8,128)(2,1)S(1)} %get-tuple-element.19), channel_id=1, source_target_pairs={{0,7},{1,4},{2,5},{3,6},{4,3},{5,0},{6,1},{7,2},{8,15},{9,12},{10,... | collective-permute-start | bytes 786440 | tf_op jit(solution)/shard_map/ppermute | solution.py:26
  81.6 4.7 %collective-permute-done.12.refs_5_ = bf16[256,512]{1,0:T(8,128)(2,1)S(1)} collective-permute-done((bf16[256,512]{1,0:T(8,128)(2,1)S(1)}, bf16[256,512]{1,0:T(8,128)(2,1)S(1)}, u32[]{:S(2)}, u32[]{:S(2)}) %collective-permute-start.12) | collective-permute-done | bytes 262176 | tf_op jit(solution)/shard_map/ppermute | solution.py:26
  86.3 5.9 %collective-permute-done.13.refs_6_ = bf16[256,512]{1,0:T(8,128)(2,1)S(1)} collective-permute-done((bf16[256,512]{1,0:T(8,128)(2,1)S(1)}, bf16[256,512]{1,0:T(8,128)(2,1)S(1)}, u32[]{:S(2)}, u32[]{:S(2)}) %collective-permute-start.13) | collective-permute-done | bytes 262176 | tf_op jit(solution)/shard_map/ppermute | solution.py:26
  92.2 3.1 %collective-permute-done.14.refs_7_ = bf16[256,512]{1,0:T(8,128)(2,1)S(1)} collective-permute-done((bf16[256,512]{1,0:T(8,128)(2,1)S(1)}, bf16[256,512]{1,0:T(8,128)(2,1)S(1)}, u32[]{:S(2)}, u32[]{:S(2)}) %collective-permute-start.14) | collective-permute-done | bytes 262176 | tf_op jit(solution)/shard_map/ppermute | solution.py:26
  95.3 6.7 %collective-permute-done.8.refs_1_ = bf16[256,512]{1,0:T(8,128)(2,1)S(1)} collective-permute-done((bf16[256,512]{1,0:T(8,128)(2,1)S(1)}, bf16[256,512]{1,0:T(8,128)(2,1)S(1)}, u32[]{:S(2)}, u32[]{:S(2)}) %collective-permute-start.8) | collective-permute-done | bytes 262176 | tf_op jit(solution)/shard_map/ppermute | solution.py:26
  102.8 3.6 %shard_map.103 = (bf16[256,512]{1,0:T(8,128)(2,1)}, bf16[256,512]{1,0:T(8,128)(2,1)}, f32[512,512]{1,0:T(8,128)}, f32[1,512]{1,0:T(1,128)}) custom-call(bf16[256,512]{1,0:T(8,128)(2,1)} %get-tuple-element.26.refs_0_, bf16[256,512]{1,0:T(8,128)(2,1)} %copy-done.11, bf16[256,512]{1,0:T(8,128)(2,1)} %copy-done.12, bf16[256,512]{1,0:T(8,128)(2,1)} %copy-done.6, ...), custom_call_target="tpu_custom_call" | custom-call | tf_op jit(solution)/shard_map/pallas_call | solution.py:174
  111.4 2.8 %collective-permute-start.18 = (bf16[256,512]{1,0:T(8,128)(2,1)}, bf16[256,512]{1,0:T(8,128)(2,1)S(1)}, u32[]{:S(2)}, u32[]{:S(2)}) collective-permute-start(bf16[256,512]{1,0:T(8,128)(2,1)} %get-tuple-element.9), channel_id=1, source_target_pairs={{0,4},{1,5},{2,6},{3,7},{4,0},{5,1},{6,2},{7,3},{8,12},{9,13},{10,... | collective-permute-start | bytes 786440 | tf_op jit(solution)/shard_map/ppermute | solution.py:26
  115.2 11.5 %collective-permute-done.15 = bf16[256,512]{1,0:T(8,128)(2,1)S(1)} collective-permute-done((bf16[256,512]{1,0:T(8,128)(2,1)}, bf16[256,512]{1,0:T(8,128)(2,1)S(1)}, u32[]{:S(2)}, u32[]{:S(2)}) %collective-permute-start.15) | collective-permute-done | bytes 262176 | tf_op jit(solution)/shard_map/ppermute | solution.py:26
  127.9 9.4 %collective-permute-done.20 = bf16[256,512]{1,0:T(8,128)(2,1)S(1)} collective-permute-done((bf16[256,512]{1,0:T(8,128)(2,1)}, bf16[256,512]{1,0:T(8,128)(2,1)S(1)}, u32[]{:S(2)}, u32[]{:S(2)}) %collective-permute-start.20) | collective-permute-done | bytes 262176 | tf_op jit(solution)/shard_map/ppermute | solution.py:26
  139.4 16.5 %shard_map.104 = bf16[16,256,512]{2,1,0:T(8,128)(2,1)} custom-call(s32[16]{0:T(128)} %pad_add_fusion.1.source_ref, s32[256]{0:T(256)} %get-tuple-element.43.slot_ref, s32[32]{0:T(128)} %bitcast.109, bf16[16,128,512]{2,1,0:T(8,128)(2,1)} %bitcast.107, bf16[32,8,128,128]{3,2,1,0:T(8,128)(2,1)} %bitcast.106), custom_call_target="tpu_custom_call" | custom-call | tf_op jit(solution)/shard_map/pallas_call | solution.py:132
  155.9 3.2 %slice.91 = bf16[8,256,512]{2,1,0:T(8,128)(2,1)} slice(bf16[16,256,512]{2,1,0:T(8,128)(2,1)} %shard_map.104), slice={[0:8], [0:256], [0:512]} | slice | bytes 4194304 | tf_op jit(solution)/shard_map/slice | solution.py:223
  160.9 46.8 %all_to_all.10 = f32[128,5,512]{2,1,0:T(8,128)S(1)} all-to-all(f32[128,5,512]{2,1,0:T(8,128)} %reshape.36), channel_id=1, replica_groups=mesh['xl'=2,'z'=4,'core'=2,'xh'=2,'y'=4] {'xl','z','core','xh','y'}, dimensions={0} | all-to-all | bytes 2621440 | tf_op jit(solution)/shard_map/all_to_all | solution.py:233
  209.5 6.7 %all-to-all-start.1 = ((f32[128,5,512]{2,1,0:T(8,128)}), f32[128,5,512]{2,1,0:T(8,128)}, u32[]{:S(2)}, u32[]{:S(2)}) async-start(f32[128,5,512]{2,1,0:T(8,128)} %broadcast_in_dim.16), calls=%async_computation.1 | async-start | bytes 4194304 | tf_op jit(solution)/shard_map/all_to_all | solution.py:235
  216.2 2.9 %add_convert_fusion = bf16[8,256,512]{2,1,0:T(8,128)(2,1)S(1)} fusion(bf16[8,256,512]{2,1,0:T(8,128)(2,1)} %collective-permute-done.22, bf16[16,256,512]{2,1,0:T(8,128)(2,1)} %shard_map.104), kind=kLoop, calls=%fused_computation | loop fusion | flops 4194304 | bytes 6291456 | tf_op jit(solution)/shard_map/convert_element_type | solution.py:224
  221.2 3.2 %collective-permute-start.24 = (bf16[256,512]{1,0:T(8,128)(2,1)S(1)}, bf16[256,512]{1,0:T(8,128)(2,1)S(1)}, u32[]{:S(2)}, u32[]{:S(2)}) collective-permute-start(bf16[256,512]{1,0:T(8,128)(2,1)S(1)} %get-tuple-element.18), channel_id=1, source_target_pairs={{0,32},{16,48},{32,0},{48,16},{64,96},{80,112},{96,64},{112,80},{1... | collective-permute-start | bytes 786440 | tf_op jit(solution)/shard_map/ppermute | solution.py:26
  227.9 22.2 %collective-permute-done.23 = bf16[256,512]{1,0:T(8,128)(2,1)S(1)} collective-permute-done((bf16[256,512]{1,0:T(8,128)(2,1)S(1)}, bf16[256,512]{1,0:T(8,128)(2,1)S(1)}, u32[]{:S(2)}, u32[]{:S(2)}) %collective-permute-start.23) | collective-permute-done | bytes 262176 | tf_op jit(solution)/shard_map/ppermute | solution.py:26
  250.1 4.4 %collective-permute-start.28 = (bf16[256,512]{1,0:T(8,128)(2,1)}, bf16[256,512]{1,0:T(8,128)(2,1)}, u32[]{:S(2)}, u32[]{:S(2)}) collective-permute-start(bf16[256,512]{1,0:T(8,128)(2,1)} %get-tuple-element.14), channel_id=1, source_target_pairs={{0,96},{16,112},{32,64},{48,80},{64,32},{80,48},{96,0},{112,16},{1... | collective-permute-start | bytes 786440 | tf_op jit(solution)/shard_map/ppermute | solution.py:26
  254.5 9.3 %collective-permute-done.24 = bf16[256,512]{1,0:T(8,128)(2,1)S(1)} collective-permute-done((bf16[256,512]{1,0:T(8,128)(2,1)S(1)}, bf16[256,512]{1,0:T(8,128)(2,1)S(1)}, u32[]{:S(2)}, u32[]{:S(2)}) %collective-permute-start.24) | collective-permute-done | bytes 262176 | tf_op jit(solution)/shard_map/ppermute | solution.py:26
  264.5 3.2 %broadcast_multiply_fusion = f32[128,5,512]{2,1,0:T(8,128)} fusion(f32[128,5,512]{2,1,0:T(8,128)} %all-to-all-done.1), kind=kLoop, calls=%fused_computation.3 | loop fusion | flops 327680 | bytes 2621440 | tf_op jit(solution)/shard_map/mul | solution.py:239
  (115 shorter events, 56.6 us)
Async XLA Ops:
  2.7 26.0 %collective-permute-start.1 = (bf16[256,512]{1,0:T(8,128)(2,1)}, bf16[256,512]{1,0:T(8,128)(2,1)S(1)}, u32[]{:S(2)}, u32[]{:S(2)}) collective-permute-start(bf16[256,512]{1,0:T(8,128)(2,1)} %param.7), channel_id=1, source_target_pairs={{0,32},{16,48},{32,0},{48,16},{64,96},{80,112},{96,64},{112,80},{1... | collective-permute-start | bytes 786440 | tf_op jit(solution)/shard_map/ppermute | solution.py:26
  6.3 23.5 %collective-permute-start.2 = (bf16[256,512]{1,0:T(8,128)(2,1)}, bf16[256,512]{1,0:T(8,128)(2,1)S(1)}, u32[]{:S(2)}, u32[]{:S(2)}) collective-permute-start(bf16[256,512]{1,0:T(8,128)(2,1)} %param.7), channel_id=1, source_target_pairs={{0,48},{16,0},{32,16},{48,32},{64,112},{80,64},{96,80},{112,96},{1... | collective-permute-start | bytes 786440 | tf_op jit(solution)/shard_map/ppermute | solution.py:26
  7.3 23.3 %collective-permute-start.3 = (bf16[256,512]{1,0:T(8,128)(2,1)}, bf16[256,512]{1,0:T(8,128)(2,1)S(1)}, u32[]{:S(2)}, u32[]{:S(2)}) collective-permute-start(bf16[256,512]{1,0:T(8,128)(2,1)} %param.7), channel_id=1, source_target_pairs={{0,64},{16,80},{32,96},{48,112},{64,0},{80,16},{96,32},{112,48},{1... | collective-permute-start | bytes 786440 | tf_op jit(solution)/shard_map/ppermute | solution.py:26
  8.8 22.7 %collective-permute-start.4 = (bf16[256,512]{1,0:T(8,128)(2,1)}, bf16[256,512]{1,0:T(8,128)(2,1)S(1)}, u32[]{:S(2)}, u32[]{:S(2)}) collective-permute-start(bf16[256,512]{1,0:T(8,128)(2,1)} %param.7), channel_id=1, source_target_pairs={{0,80},{16,96},{32,112},{48,64},{64,16},{80,32},{96,48},{112,0},{1... | collective-permute-start | bytes 786440 | tf_op jit(solution)/shard_map/ppermute | solution.py:26
  11.6 21.6 %collective-permute-start.5 = (bf16[256,512]{1,0:T(8,128)(2,1)}, bf16[256,512]{1,0:T(8,128)(2,1)S(1)}, u32[]{:S(2)}, u32[]{:S(2)}) collective-permute-start(bf16[256,512]{1,0:T(8,128)(2,1)} %param.7), channel_id=1, source_target_pairs={{0,96},{16,112},{32,64},{48,80},{64,32},{80,48},{96,0},{112,16},{1... | collective-permute-start | bytes 786440 | tf_op jit(solution)/shard_map/ppermute | solution.py:26
  62.1 17.4 %collective-permute-start.10 = (bf16[256,512]{1,0:T(8,128)(2,1)S(1)}, bf16[256,512]{1,0:T(8,128)(2,1)S(1)}, u32[]{:S(2)}, u32[]{:S(2)}) collective-permute-start(bf16[256,512]{1,0:T(8,128)(2,1)S(1)} %get-tuple-element.23), channel_id=1, source_target_pairs={{0,3},{1,0},{2,1},{3,2},{4,7},{5,4},{6,5},{7,6},{8,11},{9,8},{10,9... | collective-permute-start | bytes 786440 | tf_op jit(solution)/shard_map/ppermute | solution.py:26
  69.9 16.4 %collective-permute-start.12 = (bf16[256,512]{1,0:T(8,128)(2,1)S(1)}, bf16[256,512]{1,0:T(8,128)(2,1)S(1)}, u32[]{:S(2)}, u32[]{:S(2)}) collective-permute-start(bf16[256,512]{1,0:T(8,128)(2,1)S(1)} %get-tuple-element.21), channel_id=1, source_target_pairs={{0,5},{1,6},{2,7},{3,4},{4,1},{5,2},{6,3},{7,0},{8,13},{9,14},{10,... | collective-permute-start | bytes 786440 | tf_op jit(solution)/shard_map/ppermute | solution.py:26
  72.4 19.8 %collective-permute-start.13 = (bf16[256,512]{1,0:T(8,128)(2,1)S(1)}, bf16[256,512]{1,0:T(8,128)(2,1)S(1)}, u32[]{:S(2)}, u32[]{:S(2)}) collective-permute-start(bf16[256,512]{1,0:T(8,128)(2,1)S(1)} %get-tuple-element.20), channel_id=1, source_target_pairs={{0,6},{1,7},{2,4},{3,5},{4,2},{5,3},{6,0},{7,1},{8,14},{9,15},{10,... | collective-permute-start | bytes 786440 | tf_op jit(solution)/shard_map/ppermute | solution.py:26
  74.5 20.8 %collective-permute-start.14 = (bf16[256,512]{1,0:T(8,128)(2,1)S(1)}, bf16[256,512]{1,0:T(8,128)(2,1)S(1)}, u32[]{:S(2)}, u32[]{:S(2)}) collective-permute-start(bf16[256,512]{1,0:T(8,128)(2,1)S(1)} %get-tuple-element.19), channel_id=1, source_target_pairs={{0,7},{1,4},{2,5},{3,6},{4,3},{5,0},{6,1},{7,2},{8,15},{9,12},{10,... | collective-permute-start | bytes 786440 | tf_op jit(solution)/shard_map/ppermute | solution.py:26
  79.5 22.5 %collective-permute-start.8 = (bf16[256,512]{1,0:T(8,128)(2,1)S(1)}, bf16[256,512]{1,0:T(8,128)(2,1)S(1)}, u32[]{:S(2)}, u32[]{:S(2)}) collective-permute-start(bf16[256,512]{1,0:T(8,128)(2,1)S(1)} %get-tuple-element.25), channel_id=1, source_target_pairs={{0,1},{1,2},{2,3},{3,0},{4,5},{5,6},{6,7},{7,4},{8,9},{9,10},{10,1... | collective-permute-start | bytes 786440 | tf_op jit(solution)/shard_map/ppermute | solution.py:26
  80.1 21.9 %collective-permute-start.9 = (bf16[256,512]{1,0:T(8,128)(2,1)S(1)}, bf16[256,512]{1,0:T(8,128)(2,1)S(1)}, u32[]{:S(2)}, u32[]{:S(2)}) collective-permute-start(bf16[256,512]{1,0:T(8,128)(2,1)S(1)} %get-tuple-element.24), channel_id=1, source_target_pairs={{0,2},{1,3},{2,0},{3,1},{4,6},{5,7},{6,4},{7,5},{8,10},{9,11},{10,... | collective-permute-start | bytes 786440 | tf_op jit(solution)/shard_map/ppermute | solution.py:26
  106.4 20.3 %collective-permute-start.15 = (bf16[256,512]{1,0:T(8,128)(2,1)}, bf16[256,512]{1,0:T(8,128)(2,1)S(1)}, u32[]{:S(2)}, u32[]{:S(2)}) collective-permute-start(bf16[256,512]{1,0:T(8,128)(2,1)} %get-tuple-element.9), channel_id=1, source_target_pairs={{0,1},{1,2},{2,3},{3,0},{4,5},{5,6},{6,7},{7,4},{8,9},{9,10},{10,1... | collective-permute-start | bytes 786440 | tf_op jit(solution)/shard_map/ppermute | solution.py:26
  107.0 19.7 %collective-permute-start.16 = (bf16[256,512]{1,0:T(8,128)(2,1)}, bf16[256,512]{1,0:T(8,128)(2,1)S(1)}, u32[]{:S(2)}, u32[]{:S(2)}) collective-permute-start(bf16[256,512]{1,0:T(8,128)(2,1)} %get-tuple-element.9), channel_id=1, source_target_pairs={{0,2},{1,3},{2,0},{3,1},{4,6},{5,7},{6,4},{7,5},{8,10},{9,11},{10,... | collective-permute-start | bytes 786440 | tf_op jit(solution)/shard_map/ppermute | solution.py:26
  109.0 18.4 %collective-permute-start.17 = (bf16[256,512]{1,0:T(8,128)(2,1)}, bf16[256,512]{1,0:T(8,128)(2,1)S(1)}, u32[]{:S(2)}, u32[]{:S(2)}) collective-permute-start(bf16[256,512]{1,0:T(8,128)(2,1)} %get-tuple-element.9), channel_id=1, source_target_pairs={{0,3},{1,0},{2,1},{3,2},{4,7},{5,4},{6,5},{7,6},{8,11},{9,8},{10,9... | collective-permute-start | bytes 786440 | tf_op jit(solution)/shard_map/ppermute | solution.py:26
  111.4 16.1 %collective-permute-start.18 = (bf16[256,512]{1,0:T(8,128)(2,1)}, bf16[256,512]{1,0:T(8,128)(2,1)S(1)}, u32[]{:S(2)}, u32[]{:S(2)}) collective-permute-start(bf16[256,512]{1,0:T(8,128)(2,1)} %get-tuple-element.9), channel_id=1, source_target_pairs={{0,4},{1,5},{2,6},{3,7},{4,0},{5,1},{6,2},{7,3},{8,12},{9,13},{10,... | collective-permute-start | bytes 786440 | tf_op jit(solution)/shard_map/ppermute | solution.py:26
  114.2 13.7 %collective-permute-start.19 = (bf16[256,512]{1,0:T(8,128)(2,1)}, bf16[256,512]{1,0:T(8,128)(2,1)S(1)}, u32[]{:S(2)}, u32[]{:S(2)}) collective-permute-start(bf16[256,512]{1,0:T(8,128)(2,1)} %get-tuple-element.9), channel_id=1, source_target_pairs={{0,5},{1,6},{2,7},{3,4},{4,1},{5,2},{6,3},{7,0},{8,13},{9,14},{10,... | collective-permute-start | bytes 786440 | tf_op jit(solution)/shard_map/ppermute | solution.py:26
  159.2 57.1 %collective-permute-start.22 = (bf16[8,256,512]{2,1,0:T(8,128)(2,1)}, bf16[8,256,512]{2,1,0:T(8,128)(2,1)}, u32[]{:S(2)}, u32[]{:S(2)}) collective-permute-start(bf16[8,256,512]{2,1,0:T(8,128)(2,1)} %slice.91), channel_id=1, source_target_pairs={{0,8},{8,0},{1,9},{9,1},{2,10},{10,2},{3,11},{11,3},{4,12},{12,4},... | collective-permute-start | bytes 6291464 | tf_op jit(solution)/shard_map/ppermute | solution.py:26
  209.5 55.0 %all-to-all-start.1 = ((f32[128,5,512]{2,1,0:T(8,128)}), f32[128,5,512]{2,1,0:T(8,128)}, u32[]{:S(2)}, u32[]{:S(2)}) async-start(f32[128,5,512]{2,1,0:T(8,128)} %broadcast_in_dim.16), calls=%async_computation.1 | async-start | bytes 4194304 | tf_op jit(solution)/shard_map/all_to_all | solution.py:235
  220.2 29.9 %collective-permute-start.23 = (bf16[256,512]{1,0:T(8,128)(2,1)S(1)}, bf16[256,512]{1,0:T(8,128)(2,1)S(1)}, u32[]{:S(2)}, u32[]{:S(2)}) collective-permute-start(bf16[256,512]{1,0:T(8,128)(2,1)S(1)} %get-tuple-element.12), channel_id=1, source_target_pairs={{0,16},{16,32},{32,48},{48,0},{64,80},{80,96},{96,112},{112,64},{1... | collective-permute-start | bytes 786440 | tf_op jit(solution)/shard_map/ppermute | solution.py:26
  221.2 42.6 %collective-permute-start.24 = (bf16[256,512]{1,0:T(8,128)(2,1)S(1)}, bf16[256,512]{1,0:T(8,128)(2,1)S(1)}, u32[]{:S(2)}, u32[]{:S(2)}) collective-permute-start(bf16[256,512]{1,0:T(8,128)(2,1)S(1)} %get-tuple-element.18), channel_id=1, source_target_pairs={{0,32},{16,48},{32,0},{48,16},{64,96},{80,112},{96,64},{112,80},{1... | collective-permute-start | bytes 786440 | tf_op jit(solution)/shard_map/ppermute | solution.py:26
  224.4 46.6 %collective-permute-start.25 = (bf16[256,512]{1,0:T(8,128)(2,1)}, bf16[256,512]{1,0:T(8,128)(2,1)}, u32[]{:S(2)}, u32[]{:S(2)}) collective-permute-start(bf16[256,512]{1,0:T(8,128)(2,1)} %get-tuple-element.17), channel_id=1, source_target_pairs={{0,48},{16,0},{32,16},{48,32},{64,112},{80,64},{96,80},{112,96},{1... | collective-permute-start | bytes 786440 | tf_op jit(solution)/shard_map/ppermute | solution.py:26
  225.6 45.4 %collective-permute-start.26 = (bf16[256,512]{1,0:T(8,128)(2,1)}, bf16[256,512]{1,0:T(8,128)(2,1)}, u32[]{:S(2)}, u32[]{:S(2)}) collective-permute-start(bf16[256,512]{1,0:T(8,128)(2,1)} %get-tuple-element.16), channel_id=1, source_target_pairs={{0,64},{16,80},{32,96},{48,112},{64,0},{80,16},{96,32},{112,48},{1... | collective-permute-start | bytes 786440 | tf_op jit(solution)/shard_map/ppermute | solution.py:26
  227.1 43.9 %collective-permute-start.27 = (bf16[256,512]{1,0:T(8,128)(2,1)}, bf16[256,512]{1,0:T(8,128)(2,1)}, u32[]{:S(2)}, u32[]{:S(2)}) collective-permute-start(bf16[256,512]{1,0:T(8,128)(2,1)} %get-tuple-element.15), channel_id=1, source_target_pairs={{0,80},{16,96},{32,112},{48,64},{64,16},{80,32},{96,48},{112,0},{1... | collective-permute-start | bytes 786440 | tf_op jit(solution)/shard_map/ppermute | solution.py:26
  250.1 20.9 %collective-permute-start.28 = (bf16[256,512]{1,0:T(8,128)(2,1)}, bf16[256,512]{1,0:T(8,128)(2,1)}, u32[]{:S(2)}, u32[]{:S(2)}) collective-permute-start(bf16[256,512]{1,0:T(8,128)(2,1)} %get-tuple-element.14), channel_id=1, source_target_pairs={{0,96},{16,112},{32,64},{48,80},{64,32},{80,48},{96,0},{112,16},{1... | collective-permute-start | bytes 786440 | tf_op jit(solution)/shard_map/ppermute | solution.py:26
  (23 other events, 187.0 us)

commit v2 on v0

v2 whole, which is shorter than its diff:
```python
import itertools
import math

import jax
import jax.numpy as jnp
import numpy as np
from jax import lax
from jax.experimental import pallas as pl
from jax.experimental.pallas import tpu as pltpu
from jax.sharding import Mesh, PartitionSpec as P

SIZES = {"xl": 2, "z": 4, "core": 2, "xh": 2, "y": 4}
BLK = ("xl", "z", "core")
REP = ("xh", "y")
CHIP = ("xl", "z")
ALL = BLK + REP
VMEM = 60 << 20


def send_by(value, axes, offsets):
    sizes = [SIZES[a] for a in axes]
    pairs = []
    for at in itertools.product(*[range(n) for n in sizes]):
        to = [(i + o) % n for i, o, n in zip(at, offsets, sizes)]
        pairs.append((int(np.ravel_multi_index(at, sizes)), int(np.ravel_multi_index(to, sizes))))
    return lax.ppermute(value, axes, pairs)


def all_offsets(axes):
    return list(itertools.product(*[range(SIZES[a]) for a in axes]))


EXTRA = 16
VARIANTS = (1, 2, 3, 4, 6, 8)


def cost(flops, transferred):
    return pl.CostEstimate(flops=flops, transcendentals=0, bytes_accessed=transferred)


def start_all(pairs, sems):
    for i, (source, target) in enumerate(pairs):
        pltpu.make_async_copy(source, target, sems.at[i]).start()


def forward_kernel(shards, earlier, *refs):
    source_ref, slot_ref, count_ref, place_ref, v_ref = refs[:5]
    x_refs = refs[5 : 5 + shards]
    refs = refs[5 + shards :]
    if earlier:
        before_ref, out_refs, refs = refs[0], refs[1:9], refs[9:]
        acc_ref, x_buf, v_buf, x_sem, v_sem, before_buf, before_sem = refs
        pltpu.make_async_copy(before_ref, before_buf, before_sem).start()
    else:
        out_ref, acc_ref, x_buf, v_buf, x_sem, v_sem = refs
    slots, tile = v_ref.shape[1:3]
    for i in range(shards):
        pltpu.make_async_copy(v_ref.at[pl.ds(source_ref[i] * 2, 2)], v_buf.at[i], v_sem.at[i]).start()
        pltpu.make_async_copy(x_refs[i], x_buf.at[i], x_sem.at[i]).start()
    acc_ref[...] = jnp.zeros_like(acc_ref)

    def group_step(i, t):
        group = source_ref[i] * 2 + t
        count = count_ref[group]
        low = 0
        for n in VARIANTS:

            @pl.when((count > low) & (count <= n))
            def _():
                rows = x_buf[i, pl.ds(pl.multiple_of(t * tile, tile), tile), :]
                tiles = v_buf[i, t, pl.ds(0, n)].reshape(n * tile, tile)
                product = jnp.dot(tiles, rows, preferred_element_type=jnp.float32)
                for k in range(n):
                    acc_ref[slot_ref[group * slots + k]] += product[k * tile : (k + 1) * tile]

            low = n

    def shard_step(i, carry):
        pltpu.make_async_copy(v_ref.at[pl.ds(0, 2)], v_buf.at[i], v_sem.at[i]).wait()
        pltpu.make_async_copy(x_refs[0], x_buf.at[i], x_sem.at[i]).wait()

        def inner(t, carry):
            group_step(i, t)
            return carry

        return lax.fori_loop(0, 2, inner, carry)

    lax.fori_loop(0, shards, shard_step, 0)
    if earlier:
        pltpu.make_async_copy(before_ref, before_buf, before_sem).wait()
        for i, out_ref in enumerate(out_refs):
            for t in range(2):
                at = place_ref[i] * 2 + t
                out_ref[pl.ds(t * tile, tile), :] = (acc_ref[at] + before_buf[at]).astype(out_ref.dtype)
    else:
        out_ref[...] = acc_ref[pl.ds(0, out_ref.shape[0])]


def aggregate(sources, slots, counts, places, gathered, values, before=None):
    shards = len(gathered)
    rows, width = gathered[0].shape
    _, slot_total, tile, _ = values.shape
    parts = places.shape[0]
    anywhere = pl.BlockSpec(memory_space=pl.ANY)
    scratch = [
        pltpu.VMEM((parts * 2 + 1, tile, width), jnp.float32),
        pltpu.VMEM((shards, rows, width), jnp.bfloat16),
        pltpu.VMEM((shards, 2, slot_total, tile, tile), jnp.bfloat16),
        pltpu.SemaphoreType.DMA((shards,)),
        pltpu.SemaphoreType.DMA((shards,)),
    ]
    whole = jax.ShapeDtypeStruct((parts * 2, tile, width), jnp.float32)
    if before is None:
        out_shape, extra = whole, []
    else:
        out_shape = (jax.ShapeDtypeStruct((rows, width), jnp.bfloat16),) * parts
        extra = [before]
        scratch += [pltpu.VMEM(whole.shape, whole.dtype), pltpu.SemaphoreType.DMA(())]
    inside = pl.BlockSpec(memory_space=pltpu.VMEM)
    return pl.pallas_call(
        lambda *refs: forward_kernel(shards, before is not None, *refs),
        out_shape=out_shape,
        grid_spec=pltpu.PrefetchScalarGridSpec(
            num_scalar_prefetch=4,
            grid=(),
            in_specs=[anywhere] * (1 + shards + len(extra)),
            out_specs=inside if before is None else (inside,) * parts,
            scratch_shapes=scratch,
        ),
        compiler_params=pltpu.CompilerParams(vmem_limit_bytes=VMEM),
        cost_estimate=cost(4 << 30, 12 << 20),
        name="aggregate",
    )(sources, slots, counts, places, values, *gathered, *extra)


def backward_kernel(shards, parts, crossing, with_weight, *refs):
    source_ref, slot_ref, count_ref, v_ref = refs[:4]
    m_refs, refs = refs[4 : 4 + parts], refs[4 + parts :]
    if crossing:
        crossed_ref, mine_ref, other_ref = refs[:3]
        out_refs, refs = refs[3 : 3 + shards], refs[3 + shards :]
    else:
        out_ref, refs = refs[0], refs[1:]
        if with_weight:
            sum_ref, refs = refs[0], refs[1:]
    table_ref, v_buf, m_sem, v_sem = refs[:4]
    refs = refs[4:]
    slots, tile = v_ref.shape[1:3]
    rows = 2 * tile
    for i in range(parts):
        pltpu.make_async_copy(m_refs[i].at[pl.ds(0, rows)], table_ref.at[pl.ds(i * rows, rows)], m_sem.at[i]).start()
    for i in range(shards):
        pltpu.make_async_copy(v_ref.at[pl.ds(source_ref[i] * 2, 2)], v_buf.at[i], v_sem.at[i]).start()
    if crossing:
        term_ref, cross_buf, cross_sem = refs
        pltpu.make_async_copy(crossed_ref, cross_buf, cross_sem).start()
    elif with_weight:
        w_buf, w_sem = refs
        more = w_buf.shape[1]
        for i in range(parts):
            pltpu.make_async_copy(m_refs[i].at[pl.ds(rows, more)], w_buf.at[i], w_sem.at[i]).start()
    blank = table_ref.at[pl.ds(parts * rows, tile)]
    blank[...] = jnp.zeros_like(blank)
    for i in range(parts):
        pltpu.make_async_copy(m_refs[i].at[pl.ds(0, rows)], table_ref.at[pl.ds(i * rows, rows)], m_sem.at[i]).wait()
    if crossing:
        pltpu.make_async_copy(crossed_ref, cross_buf, cross_sem).wait()

    def group_step(i, t):
        group = source_ref[i] * 2 + t
        count = count_ref[group]
        for n in range(2, slots + 1, 2):

            @pl.when((count > n - 2) & (count <= n))
            def _():
                tiles = v_buf[i, t, pl.ds(0, n)].reshape(n * tile, tile)
                found = jnp.concatenate(
                    [
                        table_ref[pl.ds(pl.multiple_of(slot_ref[group * slots + k] * tile, tile), tile), :]
                        for k in range(n)
                    ],
                    axis=0,
                )
                product = lax.dot_general(tiles, found, (((0,), (0,)), ((), ())), preferred_element_type=jnp.float32)
                at = pl.ds(pl.multiple_of(t * tile, tile), tile)
                if crossing:
                    term_ref[i, at, :] = (product + cross_buf[i, at, :].astype(jnp.float32)).astype(jnp.bfloat16)
                else:
                    out_ref[i, at, :] = product.astype(jnp.bfloat16)

    def shard_step(i, carry):
        pltpu.make_async_copy(v_ref.at[pl.ds(0, 2)], v_buf.at[i], v_sem.at[i]).wait()

        def inner(t, carry):
            group_step(i, t)
            return carry

        return lax.fori_loop(0, 2, inner, carry)

    lax.fori_loop(0, shards, shard_step, 0)
    if crossing:
        both = mine_ref[...] + other_ref[...]
        share = both.shape[0] - EXTRA
        tail = split_rows(both[share : share + 1])
        for i in range(shards):
            out_refs[i][pl.ds(0, rows), :] = term_ref[i]
            out_refs[i][pl.ds(rows, share), :] = both[:share].astype(jnp.bfloat16)
            out_refs[i][pl.ds(rows + share, EXTRA), :] = tail
    elif with_weight:
        total = None
        for i in range(parts):
            pltpu.make_async_copy(m_refs[i].at[pl.ds(rows, more)], w_buf.at[i], w_sem.at[i]).wait()
            term = w_buf[i].astype(jnp.float32)
            total = term if total is None else total + term
        share = more - EXTRA
        sum_ref[pl.ds(0, share), :] = total[:share]
        bias = total[share : share + 1] + total[share + 1 : share + 2]
        sum_ref[pl.ds(share, EXTRA), :] = jnp.broadcast_to(bias, (EXTRA, bias.shape[1]))


def split_rows(row):
    high = row.astype(jnp.bfloat16)
    low = (row - high.astype(jnp.float32)).astype(jnp.bfloat16)
    line = lax.broadcasted_iota(jnp.int32, (EXTRA, row.shape[1]), 0)
    spread_high = jnp.broadcast_to(high.astype(jnp.float32), line.shape)
    spread_low = jnp.broadcast_to(low.astype(jnp.float32), line.shape)
    return jnp.where(line == 0, spread_high, jnp.where(line == 1, spread_low, 0.0)).astype(jnp.bfloat16)


def spread(sources, slots, counts, messages, values, crossed=None, sums=None, with_weight=False):
    parts = len(messages)
    shards = sources.shape[0]
    height, width = messages[0].shape
    slot_total, tile = values.shape[1:3]
    rows = 2 * tile
    anywhere = pl.BlockSpec(memory_space=pl.ANY)
    inside = pl.BlockSpec(memory_space=pltpu.VMEM)
    scratch = [
        pltpu.VMEM((parts * rows + tile, width), jnp.bfloat16),
        pltpu.VMEM((shards, 2, slot_total, tile, tile), jnp.bfloat16),
        pltpu.SemaphoreType.DMA((parts,)),
        pltpu.SemaphoreType.DMA((shards,)),
    ]
    crossing = crossed is not None
    in_specs = [anywhere] * (1 + parts)
    operands = []
    if crossing:
        operands = [crossed, *sums]
        in_specs += [anywhere, inside, inside]
        out_shape = (jax.ShapeDtypeStruct((height, width), jnp.bfloat16),) * shards
        out_specs = (inside,) * shards
        scratch += [
            pltpu.VMEM((shards, rows, width), jnp.bfloat16),
            pltpu.VMEM((shards, rows, width), jnp.bfloat16),
            pltpu.SemaphoreType.DMA(()),
        ]
    else:
        out_shape = (jax.ShapeDtypeStruct((shards, rows, width), jnp.bfloat16),)
        if with_weight:
            more = height - rows
            out_shape += (jax.ShapeDtypeStruct((more, width), jnp.float32),)
            scratch += [pltpu.VMEM((parts, more, width), jnp.bfloat16), pltpu.SemaphoreType.DMA((parts,))]
        out_specs = (inside,) * len(out_shape)
    return pl.pallas_call(
        lambda *refs: backward_kernel(shards, parts, crossing, with_weight, *refs),
        out_shape=out_shape,
        grid_spec=pltpu.PrefetchScalarGridSpec(
            num_scalar_prefetch=3, grid=(), in_specs=in_specs, out_specs=out_specs, scratch_shapes=scratch
        ),
        compiler_params=pltpu.CompilerParams(vmem_limit_bytes=VMEM),
        cost_estimate=cost(2 << 30, 8 << 20),
        name="spread",
    )(sources, slots, counts, values, *messages, *operands)


def middle_kernel(place_ref, *refs):
    parts = place_ref.shape[0]
    part_refs, refs = refs[:parts], refs[parts:]
    weight_ref, bias_ref, cotangent_ref, out_ref = refs[:4]
    message_refs, part_ref = refs[4 : 4 + parts], refs[4 + parts]
    f32 = jnp.float32
    total = part_refs[0][...].astype(f32)
    for part in part_refs[1:]:
        total += part[...].astype(f32)
    rows = total.astype(jnp.bfloat16)
    shifted = jnp.dot(rows, weight_ref[...], preferred_element_type=f32) + bias_ref[...]
    logistic = jax.nn.sigmoid(shifted)
    out_ref[...] = (shifted * logistic).astype(jnp.bfloat16)
    derivative = logistic * (1.0 + shifted * (1.0 - logistic))
    grad = (cotangent_ref[...].astype(f32) * derivative).astype(jnp.bfloat16)
    back = lax.dot_general(
        grad, weight_ref[...], (((1,), (1,)), ((), ())), preferred_element_type=f32
    ).astype(jnp.bfloat16)
    part_ref[...] = lax.dot_general(rows, grad, (((0,), (0,)), ((), ())), preferred_element_type=f32)
    tail = split_rows(jnp.sum(grad.astype(f32), axis=0, keepdims=True))
    share = part_ref.shape[0] // parts
    high = back.shape[0]
    for i, message_ref in enumerate(message_refs):
        message_ref[pl.ds(0, high), :] = back
        at = pl.multiple_of(place_ref[i] * share, share)
        message_ref[pl.ds(high, share), :] = part_ref[pl.ds(at, share), :].astype(jnp.bfloat16)
        message_ref[pl.ds(high + share, EXTRA), :] = tail


def middle(places, sums, weight, layer_bias, cotangent):
    rows, width = cotangent.shape
    parts = len(sums)
    inside = pl.BlockSpec(memory_space=pltpu.VMEM)
    message = jax.ShapeDtypeStruct((rows + width // parts + EXTRA, width), jnp.bfloat16)
    return pl.pallas_call(
        middle_kernel,
        out_shape=(jax.ShapeDtypeStruct((rows, width), jnp.bfloat16),) + (message,) * parts,
        grid_spec=pltpu.PrefetchScalarGridSpec(
            num_scalar_prefetch=1,
            grid=(),
            in_specs=[inside] * (parts + 3),
            out_specs=(inside,) * (parts + 1),
            scratch_shapes=[pltpu.VMEM((width, width), jnp.float32)],
        ),
        compiler_params=pltpu.CompilerParams(vmem_limit_bytes=VMEM),
        cost_estimate=cost(1 << 30, 8 << 20),
        name="middle",
    )(places, *sums, weight, layer_bias[None, :], cotangent)


def finish_kernel(rows, scale, *refs):
    messages, (grad_ref, part_ref, bias_ref) = refs[:-3], refs[-3:]
    f32 = jnp.float32
    total = messages[0][...].astype(f32)
    for message in messages[1:]:
        total += message[...].astype(f32)
    share = part_ref.shape[0]
    grad_ref[...] = total[:rows].astype(jnp.bfloat16)
    part_ref[...] = total[rows : rows + share].astype(jnp.bfloat16)
    last = rows + share
    bias_ref[...] = (total[last : last + 1] + total[last + 1 : last + 2]) * scale


def finish(messages, rows, scale):
    height, width = messages[0].shape
    return pl.pallas_call(
        lambda *refs: finish_kernel(rows, scale, *refs),
        out_shape=(
            jax.ShapeDtypeStruct((rows, width), jnp.bfloat16),
            jax.ShapeDtypeStruct((height - rows - EXTRA, width), jnp.bfloat16),
            jax.ShapeDtypeStruct((1, width), jnp.float32),
        ),
        compiler_params=pltpu.CompilerParams(vmem_limit_bytes=VMEM),
        name="finish",
    )(*messages)


def place_kernel(scale, place_ref, *refs):
    share = refs[0].shape[0]
    for i, piece in enumerate(refs[:-1]):
        at = pl.multiple_of(place_ref[i] * share, share)
        refs[-1][pl.ds(at, share), :] = piece[...].astype(jnp.float32) * scale


def place(places, pieces, scale):
    share, width = pieces[0].shape
    inside = pl.BlockSpec(memory_space=pltpu.VMEM)
    return pl.pallas_call(
        lambda *refs: place_kernel(scale, *refs),
        out_shape=jax.ShapeDtypeStruct((share * len(pieces), width), jnp.float32),
        grid_spec=pltpu.PrefetchScalarGridSpec(
            num_scalar_prefetch=1, grid=(), in_specs=[inside] * len(pieces), out_specs=inside
        ),
        compiler_params=pltpu.CompilerParams(vmem_limit_bytes=VMEM),
        name="place",
    )(places, *pieces)


CHIP_HALVES = (((0, 0), (0, 1), (0, 3), (1, 0)), ((0, 2), (1, 1), (1, 3), (1, 2)))


def at_offset(axes, offsets, sign):
    flat = jnp.int32(0)
    for axis, offset in zip(axes, offsets):
        n = SIZES[axis]
        flat = flat * n + (lax.axis_index(axis) + (n + sign * offset)) % n
    return flat


def listed(values):
    line = lax.iota(jnp.int32, len(values))
    found = jnp.zeros_like(line)
    for i, value in enumerate(values):
        found = jnp.where(line == i, value, found)
    return found


def body(features, weight, layer_bias, tile_values, tile_target, tile_counts, cotangent):
    local_rows, width = features.shape
    values = tile_values[0, 0]
    targets = tile_target[0, 0]
    counts = tile_counts[0, 0]
    tile = values.shape[-1]
    slot_total = values.shape[1]
    assert local_rows == 2 * tile and slot_total == VARIANTS[-1]
    parts = all_offsets(REP)
    dest_tiles = 2 * len(parts)

    active = lax.broadcasted_iota(jnp.int32, targets.shape, 1) < counts[:, None]
    slots = jnp.where(active, targets, dest_tiles).reshape(-1)
    owner = targets // 2
    xh, y = SIZES["xh"], SIZES["y"]
    from_part = ((lax.axis_index("xh") + xh - owner // y) % xh) * y + (lax.axis_index("y") + y - owner % y) % y
    back_slots = jnp.where(active, from_part * 2 + targets % 2, dest_tiles).reshape(-1)
    core = lax.axis_index("core")
    part_to = listed([at_offset(REP, o, 1) for o in parts])
    part_from = listed([at_offset(REP, o, -1) for o in parts])

    partial = None
    for half in CHIP_HALVES:
        own = [send_by(features, CHIP, o) if any(o) else features for o in half]
        crossed = [send_by(x, ("core",), (1,)) for x in own]
        at = [at_offset(CHIP, o, -1) * 2 for o in half]
        sources = listed([c + core for c in at] + [c + 1 - core for c in at])
        partial = aggregate(sources, slots, counts, part_to, own + crossed, values, partial)

    received = [send_by(partial[i], REP, o) if any(o) else partial[i] for i, o in enumerate(parts)]
    output, *messages = middle(part_to, received, weight, layer_bias, cotangent)
    messages = [send_by(messages[i], REP, o) if any(o) else messages[i] for i, o in enumerate(parts)]

    halves = CHIP_HALVES[::-1]
    to_chip = [[at_offset(CHIP, o, 1) * 2 for o in half] for half in halves]
    across, sums = [], None
    for i in range(2):
        sources = listed([c + 1 - core for c in to_chip[i]])
        found = spread(sources, back_slots, counts, messages, values, with_weight=i == 0)
        across.append(send_by(found[0], ("core",), (1,)))
        if i == 0:
            sums = (found[1], send_by(found[1], ("core",), (1,)))
    last = []
    for i in range(2):
        sources = listed([c + core for c in to_chip[i]])
        merged = spread(sources, back_slots, counts, messages, values, across[i], sums)
        last += [send_by(m, CHIP, o) if any(o) else m for m, o in zip(merged, halves[i])]
    norm_scale = 1.0 / math.sqrt(local_rows * math.prod(SIZES.values()))
    grad_features, piece, grad_bias = finish(last, local_rows, norm_scale)
    pieces = [send_by(piece, REP, o) if any(o) else piece for o in parts]
    grad_weight = place(part_from, pieces, norm_scale)
    return (output, grad_features, grad_weight, grad_bias[0])


def solution(mesh):
    fine = Mesh(np.asarray(mesh.devices).reshape(tuple(SIZES.values())), tuple(SIZES))
    placed = (
        P(ALL, None),
        P(),
        P(),
        P(BLK, REP, None, None, None, None),
        P(BLK, REP, None, None),
        P(BLK, REP, None),
        P(ALL, None),
    )
    return jax.shard_map(
        body,
        mesh=fine,
        in_specs=placed,
        out_specs=(P(ALL, None), P(ALL, None), P(), P()),
        check_vma=False,
    )
```

time: 918 us -> 238 us (0.26)
  waiting for transfers between devices: 314 us -> 100 us
  other arithmetic: 153 us -> 5.34 us
  loops' own time: 126 us -> 0 us
  local copies, waits for them, and re-layouts: 125 us -> 8.75 us
  matrix products: 116 us -> 0 us
  starting transfers between devices: 0.21 us -> 67.7 us
  blocking collectives: 64.4 us -> 0 us
  Pallas kernels: 0 us -> 53.1 us
  between operations: 13.8 us -> 1.11 us
    reduce_scatter x2 -> x0, waiting for transfers between devices: 158 us -> none  [the longest x1 84.7 us: body(): lax.psum_scatter(partial_value, 'rep', scatter_dimension=0, tiled=True)]
    scatter-add x32 -> x0, other arithmetic: 141 us -> none  [apply_group(): return running.at[targets[group_id]].add(products)]
    another operation x2 -> x0, loops' own time: 126 us -> none  [the longest x1 63 us: body(): lax.scan(source_group_step, jnp.zeros((), jnp.float32), jnp.arange(number...]
    dot_general x67 -> x0, matrix products: 116 us -> none  [the longest x32 63.1 us: back_group(): jnp.einsum('sij,sif->jf', masked[group_id], gathered, preferred_element_t...]
    ppermute x0 -> x46, waiting for transfers between devices: none -> 100 us  [send_by(): return lax.ppermute(value, axes, pairs)]
    psum x1 -> x0, waiting for transfers between devices: 81.6 us -> none  [body(): lax.psum((weight_part, bias_part), ('blk', 'rep'))]
    all_gather x2 -> x0, waiting for transfers between devices: 74.4 us -> none  [the longest x1 53.8 us: body(): grad_block = lax.all_gather(grad_summed, 'rep', axis=0, tiled=True)]
    gather x32 -> x0, local copies, waits for them, and re-layouts: 70.6 us -> none  [back_group(): gathered = grad_tiles[targets[group_id]]]
  transfers between devices with their start and end apart: 5 -> 46, of which waited for: 5 -> 20; matrix products, arithmetic and copies ran while one was open for 2% -> 3% of each run, Pallas kernels for 0% -> 12%
where the time goes in v2:
time: 238 us; the launch traced here: 236 us
  waiting for transfers between devices  100 us (42%)
  starting transfers between devices  67.7 us (28%)
  Pallas kernels  53.1 us (22%)
  local copies, waits for them, and re-layouts  8.75 us (4%)
  other arithmetic  5.34 us (2%)
    ppermute x46, waiting for transfers between devices, send_by(): return lax.ppermute(value, axes, pairs)  100 us
    ppermute x46, starting transfers between devices, send_by(): return lax.ppermute(value, axes, pairs)  67.7 us
    pallas_call x4, Pallas kernels, spread(): pl.pallas_call(lambda *refs: backward_kernel(shards, parts, crossing, wit...  26.5 us
    pallas_call x2, Pallas kernels, aggregate(): pl.pallas_call(lambda *refs: forward_kernel(shards, before is not None, *...  16.2 us
    unnamed x93, local copies, waits for them, and re-layouts  8.57 us
    pallas_call x1, Pallas kernels, middle(): pl.pallas_call(middle_kernel, out_shape=(jax.ShapeDtypeStruct((rows, widt...  4.86 us
  transfers between devices with their start and end apart: 46, of which 20 were waited for; matrix products, arithmetic and copies ran while one was open for 3% of the time, Pallas kernels for 12%

profile of v2, /device:TPU:0, one launch (start us, length us, event | category | flops | bytes accessed | tf_op | source)
XLA Modules:
  0.0 236.5 jit_solution(5319555585472384590)
XLA Ops:
  2.3 4.0 %collective-permute-start.9 = (bf16[256,512]{1,0:T(8,128)(2,1)}, bf16[256,512]{1,0:T(8,128)(2,1)S(1)}, u32[]{:S(2)}, u32[]{:S(2)}) collective-permute-start(bf16[256,512]{1,0:T(8,128)(2,1)} %refs_5_.1), channel_id=1, source_target_pairs={{0,48},{16,0},{32,16},{48,32},{64,112},{80,64},{96,80},{112,96},{1... | collective-permute-start | bytes 786440 | tf_op jit(solution)/shard_map/ppermute | solution.py:26
  13.4 9.8 %collective-permute-done.9.refs_7_ = bf16[256,512]{1,0:T(8,128)(2,1)S(1)} collective-permute-done((bf16[256,512]{1,0:T(8,128)(2,1)}, bf16[256,512]{1,0:T(8,128)(2,1)S(1)}, u32[]{:S(2)}, u32[]{:S(2)}) %collective-permute-start.9) | collective-permute-done | bytes 262176 | tf_op jit(solution)/shard_map/ppermute | solution.py:26
  25.3 4.3 %collective-permute-done.1.refs_6_ = bf16[256,512]{1,0:T(8,128)(2,1)S(1)} collective-permute-done((bf16[256,512]{1,0:T(8,128)(2,1)}, bf16[256,512]{1,0:T(8,128)(2,1)S(1)}, u32[]{:S(2)}, u32[]{:S(2)}) %collective-permute-start.1) | collective-permute-done | bytes 262176 | tf_op jit(solution)/shard_map/ppermute | solution.py:26
  34.9 8.5 %aggregate.2.refs_13_ = f32[16,128,512]{2,1,0:T(8,128)} custom-call(s32[8]{0:T(128)} %get-tuple-element.66.refs_0_, s32[256]{0:T(256)} %get-tuple-element.65.refs_1_, s32[32]{0:T(128)} %bitcast.13, s32[8]{0:T(128)} %get-tuple-element.67.refs_3_.place_ref, bf16[32,8,128,128]{3,2,1,0:T(8,128)(2,1)} %bitcast.6, bf16[256,512]{1,0:T(8,128)(2,1)} %refs_5_.1, ...), custom_call_target="tpu_custom_call" | custom-call | flops 4294967296 | bytes 12582912 | tf_op jit(solution)/shard_map/aggregate/pallas_call | solution.py:120
  45.0 7.7 %aggregate.3 = (bf16[256,512]{1,0:T(8,128)(2,1)}, bf16[256,512]{1,0:T(8,128)(2,1)}, bf16[256,512]{1,0:T(8,128)(2,1)}, bf16[256,512]{1,0:T(8,128)(2,1)}, bf16[256...) custom-call(s32[8]{0:T(128)} %select_select_fusion.6.refs_0_, ...), custom_call_target="tpu_custom_call" | custom-call | flops 4294967296 | bytes 12582912 | tf_op jit(solution)/shard_map/aggregate/pallas_call | solution.py:120
  62.9 6.0 %collective-permute-done.15.refs_1_ = bf16[256,512]{1,0:T(8,128)(2,1)S(1)} collective-permute-done((bf16[256,512]{1,0:T(8,128)(2,1)}, bf16[256,512]{1,0:T(8,128)(2,1)S(1)}, u32[]{:S(2)}, u32[]{:S(2)}) %collective-permute-start.15) | collective-permute-done | bytes 262176 | tf_op jit(solution)/shard_map/ppermute | solution.py:26
  69.4 4.7 %collective-permute-done.19.refs_5_ = bf16[256,512]{1,0:T(8,128)(2,1)S(1)} collective-permute-done((bf16[256,512]{1,0:T(8,128)(2,1)}, bf16[256,512]{1,0:T(8,128)(2,1)S(1)}, u32[]{:S(2)}, u32[]{:S(2)}) %collective-permute-start.19) | collective-permute-done | bytes 262176 | tf_op jit(solution)/shard_map/ppermute | solution.py:26
  74.1 7.3 %collective-permute-done.20.refs_6_ = bf16[256,512]{1,0:T(8,128)(2,1)S(1)} collective-permute-done((bf16[256,512]{1,0:T(8,128)(2,1)}, bf16[256,512]{1,0:T(8,128)(2,1)S(1)}, u32[]{:S(2)}, u32[]{:S(2)}) %collective-permute-start.20) | collective-permute-done | bytes 262176 | tf_op jit(solution)/shard_map/ppermute | solution.py:26
  81.4 5.4 %collective-permute-done.21.refs_7_ = bf16[256,512]{1,0:T(8,128)(2,1)S(1)} collective-permute-done((bf16[256,512]{1,0:T(8,128)(2,1)}, bf16[256,512]{1,0:T(8,128)(2,1)S(1)}, u32[]{:S(2)}, u32[]{:S(2)}) %collective-permute-start.21) | collective-permute-done | bytes 262176 | tf_op jit(solution)/shard_map/ppermute | solution.py:26
  87.5 4.9 %middle.1 = (bf16[256,512]{1,0:T(8,128)(2,1)}, bf16[336,512]{1,0:T(8,128)(2,1)}, bf16[336,512]{1,0:T(8,128)(2,1)}, bf16[336,512]{1,0:T(8,128)(2,1)}, bf16[336,51...) custom-call(s32[8]{0:T(128)} %get-tuple-element.67.refs_3_.place_ref, ...), custom_call_target="tpu_custom_call" | custom-call | flops 1073741824 | bytes 8388608 | tf_op jit(solution)/shard_map/middle/pallas_call | solution.py:310
  92.4 6.2 %collective-permute-start.22 = (bf16[336,512]{1,0:T(8,128)(2,1)}, bf16[336,512]{1,0:T(8,128)(2,1)S(1)}, u32[]{:S(2)}, u32[]{:S(2)}) collective-permute-start(bf16[336,512]{1,0:T(8,128)(2,1)} %get-tuple-element.44), channel_id=1, source_target_pairs={{0,1},{1,2},{2,3},{3,0},{4,5},{5,6},{6,7},{7,4},{8,9},{9,10},{10,1... | collective-permute-start | bytes 1032200 | tf_op jit(solution)/shard_map/ppermute | solution.py:26
  98.6 3.3 %collective-permute-start.23 = (bf16[336,512]{1,0:T(8,128)(2,1)}, bf16[336,512]{1,0:T(8,128)(2,1)S(1)}, u32[]{:S(2)}, u32[]{:S(2)}) collective-permute-start(bf16[336,512]{1,0:T(8,128)(2,1)} %get-tuple-element.45), channel_id=1, source_target_pairs={{0,2},{1,3},{2,0},{3,1},{4,6},{5,7},{6,4},{7,5},{8,10},{9,11},{10,... | collective-permute-start | bytes 1032200 | tf_op jit(solution)/shard_map/ppermute | solution.py:26
  111.1 21.3 %collective-permute-done.23.refs_6_ = bf16[336,512]{1,0:T(8,128)(2,1)S(1)} collective-permute-done((bf16[336,512]{1,0:T(8,128)(2,1)}, bf16[336,512]{1,0:T(8,128)(2,1)S(1)}, u32[]{:S(2)}, u32[]{:S(2)}) %collective-permute-start.23) | collective-permute-done | bytes 344096 | tf_op jit(solution)/shard_map/ppermute | solution.py:26
  133.0 11.2 %collective-permute-done.28.refs_11_ = bf16[336,512]{1,0:T(8,128)(2,1)S(1)} collective-permute-done((bf16[336,512]{1,0:T(8,128)(2,1)}, bf16[336,512]{1,0:T(8,128)(2,1)S(1)}, u32[]{:S(2)}, u32[]{:S(2)}) %collective-permute-start.28) | collective-permute-done | bytes 344096 | tf_op jit(solution)/shard_map/ppermute | solution.py:26
  144.9 5.6 %spread.6 = bf16[4,256,512]{2,1,0:T(8,128)(2,1)} custom-call(s32[4]{0:T(128)} %select_select_fusion.1.refs_0_, s32[256]{0:T(256)} %get-tuple-element.64.refs_1_, s32[32]{0:T(128)} %bitcast.15, bf16[32,8,128,128]{3,2,1,0:T(8,128)(2,1)} %bitcast.8, bf16[336,512]{1,0:T(8,128)(2,1)} %get-tuple-element.43.refs_4_, bf16[336,512]{1,0:T(8,128)(2,1)} %copy-done, ...), custom_call_target="tpu_custom_call" | custom-call | flops 2147483648 | bytes 8388608 | tf_op jit(solution)/shard_map/spread/pallas_call | solution.py:264
  151.2 6.0 %spread.4 = (bf16[4,256,512]{2,1,0:T(8,128)(2,1)}, f32[80,512]{1,0:T(8,128)}) custom-call(s32[4]{0:T(128)} %select_select_fusion.3.refs_0_, s32[256]{0:T(256)} %get-tuple-element.64.refs_1_, s32[32]{0:T(128)} %bitcast.16, bf16[32,8,128,128]{3,2,1,0:T(8,128)(2,1)} %bitcast.9, bf16[336,512]{1,0:T(8,128)(2,1)} %get-tuple-element.43.refs_4_, ...), custom_call_target="tpu_custom_call" | custom-call | flops 2147483648 | bytes 8388608 | tf_op jit(solution)/shard_map/spread/pallas_call | solution.py:264
  162.2 7.5 %spread.7 = (bf16[336,512]{1,0:T(8,128)(2,1)}, bf16[336,512]{1,0:T(8,128)(2,1)}, bf16[336,512]{1,0:T(8,128)(2,1)}, bf16[336,512]{1,0:T(8,128)(2,1)}) custom-call(s32[4]{0:T(128)} %select_select_fusion.2.refs_0_, s32[256]{0:T(256)} %get-tuple-element.64.refs_1_, s32[32]{0:T(128)} %bitcast.17, bf16[32,8,128,128]{3,2,1,0:T(8,128)(2,1)} %bitcast.10, ...), custom_call_target="tpu_custom_call" | custom-call | flops 2147483648 | bytes 8388608 | tf_op jit(solution)/shard_map/spread/pallas_call | solution.py:264
  174.6 7.4 %spread.5 = (bf16[336,512]{1,0:T(8,128)(2,1)}, bf16[336,512]{1,0:T(8,128)(2,1)}, bf16[336,512]{1,0:T(8,128)(2,1)}, bf16[336,512]{1,0:T(8,128)(2,1)}) custom-call(s32[4]{0:T(128)} %select_select_fusion.4.refs_0_, s32[256]{0:T(256)} %get-tuple-element.64.refs_1_, s32[32]{0:T(128)} %bitcast.18, bf16[32,8,128,128]{3,2,1,0:T(8,128)(2,1)} %bitcast.11, ...), custom_call_target="tpu_custom_call" | custom-call | flops 2147483648 | bytes 8388608 | tf_op jit(solution)/shard_map/spread/pallas_call | solution.py:264
  190.1 11.4 %collective-permute-done.31.refs_0_ = bf16[336,512]{1,0:T(8,128)(2,1)S(1)} collective-permute-done((bf16[336,512]{1,0:T(8,128)(2,1)}, bf16[336,512]{1,0:T(8,128)(2,1)S(1)}, u32[]{:S(2)}, u32[]{:S(2)}) %collective-permute-start.31) | collective-permute-done | bytes 344096 | tf_op jit(solution)/shard_map/ppermute | solution.py:26
  203.0 6.6 %collective-permute-done.34.refs_3_ = bf16[336,512]{1,0:T(8,128)(2,1)S(1)} collective-permute-done((bf16[336,512]{1,0:T(8,128)(2,1)}, bf16[336,512]{1,0:T(8,128)(2,1)S(1)}, u32[]{:S(2)}, u32[]{:S(2)}) %collective-permute-start.34) | collective-permute-done | bytes 344096 | tf_op jit(solution)/shard_map/ppermute | solution.py:26
  213.1 3.4 %collective-permute-start.45 = (bf16[64,512]{1,0:T(8,128)(2,1)}, bf16[64,512]{1,0:T(8,128)(2,1)S(1)}, u32[]{:S(2)}, u32[]{:S(2)}) collective-permute-start(bf16[64,512]{1,0:T(8,128)(2,1)} %get-tuple-element.62.refs_1_), channel_id=1, source_target_pairs={{0,7},{1,4},{2,5},{3,6},{4,3},{5,0},{6,1},{7,2},{8,15},{9,12},{10,... | collective-permute-start | bytes 196616 | tf_op jit(solution)/shard_map/ppermute | solution.py:26
  216.5 3.7 %collective-permute-start.44 = (bf16[64,512]{1,0:T(8,128)(2,1)}, bf16[64,512]{1,0:T(8,128)(2,1)S(1)}, u32[]{:S(2)}, u32[]{:S(2)}) collective-permute-start(bf16[64,512]{1,0:T(8,128)(2,1)} %get-tuple-element.62.refs_1_), channel_id=1, source_target_pairs={{0,6},{1,7},{2,4},{3,5},{4,2},{5,3},{6,0},{7,1},{8,14},{9,15},{10,... | collective-permute-start | bytes 196616 | tf_op jit(solution)/shard_map/ppermute | solution.py:26
  222.7 3.7 %collective-permute-start.41 = (bf16[64,512]{1,0:T(8,128)(2,1)}, bf16[64,512]{1,0:T(8,128)(2,1)S(1)}, u32[]{:S(2)}, u32[]{:S(2)}) collective-permute-start(bf16[64,512]{1,0:T(8,128)(2,1)} %get-tuple-element.62.refs_1_), channel_id=1, source_target_pairs={{0,3},{1,0},{2,1},{3,2},{4,7},{5,4},{6,5},{7,6},{8,11},{9,8},{10,9... | collective-permute-start | bytes 196616 | tf_op jit(solution)/shard_map/ppermute | solution.py:26
  229.2 3.3 %collective-permute-done.40.refs_3_ = bf16[64,512]{1,0:T(8,128)(2,1)S(1)} collective-permute-done((bf16[64,512]{1,0:T(8,128)(2,1)}, bf16[64,512]{1,0:T(8,128)(2,1)S(1)}, u32[]{:S(2)}, u32[]{:S(2)}) %collective-permute-start.40) | collective-permute-done | bytes 65568 | tf_op jit(solution)/shard_map/ppermute | solution.py:26
  (181 shorter events, 72.3 us)
Async XLA Ops:
  2.3 20.9 %collective-permute-start.9 = (bf16[256,512]{1,0:T(8,128)(2,1)}, bf16[256,512]{1,0:T(8,128)(2,1)S(1)}, u32[]{:S(2)}, u32[]{:S(2)}) collective-permute-start(bf16[256,512]{1,0:T(8,128)(2,1)} %refs_5_.1), channel_id=1, source_target_pairs={{0,48},{16,0},{32,16},{48,32},{64,112},{80,64},{96,80},{112,96},{1... | collective-permute-start | bytes 786440 | tf_op jit(solution)/shard_map/ppermute | solution.py:26
  6.3 18.3 %collective-permute-start.8 = (bf16[256,512]{1,0:T(8,128)(2,1)}, bf16[256,512]{1,0:T(8,128)(2,1)S(1)}, u32[]{:S(2)}, u32[]{:S(2)}) collective-permute-start(bf16[256,512]{1,0:T(8,128)(2,1)} %refs_5_.1), channel_id=1, source_target_pairs={{0,16},{16,32},{32,48},{48,0},{64,80},{80,96},{96,112},{112,64},{1... | collective-permute-start | bytes 786440 | tf_op jit(solution)/shard_map/ppermute | solution.py:26
  6.3 18.3 %collective-permute-start.3 = (bf16[256,512]{1,0:T(8,128)(2,1)}, bf16[256,512]{1,0:T(8,128)(2,1)S(1)}, u32[]{:S(2)}, u32[]{:S(2)}) collective-permute-start(bf16[256,512]{1,0:T(8,128)(2,1)} %refs_5_.1), channel_id=1, source_target_pairs={{0,96},{16,112},{32,64},{48,80},{64,32},{80,48},{96,0},{112,16},{1... | collective-permute-start | bytes 786440 | tf_op jit(solution)/shard_map/ppermute | solution.py:26
  8.2 17.0 %collective-permute-start.2 = (bf16[256,512]{1,0:T(8,128)(2,1)}, bf16[256,512]{1,0:T(8,128)(2,1)S(1)}, u32[]{:S(2)}, u32[]{:S(2)}) collective-permute-start(bf16[256,512]{1,0:T(8,128)(2,1)} %refs_5_.1), channel_id=1, source_target_pairs={{0,112},{16,64},{32,80},{48,96},{64,48},{80,0},{96,16},{112,32},{1... | collective-permute-start | bytes 786440 | tf_op jit(solution)/shard_map/ppermute | solution.py:26
  9.8 19.7 %collective-permute-start.1 = (bf16[256,512]{1,0:T(8,128)(2,1)}, bf16[256,512]{1,0:T(8,128)(2,1)S(1)}, u32[]{:S(2)}, u32[]{:S(2)}) collective-permute-start(bf16[256,512]{1,0:T(8,128)(2,1)} %refs_5_.1), channel_id=1, source_target_pairs={{0,80},{16,96},{32,112},{48,64},{64,16},{80,32},{96,48},{112,0},{1... | collective-permute-start | bytes 786440 | tf_op jit(solution)/shard_map/ppermute | solution.py:26
  52.8 16.1 %collective-permute-start.15 = (bf16[256,512]{1,0:T(8,128)(2,1)}, bf16[256,512]{1,0:T(8,128)(2,1)S(1)}, u32[]{:S(2)}, u32[]{:S(2)}) collective-permute-start(bf16[256,512]{1,0:T(8,128)(2,1)} %get-tuple-element.35), channel_id=1, source_target_pairs={{0,1},{1,2},{2,3},{3,0},{4,5},{5,6},{6,7},{7,4},{8,9},{9,10},{10,1... | collective-permute-start | bytes 786440 | tf_op jit(solution)/shard_map/ppermute | solution.py:26
  54.8 14.2 %collective-permute-start.16 = (bf16[256,512]{1,0:T(8,128)(2,1)}, bf16[256,512]{1,0:T(8,128)(2,1)S(1)}, u32[]{:S(2)}, u32[]{:S(2)}) collective-permute-start(bf16[256,512]{1,0:T(8,128)(2,1)} %get-tuple-element.36), channel_id=1, source_target_pairs={{0,2},{1,3},{2,0},{3,1},{4,6},{5,7},{6,4},{7,5},{8,10},{9,11},{10,... | collective-permute-start | bytes 786440 | tf_op jit(solution)/shard_map/ppermute | solution.py:26
  60.8 13.3 %collective-permute-start.19 = (bf16[256,512]{1,0:T(8,128)(2,1)}, bf16[256,512]{1,0:T(8,128)(2,1)S(1)}, u32[]{:S(2)}, u32[]{:S(2)}) collective-permute-start(bf16[256,512]{1,0:T(8,128)(2,1)} %get-tuple-element.39), channel_id=1, source_target_pairs={{0,5},{1,6},{2,7},{3,4},{4,1},{5,2},{6,3},{7,0},{8,13},{9,14},{10,... | collective-permute-start | bytes 786440 | tf_op jit(solution)/shard_map/ppermute | solution.py:26
  68.9 17.9 %collective-permute-start.21 = (bf16[256,512]{1,0:T(8,128)(2,1)}, bf16[256,512]{1,0:T(8,128)(2,1)S(1)}, u32[]{:S(2)}, u32[]{:S(2)}) collective-permute-start(bf16[256,512]{1,0:T(8,128)(2,1)} %get-tuple-element.41), channel_id=1, source_target_pairs={{0,7},{1,4},{2,5},{3,6},{4,3},{5,0},{6,1},{7,2},{8,15},{9,12},{10,... | collective-permute-start | bytes 786440 | tf_op jit(solution)/shard_map/ppermute | solution.py:26
  92.4 16.6 %collective-permute-start.22 = (bf16[336,512]{1,0:T(8,128)(2,1)}, bf16[336,512]{1,0:T(8,128)(2,1)S(1)}, u32[]{:S(2)}, u32[]{:S(2)}) collective-permute-start(bf16[336,512]{1,0:T(8,128)(2,1)} %get-tuple-element.44), channel_id=1, source_target_pairs={{0,1},{1,2},{2,3},{3,0},{4,5},{5,6},{6,7},{7,4},{8,9},{9,10},{10,1... | collective-permute-start | bytes 1032200 | tf_op jit(solution)/shard_map/ppermute | solution.py:26
  98.6 33.8 %collective-permute-start.23 = (bf16[336,512]{1,0:T(8,128)(2,1)}, bf16[336,512]{1,0:T(8,128)(2,1)S(1)}, u32[]{:S(2)}, u32[]{:S(2)}) collective-permute-start(bf16[336,512]{1,0:T(8,128)(2,1)} %get-tuple-element.45), channel_id=1, source_target_pairs={{0,2},{1,3},{2,0},{3,1},{4,6},{5,7},{6,4},{7,5},{8,10},{9,11},{10,... | collective-permute-start | bytes 1032200 | tf_op jit(solution)/shard_map/ppermute | solution.py:26
  101.9 31.0 %collective-permute-start.24 = (bf16[336,512]{1,0:T(8,128)(2,1)}, bf16[336,512]{1,0:T(8,128)(2,1)S(1)}, u32[]{:S(2)}, u32[]{:S(2)}) collective-permute-start(bf16[336,512]{1,0:T(8,128)(2,1)} %get-tuple-element.46), channel_id=1, source_target_pairs={{0,3},{1,0},{2,1},{3,2},{4,7},{5,4},{6,5},{7,6},{8,11},{9,8},{10,9... | collective-permute-start | bytes 1032200 | tf_op jit(solution)/shard_map/ppermute | solution.py:26
  101.9 31.0 %collective-permute-start.25 = (bf16[336,512]{1,0:T(8,128)(2,1)}, bf16[336,512]{1,0:T(8,128)(2,1)S(1)}, u32[]{:S(2)}, u32[]{:S(2)}) collective-permute-start(bf16[336,512]{1,0:T(8,128)(2,1)} %get-tuple-element.47), channel_id=1, source_target_pairs={{0,4},{1,5},{2,6},{3,7},{4,0},{5,1},{6,2},{7,3},{8,12},{9,13},{10,... | collective-permute-start | bytes 1032200 | tf_op jit(solution)/shard_map/ppermute | solution.py:26
  105.2 27.8 %collective-permute-start.26 = (bf16[336,512]{1,0:T(8,128)(2,1)}, bf16[336,512]{1,0:T(8,128)(2,1)S(1)}, u32[]{:S(2)}, u32[]{:S(2)}) collective-permute-start(bf16[336,512]{1,0:T(8,128)(2,1)} %get-tuple-element.48), channel_id=1, source_target_pairs={{0,5},{1,6},{2,7},{3,4},{4,1},{5,2},{6,3},{7,0},{8,13},{9,14},{10,... | collective-permute-start | bytes 1032200 | tf_op jit(solution)/shard_map/ppermute | solution.py:26
  109.0 24.1 %collective-permute-start.27 = (bf16[336,512]{1,0:T(8,128)(2,1)}, bf16[336,512]{1,0:T(8,128)(2,1)S(1)}, u32[]{:S(2)}, u32[]{:S(2)}) collective-permute-start(bf16[336,512]{1,0:T(8,128)(2,1)} %get-tuple-element.49), channel_id=1, source_target_pairs={{0,6},{1,7},{2,4},{3,5},{4,2},{5,3},{6,0},{7,1},{8,14},{9,15},{10,... | collective-permute-start | bytes 1032200 | tf_op jit(solution)/shard_map/ppermute | solution.py:26
  157.2 16.4 %collective-permute-start.29 = (bf16[4,256,512]{2,1,0:T(8,128)(2,1)}, bf16[4,256,512]{2,1,0:T(8,128)(2,1)S(1)}, u32[]{:S(2)}, u32[]{:S(2)}) collective-permute-start(bf16[4,256,512]{2,1,0:T(8,128)(2,1)} %get-tuple-element.51), channel_id=1, source_target_pairs={{0,8},{8,0},{1,9},{9,1},{2,10},{10,2},{3,11},{11,3},{4,12},{12,4},... | collective-permute-start | bytes 3145736 | tf_op jit(solution)/shard_map/ppermute | solution.py:26
  169.7 15.1 %collective-permute-start.36 = (bf16[336,512]{1,0:T(8,128)(2,1)}, bf16[336,512]{1,0:T(8,128)(2,1)S(1)}, u32[]{:S(2)}, u32[]{:S(2)}) collective-permute-start(bf16[336,512]{1,0:T(8,128)(2,1)} %get-tuple-element.58), channel_id=1, source_target_pairs={{0,16},{16,32},{32,48},{48,0},{64,80},{80,96},{96,112},{112,64},{1... | collective-permute-start | bytes 1032200 | tf_op jit(solution)/shard_map/ppermute | solution.py:26
  169.8 17.5 %collective-permute-start.37 = (bf16[336,512]{1,0:T(8,128)(2,1)}, bf16[336,512]{1,0:T(8,128)(2,1)S(1)}, u32[]{:S(2)}, u32[]{:S(2)}) collective-permute-start(bf16[336,512]{1,0:T(8,128)(2,1)} %get-tuple-element.59), channel_id=1, source_target_pairs={{0,48},{16,0},{32,16},{48,32},{64,112},{80,64},{96,80},{112,96},{1... | collective-permute-start | bytes 1032200 | tf_op jit(solution)/shard_map/ppermute | solution.py:26
  173.6 16.5 %collective-permute-start.38 = (bf16[336,512]{1,0:T(8,128)(2,1)}, bf16[336,512]{1,0:T(8,128)(2,1)S(1)}, u32[]{:S(2)}, u32[]{:S(2)}) collective-permute-start(bf16[336,512]{1,0:T(8,128)(2,1)} %get-tuple-element.60), channel_id=1, source_target_pairs={{0,64},{16,80},{32,96},{48,112},{64,0},{80,16},{96,32},{112,48},{1... | collective-permute-start | bytes 1032200 | tf_op jit(solution)/shard_map/ppermute | solution.py:26
  182.0 19.5 %collective-permute-start.31 = (bf16[336,512]{1,0:T(8,128)(2,1)}, bf16[336,512]{1,0:T(8,128)(2,1)S(1)}, u32[]{:S(2)}, u32[]{:S(2)}) collective-permute-start(bf16[336,512]{1,0:T(8,128)(2,1)} %get-tuple-element.53), channel_id=1, source_target_pairs={{0,32},{16,48},{32,0},{48,16},{64,96},{80,112},{96,64},{112,80},{1... | collective-permute-start | bytes 1032200 | tf_op jit(solution)/shard_map/ppermute | solution.py:26
  183.2 18.3 %collective-permute-start.32 = (bf16[336,512]{1,0:T(8,128)(2,1)}, bf16[336,512]{1,0:T(8,128)(2,1)S(1)}, u32[]{:S(2)}, u32[]{:S(2)}) collective-permute-start(bf16[336,512]{1,0:T(8,128)(2,1)} %get-tuple-element.54), channel_id=1, source_target_pairs={{0,80},{16,96},{32,112},{48,64},{64,16},{80,32},{96,48},{112,0},{1... | collective-permute-start | bytes 1032200 | tf_op jit(solution)/shard_map/ppermute | solution.py:26
  184.9 18.2 %collective-permute-start.33 = (bf16[336,512]{1,0:T(8,128)(2,1)}, bf16[336,512]{1,0:T(8,128)(2,1)S(1)}, u32[]{:S(2)}, u32[]{:S(2)}) collective-permute-start(bf16[336,512]{1,0:T(8,128)(2,1)} %get-tuple-element.55), channel_id=1, source_target_pairs={{0,112},{16,64},{32,80},{48,96},{64,48},{80,0},{96,16},{112,32},{1... | collective-permute-start | bytes 1032200 | tf_op jit(solution)/shard_map/ppermute | solution.py:26
  187.3 22.3 %collective-permute-start.34 = (bf16[336,512]{1,0:T(8,128)(2,1)}, bf16[336,512]{1,0:T(8,128)(2,1)S(1)}, u32[]{:S(2)}, u32[]{:S(2)}) collective-permute-start(bf16[336,512]{1,0:T(8,128)(2,1)} %get-tuple-element.56), channel_id=1, source_target_pairs={{0,96},{16,112},{32,64},{48,80},{64,32},{80,48},{96,0},{112,16},{1... | collective-permute-start | bytes 1032200 | tf_op jit(solution)/shard_map/ppermute | solution.py:26
  213.1 13.3 %collective-permute-start.45 = (bf16[64,512]{1,0:T(8,128)(2,1)}, bf16[64,512]{1,0:T(8,128)(2,1)S(1)}, u32[]{:S(2)}, u32[]{:S(2)}) collective-permute-start(bf16[64,512]{1,0:T(8,128)(2,1)} %get-tuple-element.62.refs_1_), channel_id=1, source_target_pairs={{0,7},{1,4},{2,5},{3,6},{4,3},{5,0},{6,1},{7,2},{8,15},{9,12},{10,... | collective-permute-start | bytes 196616 | tf_op jit(solution)/shard_map/ppermute | solution.py:26
  (68 other events, 608.2 us)

commit v3 on v2

v3 whole, which is shorter than its diff:
```python
import itertools
import math

import jax
import jax.numpy as jnp
import numpy as np
from jax import lax
from jax.experimental import pallas as pl
from jax.experimental.pallas import tpu as pltpu
from jax.sharding import Mesh, PartitionSpec as P

SIZES = {"xl": 2, "z": 4, "core": 2, "xh": 2, "y": 4}
BLK = ("xl", "z", "core")
REP = ("xh", "y")
CHIP = ("xl", "z")
ALL = BLK + REP
VMEM = 60 << 20


def send_by(value, axes, offsets):
    sizes = [SIZES[a] for a in axes]
    pairs = []
    for at in itertools.product(*[range(n) for n in sizes]):
        to = [(i + o) % n for i, o, n in zip(at, offsets, sizes)]
        pairs.append((int(np.ravel_multi_index(at, sizes)), int(np.ravel_multi_index(to, sizes))))
    return lax.ppermute(value, axes, pairs)


def exchange(value, axis, mask):
    return lax.ppermute(value, axis, [(i, i ^ mask) for i in range(SIZES[axis])])


def all_offsets(axes):
    return list(itertools.product(*[range(SIZES[a]) for a in axes]))


EXTRA = 16
VARIANTS = (1, 2, 3, 4, 6, 8)


def cost(flops, transferred):
    return pl.CostEstimate(flops=flops, transcendentals=0, bytes_accessed=transferred)


def of_class(count, action):
    low = 0
    for n in VARIANTS:

        @pl.when((count > low) & (count <= n))
        def _():
            action(n)

        low = n


def tiles_copy(v_ref, v_buf, sem, group, to, n):
    return pltpu.make_async_copy(v_ref.at[group, pl.ds(0, n)], v_buf.at[to, pl.ds(0, n)], sem.at[to])


def start_tiles(source_ref, count_ref, v_ref, v_buf, sem):
    def step(k, carry):
        group = source_ref[k // 2] * 2 + k % 2
        of_class(count_ref[group], lambda n: tiles_copy(v_ref, v_buf, sem, group, k, n).start())
        return carry

    lax.fori_loop(0, v_buf.shape[0], step, 0)


def forward_kernel(shards, source_ref, slot_ref, count_ref, place_ref, v_ref, *refs):
    x_refs, refs = refs[:shards], refs[shards:]
    acc_ref, x_buf, v_buf, x_sem, v_sem = refs[-5:]
    out_refs = refs[:-5]
    slots, tile = v_ref.shape[1:3]
    for i in range(shards):
        pltpu.make_async_copy(x_refs[i], x_buf.at[i], x_sem.at[i]).start()
    start_tiles(source_ref, count_ref, v_ref, v_buf, v_sem)
    acc_ref[...] = jnp.zeros_like(acc_ref)

    def group_step(k, carry):
        group = source_ref[k // 2] * 2 + k % 2

        @pl.when(k % 2 == 0)
        def _():
            pltpu.make_async_copy(x_refs[0], x_buf.at[k // 2], x_sem.at[k // 2]).wait()

        def work(n):
            tiles_copy(v_ref, v_buf, v_sem, group, k, n).wait()
            rows = x_buf[k // 2, pl.ds(pl.multiple_of(k % 2 * tile, tile), tile), :]
            tiles = v_buf[k, pl.ds(0, n)].reshape(n * tile, tile)
            product = jnp.dot(tiles, rows, preferred_element_type=jnp.float32)
            for m in range(n):
                acc_ref[slot_ref[group * slots + m]] += product[m * tile : (m + 1) * tile]

        of_class(count_ref[group], work)
        return carry

    lax.fori_loop(0, 2 * shards, group_step, 0)
    for i, out_ref in enumerate(out_refs):
        for t in range(2):
            out_ref[pl.ds(t * tile, tile), :] = acc_ref[place_ref[i] * 2 + t].astype(out_ref.dtype)


def aggregate(sources, slots, counts, places, gathered, values):
    shards = len(gathered)
    rows, width = gathered[0].shape
    _, slot_total, tile, _ = values.shape
    parts = places.shape[0]
    anywhere = pl.BlockSpec(memory_space=pl.ANY)
    inside = pl.BlockSpec(memory_space=pltpu.VMEM)
    return pl.pallas_call(
        lambda *refs: forward_kernel(shards, *refs),
        out_shape=(jax.ShapeDtypeStruct((rows, width), jnp.bfloat16),) * parts,
        grid_spec=pltpu.PrefetchScalarGridSpec(
            num_scalar_prefetch=4,
            grid=(),
            in_specs=[anywhere] * (1 + shards),
            out_specs=(inside,) * parts,
            scratch_shapes=[
                pltpu.VMEM((parts * 2 + 1, tile, width), jnp.float32),
                pltpu.VMEM((shards, rows, width), jnp.bfloat16),
                pltpu.VMEM((shards * 2, slot_total, tile, tile), jnp.bfloat16),
                pltpu.SemaphoreType.DMA((shards,)),
                pltpu.SemaphoreType.DMA((shards * 2,)),
            ],
        ),
        compiler_params=pltpu.CompilerParams(vmem_limit_bytes=VMEM),
        cost_estimate=cost(8 << 30, 16 << 20),
        name="aggregate",
    )(sources, slots, counts, places, values, *gathered)


def backward_kernel(shards, parts, crossing, with_weight, *refs):
    source_ref, slot_ref, count_ref, v_ref = refs[:4]
    m_refs, refs = refs[4 : 4 + parts], refs[4 + parts :]
    if crossing:
        crossed_refs, refs = refs[:crossing], refs[crossing:]
        out_refs, refs = refs[:shards], refs[shards:]
    else:
        out_ref, refs = refs[0], refs[1:]
        if with_weight:
            sum_ref, refs = refs[0], refs[1:]
    table_ref, v_buf, m_sem, v_sem = refs[:4]
    refs = refs[4:]
    slots, tile = v_ref.shape[1:3]
    rows = 2 * tile
    for i in range(parts):
        pltpu.make_async_copy(m_refs[i].at[pl.ds(0, rows)], table_ref.at[pl.ds(i * rows, rows)], m_sem.at[i]).start()
    start_tiles(source_ref, count_ref, v_ref, v_buf, v_sem)
    if crossing:
        term_ref, cross_buf, cross_sem = refs
        each = shards // crossing
        for i in range(crossing):
            pltpu.make_async_copy(crossed_refs[i], cross_buf.at[pl.ds(i * each, each)], cross_sem.at[i]).start()
    elif with_weight:
        w_buf, w_sem = refs
        more = w_buf.shape[1]
        for i in range(parts):
            pltpu.make_async_copy(m_refs[i].at[pl.ds(rows, more)], w_buf.at[i], w_sem.at[i]).start()
    blank = table_ref.at[pl.ds(parts * rows, tile)]
    blank[...] = jnp.zeros_like(blank)
    for i in range(parts):
        pltpu.make_async_copy(m_refs[i].at[pl.ds(0, rows)], table_ref.at[pl.ds(i * rows, rows)], m_sem.at[i]).wait()
    if crossing:
        for i in range(crossing):
            pltpu.make_async_copy(crossed_refs[i], cross_buf.at[pl.ds(i * each, each)], cross_sem.at[i]).wait()

    def group_step(k, carry):
        group = source_ref[k // 2] * 2 + k % 2
        i = k // 2
        at = pl.ds(pl.multiple_of(k % 2 * tile, tile), tile)

        def work(n):
            tiles_copy(v_ref, v_buf, v_sem, group, k, n).wait()
            tiles = v_buf[k, pl.ds(0, n)].reshape(n * tile, tile)
            found = [
                table_ref[pl.ds(pl.multiple_of(slot_ref[group * slots + m] * tile, tile), tile), :] for m in range(n)
            ]
            found = jnp.concatenate(found, axis=0) if n > 1 else found[0]
            product = lax.dot_general(tiles, found, (((0,), (0,)), ((), ())), preferred_element_type=jnp.float32)
            if crossing:
                term_ref[i, at, :] = (product + cross_buf[i, at, :].astype(jnp.float32)).astype(jnp.bfloat16)
            else:
                out_ref[i, at, :] = product.astype(jnp.bfloat16)

        of_class(count_ref[group], work)
        return carry

    lax.fori_loop(0, 2 * shards, group_step, 0)
    if crossing:
        for i in range(shards):
            out_refs[i][...] = term_ref[i]
    elif with_weight:
        total = None
        for i in range(parts):
            pltpu.make_async_copy(m_refs[i].at[pl.ds(rows, more)], w_buf.at[i], w_sem.at[i]).wait()
            term = w_buf[i].astype(jnp.float32)
            total = term if total is None else total + term
        share = more - EXTRA
        sum_ref[pl.ds(0, share), :] = total[:share]
        bias = total[share : share + 1] + total[share + 1 : share + 2]
        sum_ref[pl.ds(share, sum_ref.shape[0] - share), :] = jnp.broadcast_to(
            bias, (sum_ref.shape[0] - share, bias.shape[1])
        )


def split_rows(row):
    high = row.astype(jnp.bfloat16)
    low = (row - high.astype(jnp.float32)).astype(jnp.bfloat16)
    line = lax.broadcasted_iota(jnp.int32, (EXTRA, row.shape[1]), 0)
    spread_high = jnp.broadcast_to(high.astype(jnp.float32), line.shape)
    spread_low = jnp.broadcast_to(low.astype(jnp.float32), line.shape)
    return jnp.where(line == 0, spread_high, jnp.where(line == 1, spread_low, 0.0)).astype(jnp.bfloat16)


def spread(sources, slots, counts, messages, values, crossed=(), with_weight=False):
    parts = len(messages)
    shards = sources.shape[0]
    height, width = messages[0].shape
    slot_total, tile = values.shape[1:3]
    rows = 2 * tile
    anywhere = pl.BlockSpec(memory_space=pl.ANY)
    inside = pl.BlockSpec(memory_space=pltpu.VMEM)
    scratch = [
        pltpu.VMEM((parts * rows + tile, width), jnp.bfloat16),
        pltpu.VMEM((shards * 2, slot_total, tile, tile), jnp.bfloat16),
        pltpu.SemaphoreType.DMA((parts,)),
        pltpu.SemaphoreType.DMA((shards * 2,)),
    ]
    if crossed:
        out_shape = (jax.ShapeDtypeStruct((rows, width), jnp.bfloat16),) * shards
        scratch += [
            pltpu.VMEM((shards, rows, width), jnp.bfloat16),
            pltpu.VMEM((shards, rows, width), jnp.bfloat16),
            pltpu.SemaphoreType.DMA((len(crossed),)),
        ]
    else:
        out_shape = (jax.ShapeDtypeStruct((shards, rows, width), jnp.bfloat16),)
        if with_weight:
            more = height - rows
            out_shape += (jax.ShapeDtypeStruct((more - EXTRA + 8, width), jnp.float32),)
            scratch += [pltpu.VMEM((parts, more, width), jnp.bfloat16), pltpu.SemaphoreType.DMA((parts,))]
    return pl.pallas_call(
        lambda *refs: backward_kernel(shards, parts, len(crossed), with_weight, *refs),
        out_shape=out_shape,
        grid_spec=pltpu.PrefetchScalarGridSpec(
            num_scalar_prefetch=3,
            grid=(),
            in_specs=[anywhere] * (1 + parts + len(crossed)),
            out_specs=(inside,) * len(out_shape),
            scratch_shapes=scratch,
        ),
        compiler_params=pltpu.CompilerParams(vmem_limit_bytes=VMEM),
        cost_estimate=cost(shards << 29, shards << 20),
        name="spread",
    )(sources, slots, counts, values, *messages, *crossed)


def middle_kernel(place_ref, *refs):
    parts = place_ref.shape[0]
    part_refs, refs = refs[:parts], refs[parts:]
    weight_ref, bias_ref, cotangent_ref, out_ref = refs[:4]
    message_refs, part_ref = refs[4 : 4 + parts], refs[4 + parts]
    f32 = jnp.float32
    total = part_refs[0][...].astype(f32)
    for part in part_refs[1:]:
        total += part[...].astype(f32)
    rows = total.astype(jnp.bfloat16)
    shifted = jnp.dot(rows, weight_ref[...], preferred_element_type=f32) + bias_ref[...]
    logistic = jax.nn.sigmoid(shifted)
    out_ref[...] = (shifted * logistic).astype(jnp.bfloat16)
    derivative = logistic * (1.0 + shifted * (1.0 - logistic))
    grad = (cotangent_ref[...].astype(f32) * derivative).astype(jnp.bfloat16)
    back = lax.dot_general(
        grad, weight_ref[...], (((1,), (1,)), ((), ())), preferred_element_type=f32
    ).astype(jnp.bfloat16)
    part_ref[...] = lax.dot_general(rows, grad, (((0,), (0,)), ((), ())), preferred_element_type=f32)
    tail = split_rows(jnp.sum(grad.astype(f32), axis=0, keepdims=True))
    share = part_ref.shape[0] // parts
    high = back.shape[0]
    for i, message_ref in enumerate(message_refs):
        message_ref[pl.ds(0, high), :] = back
        at = pl.multiple_of(place_ref[i] * share, share)
        message_ref[pl.ds(high, share), :] = part_ref[pl.ds(at, share), :].astype(jnp.bfloat16)
        message_ref[pl.ds(high + share, EXTRA), :] = tail


def middle(places, sums, weight, layer_bias, cotangent):
    rows, width = cotangent.shape
    parts = len(sums)
    inside = pl.BlockSpec(memory_space=pltpu.VMEM)
    message = jax.ShapeDtypeStruct((rows + width // parts + EXTRA, width), jnp.bfloat16)
    return pl.pallas_call(
        middle_kernel,
        out_shape=(jax.ShapeDtypeStruct((rows, width), jnp.bfloat16),) + (message,) * parts,
        grid_spec=pltpu.PrefetchScalarGridSpec(
            num_scalar_prefetch=1,
            grid=(),
            in_specs=[inside] * (parts + 3),
            out_specs=(inside,) * (parts + 1),
            scratch_shapes=[pltpu.VMEM((width, width), jnp.float32)],
        ),
        compiler_params=pltpu.CompilerParams(vmem_limit_bytes=VMEM),
        cost_estimate=cost(1 << 30, 8 << 20),
        name="middle",
    )(places, *sums, weight, layer_bias[None, :], cotangent)


def place_kernel(scale, share, place_ref, *refs):
    for i, piece in enumerate(refs[:-1]):
        for k in range(piece.shape[0] // share):
            at = pl.multiple_of(place_ref[2 * i + k] * share, share)
            refs[-1][pl.ds(at, share), :] = piece[pl.ds(k * share, share), :].astype(jnp.float32) * scale


def place(places, pieces, share, scale):
    width = pieces[0].shape[1]
    inside = pl.BlockSpec(memory_space=pltpu.VMEM)
    return pl.pallas_call(
        lambda *refs: place_kernel(scale, share, *refs),
        out_shape=jax.ShapeDtypeStruct((share * places.shape[0], width), jnp.float32),
        grid_spec=pltpu.PrefetchScalarGridSpec(
            num_scalar_prefetch=1, grid=(), in_specs=[inside] * len(pieces), out_specs=inside
        ),
        compiler_params=pltpu.CompilerParams(vmem_limit_bytes=VMEM),
        name="place",
    )(places, *pieces)


CHIP_HALVES = (((0, 0), (0, 1), (0, 3), (1, 0)), ((0, 2), (1, 1), (1, 3), (1, 2)))


def at_offset(axes, offsets, sign):
    flat = jnp.int32(0)
    for axis, offset in zip(axes, offsets):
        n = SIZES[axis]
        flat = flat * n + (lax.axis_index(axis) + (n + sign * offset)) % n
    return flat


def listed(values):
    line = lax.iota(jnp.int32, len(values))
    found = jnp.zeros_like(line)
    for i, value in enumerate(values):
        found = jnp.where(line == i, value, found)
    return found


def body(features, weight, layer_bias, tile_values, tile_target, tile_counts, cotangent):
    local_rows, width = features.shape
    values = tile_values[0, 0]
    targets = tile_target[0, 0]
    counts = tile_counts[0, 0]
    tile = values.shape[-1]
    slot_total = values.shape[1]
    assert local_rows == 2 * tile and slot_total == VARIANTS[-1]
    parts = all_offsets(REP)
    dest_tiles = 2 * len(parts)

    active = lax.broadcasted_iota(jnp.int32, targets.shape, 1) < counts[:, None]
    slots = jnp.where(active, targets, dest_tiles).reshape(-1)
    owner = targets // 2
    xh, y = SIZES["xh"], SIZES["y"]
    from_part = ((lax.axis_index("xh") + xh - owner // y) % xh) * y + (lax.axis_index("y") + y - owner % y) % y
    back_slots = jnp.where(active, from_part * 2 + targets % 2, dest_tiles).reshape(-1)
    core = lax.axis_index("core")
    part_to = listed([at_offset(REP, o, 1) for o in parts])

    chips = CHIP_HALVES[0] + CHIP_HALVES[1]
    own = [send_by(features, CHIP, o) if any(o) else features for o in chips]
    crossed = [send_by(x, ("core",), (1,)) for x in own]
    at = [at_offset(CHIP, o, -1) * 2 for o in chips]
    sources = listed([c + core for c in at] + [c + 1 - core for c in at])
    partial = aggregate(sources, slots, counts, part_to, own + crossed, values)

    received = [send_by(partial[i], REP, o) if any(o) else partial[i] for i, o in enumerate(parts)]
    output, *messages = middle(part_to, received, weight, layer_bias, cotangent)
    messages = [send_by(messages[i], REP, o) if any(o) else messages[i] for i, o in enumerate(parts)]

    halves = CHIP_HALVES[::-1]
    to_chip = [[at_offset(CHIP, o, 1) * 2 for o in half] for half in halves]
    across = []
    for i in range(2):
        sources = listed([c + 1 - core for c in to_chip[i]])
        found = spread(sources, back_slots, counts, messages, values, with_weight=i == 0)
        across.append(send_by(found[0], ("core",), (1,)))
        if i == 0:
            share_sum = found[1]
    sources = listed([c + core for c in to_chip[0] + to_chip[1]])
    merged = spread(sources, back_slots, counts, messages, values, across)
    total = None
    for piece, o in zip(merged, halves[0] + halves[1]):
        piece = (send_by(piece, CHIP, o) if any(o) else piece).astype(jnp.float32)
        total = piece if total is None else total + piece
    grad_features = total.astype(jnp.bfloat16)

    share_sum = share_sum + send_by(share_sum, ("core",), (1,))
    share_sum = share_sum + send_by(share_sum, ("xl",), (1,))
    share_sum = share_sum + exchange(share_sum, "z", 1)
    share_sum = share_sum + exchange(share_sum, "z", 2)
    norm_scale = 1.0 / math.sqrt(local_rows * math.prod(SIZES.values()))
    share = width // len(parts)
    grad_bias = share_sum[share] * norm_scale
    piece = share_sum[:share].astype(jnp.bfloat16)
    pair = jnp.concatenate([piece, send_by(piece, ("xh",), (1,))])
    pieces = [send_by(pair, ("y",), (o,)) if o else pair for o in range(y)]
    at = [at_offset(REP, (k, o), -1) for o in range(y) for k in range(xh)]
    grad_weight = place(listed(at), pieces, share, norm_scale)
    return (output, grad_features, grad_weight, grad_bias)


def solution(mesh):
    fine = Mesh(np.asarray(mesh.devices).reshape(tuple(SIZES.values())), tuple(SIZES))
    placed = (
        P(ALL, None),
        P(),
        P(),
        P(BLK, REP, None, None, None, None),
        P(BLK, REP, None, None),
        P(BLK, REP, None),
        P(ALL, None),
    )
    return jax.shard_map(
        body,
        mesh=fine,
        in_specs=placed,
        out_specs=(P(ALL, None), P(ALL, None), P(), P()),
        check_vma=False,
    )
```

time: 238 us -> 224 us (0.941)
  Pallas kernels: 53.1 us -> 40.2 us
  starting transfers between devices: 67.7 us -> 71.9 us
  local copies, waits for them, and re-layouts: 8.75 us -> 5.16 us
  waiting for transfers between devices: 100 us -> 97.4 us
    ppermute x46 -> x44, waiting for transfers between devices: 100 us -> 87.5 us  [send_by(): return lax.ppermute(value, axes, pairs)]
    pallas_call x8 -> x5, Pallas kernels: 48.2 us -> 35.3 us  [the longest x3 19.9 us: spread(): pl.pallas_call(lambda *refs: backward_kernel(shards, parts, len(crossed),...]
    ppermute x0 -> x2, waiting for transfers between devices: none -> 9.85 us  [exchange(): lax.ppermute(value, axis, [(i, i ^ mask) for i in range(SIZES[axis])])]
    ppermute x0 -> x2, starting transfers between devices: none -> 3.76 us  [exchange(): lax.ppermute(value, axis, [(i, i ^ mask) for i in range(SIZES[axis])])]
    unnamed x93 -> x69, local copies, waits for them, and re-layouts: 8.57 us -> 4.97 us
    ppermute x46 -> x44, starting transfers between devices: 67.7 us -> 68.1 us  [send_by(): return lax.ppermute(value, axes, pairs)]
  transfers between devices with their start and end apart: 46 -> 46, of which waited for: 20 -> 17; matrix products, arithmetic and copies ran while one was open for 3% -> 3% of each run, Pallas kernels for 12% -> 8%
where the time goes in v3:
time: 224 us; the launch traced here: 223 us
  waiting for transfers between devices  97.4 us (43%)
  starting transfers between devices  71.9 us (32%)
  Pallas kernels  40.2 us (18%)
  other arithmetic  7.32 us (3%)
  local copies, waits for them, and re-layouts  5.16 us (2%)
    ppermute x44, waiting for transfers between devices, send_by(): return lax.ppermute(value, axes, pairs)  87.5 us
    ppermute x44, starting transfers between devices, send_by(): return lax.ppermute(value, axes, pairs)  68.1 us
    pallas_call x3, Pallas kernels, spread(): pl.pallas_call(lambda *refs: backward_kernel(shards, parts, len(crossed),...  19.9 us
    pallas_call x1, Pallas kernels, aggregate(): pl.pallas_call(lambda *refs: forward_kernel(shards, *refs), out_shape=(ja...  12.6 us
    ppermute x2, waiting for transfers between devices, exchange(): lax.ppermute(value, axis, [(i, i ^ mask) for i in range(SIZES[axis])])  9.85 us
    unnamed x69, local copies, waits for them, and re-layouts  4.97 us
    pallas_call x1, Pallas kernels, middle(): pl.pallas_call(middle_kernel, out_shape=(jax.ShapeDtypeStruct((rows, widt...  4.86 us
  transfers between devices with their start and end apart: 46, of which 17 were waited for; matrix products, arithmetic and copies ran while one was open for 3% of the time, Pallas kernels for 8%

profile of v3, /device:TPU:0, one launch (start us, length us, event | category | flops | bytes accessed | tf_op | source)
XLA Modules:
  0.0 223.0 jit_solution(17388023748937668844)
XLA Ops:
  11.3 5.4 %collective-permute-start.5 = (bf16[256,512]{1,0:T(8,128)(2,1)}, bf16[256,512]{1,0:T(8,128)(2,1)S(1)}, u32[]{:S(2)}, u32[]{:S(2)}) collective-permute-start(bf16[256,512]{1,0:T(8,128)(2,1)} %refs_5_.1), channel_id=1, source_target_pairs={{0,112},{16,64},{32,80},{48,96},{64,48},{80,0},{96,16},{112,32},{1... | collective-permute-start | bytes 786440 | tf_op jit(solution)/shard_map/ppermute | solution.py:26
  16.8 8.4 %collective-permute-start.6 = (bf16[256,512]{1,0:T(8,128)(2,1)}, bf16[256,512]{1,0:T(8,128)(2,1)S(1)}, u32[]{:S(2)}, u32[]{:S(2)}) collective-permute-start(bf16[256,512]{1,0:T(8,128)(2,1)} %refs_5_.1), channel_id=1, source_target_pairs={{0,96},{16,112},{32,64},{48,80},{64,32},{80,48},{96,0},{112,16},{1... | collective-permute-start | bytes 786440 | tf_op jit(solution)/shard_map/ppermute | solution.py:26
  28.7 3.8 %collective-permute-done.6.refs_12_ = bf16[256,512]{1,0:T(8,128)(2,1)S(1)} collective-permute-done((bf16[256,512]{1,0:T(8,128)(2,1)}, bf16[256,512]{1,0:T(8,128)(2,1)S(1)}, u32[]{:S(2)}, u32[]{:S(2)}) %collective-permute-start.6) | collective-permute-done | bytes 262176 | tf_op jit(solution)/shard_map/ppermute | solution.py:26
  36.6 12.6 %aggregate.1 = (bf16[256,512]{1,0:T(8,128)(2,1)}, bf16[256,512]{1,0:T(8,128)(2,1)}, bf16[256,512]{1,0:T(8,128)(2,1)}, bf16[256,512]{1,0:T(8,128)(2,1)}, bf16[256...) custom-call(s32[16]{0:T(128)} %compare_select_fusion.19.refs_0_, ...), custom_call_target="tpu_custom_call" | custom-call | flops 8589934592 | bytes 16777216 | tf_op jit(solution)/shard_map/aggregate/pallas_call | solution.py:110
  52.2 5.3 %collective-permute-start.16 = (bf16[256,512]{1,0:T(8,128)(2,1)}, bf16[256,512]{1,0:T(8,128)(2,1)S(1)}, u32[]{:S(2)}, u32[]{:S(2)}) collective-permute-start(bf16[256,512]{1,0:T(8,128)(2,1)} %get-tuple-element.33), channel_id=1, source_target_pairs={{0,2},{1,3},{2,0},{3,1},{4,6},{5,7},{6,4},{7,5},{8,10},{9,11},{10,... | collective-permute-start | bytes 786440 | tf_op jit(solution)/shard_map/ppermute | solution.py:26
  59.2 3.3 %collective-permute-start.19 = (bf16[256,512]{1,0:T(8,128)(2,1)}, bf16[256,512]{1,0:T(8,128)(2,1)S(1)}, u32[]{:S(2)}, u32[]{:S(2)}) collective-permute-start(bf16[256,512]{1,0:T(8,128)(2,1)} %get-tuple-element.36), channel_id=1, source_target_pairs={{0,5},{1,6},{2,7},{3,4},{4,1},{5,2},{6,3},{7,0},{8,13},{9,14},{10,... | collective-permute-start | bytes 786440 | tf_op jit(solution)/shard_map/ppermute | solution.py:26
  65.0 16.2 %collective-permute-done.16.refs_2_ = bf16[256,512]{1,0:T(8,128)(2,1)S(1)} collective-permute-done((bf16[256,512]{1,0:T(8,128)(2,1)}, bf16[256,512]{1,0:T(8,128)(2,1)S(1)}, u32[]{:S(2)}, u32[]{:S(2)}) %collective-permute-start.16) | collective-permute-done | bytes 262176 | tf_op jit(solution)/shard_map/ppermute | solution.py:26
  81.4 10.5 %collective-permute-done.21.refs_7_ = bf16[256,512]{1,0:T(8,128)(2,1)S(1)} collective-permute-done((bf16[256,512]{1,0:T(8,128)(2,1)}, bf16[256,512]{1,0:T(8,128)(2,1)S(1)}, u32[]{:S(2)}, u32[]{:S(2)}) %collective-permute-start.21) | collective-permute-done | bytes 262176 | tf_op jit(solution)/shard_map/ppermute | solution.py:26
  92.6 4.9 %middle.1 = (bf16[256,512]{1,0:T(8,128)(2,1)}, bf16[336,512]{1,0:T(8,128)(2,1)}, bf16[336,512]{1,0:T(8,128)(2,1)}, bf16[336,512]{1,0:T(8,128)(2,1)}, bf16[336,51...) custom-call(s32[8]{0:T(128)} %select_select_fusion.2.refs_3_.place_r, ...), custom_call_target="tpu_custom_call" | custom-call | flops 1073741824 | bytes 8388608 | tf_op jit(solution)/shard_map/middle/pallas_call | solution.py:292
  101.0 3.5 %collective-permute-start.26 = (bf16[336,512]{1,0:T(8,128)(2,1)}, bf16[336,512]{1,0:T(8,128)(2,1)S(1)}, u32[]{:S(2)}, u32[]{:S(2)}) collective-permute-start(bf16[336,512]{1,0:T(8,128)(2,1)} %get-tuple-element.45), channel_id=1, source_target_pairs={{0,5},{1,6},{2,7},{3,4},{4,1},{5,2},{6,3},{7,0},{8,13},{9,14},{10,... | collective-permute-start | bytes 1032200 | tf_op jit(solution)/shard_map/ppermute | solution.py:26
  104.5 18.0 %collective-permute-done.22.refs_5_ = bf16[336,512]{1,0:T(8,128)(2,1)S(1)} collective-permute-done((bf16[336,512]{1,0:T(8,128)(2,1)}, bf16[336,512]{1,0:T(8,128)(2,1)S(1)}, u32[]{:S(2)}, u32[]{:S(2)}) %collective-permute-start.22) | collective-permute-done | bytes 344096 | tf_op jit(solution)/shard_map/ppermute | solution.py:26
  122.5 4.4 %collective-permute-done.23.refs_6_ = bf16[336,512]{1,0:T(8,128)(2,1)S(1)} collective-permute-done((bf16[336,512]{1,0:T(8,128)(2,1)}, bf16[336,512]{1,0:T(8,128)(2,1)S(1)}, u32[]{:S(2)}, u32[]{:S(2)}) %collective-permute-start.23) | collective-permute-done | bytes 344096 | tf_op jit(solution)/shard_map/ppermute | solution.py:26
  128.1 9.4 %collective-permute-done.27.refs_10_ = bf16[336,512]{1,0:T(8,128)(2,1)S(1)} collective-permute-done((bf16[336,512]{1,0:T(8,128)(2,1)}, bf16[336,512]{1,0:T(8,128)(2,1)S(1)}, u32[]{:S(2)}, u32[]{:S(2)}) %collective-permute-start.27) | collective-permute-done | bytes 344096 | tf_op jit(solution)/shard_map/ppermute | solution.py:26
  139.4 5.5 %spread.3 = (bf16[4,256,512]{2,1,0:T(8,128)(2,1)}, f32[72,512]{1,0:T(8,128)}) custom-call(s32[4]{0:T(128)} %compare_select_fusion.27.refs_0_, s32[256]{0:T(256)} %get-tuple-element.58.refs_1_, s32[32]{0:T(128)} %bitcast.12, bf16[32,8,128,128]{3,2,1,0:T(8,128)(2,1)} %bitcast.7, bf16[336,512]{1,0:T(8,128)(2,1)} %get-tuple-element.40.refs_4_, ...), custom_call_target="tpu_custom_call" | custom-call | flops 2147483648 | bytes 4194304 | tf_op jit(solution)/shard_map/spread/pallas_call | solution.py:242
  145.0 5.5 %spread.4 = bf16[4,256,512]{2,1,0:T(8,128)(2,1)} custom-call(s32[4]{0:T(128)} %compare_select_fusion.26.refs_0_, s32[256]{0:T(256)} %get-tuple-element.58.refs_1_, s32[32]{0:T(128)} %bitcast.13, bf16[32,8,128,128]{3,2,1,0:T(8,128)(2,1)} %bitcast.8, bf16[336,512]{1,0:T(8,128)(2,1)} %get-tuple-element.40.refs_4_, bf16[336,512]{1,0:T(8,128)(2,1)} %copy-done, ...), custom_call_target="tpu_custom_call" | custom-call | flops 2147483648 | bytes 4194304 | tf_op jit(solution)/shard_map/spread/pallas_call | solution.py:242
  153.5 3.9 %collective-permute-start.39 = (f32[72,512]{1,0:T(8,128)S(1)}, f32[72,512]{1,0:T(8,128)S(1)}, u32[]{:S(2)}, u32[]{:S(2)}) collective-permute-start(f32[72,512]{1,0:T(8,128)S(1)} %add.575), channel_id=1, source_target_pairs={{0,64},{64,0},{1,65},{65,1},{2,66},{66,2},{3,67},{67,3},{4,68},{68... | collective-permute-start | bytes 442376 | tf_op jit(solution)/shard_map/ppermute | solution.py:26
  157.4 4.3 %collective-permute-done.39 = f32[72,512]{1,0:T(8,128)S(1)} collective-permute-done((f32[72,512]{1,0:T(8,128)S(1)}, f32[72,512]{1,0:T(8,128)S(1)}, u32[]{:S(2)}, u32[]{:S(2)}) %collective-permute-start.39) | collective-permute-done | bytes 147488 | tf_op jit(solution)/shard_map/ppermute | solution.py:26
  161.7 3.6 %collective-permute-start.40 = (f32[72,512]{1,0:T(8,128)S(1)}, f32[72,512]{1,0:T(8,128)S(1)}, u32[]{:S(2)}, u32[]{:S(2)}) collective-permute-start(f32[72,512]{1,0:T(8,128)S(1)} %add.576), channel_id=1, source_target_pairs={{0,16},{16,0},{32,48},{48,32},{1,17},{17,1},{33,49},{49,33},{2,18}... | collective-permute-start | bytes 442376 | tf_op jit(solution)/shard_map/ppermute | solution.py:30
  165.3 3.8 %collective-permute-done.40 = f32[72,512]{1,0:T(8,128)S(1)} collective-permute-done((f32[72,512]{1,0:T(8,128)S(1)}, f32[72,512]{1,0:T(8,128)S(1)}, u32[]{:S(2)}, u32[]{:S(2)}) %collective-permute-start.40) | collective-permute-done | bytes 147488 | tf_op jit(solution)/shard_map/ppermute | solution.py:30
  169.8 6.0 %collective-permute-done.41 = f32[72,512]{1,0:T(8,128)S(1)} collective-permute-done((f32[72,512]{1,0:T(8,128)S(1)}, f32[72,512]{1,0:T(8,128)S(1)}, u32[]{:S(2)}, u32[]{:S(2)}) %collective-permute-start.41) | collective-permute-done | bytes 147488 | tf_op jit(solution)/shard_map/ppermute | solution.py:30
  178.0 8.9 %spread.5 = (bf16[256,512]{1,0:T(8,128)(2,1)}, bf16[256,512]{1,0:T(8,128)(2,1)}, bf16[256,512]{1,0:T(8,128)(2,1)}, bf16[256,512]{1,0:T(8,128)(2,1)}, bf16[256,51...) custom-call(s32[8]{0:T(128)} %select_select_fusion.1.refs_0_, ...), custom_call_target="tpu_custom_call" | custom-call | flops 4294967296 | bytes 8388608 | tf_op jit(solution)/shard_map/spread/pallas_call | solution.py:242
  190.0 3.9 %collective-permute-start.44 = (bf16[128,512]{1,0:T(8,128)(2,1)S(1)}, bf16[128,512]{1,0:T(8,128)(2,1)S(1)}, u32[]{:S(2)}, u32[]{:S(2)}) collective-permute-start(bf16[128,512]{1,0:T(8,128)(2,1)S(1)} %pad_maximum_fusion.refs_1_), channel_id=1, source_target_pairs={{0,2},{1,3},{2,0},{3,1},{4,6},{5,7},{6,4},{7,5},{8,10},{9,11},{10,... | collective-permute-start | bytes 393224 | tf_op jit(solution)/shard_map/ppermute | solution.py:26
  198.2 3.6 %collective-permute-start.34 = (bf16[256,512]{1,0:T(8,128)(2,1)}, bf16[256,512]{1,0:T(8,128)(2,1)S(1)}, u32[]{:S(2)}, u32[]{:S(2)}) collective-permute-start(bf16[256,512]{1,0:T(8,128)(2,1)} %get-tuple-element.52), channel_id=1, source_target_pairs={{0,96},{16,112},{32,64},{48,80},{64,32},{80,48},{96,0},{112,16},{1... | collective-permute-start | bytes 786440 | tf_op jit(solution)/shard_map/ppermute | solution.py:26
  208.6 12.4 %collective-permute-done.35 = bf16[256,512]{1,0:T(8,128)(2,1)S(1)} collective-permute-done((bf16[256,512]{1,0:T(8,128)(2,1)}, bf16[256,512]{1,0:T(8,128)(2,1)S(1)}, u32[]{:S(2)}, u32[]{:S(2)}) %collective-permute-start.35) | collective-permute-done | bytes 262176 | tf_op jit(solution)/shard_map/ppermute | solution.py:26
  (161 shorter events, 54.6 us)
Async XLA Ops:
  4.9 20.3 %collective-permute-start.2 = (bf16[256,512]{1,0:T(8,128)(2,1)}, bf16[256,512]{1,0:T(8,128)(2,1)S(1)}, u32[]{:S(2)}, u32[]{:S(2)}) collective-permute-start(bf16[256,512]{1,0:T(8,128)(2,1)} %refs_5_.1), channel_id=1, source_target_pairs={{0,64},{16,80},{32,96},{48,112},{64,0},{80,16},{96,32},{112,48},{1... | collective-permute-start | bytes 786440 | tf_op jit(solution)/shard_map/ppermute | solution.py:26
  6.4 20.2 %collective-permute-start.3 = (bf16[256,512]{1,0:T(8,128)(2,1)}, bf16[256,512]{1,0:T(8,128)(2,1)S(1)}, u32[]{:S(2)}, u32[]{:S(2)}) collective-permute-start(bf16[256,512]{1,0:T(8,128)(2,1)} %refs_5_.1), channel_id=1, source_target_pairs={{0,32},{16,48},{32,0},{48,16},{64,96},{80,112},{96,64},{112,80},{1... | collective-permute-start | bytes 786440 | tf_op jit(solution)/shard_map/ppermute | solution.py:26
  8.2 18.5 %collective-permute-start.4 = (bf16[256,512]{1,0:T(8,128)(2,1)}, bf16[256,512]{1,0:T(8,128)(2,1)S(1)}, u32[]{:S(2)}, u32[]{:S(2)}) collective-permute-start(bf16[256,512]{1,0:T(8,128)(2,1)} %refs_5_.1), channel_id=1, source_target_pairs={{0,80},{16,96},{32,112},{48,64},{64,16},{80,32},{96,48},{112,0},{1... | collective-permute-start | bytes 786440 | tf_op jit(solution)/shard_map/ppermute | solution.py:26
  11.3 17.3 %collective-permute-start.5 = (bf16[256,512]{1,0:T(8,128)(2,1)}, bf16[256,512]{1,0:T(8,128)(2,1)S(1)}, u32[]{:S(2)}, u32[]{:S(2)}) collective-permute-start(bf16[256,512]{1,0:T(8,128)(2,1)} %refs_5_.1), channel_id=1, source_target_pairs={{0,112},{16,64},{32,80},{48,96},{64,48},{80,0},{96,16},{112,32},{1... | collective-permute-start | bytes 786440 | tf_op jit(solution)/shard_map/ppermute | solution.py:26
  16.8 15.7 %collective-permute-start.6 = (bf16[256,512]{1,0:T(8,128)(2,1)}, bf16[256,512]{1,0:T(8,128)(2,1)S(1)}, u32[]{:S(2)}, u32[]{:S(2)}) collective-permute-start(bf16[256,512]{1,0:T(8,128)(2,1)} %refs_5_.1), channel_id=1, source_target_pairs={{0,96},{16,112},{32,64},{48,80},{64,32},{80,48},{96,0},{112,16},{1... | collective-permute-start | bytes 786440 | tf_op jit(solution)/shard_map/ppermute | solution.py:26
  52.2 29.1 %collective-permute-start.16 = (bf16[256,512]{1,0:T(8,128)(2,1)}, bf16[256,512]{1,0:T(8,128)(2,1)S(1)}, u32[]{:S(2)}, u32[]{:S(2)}) collective-permute-start(bf16[256,512]{1,0:T(8,128)(2,1)} %get-tuple-element.33), channel_id=1, source_target_pairs={{0,2},{1,3},{2,0},{3,1},{4,6},{5,7},{6,4},{7,5},{8,10},{9,11},{10,... | collective-permute-start | bytes 786440 | tf_op jit(solution)/shard_map/ppermute | solution.py:26
  57.5 23.8 %collective-permute-start.17 = (bf16[256,512]{1,0:T(8,128)(2,1)}, bf16[256,512]{1,0:T(8,128)(2,1)S(1)}, u32[]{:S(2)}, u32[]{:S(2)}) collective-permute-start(bf16[256,512]{1,0:T(8,128)(2,1)} %get-tuple-element.34), channel_id=1, source_target_pairs={{0,3},{1,0},{2,1},{3,2},{4,7},{5,4},{6,5},{7,6},{8,11},{9,8},{10,9... | collective-permute-start | bytes 786440 | tf_op jit(solution)/shard_map/ppermute | solution.py:26
  57.5 23.8 %collective-permute-start.18 = (bf16[256,512]{1,0:T(8,128)(2,1)}, bf16[256,512]{1,0:T(8,128)(2,1)S(1)}, u32[]{:S(2)}, u32[]{:S(2)}) collective-permute-start(bf16[256,512]{1,0:T(8,128)(2,1)} %get-tuple-element.35), channel_id=1, source_target_pairs={{0,4},{1,5},{2,6},{3,7},{4,0},{5,1},{6,2},{7,3},{8,12},{9,13},{10,... | collective-permute-start | bytes 786440 | tf_op jit(solution)/shard_map/ppermute | solution.py:26
  59.2 22.2 %collective-permute-start.19 = (bf16[256,512]{1,0:T(8,128)(2,1)}, bf16[256,512]{1,0:T(8,128)(2,1)S(1)}, u32[]{:S(2)}, u32[]{:S(2)}) collective-permute-start(bf16[256,512]{1,0:T(8,128)(2,1)} %get-tuple-element.36), channel_id=1, source_target_pairs={{0,5},{1,6},{2,7},{3,4},{4,1},{5,2},{6,3},{7,0},{8,13},{9,14},{10,... | collective-permute-start | bytes 786440 | tf_op jit(solution)/shard_map/ppermute | solution.py:26
  63.2 18.1 %collective-permute-start.20 = (bf16[256,512]{1,0:T(8,128)(2,1)}, bf16[256,512]{1,0:T(8,128)(2,1)S(1)}, u32[]{:S(2)}, u32[]{:S(2)}) collective-permute-start(bf16[256,512]{1,0:T(8,128)(2,1)} %get-tuple-element.37), channel_id=1, source_target_pairs={{0,6},{1,7},{2,4},{3,5},{4,2},{5,3},{6,0},{7,1},{8,14},{9,15},{10,... | collective-permute-start | bytes 786440 | tf_op jit(solution)/shard_map/ppermute | solution.py:26
  97.4 25.0 %collective-permute-start.22 = (bf16[336,512]{1,0:T(8,128)(2,1)}, bf16[336,512]{1,0:T(8,128)(2,1)S(1)}, u32[]{:S(2)}, u32[]{:S(2)}) collective-permute-start(bf16[336,512]{1,0:T(8,128)(2,1)} %get-tuple-element.41), channel_id=1, source_target_pairs={{0,1},{1,2},{2,3},{3,0},{4,5},{5,6},{6,7},{7,4},{8,9},{9,10},{10,1... | collective-permute-start | bytes 1032200 | tf_op jit(solution)/shard_map/ppermute | solution.py:26
  97.4 29.4 %collective-permute-start.23 = (bf16[336,512]{1,0:T(8,128)(2,1)}, bf16[336,512]{1,0:T(8,128)(2,1)S(1)}, u32[]{:S(2)}, u32[]{:S(2)}) collective-permute-start(bf16[336,512]{1,0:T(8,128)(2,1)} %get-tuple-element.42), channel_id=1, source_target_pairs={{0,2},{1,3},{2,0},{3,1},{4,6},{5,7},{6,4},{7,5},{8,10},{9,11},{10,... | collective-permute-start | bytes 1032200 | tf_op jit(solution)/shard_map/ppermute | solution.py:26
  97.5 30.6 %collective-permute-start.24 = (bf16[336,512]{1,0:T(8,128)(2,1)}, bf16[336,512]{1,0:T(8,128)(2,1)S(1)}, u32[]{:S(2)}, u32[]{:S(2)}) collective-permute-start(bf16[336,512]{1,0:T(8,128)(2,1)} %get-tuple-element.43), channel_id=1, source_target_pairs={{0,3},{1,0},{2,1},{3,2},{4,7},{5,4},{6,5},{7,6},{8,11},{9,8},{10,9... | collective-permute-start | bytes 1032200 | tf_op jit(solution)/shard_map/ppermute | solution.py:26
  100.7 27.4 %collective-permute-start.25 = (bf16[336,512]{1,0:T(8,128)(2,1)}, bf16[336,512]{1,0:T(8,128)(2,1)S(1)}, u32[]{:S(2)}, u32[]{:S(2)}) collective-permute-start(bf16[336,512]{1,0:T(8,128)(2,1)} %get-tuple-element.44), channel_id=1, source_target_pairs={{0,4},{1,5},{2,6},{3,7},{4,0},{5,1},{6,2},{7,3},{8,12},{9,13},{10,... | collective-permute-start | bytes 1032200 | tf_op jit(solution)/shard_map/ppermute | solution.py:26
  101.0 27.2 %collective-permute-start.26 = (bf16[336,512]{1,0:T(8,128)(2,1)}, bf16[336,512]{1,0:T(8,128)(2,1)S(1)}, u32[]{:S(2)}, u32[]{:S(2)}) collective-permute-start(bf16[336,512]{1,0:T(8,128)(2,1)} %get-tuple-element.45), channel_id=1, source_target_pairs={{0,5},{1,6},{2,7},{3,4},{4,1},{5,2},{6,3},{7,0},{8,13},{9,14},{10,... | collective-permute-start | bytes 1032200 | tf_op jit(solution)/shard_map/ppermute | solution.py:26
  144.9 31.1 %collective-permute-start.29 = (bf16[4,256,512]{2,1,0:T(8,128)(2,1)}, bf16[4,256,512]{2,1,0:T(8,128)(2,1)S(1)}, u32[]{:S(2)}, u32[]{:S(2)}) collective-permute-start(bf16[4,256,512]{2,1,0:T(8,128)(2,1)} %get-tuple-element.48), channel_id=1, source_target_pairs={{0,8},{8,0},{1,9},{9,1},{2,10},{10,2},{3,11},{11,3},{4,12},{12,4},... | collective-permute-start | bytes 3145736 | tf_op jit(solution)/shard_map/ppermute | solution.py:26
  150.5 25.5 %collective-permute-start.30 = (bf16[4,256,512]{2,1,0:T(8,128)(2,1)}, bf16[4,256,512]{2,1,0:T(8,128)(2,1)S(1)}, u32[]{:S(2)}, u32[]{:S(2)}) collective-permute-start(bf16[4,256,512]{2,1,0:T(8,128)(2,1)} %spread.4), channel_id=1, source_target_pairs={{0,8},{8,0},{1,9},{9,1},{2,10},{10,2},{3,11},{11,3},{4,12},{12,4},... | collective-permute-start | bytes 3145736 | tf_op jit(solution)/shard_map/ppermute | solution.py:26
  186.9 15.9 %collective-permute-start.37 = (bf16[256,512]{1,0:T(8,128)(2,1)}, bf16[256,512]{1,0:T(8,128)(2,1)S(1)}, u32[]{:S(2)}, u32[]{:S(2)}) collective-permute-start(bf16[256,512]{1,0:T(8,128)(2,1)} %get-tuple-element.56), channel_id=1, source_target_pairs={{0,64},{16,80},{32,96},{48,112},{64,0},{80,16},{96,32},{112,48},{1... | collective-permute-start | bytes 786440 | tf_op jit(solution)/shard_map/ppermute | solution.py:26
  189.2 15.5 %collective-permute-start.36 = (bf16[256,512]{1,0:T(8,128)(2,1)}, bf16[256,512]{1,0:T(8,128)(2,1)S(1)}, u32[]{:S(2)}, u32[]{:S(2)}) collective-permute-start(bf16[256,512]{1,0:T(8,128)(2,1)} %get-tuple-element.55), channel_id=1, source_target_pairs={{0,48},{16,0},{32,16},{48,32},{64,112},{80,64},{96,80},{112,96},{1... | collective-permute-start | bytes 786440 | tf_op jit(solution)/shard_map/ppermute | solution.py:26
  196.4 24.6 %collective-permute-start.35 = (bf16[256,512]{1,0:T(8,128)(2,1)}, bf16[256,512]{1,0:T(8,128)(2,1)S(1)}, u32[]{:S(2)}, u32[]{:S(2)}) collective-permute-start(bf16[256,512]{1,0:T(8,128)(2,1)} %get-tuple-element.54), channel_id=1, source_target_pairs={{0,16},{16,32},{32,48},{48,0},{64,80},{80,96},{96,112},{112,64},{1... | collective-permute-start | bytes 786440 | tf_op jit(solution)/shard_map/ppermute | solution.py:26
  198.2 22.9 %collective-permute-start.34 = (bf16[256,512]{1,0:T(8,128)(2,1)}, bf16[256,512]{1,0:T(8,128)(2,1)S(1)}, u32[]{:S(2)}, u32[]{:S(2)}) collective-permute-start(bf16[256,512]{1,0:T(8,128)(2,1)} %get-tuple-element.52), channel_id=1, source_target_pairs={{0,96},{16,112},{32,64},{48,80},{64,32},{80,48},{96,0},{112,16},{1... | collective-permute-start | bytes 786440 | tf_op jit(solution)/shard_map/ppermute | solution.py:26
  201.8 19.2 %collective-permute-start.33 = (bf16[256,512]{1,0:T(8,128)(2,1)}, bf16[256,512]{1,0:T(8,128)(2,1)S(1)}, u32[]{:S(2)}, u32[]{:S(2)}) collective-permute-start(bf16[256,512]{1,0:T(8,128)(2,1)} %get-tuple-element.51), channel_id=1, source_target_pairs={{0,112},{16,64},{32,80},{48,96},{64,48},{80,0},{96,16},{112,32},{1... | collective-permute-start | bytes 786440 | tf_op jit(solution)/shard_map/ppermute | solution.py:26
  202.8 18.3 %collective-permute-start.32 = (bf16[256,512]{1,0:T(8,128)(2,1)}, bf16[256,512]{1,0:T(8,128)(2,1)S(1)}, u32[]{:S(2)}, u32[]{:S(2)}) collective-permute-start(bf16[256,512]{1,0:T(8,128)(2,1)} %get-tuple-element.50), channel_id=1, source_target_pairs={{0,80},{16,96},{32,112},{48,64},{64,16},{80,32},{96,48},{112,0},{1... | collective-permute-start | bytes 786440 | tf_op jit(solution)/shard_map/ppermute | solution.py:26
  204.7 16.3 %collective-permute-start.31 = (bf16[256,512]{1,0:T(8,128)(2,1)}, bf16[256,512]{1,0:T(8,128)(2,1)S(1)}, u32[]{:S(2)}, u32[]{:S(2)}) collective-permute-start(bf16[256,512]{1,0:T(8,128)(2,1)} %get-tuple-element.49), channel_id=1, source_target_pairs={{0,32},{16,48},{32,0},{48,16},{64,96},{80,112},{96,64},{112,80},{1... | collective-permute-start | bytes 786440 | tf_op jit(solution)/shard_map/ppermute | solution.py:26
  (56 other events, 458.5 us)

commit v4 on v3

--- a/solution.py
+++ b/solution.py
@@ -42,6 +42,14 @@
     return pl.CostEstimate(flops=flops, transcendentals=0, bytes_accessed=transferred)
 
 
+class Window:
+    def __init__(self, ref, base, length):
+        self.ref, self.base, self.shape = ref, base, (length,)
+
+    def __getitem__(self, i):
+        return self.ref[self.base + i]
+
+
 def of_class(count, action):
     low = 0
     for n in VARIANTS:
@@ -66,11 +74,14 @@
     lax.fori_loop(0, v_buf.shape[0], step, 0)
 
 
-def forward_kernel(shards, source_ref, slot_ref, count_ref, place_ref, v_ref, *refs):
+def forward_kernel(shards, at_source, at_place, index_ref, target_ref, count_ref, v_ref, *refs):
+    source_ref = Window(index_ref, at_source, shards)
+    place_ref = Window(index_ref, at_place, len(refs) - 5 - shards)
     x_refs, refs = refs[:shards], refs[shards:]
     acc_ref, x_buf, v_buf, x_sem, v_sem = refs[-5:]
     out_refs = refs[:-5]
-    slots, tile = v_ref.shape[1:3]
+    tile = v_ref.shape[-1]
+    dummy = acc_ref.shape[0] - 1
     for i in range(shards):
         pltpu.make_async_copy(x_refs[i], x_buf.at[i], x_sem.at[i]).start()
     start_tiles(source_ref, count_ref, v_ref, v_buf, v_sem)
@@ -89,7 +100,8 @@
             tiles = v_buf[k, pl.ds(0, n)].reshape(n * tile, tile)
             product = jnp.dot(tiles, rows, preferred_element_type=jnp.float32)
             for m in range(n):
-                acc_ref[slot_ref[group * slots + m]] += product[m * tile : (m + 1) * tile]
+                to = jnp.where(m < count_ref[group], target_ref[group, m], dummy)
+                acc_ref[to] += product[m * tile : (m + 1) * tile]
 
         of_class(count_ref[group], work)
         return carry
@@ -100,18 +112,17 @@
             out_ref[pl.ds(t * tile, tile), :] = acc_ref[place_ref[i] * 2 + t].astype(out_ref.dtype)
 
 
-def aggregate(sources, slots, counts, places, gathered, values):
+def aggregate(at_source, at_place, parts, index, targets, counts, gathered, values):
     shards = len(gathered)
     rows, width = gathered[0].shape
     _, slot_total, tile, _ = values.shape
-    parts = places.shape[0]
     anywhere = pl.BlockSpec(memory_space=pl.ANY)
     inside = pl.BlockSpec(memory_space=pltpu.VMEM)
     return pl.pallas_call(
-        lambda *refs: forward_kernel(shards, *refs),
+        lambda *refs: forward_kernel(shards, at_source, at_place, *refs),
         out_shape=(jax.ShapeDtypeStruct((rows, width), jnp.bfloat16),) * parts,
         grid_spec=pltpu.PrefetchScalarGridSpec(
-            num_scalar_prefetch=4,
+            num_scalar_prefetch=3,
             grid=(),
             in_specs=[anywhere] * (1 + shards),
             out_specs=(inside,) * parts,
@@ -126,22 +137,21 @@
         compiler_params=pltpu.CompilerParams(vmem_limit_bytes=VMEM),
         cost_estimate=cost(8 << 30, 16 << 20),
         name="aggregate",
-    )(sources, slots, counts, places, values, *gathered)
-
-
-def backward_kernel(shards, parts, crossing, with_weight, *refs):
-    source_ref, slot_ref, count_ref, v_ref = refs[:4]
+    )(index, targets, counts, values, *gathered)
+
+
+def backward_kernel(shards, parts, at_source, at_turn, crossing, *refs):
+    index_ref, target_ref, count_ref, v_ref = refs[:4]
+    source_ref = Window(index_ref, at_source, shards)
     m_refs, refs = refs[4 : 4 + parts], refs[4 + parts :]
     if crossing:
         crossed_refs, refs = refs[:crossing], refs[crossing:]
         out_refs, refs = refs[:shards], refs[shards:]
     else:
         out_ref, refs = refs[0], refs[1:]
-        if with_weight:
-            sum_ref, refs = refs[0], refs[1:]
     table_ref, v_buf, m_sem, v_sem = refs[:4]
     refs = refs[4:]
-    slots, tile = v_ref.shape[1:3]
+    tile = v_ref.shape[-1]
     rows = 2 * tile
     for i in range(parts):
         pltpu.make_async_copy(m_refs[i].at[pl.ds(0, rows)], table_ref.at[pl.ds(i * rows, rows)], m_sem.at[i]).start()
@@ -151,11 +161,6 @@
         each = shards // crossing
         for i in range(crossing):
             pltpu.make_async_copy(crossed_refs[i], cross_buf.at[pl.ds(i * each, each)], cross_sem.at[i]).start()
-    elif with_weight:
-        w_buf, w_sem = refs
-        more = w_buf.shape[1]
-        for i in range(parts):
-            pltpu.make_async_copy(m_refs[i].at[pl.ds(rows, more)], w_buf.at[i], w_sem.at[i]).start()
     blank = table_ref.at[pl.ds(parts * rows, tile)]
     blank[...] = jnp.zeros_like(blank)
     for i in range(parts):
@@ -172,9 +177,12 @@
         def work(n):
             tiles_copy(v_ref, v_buf, v_sem, group, k, n).wait()
             tiles = v_buf[k, pl.ds(0, n)].reshape(n * tile, tile)
-            found = [
-                table_ref[pl.ds(pl.multiple_of(slot_ref[group * slots + m] * tile, tile), tile), :] for m in range(n)
-            ]
+            found = []
+            for m in range(n):
+                target = target_ref[group, m]
+                held = index_ref[at_turn + target // 2] * 2 + target % 2
+                held = jnp.where(m < count_ref[group], held, 2 * parts)
+                found.append(table_ref[pl.ds(pl.multiple_of(held * tile, tile), tile), :])
             found = jnp.concatenate(found, axis=0) if n > 1 else found[0]
             product = lax.dot_general(tiles, found, (((0,), (0,)), ((), ())), preferred_element_type=jnp.float32)
             if crossing:
@@ -189,18 +197,44 @@
     if crossing:
         for i in range(shards):
             out_refs[i][...] = term_ref[i]
-    elif with_weight:
-        total = None
-        for i in range(parts):
-            pltpu.make_async_copy(m_refs[i].at[pl.ds(rows, more)], w_buf.at[i], w_sem.at[i]).wait()
-            term = w_buf[i].astype(jnp.float32)
-            total = term if total is None else total + term
-        share = more - EXTRA
-        sum_ref[pl.ds(0, share), :] = total[:share]
-        bias = total[share : share + 1] + total[share + 1 : share + 2]
-        sum_ref[pl.ds(share, sum_ref.shape[0] - share), :] = jnp.broadcast_to(
-            bias, (sum_ref.shape[0] - share, bias.shape[1])
-        )
+
+
+def share_kernel(*refs):
+    m_refs, (sum_ref, w_buf, w_sem) = refs[:-3], refs[-3:]
+    more = w_buf.shape[1]
+    copies = [
+        pltpu.make_async_copy(m_ref.at[pl.ds(m_ref.shape[0] - more, more)], w_buf.at[i], w_sem.at[i])
+        for i, m_ref in enumerate(m_refs)
+    ]
+    for copy in copies:
+        copy.start()
+    total = None
+    for i, copy in enumerate(copies):
+        copy.wait()
+        term = w_buf[i].astype(jnp.float32)
+        total = term if total is None else total + term
+    share = more - EXTRA
+    sum_ref[pl.ds(0, share), :] = total[:share]
+    bias = total[share : share + 1] + total[share + 1 : share + 2]
+    rest = sum_ref.shape[0] - share
+    sum_ref[pl.ds(share, rest), :] = jnp.broadcast_to(bias, (rest, bias.shape[1]))
+
+
+def add_shares(messages, share):
+    width = messages[0].shape[1]
+    return pl.pallas_call(
+        share_kernel,
+        out_shape=jax.ShapeDtypeStruct((share + 8, width), jnp.float32),
+        in_specs=[pl.BlockSpec(memory_space=pl.ANY)] * len(messages),
+        out_specs=pl.BlockSpec(memory_space=pltpu.VMEM),
+        scratch_shapes=[
+            pltpu.VMEM((len(messages), share + EXTRA, width), jnp.bfloat16),
+            pltpu.SemaphoreType.DMA((len(messages),)),
+        ],
+        compiler_params=pltpu.CompilerParams(vmem_limit_bytes=VMEM),
+        cost_estimate=cost(1 << 20, 1 << 20),
+        name="add_shares",
+    )(*messages)
 
 
 def split_rows(row):
@@ -212,10 +246,9 @@
     return jnp.where(line == 0, spread_high, jnp.where(line == 1, spread_low, 0.0)).astype(jnp.bfloat16)
 
 
-def spread(sources, slots, counts, messages, values, crossed=(), with_weight=False):
+def spread(shards, at_source, at_turn, index, targets, counts, messages, values, crossed=()):
     parts = len(messages)
-    shards = sources.shape[0]
-    height, width = messages[0].shape
+    width = messages[0].shape[1]
     slot_total, tile = values.shape[1:3]
     rows = 2 * tile
     anywhere = pl.BlockSpec(memory_space=pl.ANY)
@@ -235,12 +268,10 @@
         ]
     else:
         out_shape = (jax.ShapeDtypeStruct((shards, rows, width), jnp.bfloat16),)
-        if with_weight:
-            more = height - rows
-            out_shape += (jax.ShapeDtypeStruct((more - EXTRA + 8, width), jnp.float32),)
-            scratch += [pltpu.VMEM((parts, more, width), jnp.bfloat16), pltpu.SemaphoreType.DMA((parts,))]
     return pl.pallas_call(
-        lambda *refs: backward_kernel(shards, parts, len(crossed), with_weight, *refs),
+        lambda *refs: backward_kernel(
+            shards, parts, at_source, at_turn, len(crossed), *refs
+        ),
         out_shape=out_shape,
         grid_spec=pltpu.PrefetchScalarGridSpec(
             num_scalar_prefetch=3,
@@ -252,11 +283,11 @@
         compiler_params=pltpu.CompilerParams(vmem_limit_bytes=VMEM),
         cost_estimate=cost(shards << 29, shards << 20),
         name="spread",
-    )(sources, slots, counts, values, *messages, *crossed)
-
-
-def middle_kernel(place_ref, *refs):
-    parts = place_ref.shape[0]
+    )(index, targets, counts, values, *messages, *crossed)
+
+
+def middle_kernel(parts, at_place, index_ref, *refs):
+    place_ref = Window(index_ref, at_place, parts)
     part_refs, refs = refs[:parts], refs[parts:]
     weight_ref, bias_ref, cotangent_ref, out_ref = refs[:4]
     message_refs, part_ref = refs[4 : 4 + parts], refs[4 + parts]
@@ -284,13 +315,13 @@
         message_ref[pl.ds(high + share, EXTRA), :] = tail
 
 
-def middle(places, sums, weight, layer_bias, cotangent):
+def middle(at_place, index, sums, weight, layer_bias, cotangent):
     rows, width = cotangent.shape
     parts = len(sums)
     inside = pl.BlockSpec(memory_space=pltpu.VMEM)
     message = jax.ShapeDtypeStruct((rows + width // parts + EXTRA, width), jnp.bfloat16)
     return pl.pallas_call(
-        middle_kernel,
+        lambda *refs: middle_kernel(parts, at_place, *refs),
         out_shape=(jax.ShapeDtypeStruct((rows, width), jnp.bfloat16),) + (message,) * parts,
         grid_spec=pltpu.PrefetchScalarGridSpec(
             num_scalar_prefetch=1,
@@ -302,47 +333,62 @@
         compiler_params=pltpu.CompilerParams(vmem_limit_bytes=VMEM),
         cost_estimate=cost(1 << 30, 8 << 20),
         name="middle",
-    )(places, *sums, weight, layer_bias[None, :], cotangent)
-
-
-def place_kernel(scale, share, place_ref, *refs):
+    )(index, *sums, weight, layer_bias[None, :], cotangent)
+
+
+def place_kernel(scale, share, at_place, index_ref, *refs):
+    place_ref = Window(index_ref, at_place, refs[-1].shape[0] // share)
     for i, piece in enumerate(refs[:-1]):
         for k in range(piece.shape[0] // share):
             at = pl.multiple_of(place_ref[2 * i + k] * share, share)
             refs[-1][pl.ds(at, share), :] = piece[pl.ds(k * share, share), :].astype(jnp.float32) * scale
 
 
-def place(places, pieces, share, scale):
+def place(at_place, count, index, pieces, share, scale):
     width = pieces[0].shape[1]
     inside = pl.BlockSpec(memory_space=pltpu.VMEM)
     return pl.pallas_call(
-        lambda *refs: place_kernel(scale, share, *refs),
-        out_shape=jax.ShapeDtypeStruct((share * places.shape[0], width), jnp.float32),
+        lambda *refs: place_kernel(scale, share, at_place, *refs),
+        out_shape=jax.ShapeDtypeStruct((share * count, width), jnp.float32),
         grid_spec=pltpu.PrefetchScalarGridSpec(
             num_scalar_prefetch=1, grid=(), in_specs=[inside] * len(pieces), out_specs=inside
         ),
         compiler_params=pltpu.CompilerParams(vmem_limit_bytes=VMEM),
         name="place",
-    )(places, *pieces)
+    )(index, *pieces)
 
 
 CHIP_HALVES = (((0, 0), (0, 1), (0, 3), (1, 0)), ((0, 2), (1, 1), (1, 3), (1, 2)))
 
 
-def at_offset(axes, offsets, sign):
-    flat = jnp.int32(0)
-    for axis, offset in zip(axes, offsets):
-        n = SIZES[axis]
-        flat = flat * n + (lax.axis_index(axis) + (n + sign * offset)) % n
-    return flat
-
-
-def listed(values):
-    line = lax.iota(jnp.int32, len(values))
-    found = jnp.zeros_like(line)
-    for i, value in enumerate(values):
-        found = jnp.where(line == i, value, found)
-    return found
+def lists_of_numbers(halves, chips, parts):
+    table, begin = [], {}
+    for place in itertools.product(*[range(n) for n in SIZES.values()]):
+        at = dict(zip(SIZES, place))
+
+        def number(axes, offsets, sign):
+            flat = 0
+            for axis, offset in zip(axes, offsets):
+                flat = flat * SIZES[axis] + (at[axis] + sign * offset) % SIZES[axis]
+            return flat
+
+        core = at["core"]
+        come = [number(CHIP, o, -1) * 2 for o in chips]
+        go = [number(CHIP, o, 1) * 2 for o in halves[0] + halves[1]]
+        lists = {
+            "come": [c + core for c in come] + [c + 1 - core for c in come],
+            "to": [number(REP, o, 1) for o in parts],
+            "cross": [c + 1 - core for c in go],
+            "stay": [c + core for c in go],
+            "turn": [(at["xh"] - o[0]) % SIZES["xh"] * SIZES["y"] + (at["y"] - o[1]) % SIZES["y"] for o in parts],
+            "piece": [number(REP, (k, o), -1) for o in range(SIZES["y"]) for k in range(SIZES["xh"])],
+        }
+        row = []
+        for name, numbers in lists.items():
+            begin[name] = len(row)
+            row += numbers
+        table.append(row)
+    return np.asarray(table, np.int32), begin
 
 
 def body(features, weight, layer_bias, tile_values, tile_target, tile_counts, cotangent):
@@ -354,57 +400,50 @@
     slot_total = values.shape[1]
     assert local_rows == 2 * tile and slot_total == VARIANTS[-1]
     parts = all_offsets(REP)
-    dest_tiles = 2 * len(parts)
-
-    active = lax.broadcasted_iota(jnp.int32, targets.shape, 1) < counts[:, None]
-    slots = jnp.where(active, targets, dest_tiles).reshape(-1)
-    owner = targets // 2
-    xh, y = SIZES["xh"], SIZES["y"]
-    from_part = ((lax.axis_index("xh") + xh - owner // y) % xh) * y + (lax.axis_index("y") + y - owner % y) % y
-    back_slots = jnp.where(active, from_part * 2 + targets % 2, dest_tiles).reshape(-1)
-    core = lax.axis_index("core")
-    part_to = listed([at_offset(REP, o, 1) for o in parts])
-
+    halves = CHIP_HALVES[::-1]
     chips = CHIP_HALVES[0] + CHIP_HALVES[1]
+    y = SIZES["y"]
+    table, begin = lists_of_numbers(halves, chips, parts)
+    index = lax.dynamic_slice_in_dim(jnp.asarray(table), lax.axis_index(ALL), 1)[0]
+
     own = [send_by(features, CHIP, o) if any(o) else features for o in chips]
     crossed = [send_by(x, ("core",), (1,)) for x in own]
-    at = [at_offset(CHIP, o, -1) * 2 for o in chips]
-    sources = listed([c + core for c in at] + [c + 1 - core for c in at])
-    partial = aggregate(sources, slots, counts, part_to, own + crossed, values)
+    partial = aggregate(begin["come"], begin["to"], len(parts), index, targets, counts, own + crossed, values)
 
     received = [send_by(partial[i], REP, o) if any(o) else partial[i] for i, o in enumerate(parts)]
-    output, *messages = middle(part_to, received, weight, layer_bias, cotangent)
+    output, *messages = middle(begin["to"], index, received, weight, layer_bias, cotangent)
     messages = [send_by(messages[i], REP, o) if any(o) else messages[i] for i, o in enumerate(parts)]
 
-    halves = CHIP_HALVES[::-1]
-    to_chip = [[at_offset(CHIP, o, 1) * 2 for o in half] for half in halves]
-    across = []
-    for i in range(2):
-        sources = listed([c + 1 - core for c in to_chip[i]])
-        found = spread(sources, back_slots, counts, messages, values, with_weight=i == 0)
-        across.append(send_by(found[0], ("core",), (1,)))
-        if i == 0:
-            share_sum = found[1]
-    sources = listed([c + core for c in to_chip[0] + to_chip[1]])
-    merged = spread(sources, back_slots, counts, messages, values, across)
+    share = width // len(parts)
+    share_sum = add_shares(messages, share)
+    steps = (("xl", 1), ("z", 1), ("z", 2))
+    across, each = [], len(halves[0])
+    for i, step in enumerate(steps):
+        index, share_sum = lax.optimization_barrier((index, share_sum))
+        arriving = exchange(share_sum, *step)
+        if i < 2:
+            found = spread(each, begin["cross"] + each * i, begin["turn"], index, targets, counts, messages, values)
+            across.append(send_by(found[0], ("core",), (1,)))
+        else:
+            found = spread(
+                2 * each, begin["stay"], begin["turn"], index, targets, counts, messages, values, across
+            )
+        _, share_sum, arriving = lax.optimization_barrier((found, share_sum, arriving))
+        share_sum = share_sum + arriving
+    merged = found
     total = None
     for piece, o in zip(merged, halves[0] + halves[1]):
         piece = (send_by(piece, CHIP, o) if any(o) else piece).astype(jnp.float32)
         total = piece if total is None else total + piece
     grad_features = total.astype(jnp.bfloat16)
 
-    share_sum = share_sum + send_by(share_sum, ("core",), (1,))
-    share_sum = share_sum + send_by(share_sum, ("xl",), (1,))
-    share_sum = share_sum + exchange(share_sum, "z", 1)
-    share_sum = share_sum + exchange(share_sum, "z", 2)
+    share_sum = share_sum + exchange(share_sum, "core", 1)
     norm_scale = 1.0 / math.sqrt(local_rows * math.prod(SIZES.values()))
-    share = width // len(parts)
     grad_bias = share_sum[share] * norm_scale
     piece = share_sum[:share].astype(jnp.bfloat16)
     pair = jnp.concatenate([piece, send_by(piece, ("xh",), (1,))])
     pieces = [send_by(pair, ("y",), (o,)) if o else pair for o in range(y)]
-    at = [at_offset(REP, (k, o), -1) for o in range(y) for k in range(xh)]
-    grad_weight = place(listed(at), pieces, share, norm_scale)
+    grad_weight = place(begin["piece"], len(parts), index, pieces, share, norm_scale)
     return (output, grad_features, grad_weight, grad_bias)
 
 

time: 224 us -> 225 us (level)
  waiting for transfers between devices: 97.4 us -> 89.1 us
  starting transfers between devices: 71.9 us -> 79.1 us
  other arithmetic: 7.32 us -> 2.61 us
  Pallas kernels: 40.2 us -> 44.8 us
    ppermute x44 -> x42, starting transfers between devices: 68.1 us -> 73.9 us  [send_by(): return lax.ppermute(value, axes, pairs)]
    pallas_call x6 -> x7, Pallas kernels: 40.2 us -> 44.8 us  [the longest x3 21.2 us: spread(): pl.pallas_call(lambda *refs: backward_kernel(shards, parts, at_source, at...]
    ppermute x44 -> x42, waiting for transfers between devices: 87.5 us -> 83.3 us  [send_by(): return lax.ppermute(value, axes, pairs)]
    ppermute x2 -> x4, waiting for transfers between devices: 9.85 us -> 5.78 us  [exchange(): lax.ppermute(value, axis, [(i, i ^ mask) for i in range(SIZES[axis])])]
    select_n x7 -> x0, other arithmetic: 3.99 us -> none  [the longest x6 3.39 us: listed(): found = jnp.where(line == i, value, found)]
    ppermute x2 -> x4, starting transfers between devices: 3.76 us -> 5.2 us  [exchange(): lax.ppermute(value, axis, [(i, i ^ mask) for i in range(SIZES[axis])])]
  transfers between devices with their start and end apart: 46 -> 46, of which waited for: 17 -> 16; matrix products, arithmetic and copies ran while one was open for 3% -> 2% of each run, Pallas kernels for 8% -> 9%
where the time goes in v4:
time: 225 us; the launch traced here: 224 us
  waiting for transfers between devices  89.1 us (40%)
  starting transfers between devices  79.1 us (35%)
  Pallas kernels  44.8 us (20%)
  local copies, waits for them, and re-layouts  7.37 us (3%)
  other arithmetic  2.61 us (1%)
    ppermute x42, waiting for transfers between devices, send_by(): return lax.ppermute(value, axes, pairs)  83.3 us
    ppermute x42, starting transfers between devices, send_by(): return lax.ppermute(value, axes, pairs)  73.9 us
    pallas_call x3, Pallas kernels, spread(): pl.pallas_call(lambda *refs: backward_kernel(shards, parts, at_source, at...  21.2 us
    pallas_call x1, Pallas kernels, aggregate(): pl.pallas_call(lambda *refs: forward_kernel(shards, at_source, at_place,...  14 us
    unnamed x69, local copies, waits for them, and re-layouts  6.19 us
    ppermute x4, waiting for transfers between devices, exchange(): lax.ppermute(value, axis, [(i, i ^ mask) for i in range(SIZES[axis])])  5.78 us
    ppermute x4, starting transfers between devices, exchange(): lax.ppermute(value, axis, [(i, i ^ mask) for i in range(SIZES[axis])])  5.2 us
    pallas_call x1, Pallas kernels, middle(): pl.pallas_call(lambda *refs: middle_kernel(parts, at_place, *refs), out_s...  4.87 us
  transfers between devices with their start and end apart: 46, of which 16 were waited for; matrix products, arithmetic and copies ran while one was open for 2% of the time, Pallas kernels for 9%

profile of v4, /device:TPU:0, one launch (start us, length us, event | category | flops | bytes accessed | tf_op | source)
XLA Modules:
  0.0 224.0 jit_solution(17085156588674493779)
XLA Ops:
  11.3 5.4 %collective-permute-start.5 = (bf16[256,512]{1,0:T(8,128)(2,1)}, bf16[256,512]{1,0:T(8,128)(2,1)S(1)}, u32[]{:S(2)}, u32[]{:S(2)}) collective-permute-start(bf16[256,512]{1,0:T(8,128)(2,1)} %refs_4_.1), channel_id=1, source_target_pairs={{0,112},{16,64},{32,80},{48,96},{64,48},{80,0},{96,16},{112,32},{1... | collective-permute-start | bytes 786440 | tf_op jit(solution)/shard_map/ppermute | solution.py:26
  16.8 8.4 %collective-permute-start.6 = (bf16[256,512]{1,0:T(8,128)(2,1)}, bf16[256,512]{1,0:T(8,128)(2,1)S(1)}, u32[]{:S(2)}, u32[]{:S(2)}) collective-permute-start(bf16[256,512]{1,0:T(8,128)(2,1)} %refs_4_.1), channel_id=1, source_target_pairs={{0,96},{16,112},{32,64},{48,80},{64,32},{80,48},{96,0},{112,16},{1... | collective-permute-start | bytes 786440 | tf_op jit(solution)/shard_map/ppermute | solution.py:26
  28.7 3.8 %collective-permute-done.6.refs_11_ = bf16[256,512]{1,0:T(8,128)(2,1)S(1)} collective-permute-done((bf16[256,512]{1,0:T(8,128)(2,1)}, bf16[256,512]{1,0:T(8,128)(2,1)S(1)}, u32[]{:S(2)}, u32[]{:S(2)}) %collective-permute-start.6) | collective-permute-done | bytes 262176 | tf_op jit(solution)/shard_map/ppermute | solution.py:26
  36.9 14.0 %aggregate.1 = (bf16[256,512]{1,0:T(8,128)(2,1)}, bf16[256,512]{1,0:T(8,128)(2,1)}, bf16[256,512]{1,0:T(8,128)(2,1)}, bf16[256,512]{1,0:T(8,128)(2,1)}, bf16[256...) custom-call(s32[56]{0:T(128)} %dynamic-slice_bitcast_fusion.refs_0_, ...), custom_call_target="tpu_custom_call" | custom-call | flops 8589934592 | bytes 16777216 | tf_op jit(solution)/shard_map/aggregate/pallas_call | solution.py:121
  52.7 6.0 %collective-permute-start.16 = (bf16[256,512]{1,0:T(8,128)(2,1)}, bf16[256,512]{1,0:T(8,128)(2,1)S(1)}, u32[]{:S(2)}, u32[]{:S(2)}) collective-permute-start(bf16[256,512]{1,0:T(8,128)(2,1)} %get-tuple-element.43), channel_id=1, source_target_pairs={{0,2},{1,3},{2,0},{3,1},{4,6},{5,7},{6,4},{7,5},{8,10},{9,11},{10,... | collective-permute-start | bytes 786440 | tf_op jit(solution)/shard_map/ppermute | solution.py:26
  63.7 3.7 %collective-permute-start.20 = (bf16[256,512]{1,0:T(8,128)(2,1)}, bf16[256,512]{1,0:T(8,128)(2,1)S(1)}, u32[]{:S(2)}, u32[]{:S(2)}) collective-permute-start(bf16[256,512]{1,0:T(8,128)(2,1)} %get-tuple-element.47), channel_id=1, source_target_pairs={{0,6},{1,7},{2,4},{3,5},{4,2},{5,3},{6,0},{7,1},{8,14},{9,15},{10,... | collective-permute-start | bytes 786440 | tf_op jit(solution)/shard_map/ppermute | solution.py:26
  67.4 3.2 %collective-permute-start.21 = (bf16[256,512]{1,0:T(8,128)(2,1)}, bf16[256,512]{1,0:T(8,128)(2,1)S(1)}, u32[]{:S(2)}, u32[]{:S(2)}) collective-permute-start(bf16[256,512]{1,0:T(8,128)(2,1)} %get-tuple-element.48), channel_id=1, source_target_pairs={{0,7},{1,4},{2,5},{3,6},{4,3},{5,0},{6,1},{7,2},{8,15},{9,12},{10,... | collective-permute-start | bytes 786440 | tf_op jit(solution)/shard_map/ppermute | solution.py:26
  70.6 4.3 %collective-permute-done.19.refs_6_ = bf16[256,512]{1,0:T(8,128)(2,1)S(1)} collective-permute-done((bf16[256,512]{1,0:T(8,128)(2,1)}, bf16[256,512]{1,0:T(8,128)(2,1)S(1)}, u32[]{:S(2)}, u32[]{:S(2)}) %collective-permute-start.19) | collective-permute-done | bytes 262176 | tf_op jit(solution)/shard_map/ppermute | solution.py:26
  74.9 5.2 %collective-permute-done.20.refs_7_ = bf16[256,512]{1,0:T(8,128)(2,1)S(1)} collective-permute-done((bf16[256,512]{1,0:T(8,128)(2,1)}, bf16[256,512]{1,0:T(8,128)(2,1)S(1)}, u32[]{:S(2)}, u32[]{:S(2)}) %collective-permute-start.20) | collective-permute-done | bytes 262176 | tf_op jit(solution)/shard_map/ppermute | solution.py:26
  80.2 5.0 %collective-permute-done.21.refs_8_ = bf16[256,512]{1,0:T(8,128)(2,1)S(1)} collective-permute-done((bf16[256,512]{1,0:T(8,128)(2,1)}, bf16[256,512]{1,0:T(8,128)(2,1)S(1)}, u32[]{:S(2)}, u32[]{:S(2)}) %collective-permute-start.21) | collective-permute-done | bytes 262176 | tf_op jit(solution)/shard_map/ppermute | solution.py:26
  85.8 4.9 %middle.1 = (bf16[256,512]{1,0:T(8,128)(2,1)}, bf16[336,512]{1,0:T(8,128)(2,1)}, bf16[336,512]{1,0:T(8,128)(2,1)}, bf16[336,512]{1,0:T(8,128)(2,1)}, bf16[336,51...) custom-call(s32[56]{0:T(128)} %dynamic-slice_bitcast_fusion.refs_0_,, ...), custom_call_target="tpu_custom_call" | custom-call | flops 1073741824 | bytes 8388608 | tf_op jit(solution)/shard_map/middle/pallas_call | solution.py:323
  90.7 3.6 %collective-permute-start.22 = (bf16[336,512]{1,0:T(8,128)(2,1)}, bf16[336,512]{1,0:T(8,128)(2,1)S(1)}, u32[]{:S(2)}, u32[]{:S(2)}) collective-permute-start(bf16[336,512]{1,0:T(8,128)(2,1)} %get-tuple-element.51), channel_id=1, source_target_pairs={{0,1},{1,2},{2,3},{3,0},{4,5},{5,6},{6,7},{7,4},{8,9},{9,10},{10,1... | collective-permute-start | bytes 1032200 | tf_op jit(solution)/shard_map/ppermute | solution.py:26
  97.1 3.8 %collective-permute-start.25 = (bf16[336,512]{1,0:T(8,128)(2,1)}, bf16[336,512]{1,0:T(8,128)(2,1)S(1)}, u32[]{:S(2)}, u32[]{:S(2)}) collective-permute-start(bf16[336,512]{1,0:T(8,128)(2,1)} %get-tuple-element.54), channel_id=1, source_target_pairs={{0,4},{1,5},{2,6},{3,7},{4,0},{5,1},{6,2},{7,3},{8,12},{9,13},{10,... | collective-permute-start | bytes 1032200 | tf_op jit(solution)/shard_map/ppermute | solution.py:26
  107.1 21.0 %collective-permute-done.23.refs_2_.refs_6_ = bf16[336,512]{1,0:T(8,128)(2,1)S(1)} collective-permute-done((bf16[336,512]{1,0:T(8,128)(2,1)}, bf16[336,512]{1,0:T(8,128)(2,1)S(1)}, u32[]{:S(2)}, u32[]{:S(2)}) %collective-permute-start.23) | collective-permute-done | bytes 344096 | tf_op jit(solution)/shard_map/ppermute | solution.py:26
  128.2 12.4 %collective-permute-done.28.refs_7_.refs_11_ = bf16[336,512]{1,0:T(8,128)(2,1)S(1)} collective-permute-done((bf16[336,512]{1,0:T(8,128)(2,1)}, bf16[336,512]{1,0:T(8,128)(2,1)S(1)}, u32[]{:S(2)}, u32[]{:S(2)}) %collective-permute-start.28) | collective-permute-done | bytes 344096 | tf_op jit(solution)/shard_map/ppermute | solution.py:26
  143.3 5.7 %spread.3 = bf16[4,256,512]{2,1,0:T(8,128)(2,1)} custom-call(s32[56]{0:T(128)} %dynamic-slice_bitcast_fusion.refs_0_, s32[32,8]{1,0:T(8,128)} %bitcast.12, s32[32]{0:T(128)} %bitcast.16, bf16[32,8,128,128]{3,2,1,0:T(8,128)(2,1)} %bitcast.8, bf16[336,512]{1,0:T(8,128)(2,1)} %get-tuple-element.50.refs_0_.refs_4_, bf16[336,512]{1,0:T(8,128)(2,1)} %copy-done, ...), custom_call_target="tpu_custom_call" | custom-call | flops 2147483648 | bytes 4194304 | tf_op jit(solution)/shard_map/spread/pallas_call | solution.py:271
  149.2 5.9 %spread.4 = bf16[4,256,512]{2,1,0:T(8,128)(2,1)} custom-call(s32[56]{0:T(128)} %dynamic-slice_bitcast_fusion.refs_0_, s32[32,8]{1,0:T(8,128)} %bitcast.13, s32[32]{0:T(128)} %bitcast.17, bf16[32,8,128,128]{3,2,1,0:T(8,128)(2,1)} %bitcast.9, bf16[336,512]{1,0:T(8,128)(2,1)} %get-tuple-element.50.refs_0_.refs_4_, bf16[336,512]{1,0:T(8,128)(2,1)} %copy-done, ...), custom_call_target="tpu_custom_call" | custom-call | flops 2147483648 | bytes 4194304 | tf_op jit(solution)/shard_map/spread/pallas_call | solution.py:271
  157.0 4.4 %collective-permute-done.30 = f32[72,512]{1,0:T(8,128)S(1)} collective-permute-done((f32[72,512]{1,0:T(8,128)S(1)}, f32[72,512]{1,0:T(8,128)S(1)}, u32[]{:S(2)}, u32[]{:S(2)}) %collective-permute-start.30) | collective-permute-done | bytes 147488 | tf_op jit(solution)/shard_map/ppermute | solution.py:30
  161.4 3.4 %collective-permute-start.40 = (f32[72,512]{1,0:T(8,128)S(1)}, f32[72,512]{1,0:T(8,128)S(1)}, u32[]{:S(2)}, u32[]{:S(2)}) collective-permute-start(f32[72,512]{1,0:T(8,128)S(1)} %add.54), channel_id=1, source_target_pairs={{0,32},{16,48},{32,0},{48,16},{1,33},{17,49},{33,1},{49,17},{2,34}... | collective-permute-start | bytes 442376 | tf_op jit(solution)/shard_map/ppermute | solution.py:30
  166.8 9.7 %spread.5 = (bf16[256,512]{1,0:T(8,128)(2,1)}, bf16[256,512]{1,0:T(8,128)(2,1)}, bf16[256,512]{1,0:T(8,128)(2,1)}, bf16[256,512]{1,0:T(8,128)(2,1)}, bf16[256,51...) custom-call(s32[56]{0:T(128)} %dynamic-slice_bitcast_fusion.refs_0_, ...), custom_call_target="tpu_custom_call" | custom-call | flops 4294967296 | bytes 8388608 | tf_op jit(solution)/shard_map/spread/pallas_call | solution.py:271
  179.8 5.9 %collective-permute-start.42 = (bf16[64,512]{1,0:T(8,128)(2,1)S(1)}, bf16[64,512]{1,0:T(8,128)(2,1)S(1)}, u32[]{:S(2)}, u32[]{:S(2)}) collective-permute-start(bf16[64,512]{1,0:T(8,128)(2,1)S(1)} %slice.13), channel_id=1, source_target_pairs={{0,4},{4,0},{1,5},{5,1},{2,6},{6,2},{3,7},{7,3},{8,12},{12,8},{9,1... | collective-permute-start | bytes 196616 | tf_op jit(solution)/shard_map/ppermute | solution.py:26
  187.3 3.7 %collective-permute-done.42 = bf16[64,512]{1,0:T(8,128)(2,1)S(1)} collective-permute-done((bf16[64,512]{1,0:T(8,128)(2,1)S(1)}, bf16[64,512]{1,0:T(8,128)(2,1)S(1)}, u32[]{:S(2)}, u32[]{:S(2)}) %collective-permute-start.42) | collective-permute-done | bytes 65568 | tf_op jit(solution)/shard_map/ppermute | solution.py:26
  195.2 16.9 %collective-permute-done.37 = bf16[256,512]{1,0:T(8,128)(2,1)S(1)} collective-permute-done((bf16[256,512]{1,0:T(8,128)(2,1)}, bf16[256,512]{1,0:T(8,128)(2,1)S(1)}, u32[]{:S(2)}, u32[]{:S(2)}) %collective-permute-start.37) | collective-permute-done | bytes 262176 | tf_op jit(solution)/shard_map/ppermute | solution.py:26
  212.1 3.3 %collective-permute-start.45 = (bf16[128,512]{1,0:T(8,128)(2,1)S(1)}, bf16[128,512]{1,0:T(8,128)(2,1)S(1)}, u32[]{:S(2)}, u32[]{:S(2)}) collective-permute-start(bf16[128,512]{1,0:T(8,128)(2,1)S(1)} %pad_maximum_fusion.refs_1_), channel_id=1, source_target_pairs={{0,3},{1,0},{2,1},{3,2},{4,7},{5,4},{6,5},{7,6},{8,11},{9,8},{10,9... | collective-permute-start | bytes 393224 | tf_op jit(solution)/shard_map/ppermute | solution.py:26
  (153 shorter events, 59.4 us)
Async XLA Ops:
  2.7 14.1 %collective-permute-start.1 = (bf16[256,512]{1,0:T(8,128)(2,1)}, bf16[256,512]{1,0:T(8,128)(2,1)S(1)}, u32[]{:S(2)}, u32[]{:S(2)}) collective-permute-start(bf16[256,512]{1,0:T(8,128)(2,1)} %refs_4_.1), channel_id=1, source_target_pairs={{0,48},{16,0},{32,16},{48,32},{64,112},{80,64},{96,80},{112,96},{1... | collective-permute-start | bytes 786440 | tf_op jit(solution)/shard_map/ppermute | solution.py:26
  4.9 20.3 %collective-permute-start.2 = (bf16[256,512]{1,0:T(8,128)(2,1)}, bf16[256,512]{1,0:T(8,128)(2,1)S(1)}, u32[]{:S(2)}, u32[]{:S(2)}) collective-permute-start(bf16[256,512]{1,0:T(8,128)(2,1)} %refs_4_.1), channel_id=1, source_target_pairs={{0,64},{16,80},{32,96},{48,112},{64,0},{80,16},{96,32},{112,48},{1... | collective-permute-start | bytes 786440 | tf_op jit(solution)/shard_map/ppermute | solution.py:26
  6.4 20.2 %collective-permute-start.3 = (bf16[256,512]{1,0:T(8,128)(2,1)}, bf16[256,512]{1,0:T(8,128)(2,1)S(1)}, u32[]{:S(2)}, u32[]{:S(2)}) collective-permute-start(bf16[256,512]{1,0:T(8,128)(2,1)} %refs_4_.1), channel_id=1, source_target_pairs={{0,32},{16,48},{32,0},{48,16},{64,96},{80,112},{96,64},{112,80},{1... | collective-permute-start | bytes 786440 | tf_op jit(solution)/shard_map/ppermute | solution.py:26
  8.2 18.5 %collective-permute-start.4 = (bf16[256,512]{1,0:T(8,128)(2,1)}, bf16[256,512]{1,0:T(8,128)(2,1)S(1)}, u32[]{:S(2)}, u32[]{:S(2)}) collective-permute-start(bf16[256,512]{1,0:T(8,128)(2,1)} %refs_4_.1), channel_id=1, source_target_pairs={{0,80},{16,96},{32,112},{48,64},{64,16},{80,32},{96,48},{112,0},{1... | collective-permute-start | bytes 786440 | tf_op jit(solution)/shard_map/ppermute | solution.py:26
  11.3 17.3 %collective-permute-start.5 = (bf16[256,512]{1,0:T(8,128)(2,1)}, bf16[256,512]{1,0:T(8,128)(2,1)S(1)}, u32[]{:S(2)}, u32[]{:S(2)}) collective-permute-start(bf16[256,512]{1,0:T(8,128)(2,1)} %refs_4_.1), channel_id=1, source_target_pairs={{0,112},{16,64},{32,80},{48,96},{64,48},{80,0},{96,16},{112,32},{1... | collective-permute-start | bytes 786440 | tf_op jit(solution)/shard_map/ppermute | solution.py:26
  16.8 15.7 %collective-permute-start.6 = (bf16[256,512]{1,0:T(8,128)(2,1)}, bf16[256,512]{1,0:T(8,128)(2,1)S(1)}, u32[]{:S(2)}, u32[]{:S(2)}) collective-permute-start(bf16[256,512]{1,0:T(8,128)(2,1)} %refs_4_.1), channel_id=1, source_target_pairs={{0,96},{16,112},{32,64},{48,80},{64,32},{80,48},{96,0},{112,16},{1... | collective-permute-start | bytes 786440 | tf_op jit(solution)/shard_map/ppermute | solution.py:26
  52.7 14.7 %collective-permute-start.16 = (bf16[256,512]{1,0:T(8,128)(2,1)}, bf16[256,512]{1,0:T(8,128)(2,1)S(1)}, u32[]{:S(2)}, u32[]{:S(2)}) collective-permute-start(bf16[256,512]{1,0:T(8,128)(2,1)} %get-tuple-element.43), channel_id=1, source_target_pairs={{0,2},{1,3},{2,0},{3,1},{4,6},{5,7},{6,4},{7,5},{8,10},{9,11},{10,... | collective-permute-start | bytes 786440 | tf_op jit(solution)/shard_map/ppermute | solution.py:26
  63.7 16.5 %collective-permute-start.20 = (bf16[256,512]{1,0:T(8,128)(2,1)}, bf16[256,512]{1,0:T(8,128)(2,1)S(1)}, u32[]{:S(2)}, u32[]{:S(2)}) collective-permute-start(bf16[256,512]{1,0:T(8,128)(2,1)} %get-tuple-element.47), channel_id=1, source_target_pairs={{0,6},{1,7},{2,4},{3,5},{4,2},{5,3},{6,0},{7,1},{8,14},{9,15},{10,... | collective-permute-start | bytes 786440 | tf_op jit(solution)/shard_map/ppermute | solution.py:26
  67.4 17.8 %collective-permute-start.21 = (bf16[256,512]{1,0:T(8,128)(2,1)}, bf16[256,512]{1,0:T(8,128)(2,1)S(1)}, u32[]{:S(2)}, u32[]{:S(2)}) collective-permute-start(bf16[256,512]{1,0:T(8,128)(2,1)} %get-tuple-element.48), channel_id=1, source_target_pairs={{0,7},{1,4},{2,5},{3,6},{4,3},{5,0},{6,1},{7,2},{8,15},{9,12},{10,... | collective-permute-start | bytes 786440 | tf_op jit(solution)/shard_map/ppermute | solution.py:26
  90.7 13.9 %collective-permute-start.22 = (bf16[336,512]{1,0:T(8,128)(2,1)}, bf16[336,512]{1,0:T(8,128)(2,1)S(1)}, u32[]{:S(2)}, u32[]{:S(2)}) collective-permute-start(bf16[336,512]{1,0:T(8,128)(2,1)} %get-tuple-element.51), channel_id=1, source_target_pairs={{0,1},{1,2},{2,3},{3,0},{4,5},{5,6},{6,7},{7,4},{8,9},{9,10},{10,1... | collective-permute-start | bytes 1032200 | tf_op jit(solution)/shard_map/ppermute | solution.py:26
  94.3 33.8 %collective-permute-start.23 = (bf16[336,512]{1,0:T(8,128)(2,1)}, bf16[336,512]{1,0:T(8,128)(2,1)S(1)}, u32[]{:S(2)}, u32[]{:S(2)}) collective-permute-start(bf16[336,512]{1,0:T(8,128)(2,1)} %get-tuple-element.52), channel_id=1, source_target_pairs={{0,2},{1,3},{2,0},{3,1},{4,6},{5,7},{6,4},{7,5},{8,10},{9,11},{10,... | collective-permute-start | bytes 1032200 | tf_op jit(solution)/shard_map/ppermute | solution.py:26
  97.0 31.1 %collective-permute-start.24 = (bf16[336,512]{1,0:T(8,128)(2,1)}, bf16[336,512]{1,0:T(8,128)(2,1)S(1)}, u32[]{:S(2)}, u32[]{:S(2)}) collective-permute-start(bf16[336,512]{1,0:T(8,128)(2,1)} %get-tuple-element.53), channel_id=1, source_target_pairs={{0,3},{1,0},{2,1},{3,2},{4,7},{5,4},{6,5},{7,6},{8,11},{9,8},{10,9... | collective-permute-start | bytes 1032200 | tf_op jit(solution)/shard_map/ppermute | solution.py:26
  97.1 31.0 %collective-permute-start.25 = (bf16[336,512]{1,0:T(8,128)(2,1)}, bf16[336,512]{1,0:T(8,128)(2,1)S(1)}, u32[]{:S(2)}, u32[]{:S(2)}) collective-permute-start(bf16[336,512]{1,0:T(8,128)(2,1)} %get-tuple-element.54), channel_id=1, source_target_pairs={{0,4},{1,5},{2,6},{3,7},{4,0},{5,1},{6,2},{7,3},{8,12},{9,13},{10,... | collective-permute-start | bytes 1032200 | tf_op jit(solution)/shard_map/ppermute | solution.py:26
  100.9 27.2 %collective-permute-start.26 = (bf16[336,512]{1,0:T(8,128)(2,1)}, bf16[336,512]{1,0:T(8,128)(2,1)S(1)}, u32[]{:S(2)}, u32[]{:S(2)}) collective-permute-start(bf16[336,512]{1,0:T(8,128)(2,1)} %get-tuple-element.55), channel_id=1, source_target_pairs={{0,5},{1,6},{2,7},{3,4},{4,1},{5,2},{6,3},{7,0},{8,13},{9,14},{10,... | collective-permute-start | bytes 1032200 | tf_op jit(solution)/shard_map/ppermute | solution.py:26
  104.6 23.5 %collective-permute-start.27 = (bf16[336,512]{1,0:T(8,128)(2,1)}, bf16[336,512]{1,0:T(8,128)(2,1)S(1)}, u32[]{:S(2)}, u32[]{:S(2)}) collective-permute-start(bf16[336,512]{1,0:T(8,128)(2,1)} %get-tuple-element.56), channel_id=1, source_target_pairs={{0,6},{1,7},{2,4},{3,5},{4,2},{5,3},{6,0},{7,1},{8,14},{9,15},{10,... | collective-permute-start | bytes 1032200 | tf_op jit(solution)/shard_map/ppermute | solution.py:26
  149.0 15.8 %collective-permute-start.31 = (bf16[4,256,512]{2,1,0:T(8,128)(2,1)}, bf16[4,256,512]{2,1,0:T(8,128)(2,1)S(1)}, u32[]{:S(2)}, u32[]{:S(2)}) collective-permute-start(bf16[4,256,512]{2,1,0:T(8,128)(2,1)} %spread.3), channel_id=1, source_target_pairs={{0,8},{8,0},{1,9},{9,1},{2,10},{10,2},{3,11},{11,3},{4,12},{12,4},... | collective-permute-start | bytes 3145736 | tf_op jit(solution)/shard_map/ppermute | solution.py:26
  161.4 16.9 %collective-permute-start.40 = (f32[72,512]{1,0:T(8,128)S(1)}, f32[72,512]{1,0:T(8,128)S(1)}, u32[]{:S(2)}, u32[]{:S(2)}) collective-permute-start(f32[72,512]{1,0:T(8,128)S(1)} %add.54), channel_id=1, source_target_pairs={{0,32},{16,48},{32,0},{48,16},{1,33},{17,49},{33,1},{49,17},{2,34}... | collective-permute-start | bytes 442376 | tf_op jit(solution)/shard_map/ppermute | solution.py:30
  176.5 14.7 %collective-permute-start.39 = (bf16[256,512]{1,0:T(8,128)(2,1)}, bf16[256,512]{1,0:T(8,128)(2,1)S(1)}, u32[]{:S(2)}, u32[]{:S(2)}) collective-permute-start(bf16[256,512]{1,0:T(8,128)(2,1)} %get-tuple-element.74), channel_id=1, source_target_pairs={{0,64},{16,80},{32,96},{48,112},{64,0},{80,16},{96,32},{112,48},{1... | collective-permute-start | bytes 786440 | tf_op jit(solution)/shard_map/ppermute | solution.py:26
  176.7 17.3 %collective-permute-start.38 = (bf16[256,512]{1,0:T(8,128)(2,1)}, bf16[256,512]{1,0:T(8,128)(2,1)S(1)}, u32[]{:S(2)}, u32[]{:S(2)}) collective-permute-start(bf16[256,512]{1,0:T(8,128)(2,1)} %get-tuple-element.73), channel_id=1, source_target_pairs={{0,48},{16,0},{32,16},{48,32},{64,112},{80,64},{96,80},{112,96},{1... | collective-permute-start | bytes 786440 | tf_op jit(solution)/shard_map/ppermute | solution.py:26
  185.7 26.4 %collective-permute-start.37 = (bf16[256,512]{1,0:T(8,128)(2,1)}, bf16[256,512]{1,0:T(8,128)(2,1)S(1)}, u32[]{:S(2)}, u32[]{:S(2)}) collective-permute-start(bf16[256,512]{1,0:T(8,128)(2,1)} %get-tuple-element.72), channel_id=1, source_target_pairs={{0,16},{16,32},{32,48},{48,0},{64,80},{80,96},{96,112},{112,64},{1... | collective-permute-start | bytes 786440 | tf_op jit(solution)/shard_map/ppermute | solution.py:26
  186.7 25.3 %collective-permute-start.36 = (bf16[256,512]{1,0:T(8,128)(2,1)}, bf16[256,512]{1,0:T(8,128)(2,1)S(1)}, u32[]{:S(2)}, u32[]{:S(2)}) collective-permute-start(bf16[256,512]{1,0:T(8,128)(2,1)} %get-tuple-element.70), channel_id=1, source_target_pairs={{0,96},{16,112},{32,64},{48,80},{64,32},{80,48},{96,0},{112,16},{1... | collective-permute-start | bytes 786440 | tf_op jit(solution)/shard_map/ppermute | solution.py:26
  191.1 21.0 %collective-permute-start.35 = (bf16[256,512]{1,0:T(8,128)(2,1)}, bf16[256,512]{1,0:T(8,128)(2,1)S(1)}, u32[]{:S(2)}, u32[]{:S(2)}) collective-permute-start(bf16[256,512]{1,0:T(8,128)(2,1)} %get-tuple-element.69), channel_id=1, source_target_pairs={{0,112},{16,64},{32,80},{48,96},{64,48},{80,0},{96,16},{112,32},{1... | collective-permute-start | bytes 786440 | tf_op jit(solution)/shard_map/ppermute | solution.py:26
  191.2 24.2 %collective-permute-start.34 = (bf16[256,512]{1,0:T(8,128)(2,1)}, bf16[256,512]{1,0:T(8,128)(2,1)S(1)}, u32[]{:S(2)}, u32[]{:S(2)}) collective-permute-start(bf16[256,512]{1,0:T(8,128)(2,1)} %get-tuple-element.68), channel_id=1, source_target_pairs={{0,80},{16,96},{32,112},{48,64},{64,16},{80,32},{96,48},{112,0},{1... | collective-permute-start | bytes 786440 | tf_op jit(solution)/shard_map/ppermute | solution.py:26
  194.0 21.4 %collective-permute-start.33 = (bf16[256,512]{1,0:T(8,128)(2,1)}, bf16[256,512]{1,0:T(8,128)(2,1)S(1)}, u32[]{:S(2)}, u32[]{:S(2)}) collective-permute-start(bf16[256,512]{1,0:T(8,128)(2,1)} %get-tuple-element.67), channel_id=1, source_target_pairs={{0,32},{16,48},{32,0},{48,16},{64,96},{80,112},{96,64},{112,80},{1... | collective-permute-start | bytes 786440 | tf_op jit(solution)/shard_map/ppermute | solution.py:26
  (56 other events, 488.0 us)

commit v5 on v4

--- a/solution.py
+++ b/solution.py
@@ -14,7 +14,7 @@
 REP = ("xh", "y")
 CHIP = ("xl", "z")
 ALL = BLK + REP
-VMEM = 60 << 20
+VMEM = 26 << 20
 
 
 def send_by(value, axes, offsets):
@@ -100,7 +100,7 @@
             tiles = v_buf[k, pl.ds(0, n)].reshape(n * tile, tile)
             product = jnp.dot(tiles, rows, preferred_element_type=jnp.float32)
             for m in range(n):
-                to = jnp.where(m < count_ref[group], target_ref[group, m], dummy)
+                to = jnp.where(m < count_ref[group], target_ref[m, group], dummy)
                 acc_ref[to] += product[m * tile : (m + 1) * tile]
 
         of_class(count_ref[group], work)
@@ -179,7 +179,7 @@
             tiles = v_buf[k, pl.ds(0, n)].reshape(n * tile, tile)
             found = []
             for m in range(n):
-                target = target_ref[group, m]
+                target = target_ref[m, group]
                 held = index_ref[at_turn + target // 2] * 2 + target % 2
                 held = jnp.where(m < count_ref[group], held, 2 * parts)
                 found.append(table_ref[pl.ds(pl.multiple_of(held * tile, tile), tile), :])
@@ -281,7 +281,7 @@
             scratch_shapes=scratch,
         ),
         compiler_params=pltpu.CompilerParams(vmem_limit_bytes=VMEM),
-        cost_estimate=cost(shards << 29, shards << 20),
+        cost_estimate=cost(shards << 32, shards << 20),
         name="spread",
     )(index, targets, counts, values, *messages, *crossed)
 
@@ -394,7 +394,7 @@
 def body(features, weight, layer_bias, tile_values, tile_target, tile_counts, cotangent):
     local_rows, width = features.shape
     values = tile_values[0, 0]
-    targets = tile_target[0, 0]
+    targets = tile_target[0, 0].T
     counts = tile_counts[0, 0]
     tile = values.shape[-1]
     slot_total = values.shape[1]
@@ -407,6 +407,7 @@
     index = lax.dynamic_slice_in_dim(jnp.asarray(table), lax.axis_index(ALL), 1)[0]
 
     own = [send_by(features, CHIP, o) if any(o) else features for o in chips]
+    index, own[1] = lax.optimization_barrier((index, own[1]))
     crossed = [send_by(x, ("core",), (1,)) for x in own]
     partial = aggregate(begin["come"], begin["to"], len(parts), index, targets, counts, own + crossed, values)
 
@@ -416,32 +417,34 @@
 
     share = width // len(parts)
     share_sum = add_shares(messages, share)
-    steps = (("xl", 1), ("z", 1), ("z", 2))
-    across, each = [], len(halves[0])
-    for i, step in enumerate(steps):
+    each = len(halves[0])
+    across, merged = [], []
+    for i, step in enumerate((("xl", 1), ("z", 1), ("z", 2), ("xh", 1))):
         index, share_sum = lax.optimization_barrier((index, share_sum))
         arriving = exchange(share_sum, *step)
+        k = i % 2
         if i < 2:
-            found = spread(each, begin["cross"] + each * i, begin["turn"], index, targets, counts, messages, values)
+            found = spread(each, begin["cross"] + each * k, begin["turn"], index, targets, counts, messages, values)
             across.append(send_by(found[0], ("core",), (1,)))
         else:
             found = spread(
-                2 * each, begin["stay"], begin["turn"], index, targets, counts, messages, values, across
+                each, begin["stay"] + each * k, begin["turn"], index, targets, counts, messages, values, across[k : k + 1]
             )
+            merged += found
         _, share_sum, arriving = lax.optimization_barrier((found, share_sum, arriving))
-        share_sum = share_sum + arriving
-    merged = found
+        if i < 3:
+            share_sum = share_sum + arriving
+        if i == 2:
+            share_sum = share_sum + exchange(share_sum, "core", 1)
     total = None
     for piece, o in zip(merged, halves[0] + halves[1]):
         piece = (send_by(piece, CHIP, o) if any(o) else piece).astype(jnp.float32)
         total = piece if total is None else total + piece
     grad_features = total.astype(jnp.bfloat16)
 
-    share_sum = share_sum + exchange(share_sum, "core", 1)
     norm_scale = 1.0 / math.sqrt(local_rows * math.prod(SIZES.values()))
     grad_bias = share_sum[share] * norm_scale
-    piece = share_sum[:share].astype(jnp.bfloat16)
-    pair = jnp.concatenate([piece, send_by(piece, ("xh",), (1,))])
+    pair = jnp.concatenate([share_sum[:share], arriving[:share]]).astype(jnp.bfloat16)
     pieces = [send_by(pair, ("y",), (o,)) if o else pair for o in range(y)]
     grad_weight = place(begin["piece"], len(parts), index, pieces, share, norm_scale)
     return (output, grad_features, grad_weight, grad_bias)

time: 225 us -> 209 us (0.929)
  Pallas kernels: 44.8 us -> 34.4 us
  starting transfers between devices: 79.1 us -> 76.4 us
    ppermute x42 -> x41, starting transfers between devices: 73.9 us -> 66.3 us  [send_by(): return lax.ppermute(value, axes, pairs)]
    pallas_call x3 -> x4, Pallas kernels: 21.2 us -> 16.1 us  [spread(): pl.pallas_call(lambda *refs: backward_kernel(shards, parts, at_source, at...]
    ppermute x4 -> x5, starting transfers between devices: 5.2 us -> 10.1 us  [exchange(): lax.ppermute(value, axis, [(i, i ^ mask) for i in range(SIZES[axis])])]
    ppermute x42 -> x41, waiting for transfers between devices: 83.3 us -> 79 us  [send_by(): return lax.ppermute(value, axes, pairs)]
    pallas_call x1, Pallas kernels: 4.87 us -> 1.81 us  [middle(): pl.pallas_call(lambda *refs: middle_kernel(parts, at_place, *refs), out_s...]
    ppermute x4 -> x5, waiting for transfers between devices: 5.78 us -> 8.59 us  [exchange(): lax.ppermute(value, axis, [(i, i ^ mask) for i in range(SIZES[axis])])]
    unnamed x69 -> x18, local copies, waits for them, and re-layouts: 6.19 us -> 5.69 us
  transfers between devices with their start and end apart: 46 -> 46, of which waited for: 16 -> 20; matrix products, arithmetic and copies ran while one was open for 2% -> 1% of each run, Pallas kernels for 9% -> 9%
where the time goes in v5:
time: 209 us; the launch traced here: 207 us
  waiting for transfers between devices  87.6 us (42%)
  starting transfers between devices  76.4 us (37%)
  Pallas kernels  34.4 us (16%)
  local copies, waits for them, and re-layouts  6.4 us (3%)
    ppermute x41, waiting for transfers between devices, send_by(): return lax.ppermute(value, axes, pairs)  79 us
    ppermute x41, starting transfers between devices, send_by(): return lax.ppermute(value, axes, pairs)  66.3 us
    pallas_call x4, Pallas kernels, spread(): pl.pallas_call(lambda *refs: backward_kernel(shards, parts, at_source, at...  16.1 us
    pallas_call x1, Pallas kernels, aggregate(): pl.pallas_call(lambda *refs: forward_kernel(shards, at_source, at_place,...  13.9 us
    ppermute x5, starting transfers between devices, exchange(): lax.ppermute(value, axis, [(i, i ^ mask) for i in range(SIZES[axis])])  10.1 us
    ppermute x5, waiting for transfers between devices, exchange(): lax.ppermute(value, axis, [(i, i ^ mask) for i in range(SIZES[axis])])  8.59 us
    unnamed x18, local copies, waits for them, and re-layouts  5.69 us
  transfers between devices with their start and end apart: 46, of which 20 were waited for; matrix products, arithmetic and copies ran while one was open for 1% of the time, Pallas kernels for 9%

profile of v5, /device:TPU:0, one launch (start us, length us, event | category | flops | bytes accessed | tf_op | source)
XLA Modules:
  0.0 207.3 jit_solution(2088176011241000466)
XLA Ops:
  11.3 5.4 %collective-permute-start.5 = (bf16[256,512]{1,0:T(8,128)(2,1)}, bf16[256,512]{1,0:T(8,128)(2,1)S(1)}, u32[]{:S(2)}, u32[]{:S(2)}) collective-permute-start(bf16[256,512]{1,0:T(8,128)(2,1)} %refs_4_.1), channel_id=1, source_target_pairs={{0,112},{16,64},{32,80},{48,96},{64,48},{80,0},{96,16},{112,32},{1... | collective-permute-start | bytes 786440 | tf_op jit(solution)/shard_map/ppermute | solution.py:26
  16.7 8.3 %collective-permute-start.6 = (bf16[256,512]{1,0:T(8,128)(2,1)}, bf16[256,512]{1,0:T(8,128)(2,1)S(1)}, u32[]{:S(2)}, u32[]{:S(2)}) collective-permute-start(bf16[256,512]{1,0:T(8,128)(2,1)} %refs_4_.1), channel_id=1, source_target_pairs={{0,96},{16,112},{32,64},{48,80},{64,32},{80,48},{96,0},{112,16},{1... | collective-permute-start | bytes 786440 | tf_op jit(solution)/shard_map/ppermute | solution.py:26
  28.7 3.8 %collective-permute-done.6.refs_11_ = bf16[256,512]{1,0:T(8,128)(2,1)S(1)} collective-permute-done((bf16[256,512]{1,0:T(8,128)(2,1)}, bf16[256,512]{1,0:T(8,128)(2,1)S(1)}, u32[]{:S(2)}, u32[]{:S(2)}) %collective-permute-start.6) | collective-permute-done | bytes 262176 | tf_op jit(solution)/shard_map/ppermute | solution.py:26
  35.1 3.4 %copy-done = bf16[1,1,32,8,128,128]{5,4,3,2,1,0:T(8,128)(2,1)S(1)} copy-done((bf16[1,1,32,8,128,128]{5,4,3,2,1,0:T(8,128)(2,1)S(1)}, bf16[1,1,32,8,128,128]{5,4,3,2,1,0:T(8,128)(2,1)}, u32[]{:S(2)}) %copy-start) | copy-done | bytes 8388632
  40.8 13.9 %aggregate.1 = (bf16[256,512]{1,0:T(8,128)(2,1)S(1)}, bf16[256,512]{1,0:T(8,128)(2,1)S(1)}, bf16[256,512]{1,0:T(8,128)(2,1)S(1)}, bf16[256,512]{1,0:T(8,128)(2,1...) custom-call(s32[56]{0:T(128)S(1)} %dynamic-slice_bitcast_fusion.refs, ...), custom_call_target="tpu_custom_call" | custom-call | flops 8589934592 | bytes 16777216 | tf_op jit(solution)/shard_map/aggregate/pallas_call | solution.py:121
  54.7 6.4 %collective-permute-start.15 = (bf16[256,512]{1,0:T(8,128)(2,1)S(1)}, bf16[256,512]{1,0:T(8,128)(2,1)S(1)}, u32[]{:S(2)}, u32[]{:S(2)}) collective-permute-start(bf16[256,512]{1,0:T(8,128)(2,1)S(1)} %get-tuple-element.50), channel_id=1, source_target_pairs={{0,1},{1,2},{2,3},{3,0},{4,5},{5,6},{6,7},{7,4},{8,9},{9,10},{10,1... | collective-permute-start | bytes 786440 | tf_op jit(solution)/shard_map/ppermute | solution.py:26
  61.1 3.0 %collective-permute-start.16 = (bf16[256,512]{1,0:T(8,128)(2,1)S(1)}, bf16[256,512]{1,0:T(8,128)(2,1)S(1)}, u32[]{:S(2)}, u32[]{:S(2)}) collective-permute-start(bf16[256,512]{1,0:T(8,128)(2,1)S(1)} %get-tuple-element.51), channel_id=1, source_target_pairs={{0,2},{1,3},{2,0},{3,1},{4,6},{5,7},{6,4},{7,5},{8,10},{9,11},{10,... | collective-permute-start | bytes 786440 | tf_op jit(solution)/shard_map/ppermute | solution.py:26
  69.1 2.9 %collective-permute-start.20 = (bf16[256,512]{1,0:T(8,128)(2,1)S(1)}, bf16[256,512]{1,0:T(8,128)(2,1)S(1)}, u32[]{:S(2)}, u32[]{:S(2)}) collective-permute-start(bf16[256,512]{1,0:T(8,128)(2,1)S(1)} %get-tuple-element.55), channel_id=1, source_target_pairs={{0,6},{1,7},{2,4},{3,5},{4,2},{5,3},{6,0},{7,1},{8,14},{9,15},{10,... | collective-permute-start | bytes 786440 | tf_op jit(solution)/shard_map/ppermute | solution.py:26
  71.9 15.4 %collective-permute-done.16.refs_3_ = bf16[256,512]{1,0:T(8,128)(2,1)S(1)} collective-permute-done((bf16[256,512]{1,0:T(8,128)(2,1)S(1)}, bf16[256,512]{1,0:T(8,128)(2,1)S(1)}, u32[]{:S(2)}, u32[]{:S(2)}) %collective-permute-start.16) | collective-permute-done | bytes 262176 | tf_op jit(solution)/shard_map/ppermute | solution.py:26
  87.3 8.7 %collective-permute-done.21.refs_8_ = bf16[256,512]{1,0:T(8,128)(2,1)S(1)} collective-permute-done((bf16[256,512]{1,0:T(8,128)(2,1)S(1)}, bf16[256,512]{1,0:T(8,128)(2,1)S(1)}, u32[]{:S(2)}, u32[]{:S(2)}) %collective-permute-start.21) | collective-permute-done | bytes 262176 | tf_op jit(solution)/shard_map/ppermute | solution.py:26
  98.0 3.2 %collective-permute-start.24 = (bf16[336,512]{1,0:T(8,128)(2,1)S(1)}, bf16[336,512]{1,0:T(8,128)(2,1)S(1)}, u32[]{:S(2)}, u32[]{:S(2)}) collective-permute-start(bf16[336,512]{1,0:T(8,128)(2,1)S(1)} %get-tuple-element.61), channel_id=1, source_target_pairs={{0,3},{1,0},{2,1},{3,2},{4,7},{5,4},{6,5},{7,6},{8,11},{9,8},{10,9... | collective-permute-start | bytes 1032200 | tf_op jit(solution)/shard_map/ppermute | solution.py:26
  101.9 3.0 %collective-permute-start.26 = (bf16[336,512]{1,0:T(8,128)(2,1)S(1)}, bf16[336,512]{1,0:T(8,128)(2,1)S(1)}, u32[]{:S(2)}, u32[]{:S(2)}) collective-permute-start(bf16[336,512]{1,0:T(8,128)(2,1)S(1)} %get-tuple-element.63), channel_id=1, source_target_pairs={{0,5},{1,6},{2,7},{3,4},{4,1},{5,2},{6,3},{7,0},{8,13},{9,14},{10,... | collective-permute-start | bytes 1032200 | tf_op jit(solution)/shard_map/ppermute | solution.py:26
  105.0 17.5 %collective-permute-done.22.refs_1_.refs_5_ = bf16[336,512]{1,0:T(8,128)(2,1)S(1)} collective-permute-done((bf16[336,512]{1,0:T(8,128)(2,1)S(1)}, bf16[336,512]{1,0:T(8,128)(2,1)S(1)}, u32[]{:S(2)}, u32[]{:S(2)}) %collective-permute-start.22) | collective-permute-done | bytes 344096 | tf_op jit(solution)/shard_map/ppermute | solution.py:26
  125.3 9.7 %collective-permute-done.27.refs_6_.refs_10_ = bf16[336,512]{1,0:T(8,128)(2,1)S(1)} collective-permute-done((bf16[336,512]{1,0:T(8,128)(2,1)S(1)}, bf16[336,512]{1,0:T(8,128)(2,1)S(1)}, u32[]{:S(2)}, u32[]{:S(2)}) %collective-permute-start.27) | collective-permute-done | bytes 344096 | tf_op jit(solution)/shard_map/ppermute | solution.py:26
  139.7 3.8 %spread.4 = bf16[4,256,512]{2,1,0:T(8,128)(2,1)S(1)} custom-call(s32[56]{0:T(128)S(1)} %dynamic-slice_bitcast_fusion.refs_0_, s32[8,32]{1,0:T(8,128)S(1)} %bitcast.15, s32[32]{0:T(128)S(1)} %bitcast.21, bf16[32,8,128,128]{3,2,1,0:T(8,128)(2,1)S(1)} %bitcast.10, bf16[336,512]{1,0:T(8,128)(2,1)S(1)} %get-tuple-element.58.refs_0_.refs_4_, ...), custom_call_target="tpu_custom_call" | custom-call | flops 17179869184 | bytes 4194304 | tf_op jit(solution)/shard_map/spread/pallas_call | solution.py:271
  143.7 3.0 %collective-permute-start.30 = (f32[72,512]{1,0:T(8,128)S(1)}, f32[72,512]{1,0:T(8,128)S(1)}, u32[]{:S(2)}, u32[]{:S(2)}) collective-permute-start(f32[72,512]{1,0:T(8,128)S(1)} %add.53), channel_id=1, source_target_pairs={{0,16},{16,0},{32,48},{48,32},{1,17},{17,1},{33,49},{49,33},{2,18}... | collective-permute-start | bytes 442376 | tf_op jit(solution)/shard_map/ppermute | solution.py:30
  146.7 4.0 %spread.5 = bf16[4,256,512]{2,1,0:T(8,128)(2,1)S(1)} custom-call(s32[56]{0:T(128)S(1)} %dynamic-slice_bitcast_fusion.refs_0_, s32[8,32]{1,0:T(8,128)S(1)} %bitcast.16, s32[32]{0:T(128)S(1)} %bitcast.22, bf16[32,8,128,128]{3,2,1,0:T(8,128)(2,1)S(1)} %bitcast.11, bf16[336,512]{1,0:T(8,128)(2,1)S(1)} %get-tuple-element.58.refs_0_.refs_4_, ...), custom_call_target="tpu_custom_call" | custom-call | flops 17179869184 | bytes 4194304 | tf_op jit(solution)/shard_map/spread/pallas_call | solution.py:271
  153.8 4.2 %spread.6 = (bf16[256,512]{1,0:T(8,128)(2,1)S(1)}, bf16[256,512]{1,0:T(8,128)(2,1)S(1)}, bf16[256,512]{1,0:T(8,128)(2,1)S(1)}, bf16[256,512]{1,0:T(8,128)(2,1)S(1)}) custom-call(s32[56]{0:T(128)S(1)} %dynamic-slice_bitcast_fusion.refs_0_, s32[8,32]{1,0:T(8,128)S(1)} %bitcast.17, s32[32]{0:T(128)S(1)} %bitcast.23, bf16[32,8,128,128]{3,2,1,0:T(8,128)(2,1)S(1)} %bitcast.12, ...), custom_call_target="tpu_custom_call" | custom-call | flops 17179869184 | bytes 4194304 | tf_op jit(solution)/shard_map/spread/pallas_call | solution.py:271
  163.8 3.2 %collective-permute-start.42 = (bf16[72,512]{1,0:T(8,128)(2,1)S(1)}, bf16[72,512]{1,0:T(8,128)(2,1)S(1)}, u32[]{:S(2)}, u32[]{:S(2)}) collective-permute-start(bf16[72,512]{1,0:T(8,128)(2,1)S(1)} %convert.12), channel_id=1, source_target_pairs={{0,4},{4,0},{1,5},{5,1},{2,6},{6,2},{3,7},{7,3},{8,12},{12,8},{9,1... | collective-permute-start | bytes 221192 | tf_op jit(solution)/shard_map/ppermute | solution.py:30
  167.1 4.1 %spread.7 = (bf16[256,512]{1,0:T(8,128)(2,1)S(1)}, bf16[256,512]{1,0:T(8,128)(2,1)S(1)}, bf16[256,512]{1,0:T(8,128)(2,1)S(1)}, bf16[256,512]{1,0:T(8,128)(2,1)S(1)}) custom-call(s32[56]{0:T(128)S(1)} %dynamic-slice_bitcast_fusion.refs_0_, s32[8,32]{1,0:T(8,128)S(1)} %bitcast.18, s32[32]{0:T(128)S(1)} %bitcast.24, bf16[32,8,128,128]{3,2,1,0:T(8,128)(2,1)S(1)} %bitcast.13, ...), custom_call_target="tpu_custom_call" | custom-call | flops 17179869184 | bytes 4194304 | tf_op jit(solution)/shard_map/spread/pallas_call | solution.py:271
  171.2 7.6 %collective-permute-done.42 = bf16[72,512]{1,0:T(8,128)(2,1)S(1)} collective-permute-done((bf16[72,512]{1,0:T(8,128)(2,1)S(1)}, bf16[72,512]{1,0:T(8,128)(2,1)S(1)}, u32[]{:S(2)}, u32[]{:S(2)}) %collective-permute-start.42) | collective-permute-done | bytes 73760 | tf_op jit(solution)/shard_map/ppermute | solution.py:30
  178.8 4.2 %collective-permute-start.43 = (bf16[128,512]{1,0:T(8,128)(2,1)S(1)}, bf16[128,512]{1,0:T(8,128)(2,1)S(1)}, u32[]{:S(2)}, u32[]{:S(2)}) collective-permute-start(bf16[128,512]{1,0:T(8,128)(2,1)S(1)} %pad_maximum_fusion.refs_1_), channel_id=1, source_target_pairs={{0,1},{1,2},{2,3},{3,0},{4,5},{5,6},{6,7},{7,4},{8,9},{9,10},{10,1... | collective-permute-start | bytes 393224 | tf_op jit(solution)/shard_map/ppermute | solution.py:26
  193.7 4.6 %collective-permute-done.33 = bf16[256,512]{1,0:T(8,128)(2,1)S(1)} collective-permute-done((bf16[256,512]{1,0:T(8,128)(2,1)S(1)}, bf16[256,512]{1,0:T(8,128)(2,1)S(1)}, u32[]{:S(2)}, u32[]{:S(2)}) %collective-permute-start.33) | collective-permute-done | bytes 262176 | tf_op jit(solution)/shard_map/ppermute | solution.py:26
  200.9 5.5 %collective-permute-done.39 = bf16[256,512]{1,0:T(8,128)(2,1)S(1)} collective-permute-done((bf16[256,512]{1,0:T(8,128)(2,1)S(1)}, bf16[256,512]{1,0:T(8,128)(2,1)S(1)}, u32[]{:S(2)}, u32[]{:S(2)}) %collective-permute-start.39) | collective-permute-done | bytes 262176 | tf_op jit(solution)/shard_map/ppermute | solution.py:26
  (105 shorter events, 57.7 us)
Async XLA Ops:
  2.7 14.1 %collective-permute-start.1 = (bf16[256,512]{1,0:T(8,128)(2,1)}, bf16[256,512]{1,0:T(8,128)(2,1)S(1)}, u32[]{:S(2)}, u32[]{:S(2)}) collective-permute-start(bf16[256,512]{1,0:T(8,128)(2,1)} %refs_4_.1), channel_id=1, source_target_pairs={{0,48},{16,0},{32,16},{48,32},{64,112},{80,64},{96,80},{112,96},{1... | collective-permute-start | bytes 786440 | tf_op jit(solution)/shard_map/ppermute | solution.py:26
  4.9 20.2 %collective-permute-start.2 = (bf16[256,512]{1,0:T(8,128)(2,1)}, bf16[256,512]{1,0:T(8,128)(2,1)S(1)}, u32[]{:S(2)}, u32[]{:S(2)}) collective-permute-start(bf16[256,512]{1,0:T(8,128)(2,1)} %refs_4_.1), channel_id=1, source_target_pairs={{0,64},{16,80},{32,96},{48,112},{64,0},{80,16},{96,32},{112,48},{1... | collective-permute-start | bytes 786440 | tf_op jit(solution)/shard_map/ppermute | solution.py:26
  6.4 20.2 %collective-permute-start.3 = (bf16[256,512]{1,0:T(8,128)(2,1)}, bf16[256,512]{1,0:T(8,128)(2,1)S(1)}, u32[]{:S(2)}, u32[]{:S(2)}) collective-permute-start(bf16[256,512]{1,0:T(8,128)(2,1)} %refs_4_.1), channel_id=1, source_target_pairs={{0,32},{16,48},{32,0},{48,16},{64,96},{80,112},{96,64},{112,80},{1... | collective-permute-start | bytes 786440 | tf_op jit(solution)/shard_map/ppermute | solution.py:26
  8.2 18.5 %collective-permute-start.4 = (bf16[256,512]{1,0:T(8,128)(2,1)}, bf16[256,512]{1,0:T(8,128)(2,1)S(1)}, u32[]{:S(2)}, u32[]{:S(2)}) collective-permute-start(bf16[256,512]{1,0:T(8,128)(2,1)} %refs_4_.1), channel_id=1, source_target_pairs={{0,80},{16,96},{32,112},{48,64},{64,16},{80,32},{96,48},{112,0},{1... | collective-permute-start | bytes 786440 | tf_op jit(solution)/shard_map/ppermute | solution.py:26
  11.3 17.3 %collective-permute-start.5 = (bf16[256,512]{1,0:T(8,128)(2,1)}, bf16[256,512]{1,0:T(8,128)(2,1)S(1)}, u32[]{:S(2)}, u32[]{:S(2)}) collective-permute-start(bf16[256,512]{1,0:T(8,128)(2,1)} %refs_4_.1), channel_id=1, source_target_pairs={{0,112},{16,64},{32,80},{48,96},{64,48},{80,0},{96,16},{112,32},{1... | collective-permute-start | bytes 786440 | tf_op jit(solution)/shard_map/ppermute | solution.py:26
  16.7 15.7 %collective-permute-start.6 = (bf16[256,512]{1,0:T(8,128)(2,1)}, bf16[256,512]{1,0:T(8,128)(2,1)S(1)}, u32[]{:S(2)}, u32[]{:S(2)}) collective-permute-start(bf16[256,512]{1,0:T(8,128)(2,1)} %refs_4_.1), channel_id=1, source_target_pairs={{0,96},{16,112},{32,64},{48,80},{64,32},{80,48},{96,0},{112,16},{1... | collective-permute-start | bytes 786440 | tf_op jit(solution)/shard_map/ppermute | solution.py:26
  54.7 14.4 %collective-permute-start.15 = (bf16[256,512]{1,0:T(8,128)(2,1)S(1)}, bf16[256,512]{1,0:T(8,128)(2,1)S(1)}, u32[]{:S(2)}, u32[]{:S(2)}) collective-permute-start(bf16[256,512]{1,0:T(8,128)(2,1)S(1)} %get-tuple-element.50), channel_id=1, source_target_pairs={{0,1},{1,2},{2,3},{3,0},{4,5},{5,6},{6,7},{7,4},{8,9},{9,10},{10,1... | collective-permute-start | bytes 786440 | tf_op jit(solution)/shard_map/ppermute | solution.py:26
  61.1 26.2 %collective-permute-start.16 = (bf16[256,512]{1,0:T(8,128)(2,1)S(1)}, bf16[256,512]{1,0:T(8,128)(2,1)S(1)}, u32[]{:S(2)}, u32[]{:S(2)}) collective-permute-start(bf16[256,512]{1,0:T(8,128)(2,1)S(1)} %get-tuple-element.51), channel_id=1, source_target_pairs={{0,2},{1,3},{2,0},{3,1},{4,6},{5,7},{6,4},{7,5},{8,10},{9,11},{10,... | collective-permute-start | bytes 786440 | tf_op jit(solution)/shard_map/ppermute | solution.py:26
  64.1 23.2 %collective-permute-start.17 = (bf16[256,512]{1,0:T(8,128)(2,1)S(1)}, bf16[256,512]{1,0:T(8,128)(2,1)S(1)}, u32[]{:S(2)}, u32[]{:S(2)}) collective-permute-start(bf16[256,512]{1,0:T(8,128)(2,1)S(1)} %get-tuple-element.52), channel_id=1, source_target_pairs={{0,3},{1,0},{2,1},{3,2},{4,7},{5,4},{6,5},{7,6},{8,11},{9,8},{10,9... | collective-permute-start | bytes 786440 | tf_op jit(solution)/shard_map/ppermute | solution.py:26
  64.1 23.2 %collective-permute-start.18 = (bf16[256,512]{1,0:T(8,128)(2,1)S(1)}, bf16[256,512]{1,0:T(8,128)(2,1)S(1)}, u32[]{:S(2)}, u32[]{:S(2)}) collective-permute-start(bf16[256,512]{1,0:T(8,128)(2,1)S(1)} %get-tuple-element.53), channel_id=1, source_target_pairs={{0,4},{1,5},{2,6},{3,7},{4,0},{5,1},{6,2},{7,3},{8,12},{9,13},{10,... | collective-permute-start | bytes 786440 | tf_op jit(solution)/shard_map/ppermute | solution.py:26
  66.7 20.6 %collective-permute-start.19 = (bf16[256,512]{1,0:T(8,128)(2,1)S(1)}, bf16[256,512]{1,0:T(8,128)(2,1)S(1)}, u32[]{:S(2)}, u32[]{:S(2)}) collective-permute-start(bf16[256,512]{1,0:T(8,128)(2,1)S(1)} %get-tuple-element.54), channel_id=1, source_target_pairs={{0,5},{1,6},{2,7},{3,4},{4,1},{5,2},{6,3},{7,0},{8,13},{9,14},{10,... | collective-permute-start | bytes 786440 | tf_op jit(solution)/shard_map/ppermute | solution.py:26
  69.1 18.2 %collective-permute-start.20 = (bf16[256,512]{1,0:T(8,128)(2,1)S(1)}, bf16[256,512]{1,0:T(8,128)(2,1)S(1)}, u32[]{:S(2)}, u32[]{:S(2)}) collective-permute-start(bf16[256,512]{1,0:T(8,128)(2,1)S(1)} %get-tuple-element.55), channel_id=1, source_target_pairs={{0,6},{1,7},{2,4},{3,5},{4,2},{5,3},{6,0},{7,1},{8,14},{9,15},{10,... | collective-permute-start | bytes 786440 | tf_op jit(solution)/shard_map/ppermute | solution.py:26
  97.9 24.6 %collective-permute-start.22 = (bf16[336,512]{1,0:T(8,128)(2,1)S(1)}, bf16[336,512]{1,0:T(8,128)(2,1)S(1)}, u32[]{:S(2)}, u32[]{:S(2)}) collective-permute-start(bf16[336,512]{1,0:T(8,128)(2,1)S(1)} %get-tuple-element.59), channel_id=1, source_target_pairs={{0,1},{1,2},{2,3},{3,0},{4,5},{5,6},{6,7},{7,4},{8,9},{9,10},{10,1... | collective-permute-start | bytes 1032200 | tf_op jit(solution)/shard_map/ppermute | solution.py:26
  97.9 27.3 %collective-permute-start.23 = (bf16[336,512]{1,0:T(8,128)(2,1)S(1)}, bf16[336,512]{1,0:T(8,128)(2,1)S(1)}, u32[]{:S(2)}, u32[]{:S(2)}) collective-permute-start(bf16[336,512]{1,0:T(8,128)(2,1)S(1)} %get-tuple-element.60), channel_id=1, source_target_pairs={{0,2},{1,3},{2,0},{3,1},{4,6},{5,7},{6,4},{7,5},{8,10},{9,11},{10,... | collective-permute-start | bytes 1032200 | tf_op jit(solution)/shard_map/ppermute | solution.py:26
  98.0 27.3 %collective-permute-start.24 = (bf16[336,512]{1,0:T(8,128)(2,1)S(1)}, bf16[336,512]{1,0:T(8,128)(2,1)S(1)}, u32[]{:S(2)}, u32[]{:S(2)}) collective-permute-start(bf16[336,512]{1,0:T(8,128)(2,1)S(1)} %get-tuple-element.61), channel_id=1, source_target_pairs={{0,3},{1,0},{2,1},{3,2},{4,7},{5,4},{6,5},{7,6},{8,11},{9,8},{10,9... | collective-permute-start | bytes 1032200 | tf_op jit(solution)/shard_map/ppermute | solution.py:26
  101.1 24.1 %collective-permute-start.25 = (bf16[336,512]{1,0:T(8,128)(2,1)S(1)}, bf16[336,512]{1,0:T(8,128)(2,1)S(1)}, u32[]{:S(2)}, u32[]{:S(2)}) collective-permute-start(bf16[336,512]{1,0:T(8,128)(2,1)S(1)} %get-tuple-element.62), channel_id=1, source_target_pairs={{0,4},{1,5},{2,6},{3,7},{4,0},{5,1},{6,2},{7,3},{8,12},{9,13},{10,... | collective-permute-start | bytes 1032200 | tf_op jit(solution)/shard_map/ppermute | solution.py:26
  101.9 23.3 %collective-permute-start.26 = (bf16[336,512]{1,0:T(8,128)(2,1)S(1)}, bf16[336,512]{1,0:T(8,128)(2,1)S(1)}, u32[]{:S(2)}, u32[]{:S(2)}) collective-permute-start(bf16[336,512]{1,0:T(8,128)(2,1)S(1)} %get-tuple-element.63), channel_id=1, source_target_pairs={{0,5},{1,6},{2,7},{3,4},{4,1},{5,2},{6,3},{7,0},{8,13},{9,14},{10,... | collective-permute-start | bytes 1032200 | tf_op jit(solution)/shard_map/ppermute | solution.py:26
  150.7 16.4 %collective-permute-start.38 = (bf16[4,256,512]{2,1,0:T(8,128)(2,1)S(1)}, bf16[4,256,512]{2,1,0:T(8,128)(2,1)S(1)}, u32[]{:S(2)}, u32[]{:S(2)}) collective-permute-start(bf16[4,256,512]{2,1,0:T(8,128)(2,1)S(1)} %spread.5), channel_id=1, source_target_pairs={{0,8},{8,0},{1,9},{9,1},{2,10},{10,2},{3,11},{11,3},{4,12},{12,4},... | collective-permute-start | bytes 3145736 | tf_op jit(solution)/shard_map/ppermute | solution.py:26
  159.1 26.7 %collective-permute-start.35 = (bf16[256,512]{1,0:T(8,128)(2,1)S(1)}, bf16[256,512]{1,0:T(8,128)(2,1)S(1)}, u32[]{:S(2)}, u32[]{:S(2)}) collective-permute-start(bf16[256,512]{1,0:T(8,128)(2,1)S(1)} %get-tuple-element.78), channel_id=1, source_target_pairs={{0,96},{16,112},{32,64},{48,80},{64,32},{80,48},{96,0},{112,16},{1... | collective-permute-start | bytes 786440 | tf_op jit(solution)/shard_map/ppermute | solution.py:26
  161.8 23.9 %collective-permute-start.34 = (bf16[256,512]{1,0:T(8,128)(2,1)S(1)}, bf16[256,512]{1,0:T(8,128)(2,1)S(1)}, u32[]{:S(2)}, u32[]{:S(2)}) collective-permute-start(bf16[256,512]{1,0:T(8,128)(2,1)S(1)} %get-tuple-element.77), channel_id=1, source_target_pairs={{0,112},{16,64},{32,80},{48,96},{64,48},{80,0},{96,16},{112,32},{1... | collective-permute-start | bytes 786440 | tf_op jit(solution)/shard_map/ppermute | solution.py:26
  163.8 15.0 %collective-permute-start.42 = (bf16[72,512]{1,0:T(8,128)(2,1)S(1)}, bf16[72,512]{1,0:T(8,128)(2,1)S(1)}, u32[]{:S(2)}, u32[]{:S(2)}) collective-permute-start(bf16[72,512]{1,0:T(8,128)(2,1)S(1)} %convert.12), channel_id=1, source_target_pairs={{0,4},{4,0},{1,5},{5,1},{2,6},{6,2},{3,7},{7,3},{8,12},{12,8},{9,1... | collective-permute-start | bytes 221192 | tf_op jit(solution)/shard_map/ppermute | solution.py:30
  185.8 15.1 %collective-permute-start.32 = (bf16[256,512]{1,0:T(8,128)(2,1)S(1)}, bf16[256,512]{1,0:T(8,128)(2,1)S(1)}, u32[]{:S(2)}, u32[]{:S(2)}) collective-permute-start(bf16[256,512]{1,0:T(8,128)(2,1)S(1)} %get-tuple-element.75), channel_id=1, source_target_pairs={{0,32},{16,48},{32,0},{48,16},{64,96},{80,112},{96,64},{112,80},{1... | collective-permute-start | bytes 786440 | tf_op jit(solution)/shard_map/ppermute | solution.py:26
  187.1 13.8 %collective-permute-start.41 = (bf16[256,512]{1,0:T(8,128)(2,1)S(1)}, bf16[256,512]{1,0:T(8,128)(2,1)S(1)}, u32[]{:S(2)}, u32[]{:S(2)}) collective-permute-start(bf16[256,512]{1,0:T(8,128)(2,1)S(1)} %get-tuple-element.86), channel_id=1, source_target_pairs={{0,64},{16,80},{32,96},{48,112},{64,0},{80,16},{96,32},{112,48},{1... | collective-permute-start | bytes 786440 | tf_op jit(solution)/shard_map/ppermute | solution.py:26
  191.1 15.2 %collective-permute-start.39 = (bf16[256,512]{1,0:T(8,128)(2,1)S(1)}, bf16[256,512]{1,0:T(8,128)(2,1)S(1)}, u32[]{:S(2)}, u32[]{:S(2)}) collective-permute-start(bf16[256,512]{1,0:T(8,128)(2,1)S(1)} %get-tuple-element.84), channel_id=1, source_target_pairs={{0,16},{16,32},{32,48},{48,0},{64,80},{80,96},{96,112},{112,64},{1... | collective-permute-start | bytes 786440 | tf_op jit(solution)/shard_map/ppermute | solution.py:26
  (31 other events, 528.0 us)

commit v6 on v5

--- a/solution.py
+++ b/solution.py
@@ -61,43 +61,52 @@
         low = n
 
 
-def tiles_copy(v_ref, v_buf, sem, group, to, n):
-    return pltpu.make_async_copy(v_ref.at[group, pl.ds(0, n)], v_buf.at[to, pl.ds(0, n)], sem.at[to])
-
-
-def start_tiles(source_ref, count_ref, v_ref, v_buf, sem):
-    def step(k, carry):
-        group = source_ref[k // 2] * 2 + k % 2
-        of_class(count_ref[group], lambda n: tiles_copy(v_ref, v_buf, sem, group, k, n).start())
-        return carry
-
-    lax.fori_loop(0, v_buf.shape[0], step, 0)
+def fetch_kernel(index_ref, v_ref, out_ref, again_ref, sem):
+    parts = sem.shape[0]
+    each = v_ref.shape[0] // parts
+    copies = [
+        pltpu.make_async_copy(v_ref.at[pl.ds(i * each, each)], out_ref.at[pl.ds(i * each, each)], sem.at[i])
+        for i in range(parts)
+    ]
+    for copy in copies:
+        copy.start()
+    for copy in copies:
+        copy.wait()
+    for i in range(index_ref.shape[0]):
+        again_ref[i] = index_ref[i]
+
+
+def fetch(values, index):
+    return pl.pallas_call(
+        fetch_kernel,
+        out_shape=(pltpu.VMEM(values.shape, values.dtype), jax.ShapeDtypeStruct(index.shape, index.dtype)),
+        in_specs=[pl.BlockSpec(memory_space=pltpu.SMEM), pl.BlockSpec(memory_space=pl.ANY)],
+        out_specs=(pl.BlockSpec(memory_space=pltpu.VMEM), pl.BlockSpec(memory_space=pltpu.SMEM)),
+        scratch_shapes=[pltpu.SemaphoreType.DMA((8,))],
+        compiler_params=pltpu.CompilerParams(vmem_limit_bytes=VMEM),
+        cost_estimate=cost(0, 16 << 20),
+        name="fetch",
+    )(index, pltpu.with_memory_space_constraint(values, pltpu.HBM))
 
 
 def forward_kernel(shards, at_source, at_place, index_ref, target_ref, count_ref, v_ref, *refs):
     source_ref = Window(index_ref, at_source, shards)
-    place_ref = Window(index_ref, at_place, len(refs) - 5 - shards)
+    place_ref = Window(index_ref, at_place, len(refs) - 2 - shards)
     x_refs, refs = refs[:shards], refs[shards:]
-    acc_ref, x_buf, v_buf, x_sem, v_sem = refs[-5:]
-    out_refs = refs[:-5]
+    acc_ref, x_buf = refs[-2:]
+    out_refs = refs[:-2]
     tile = v_ref.shape[-1]
     dummy = acc_ref.shape[0] - 1
     for i in range(shards):
-        pltpu.make_async_copy(x_refs[i], x_buf.at[i], x_sem.at[i]).start()
-    start_tiles(source_ref, count_ref, v_ref, v_buf, v_sem)
+        x_buf[i] = x_refs[i][...]
     acc_ref[...] = jnp.zeros_like(acc_ref)
 
     def group_step(k, carry):
         group = source_ref[k // 2] * 2 + k % 2
 
-        @pl.when(k % 2 == 0)
-        def _():
-            pltpu.make_async_copy(x_refs[0], x_buf.at[k // 2], x_sem.at[k // 2]).wait()
-
         def work(n):
-            tiles_copy(v_ref, v_buf, v_sem, group, k, n).wait()
             rows = x_buf[k // 2, pl.ds(pl.multiple_of(k % 2 * tile, tile), tile), :]
-            tiles = v_buf[k, pl.ds(0, n)].reshape(n * tile, tile)
+            tiles = v_ref[group, pl.ds(0, n)].reshape(n * tile, tile)
             product = jnp.dot(tiles, rows, preferred_element_type=jnp.float32)
             for m in range(n):
                 to = jnp.where(m < count_ref[group], target_ref[m, group], dummy)
@@ -115,8 +124,7 @@
 def aggregate(at_source, at_place, parts, index, targets, counts, gathered, values):
     shards = len(gathered)
     rows, width = gathered[0].shape
-    _, slot_total, tile, _ = values.shape
-    anywhere = pl.BlockSpec(memory_space=pl.ANY)
+    tile = values.shape[-1]
     inside = pl.BlockSpec(memory_space=pltpu.VMEM)
     return pl.pallas_call(
         lambda *refs: forward_kernel(shards, at_source, at_place, *refs),
@@ -124,20 +132,17 @@
         grid_spec=pltpu.PrefetchScalarGridSpec(
             num_scalar_prefetch=3,
             grid=(),
-            in_specs=[anywhere] * (1 + shards),
+            in_specs=[inside] * (1 + shards),
             out_specs=(inside,) * parts,
             scratch_shapes=[
                 pltpu.VMEM((parts * 2 + 1, tile, width), jnp.float32),
                 pltpu.VMEM((shards, rows, width), jnp.bfloat16),
-                pltpu.VMEM((shards * 2, slot_total, tile, tile), jnp.bfloat16),
-                pltpu.SemaphoreType.DMA((shards,)),
-                pltpu.SemaphoreType.DMA((shards * 2,)),
             ],
         ),
         compiler_params=pltpu.CompilerParams(vmem_limit_bytes=VMEM),
         cost_estimate=cost(8 << 30, 16 << 20),
         name="aggregate",
-    )(index, targets, counts, values, *gathered)
+    )(index, targets, counts, pltpu.with_memory_space_constraint(values, pltpu.VMEM), *gathered)
 
 
 def backward_kernel(shards, parts, at_source, at_turn, crossing, *refs):
@@ -149,25 +154,15 @@
         out_refs, refs = refs[:shards], refs[shards:]
     else:
         out_ref, refs = refs[0], refs[1:]
-    table_ref, v_buf, m_sem, v_sem = refs[:4]
-    refs = refs[4:]
+    table_ref = refs[0]
     tile = v_ref.shape[-1]
     rows = 2 * tile
     for i in range(parts):
-        pltpu.make_async_copy(m_refs[i].at[pl.ds(0, rows)], table_ref.at[pl.ds(i * rows, rows)], m_sem.at[i]).start()
-    start_tiles(source_ref, count_ref, v_ref, v_buf, v_sem)
-    if crossing:
-        term_ref, cross_buf, cross_sem = refs
-        each = shards // crossing
-        for i in range(crossing):
-            pltpu.make_async_copy(crossed_refs[i], cross_buf.at[pl.ds(i * each, each)], cross_sem.at[i]).start()
+        table_ref[pl.ds(i * rows, rows), :] = m_refs[i][pl.ds(0, rows), :]
     blank = table_ref.at[pl.ds(parts * rows, tile)]
     blank[...] = jnp.zeros_like(blank)
-    for i in range(parts):
-        pltpu.make_async_copy(m_refs[i].at[pl.ds(0, rows)], table_ref.at[pl.ds(i * rows, rows)], m_sem.at[i]).wait()
     if crossing:
-        for i in range(crossing):
-            pltpu.make_async_copy(crossed_refs[i], cross_buf.at[pl.ds(i * each, each)], cross_sem.at[i]).wait()
+        term_ref = refs[1]
 
     def group_step(k, carry):
         group = source_ref[k // 2] * 2 + k % 2
@@ -175,8 +170,7 @@
         at = pl.ds(pl.multiple_of(k % 2 * tile, tile), tile)
 
         def work(n):
-            tiles_copy(v_ref, v_buf, v_sem, group, k, n).wait()
-            tiles = v_buf[k, pl.ds(0, n)].reshape(n * tile, tile)
+            tiles = v_ref[group, pl.ds(0, n)].reshape(n * tile, tile)
             found = []
             for m in range(n):
                 target = target_ref[m, group]
@@ -186,7 +180,7 @@
             found = jnp.concatenate(found, axis=0) if n > 1 else found[0]
             product = lax.dot_general(tiles, found, (((0,), (0,)), ((), ())), preferred_element_type=jnp.float32)
             if crossing:
-                term_ref[i, at, :] = (product + cross_buf[i, at, :].astype(jnp.float32)).astype(jnp.bfloat16)
+                term_ref[i, at, :] = (product + crossed_refs[0][i, at, :].astype(jnp.float32)).astype(jnp.bfloat16)
             else:
                 out_ref[i, at, :] = product.astype(jnp.bfloat16)
 
@@ -200,24 +194,16 @@
 
 
 def share_kernel(*refs):
-    m_refs, (sum_ref, w_buf, w_sem) = refs[:-3], refs[-3:]
-    more = w_buf.shape[1]
-    copies = [
-        pltpu.make_async_copy(m_ref.at[pl.ds(m_ref.shape[0] - more, more)], w_buf.at[i], w_sem.at[i])
-        for i, m_ref in enumerate(m_refs)
-    ]
-    for copy in copies:
-        copy.start()
+    m_refs, sum_ref = refs[:-1], refs[-1]
+    share = sum_ref.shape[0] - 8
+    more = share + EXTRA
     total = None
-    for i, copy in enumerate(copies):
-        copy.wait()
-        term = w_buf[i].astype(jnp.float32)
+    for m_ref in m_refs:
+        term = m_ref[pl.ds(m_ref.shape[0] - more, more), :].astype(jnp.float32)
         total = term if total is None else total + term
-    share = more - EXTRA
     sum_ref[pl.ds(0, share), :] = total[:share]
     bias = total[share : share + 1] + total[share + 1 : share + 2]
-    rest = sum_ref.shape[0] - share
-    sum_ref[pl.ds(share, rest), :] = jnp.broadcast_to(bias, (rest, bias.shape[1]))
+    sum_ref[pl.ds(share, 8), :] = jnp.broadcast_to(bias, (8, bias.shape[1]))
 
 
 def add_shares(messages, share):
@@ -225,12 +211,8 @@
     return pl.pallas_call(
         share_kernel,
         out_shape=jax.ShapeDtypeStruct((share + 8, width), jnp.float32),
-        in_specs=[pl.BlockSpec(memory_space=pl.ANY)] * len(messages),
+        in_specs=[pl.BlockSpec(memory_space=pltpu.VMEM)] * len(messages),
         out_specs=pl.BlockSpec(memory_space=pltpu.VMEM),
-        scratch_shapes=[
-            pltpu.VMEM((len(messages), share + EXTRA, width), jnp.bfloat16),
-            pltpu.SemaphoreType.DMA((len(messages),)),
-        ],
         compiler_params=pltpu.CompilerParams(vmem_limit_bytes=VMEM),
         cost_estimate=cost(1 << 20, 1 << 20),
         name="add_shares",
@@ -249,23 +231,13 @@
 def spread(shards, at_source, at_turn, index, targets, counts, messages, values, crossed=()):
     parts = len(messages)
     width = messages[0].shape[1]
-    slot_total, tile = values.shape[1:3]
+    tile = values.shape[-1]
     rows = 2 * tile
-    anywhere = pl.BlockSpec(memory_space=pl.ANY)
     inside = pl.BlockSpec(memory_space=pltpu.VMEM)
-    scratch = [
-        pltpu.VMEM((parts * rows + tile, width), jnp.bfloat16),
-        pltpu.VMEM((shards * 2, slot_total, tile, tile), jnp.bfloat16),
-        pltpu.SemaphoreType.DMA((parts,)),
-        pltpu.SemaphoreType.DMA((shards * 2,)),
-    ]
+    scratch = [pltpu.VMEM((parts * rows + tile, width), jnp.bfloat16)]
     if crossed:
         out_shape = (jax.ShapeDtypeStruct((rows, width), jnp.bfloat16),) * shards
-        scratch += [
-            pltpu.VMEM((shards, rows, width), jnp.bfloat16),
-            pltpu.VMEM((shards, rows, width), jnp.bfloat16),
-            pltpu.SemaphoreType.DMA((len(crossed),)),
-        ]
+        scratch.append(pltpu.VMEM((shards, rows, width), jnp.bfloat16))
     else:
         out_shape = (jax.ShapeDtypeStruct((shards, rows, width), jnp.bfloat16),)
     return pl.pallas_call(
@@ -276,14 +248,14 @@
         grid_spec=pltpu.PrefetchScalarGridSpec(
             num_scalar_prefetch=3,
             grid=(),
-            in_specs=[anywhere] * (1 + parts + len(crossed)),
+            in_specs=[inside] * (1 + parts + len(crossed)),
             out_specs=(inside,) * len(out_shape),
             scratch_shapes=scratch,
         ),
         compiler_params=pltpu.CompilerParams(vmem_limit_bytes=VMEM),
         cost_estimate=cost(shards << 32, shards << 20),
         name="spread",
-    )(index, targets, counts, values, *messages, *crossed)
+    )(index, targets, counts, pltpu.with_memory_space_constraint(values, pltpu.VMEM), *messages, *crossed)
 
 
 def middle_kernel(parts, at_place, index_ref, *refs):
@@ -407,6 +379,7 @@
     index = lax.dynamic_slice_in_dim(jnp.asarray(table), lax.axis_index(ALL), 1)[0]
 
     own = [send_by(features, CHIP, o) if any(o) else features for o in chips]
+    values, index = fetch(values, index)
     index, own[1] = lax.optimization_barrier((index, own[1]))
     crossed = [send_by(x, ("core",), (1,)) for x in own]
     partial = aggregate(begin["come"], begin["to"], len(parts), index, targets, counts, own + crossed, values)

time: 209 us -> 196 us (0.938)
  local copies, waits for them, and re-layouts: 6.4 us -> 0.73 us
  Pallas kernels: 34.4 us -> 28.8 us
  waiting for transfers between devices: 87.6 us -> 83.4 us
    ppermute x41, waiting for transfers between devices: 79 us -> 64.7 us  [send_by(): return lax.ppermute(value, axes, pairs)]
    ppermute x5, waiting for transfers between devices: 8.59 us -> 18.7 us  [exchange(): lax.ppermute(value, axis, [(i, i ^ mask) for i in range(SIZES[axis])])]
    ppermute x41, starting transfers between devices: 66.3 us -> 74.6 us  [send_by(): return lax.ppermute(value, axes, pairs)]
    ppermute x5, starting transfers between devices: 10.1 us -> 2.5 us  [exchange(): lax.ppermute(value, axis, [(i, i ^ mask) for i in range(SIZES[axis])])]
    unnamed x18 -> x12, local copies, waits for them, and re-layouts: 5.69 us -> 0.03 us
    pallas_call x4, Pallas kernels: 16.1 us -> 11.4 us  [spread(): pl.pallas_call(lambda *refs: backward_kernel(shards, parts, at_source, at...]
    pallas_call x0 -> x1, Pallas kernels: none -> 4.61 us  [fetch(): pl.pallas_call(fetch_kernel, out_shape=(pltpu.VMEM(values.shape, values.d...]
    pallas_call x1, Pallas kernels: 13.9 us -> 9.27 us  [aggregate(): pl.pallas_call(lambda *refs: forward_kernel(shards, at_source, at_place,...]
  transfers between devices with their start and end apart: 46 -> 46, of which waited for: 20 -> 21; matrix products, arithmetic and copies ran while one was open for 1% -> 1% of each run, Pallas kernels for 9% -> 9%
where the time goes in v6:
time: 196 us; the launch traced here: 193 us
  waiting for transfers between devices  83.4 us (43%)
  starting transfers between devices  77.1 us (39%)
  Pallas kernels  28.8 us (15%)
    ppermute x41, starting transfers between devices, send_by(): return lax.ppermute(value, axes, pairs)  74.6 us
    ppermute x41, waiting for transfers between devices, send_by(): return lax.ppermute(value, axes, pairs)  64.7 us
    ppermute x5, waiting for transfers between devices, exchange(): lax.ppermute(value, axis, [(i, i ^ mask) for i in range(SIZES[axis])])  18.7 us
    pallas_call x4, Pallas kernels, spread(): pl.pallas_call(lambda *refs: backward_kernel(shards, parts, at_source, at...  11.4 us
    pallas_call x1, Pallas kernels, aggregate(): pl.pallas_call(lambda *refs: forward_kernel(shards, at_source, at_place,...  9.27 us
    pallas_call x1, Pallas kernels, fetch(): pl.pallas_call(fetch_kernel, out_shape=(pltpu.VMEM(values.shape, values.d...  4.61 us
  transfers between devices with their start and end apart: 46, of which 21 were waited for; matrix products, arithmetic and copies ran while one was open for 1% of the time, Pallas kernels for 9%

profile of v6, /device:TPU:0, one launch (start us, length us, event | category | flops | bytes accessed | tf_op | source)
XLA Modules:
  0.0 192.5 jit_solution(16345224254255240840)
XLA Ops:
  9.9 4.6 %fetch.1 = (bf16[32,8,128,128]{3,2,1,0:T(8,128)(2,1)S(1)}, s32[56]{0:T(128)S(1)}) custom-call(s32[56]{0:T(128)S(1)} %dynamic-slice_bitcast_fusion.index_ref, bf16[32,8,128,128]{3,2,1,0:T(8,128)(2,1)} %bitcast.20), custom_call_target="tpu_custom_call" | custom-call | bytes 16777216 | tf_op jit(solution)/shard_map/fetch/pallas_call | solution.py:80
  14.5 3.2 %collective-permute-start.5 = (bf16[256,512]{1,0:T(8,128)(2,1)S(1)}, bf16[256,512]{1,0:T(8,128)(2,1)S(1)}, u32[]{:S(2)}, u32[]{:S(2)}) collective-permute-start(bf16[256,512]{1,0:T(8,128)(2,1)S(1)} %copy-done.1), channel_id=1, source_target_pairs={{0,112},{16,64},{32,80},{48,96},{64,48},{80,0},{96,16},{112,32},{1... | collective-permute-start | bytes 786440 | tf_op jit(solution)/shard_map/ppermute | solution.py:26
  17.7 7.5 %collective-permute-start.6 = (bf16[256,512]{1,0:T(8,128)(2,1)S(1)}, bf16[256,512]{1,0:T(8,128)(2,1)S(1)}, u32[]{:S(2)}, u32[]{:S(2)}) collective-permute-start(bf16[256,512]{1,0:T(8,128)(2,1)S(1)} %copy-done.1), channel_id=1, source_target_pairs={{0,96},{16,112},{32,64},{48,80},{64,32},{80,48},{96,0},{112,16},{1... | collective-permute-start | bytes 786440 | tf_op jit(solution)/shard_map/ppermute | solution.py:26
  28.7 3.6 %collective-permute-done.6.refs_11_ = bf16[256,512]{1,0:T(8,128)(2,1)S(1)} collective-permute-done((bf16[256,512]{1,0:T(8,128)(2,1)S(1)}, bf16[256,512]{1,0:T(8,128)(2,1)S(1)}, u32[]{:S(2)}, u32[]{:S(2)}) %collective-permute-start.6) | collective-permute-done | bytes 262176 | tf_op jit(solution)/shard_map/ppermute | solution.py:26
  35.0 9.3 %aggregate.1 = (bf16[256,512]{1,0:T(8,128)(2,1)S(1)}, bf16[256,512]{1,0:T(8,128)(2,1)S(1)}, bf16[256,512]{1,0:T(8,128)(2,1)S(1)}, bf16[256,512]{1,0:T(8,128)(2,1...) custom-call(s32[56]{0:T(128)S(1)} %get-tuple-element.86.refs_0_, ...), custom_call_target="tpu_custom_call" | custom-call | flops 8589934592 | bytes 16777216 | tf_op jit(solution)/shard_map/aggregate/pallas_call | solution.py:129
  46.1 4.3 %collective-permute-start.16 = (bf16[256,512]{1,0:T(8,128)(2,1)S(1)}, bf16[256,512]{1,0:T(8,128)(2,1)S(1)}, u32[]{:S(2)}, u32[]{:S(2)}) collective-permute-start(bf16[256,512]{1,0:T(8,128)(2,1)S(1)} %get-tuple-element.55), channel_id=1, source_target_pairs={{0,2},{1,3},{2,0},{3,1},{4,6},{5,7},{6,4},{7,5},{8,10},{9,11},{10,... | collective-permute-start | bytes 786440 | tf_op jit(solution)/shard_map/ppermute | solution.py:26
  56.1 11.2 %collective-permute-start.20 = (bf16[256,512]{1,0:T(8,128)(2,1)S(1)}, bf16[256,512]{1,0:T(8,128)(2,1)S(1)}, u32[]{:S(2)}, u32[]{:S(2)}) collective-permute-start(bf16[256,512]{1,0:T(8,128)(2,1)S(1)} %get-tuple-element.59), channel_id=1, source_target_pairs={{0,6},{1,7},{2,4},{3,5},{4,2},{5,3},{6,0},{7,1},{8,14},{9,15},{10,... | collective-permute-start | bytes 786440 | tf_op jit(solution)/shard_map/ppermute | solution.py:26
  67.3 3.0 %collective-permute-start.21 = (bf16[256,512]{1,0:T(8,128)(2,1)S(1)}, bf16[256,512]{1,0:T(8,128)(2,1)S(1)}, u32[]{:S(2)}, u32[]{:S(2)}) collective-permute-start(bf16[256,512]{1,0:T(8,128)(2,1)S(1)} %get-tuple-element.60), channel_id=1, source_target_pairs={{0,7},{1,4},{2,5},{3,6},{4,3},{5,0},{6,1},{7,2},{8,15},{9,12},{10,... | collective-permute-start | bytes 786440 | tf_op jit(solution)/shard_map/ppermute | solution.py:26
  70.3 3.7 %collective-permute-done.20.refs_7_ = bf16[256,512]{1,0:T(8,128)(2,1)S(1)} collective-permute-done((bf16[256,512]{1,0:T(8,128)(2,1)S(1)}, bf16[256,512]{1,0:T(8,128)(2,1)S(1)}, u32[]{:S(2)}, u32[]{:S(2)}) %collective-permute-start.20) | collective-permute-done | bytes 262176 | tf_op jit(solution)/shard_map/ppermute | solution.py:26
  74.0 6.9 %collective-permute-done.21.refs_8_ = bf16[256,512]{1,0:T(8,128)(2,1)S(1)} collective-permute-done((bf16[256,512]{1,0:T(8,128)(2,1)S(1)}, bf16[256,512]{1,0:T(8,128)(2,1)S(1)}, u32[]{:S(2)}, u32[]{:S(2)}) %collective-permute-start.21) | collective-permute-done | bytes 262176 | tf_op jit(solution)/shard_map/ppermute | solution.py:26
  84.1 4.8 %collective-permute-start.23 = (bf16[336,512]{1,0:T(8,128)(2,1)S(1)}, bf16[336,512]{1,0:T(8,128)(2,1)S(1)}, u32[]{:S(2)}, u32[]{:S(2)}) collective-permute-start(bf16[336,512]{1,0:T(8,128)(2,1)S(1)} %get-tuple-element.64), channel_id=1, source_target_pairs={{0,2},{1,3},{2,0},{3,1},{4,6},{5,7},{6,4},{7,5},{8,10},{9,11},{10,... | collective-permute-start | bytes 1032200 | tf_op jit(solution)/shard_map/ppermute | solution.py:26
  89.6 3.4 %collective-permute-start.25 = (bf16[336,512]{1,0:T(8,128)(2,1)S(1)}, bf16[336,512]{1,0:T(8,128)(2,1)S(1)}, u32[]{:S(2)}, u32[]{:S(2)}) collective-permute-start(bf16[336,512]{1,0:T(8,128)(2,1)S(1)} %get-tuple-element.66), channel_id=1, source_target_pairs={{0,4},{1,5},{2,6},{3,7},{4,0},{5,1},{6,2},{7,3},{8,12},{9,13},{10,... | collective-permute-start | bytes 1032200 | tf_op jit(solution)/shard_map/ppermute | solution.py:26
  95.5 4.4 %collective-permute-start.27 = (bf16[336,512]{1,0:T(8,128)(2,1)S(1)}, bf16[336,512]{1,0:T(8,128)(2,1)S(1)}, u32[]{:S(2)}, u32[]{:S(2)}) collective-permute-start(bf16[336,512]{1,0:T(8,128)(2,1)S(1)} %get-tuple-element.68), channel_id=1, source_target_pairs={{0,6},{1,7},{2,4},{3,5},{4,2},{5,3},{6,0},{7,1},{8,14},{9,15},{10,... | collective-permute-start | bytes 1032200 | tf_op jit(solution)/shard_map/ppermute | solution.py:26
  100.0 18.3 %collective-permute-done.23.refs_2_.refs_6_ = bf16[336,512]{1,0:T(8,128)(2,1)S(1)} collective-permute-done((bf16[336,512]{1,0:T(8,128)(2,1)S(1)}, bf16[336,512]{1,0:T(8,128)(2,1)S(1)}, u32[]{:S(2)}, u32[]{:S(2)}) %collective-permute-start.23) | collective-permute-done | bytes 344096 | tf_op jit(solution)/shard_map/ppermute | solution.py:26
  118.3 11.2 %collective-permute-done.28.refs_7_.refs_11_ = bf16[336,512]{1,0:T(8,128)(2,1)S(1)} collective-permute-done((bf16[336,512]{1,0:T(8,128)(2,1)S(1)}, bf16[336,512]{1,0:T(8,128)(2,1)S(1)}, u32[]{:S(2)}, u32[]{:S(2)}) %collective-permute-start.28) | collective-permute-done | bytes 344096 | tf_op jit(solution)/shard_map/ppermute | solution.py:26
  135.3 2.9 %spread.5 = bf16[4,256,512]{2,1,0:T(8,128)(2,1)S(1)} custom-call(s32[56]{0:T(128)S(1)} %get-tuple-element.86.refs_0_, s32[8,32]{1,0:T(8,128)S(1)} %bitcast.11, s32[32]{0:T(128)S(1)} %bitcast.17, bf16[32,8,128,128]{3,2,1,0:T(8,128)(2,1)S(1)} %get-tuple-element.51.refs_3_, bf16[336,512]{1,0:T(8,128)(2,1)S(1)} %get-tuple-element.62.refs_0_.refs_4_, ...), custom_call_target="tpu_custom_call" | custom-call | flops 17179869184 | bytes 4194304 | tf_op jit(solution)/shard_map/spread/pallas_call | solution.py:243
  140.2 2.9 %spread.6 = (bf16[256,512]{1,0:T(8,128)(2,1)S(1)}, bf16[256,512]{1,0:T(8,128)(2,1)S(1)}, bf16[256,512]{1,0:T(8,128)(2,1)S(1)}, bf16[256,512]{1,0:T(8,128)(2,1)S(1)}) custom-call(s32[56]{0:T(128)S(1)} %get-tuple-element.86.refs_0_, s32[8,32]{1,0:T(8,128)S(1)} %bitcast.12, s32[32]{0:T(128)S(1)} %bitcast.18, ...), custom_call_target="tpu_custom_call" | custom-call | flops 17179869184 | bytes 4194304 | tf_op jit(solution)/shard_map/spread/pallas_call | solution.py:243
  143.1 3.7 %collective-permute-done.36 = f32[72,512]{1,0:T(8,128)S(1)} collective-permute-done((f32[72,512]{1,0:T(8,128)S(1)}, f32[72,512]{1,0:T(8,128)S(1)}, u32[]{:S(2)}, u32[]{:S(2)}) %collective-permute-start.36) | collective-permute-done | bytes 147488 | tf_op jit(solution)/shard_map/ppermute | solution.py:30
  148.6 3.3 %collective-permute-start.34 = (bf16[256,512]{1,0:T(8,128)(2,1)S(1)}, bf16[256,512]{1,0:T(8,128)(2,1)S(1)}, u32[]{:S(2)}, u32[]{:S(2)}) collective-permute-start(bf16[256,512]{1,0:T(8,128)(2,1)S(1)} %get-tuple-element.81), channel_id=1, source_target_pairs={{0,112},{16,64},{32,80},{48,96},{64,48},{80,0},{96,16},{112,32},{1... | collective-permute-start | bytes 786440 | tf_op jit(solution)/shard_map/ppermute | solution.py:26
  156.6 11.0 %collective-permute-done.42 = bf16[72,512]{1,0:T(8,128)(2,1)S(1)} collective-permute-done((bf16[72,512]{1,0:T(8,128)(2,1)S(1)}, bf16[72,512]{1,0:T(8,128)(2,1)S(1)}, u32[]{:S(2)}, u32[]{:S(2)}) %collective-permute-start.42) | collective-permute-done | bytes 73760 | tf_op jit(solution)/shard_map/ppermute | solution.py:30
  167.8 3.1 %collective-permute-start.45 = (bf16[128,512]{1,0:T(8,128)(2,1)S(1)}, bf16[128,512]{1,0:T(8,128)(2,1)S(1)}, u32[]{:S(2)}, u32[]{:S(2)}) collective-permute-start(bf16[128,512]{1,0:T(8,128)(2,1)S(1)} %pad_maximum_fusion.refs_1_), channel_id=1, source_target_pairs={{0,3},{1,0},{2,1},{3,2},{4,7},{5,4},{6,5},{7,6},{8,11},{9,8},{10,9... | collective-permute-start | bytes 393224 | tf_op jit(solution)/shard_map/ppermute | solution.py:26
  173.1 3.6 %collective-permute-done.43.refs_2_ = bf16[128,512]{1,0:T(8,128)(2,1)S(1)} collective-permute-done((bf16[128,512]{1,0:T(8,128)(2,1)S(1)}, bf16[128,512]{1,0:T(8,128)(2,1)S(1)}, u32[]{:S(2)}, u32[]{:S(2)}) %collective-permute-start.43) | collective-permute-done | bytes 131104 | tf_op jit(solution)/shard_map/ppermute | solution.py:26
  183.1 3.0 %collective-permute-done.32 = bf16[256,512]{1,0:T(8,128)(2,1)S(1)} collective-permute-done((bf16[256,512]{1,0:T(8,128)(2,1)S(1)}, bf16[256,512]{1,0:T(8,128)(2,1)S(1)}, u32[]{:S(2)}, u32[]{:S(2)}) %collective-permute-start.32) | collective-permute-done | bytes 262176 | tf_op jit(solution)/shard_map/ppermute | solution.py:26
  186.1 5.5 %collective-permute-done.39 = bf16[256,512]{1,0:T(8,128)(2,1)S(1)} collective-permute-done((bf16[256,512]{1,0:T(8,128)(2,1)S(1)}, bf16[256,512]{1,0:T(8,128)(2,1)S(1)}, u32[]{:S(2)}, u32[]{:S(2)}) %collective-permute-start.39) | collective-permute-done | bytes 262176 | tf_op jit(solution)/shard_map/ppermute | solution.py:26
  (100 shorter events, 53.3 us)
Async XLA Ops:
  0.7 13.8 %collective-permute-start = (bf16[256,512]{1,0:T(8,128)(2,1)}, bf16[256,512]{1,0:T(8,128)(2,1)S(1)}, u32[]{:S(2)}, u32[]{:S(2)}) collective-permute-start(bf16[256,512]{1,0:T(8,128)(2,1)} %refs_4_.1), channel_id=1, source_target_pairs={{0,16},{16,32},{32,48},{48,0},{64,80},{80,96},{96,112},{112,64},{1... | collective-permute-start | bytes 786440 | tf_op jit(solution)/shard_map/ppermute | solution.py:26
  2.7 15.0 %collective-permute-start.1 = (bf16[256,512]{1,0:T(8,128)(2,1)}, bf16[256,512]{1,0:T(8,128)(2,1)S(1)}, u32[]{:S(2)}, u32[]{:S(2)}) collective-permute-start(bf16[256,512]{1,0:T(8,128)(2,1)} %refs_4_.1), channel_id=1, source_target_pairs={{0,48},{16,0},{32,16},{48,32},{64,112},{80,64},{96,80},{112,96},{1... | collective-permute-start | bytes 786440 | tf_op jit(solution)/shard_map/ppermute | solution.py:26
  4.9 20.3 %collective-permute-start.2 = (bf16[256,512]{1,0:T(8,128)(2,1)}, bf16[256,512]{1,0:T(8,128)(2,1)S(1)}, u32[]{:S(2)}, u32[]{:S(2)}) collective-permute-start(bf16[256,512]{1,0:T(8,128)(2,1)} %refs_4_.1), channel_id=1, source_target_pairs={{0,64},{16,80},{32,96},{48,112},{64,0},{80,16},{96,32},{112,48},{1... | collective-permute-start | bytes 786440 | tf_op jit(solution)/shard_map/ppermute | solution.py:26
  6.4 20.2 %collective-permute-start.3 = (bf16[256,512]{1,0:T(8,128)(2,1)}, bf16[256,512]{1,0:T(8,128)(2,1)S(1)}, u32[]{:S(2)}, u32[]{:S(2)}) collective-permute-start(bf16[256,512]{1,0:T(8,128)(2,1)} %refs_4_.1), channel_id=1, source_target_pairs={{0,32},{16,48},{32,0},{48,16},{64,96},{80,112},{96,64},{112,80},{1... | collective-permute-start | bytes 786440 | tf_op jit(solution)/shard_map/ppermute | solution.py:26
  8.2 18.5 %collective-permute-start.4 = (bf16[256,512]{1,0:T(8,128)(2,1)}, bf16[256,512]{1,0:T(8,128)(2,1)S(1)}, u32[]{:S(2)}, u32[]{:S(2)}) collective-permute-start(bf16[256,512]{1,0:T(8,128)(2,1)} %refs_4_.1), channel_id=1, source_target_pairs={{0,80},{16,96},{32,112},{48,64},{64,16},{80,32},{96,48},{112,0},{1... | collective-permute-start | bytes 786440 | tf_op jit(solution)/shard_map/ppermute | solution.py:26
  14.5 14.2 %collective-permute-start.5 = (bf16[256,512]{1,0:T(8,128)(2,1)S(1)}, bf16[256,512]{1,0:T(8,128)(2,1)S(1)}, u32[]{:S(2)}, u32[]{:S(2)}) collective-permute-start(bf16[256,512]{1,0:T(8,128)(2,1)S(1)} %copy-done.1), channel_id=1, source_target_pairs={{0,112},{16,64},{32,80},{48,96},{64,48},{80,0},{96,16},{112,32},{1... | collective-permute-start | bytes 786440 | tf_op jit(solution)/shard_map/ppermute | solution.py:26
  17.7 14.5 %collective-permute-start.6 = (bf16[256,512]{1,0:T(8,128)(2,1)S(1)}, bf16[256,512]{1,0:T(8,128)(2,1)S(1)}, u32[]{:S(2)}, u32[]{:S(2)}) collective-permute-start(bf16[256,512]{1,0:T(8,128)(2,1)S(1)} %copy-done.1), channel_id=1, source_target_pairs={{0,96},{16,112},{32,64},{48,80},{64,32},{80,48},{96,0},{112,16},{1... | collective-permute-start | bytes 786440 | tf_op jit(solution)/shard_map/ppermute | solution.py:26
  46.1 21.2 %collective-permute-start.16 = (bf16[256,512]{1,0:T(8,128)(2,1)S(1)}, bf16[256,512]{1,0:T(8,128)(2,1)S(1)}, u32[]{:S(2)}, u32[]{:S(2)}) collective-permute-start(bf16[256,512]{1,0:T(8,128)(2,1)S(1)} %get-tuple-element.55), channel_id=1, source_target_pairs={{0,2},{1,3},{2,0},{3,1},{4,6},{5,7},{6,4},{7,5},{8,10},{9,11},{10,... | collective-permute-start | bytes 786440 | tf_op jit(solution)/shard_map/ppermute | solution.py:26
  50.4 19.9 %collective-permute-start.17 = (bf16[256,512]{1,0:T(8,128)(2,1)S(1)}, bf16[256,512]{1,0:T(8,128)(2,1)S(1)}, u32[]{:S(2)}, u32[]{:S(2)}) collective-permute-start(bf16[256,512]{1,0:T(8,128)(2,1)S(1)} %get-tuple-element.56), channel_id=1, source_target_pairs={{0,3},{1,0},{2,1},{3,2},{4,7},{5,4},{6,5},{7,6},{8,11},{9,8},{10,9... | collective-permute-start | bytes 786440 | tf_op jit(solution)/shard_map/ppermute | solution.py:26
  52.9 17.4 %collective-permute-start.18 = (bf16[256,512]{1,0:T(8,128)(2,1)S(1)}, bf16[256,512]{1,0:T(8,128)(2,1)S(1)}, u32[]{:S(2)}, u32[]{:S(2)}) collective-permute-start(bf16[256,512]{1,0:T(8,128)(2,1)S(1)} %get-tuple-element.57), channel_id=1, source_target_pairs={{0,4},{1,5},{2,6},{3,7},{4,0},{5,1},{6,2},{7,3},{8,12},{9,13},{10,... | collective-permute-start | bytes 786440 | tf_op jit(solution)/shard_map/ppermute | solution.py:26
  54.6 15.6 %collective-permute-start.19 = (bf16[256,512]{1,0:T(8,128)(2,1)S(1)}, bf16[256,512]{1,0:T(8,128)(2,1)S(1)}, u32[]{:S(2)}, u32[]{:S(2)}) collective-permute-start(bf16[256,512]{1,0:T(8,128)(2,1)S(1)} %get-tuple-element.58), channel_id=1, source_target_pairs={{0,5},{1,6},{2,7},{3,4},{4,1},{5,2},{6,3},{7,0},{8,13},{9,14},{10,... | collective-permute-start | bytes 786440 | tf_op jit(solution)/shard_map/ppermute | solution.py:26
  56.1 17.9 %collective-permute-start.20 = (bf16[256,512]{1,0:T(8,128)(2,1)S(1)}, bf16[256,512]{1,0:T(8,128)(2,1)S(1)}, u32[]{:S(2)}, u32[]{:S(2)}) collective-permute-start(bf16[256,512]{1,0:T(8,128)(2,1)S(1)} %get-tuple-element.59), channel_id=1, source_target_pairs={{0,6},{1,7},{2,4},{3,5},{4,2},{5,3},{6,0},{7,1},{8,14},{9,15},{10,... | collective-permute-start | bytes 786440 | tf_op jit(solution)/shard_map/ppermute | solution.py:26
  67.3 13.6 %collective-permute-start.21 = (bf16[256,512]{1,0:T(8,128)(2,1)S(1)}, bf16[256,512]{1,0:T(8,128)(2,1)S(1)}, u32[]{:S(2)}, u32[]{:S(2)}) collective-permute-start(bf16[256,512]{1,0:T(8,128)(2,1)S(1)} %get-tuple-element.60), channel_id=1, source_target_pairs={{0,7},{1,4},{2,5},{3,6},{4,3},{5,0},{6,1},{7,2},{8,15},{9,12},{10,... | collective-permute-start | bytes 786440 | tf_op jit(solution)/shard_map/ppermute | solution.py:26
  84.1 34.2 %collective-permute-start.23 = (bf16[336,512]{1,0:T(8,128)(2,1)S(1)}, bf16[336,512]{1,0:T(8,128)(2,1)S(1)}, u32[]{:S(2)}, u32[]{:S(2)}) collective-permute-start(bf16[336,512]{1,0:T(8,128)(2,1)S(1)} %get-tuple-element.64), channel_id=1, source_target_pairs={{0,2},{1,3},{2,0},{3,1},{4,6},{5,7},{6,4},{7,5},{8,10},{9,11},{10,... | collective-permute-start | bytes 1032200 | tf_op jit(solution)/shard_map/ppermute | solution.py:26
  88.9 29.4 %collective-permute-start.24 = (bf16[336,512]{1,0:T(8,128)(2,1)S(1)}, bf16[336,512]{1,0:T(8,128)(2,1)S(1)}, u32[]{:S(2)}, u32[]{:S(2)}) collective-permute-start(bf16[336,512]{1,0:T(8,128)(2,1)S(1)} %get-tuple-element.65), channel_id=1, source_target_pairs={{0,3},{1,0},{2,1},{3,2},{4,7},{5,4},{6,5},{7,6},{8,11},{9,8},{10,9... | collective-permute-start | bytes 1032200 | tf_op jit(solution)/shard_map/ppermute | solution.py:26
  89.6 28.7 %collective-permute-start.25 = (bf16[336,512]{1,0:T(8,128)(2,1)S(1)}, bf16[336,512]{1,0:T(8,128)(2,1)S(1)}, u32[]{:S(2)}, u32[]{:S(2)}) collective-permute-start(bf16[336,512]{1,0:T(8,128)(2,1)S(1)} %get-tuple-element.66), channel_id=1, source_target_pairs={{0,4},{1,5},{2,6},{3,7},{4,0},{5,1},{6,2},{7,3},{8,12},{9,13},{10,... | collective-permute-start | bytes 1032200 | tf_op jit(solution)/shard_map/ppermute | solution.py:26
  93.1 25.2 %collective-permute-start.26 = (bf16[336,512]{1,0:T(8,128)(2,1)S(1)}, bf16[336,512]{1,0:T(8,128)(2,1)S(1)}, u32[]{:S(2)}, u32[]{:S(2)}) collective-permute-start(bf16[336,512]{1,0:T(8,128)(2,1)S(1)} %get-tuple-element.67), channel_id=1, source_target_pairs={{0,5},{1,6},{2,7},{3,4},{4,1},{5,2},{6,3},{7,0},{8,13},{9,14},{10,... | collective-permute-start | bytes 1032200 | tf_op jit(solution)/shard_map/ppermute | solution.py:26
  95.5 22.8 %collective-permute-start.27 = (bf16[336,512]{1,0:T(8,128)(2,1)S(1)}, bf16[336,512]{1,0:T(8,128)(2,1)S(1)}, u32[]{:S(2)}, u32[]{:S(2)}) collective-permute-start(bf16[336,512]{1,0:T(8,128)(2,1)S(1)} %get-tuple-element.68), channel_id=1, source_target_pairs={{0,6},{1,7},{2,4},{3,5},{4,2},{5,3},{6,0},{7,1},{8,14},{9,15},{10,... | collective-permute-start | bytes 1032200 | tf_op jit(solution)/shard_map/ppermute | solution.py:26
  138.2 15.5 %collective-permute-start.38 = (bf16[4,256,512]{2,1,0:T(8,128)(2,1)S(1)}, bf16[4,256,512]{2,1,0:T(8,128)(2,1)S(1)}, u32[]{:S(2)}, u32[]{:S(2)}) collective-permute-start(bf16[4,256,512]{2,1,0:T(8,128)(2,1)S(1)} %spread.5), channel_id=1, source_target_pairs={{0,8},{8,0},{1,9},{9,1},{2,10},{10,2},{3,11},{11,3},{4,12},{12,4},... | collective-permute-start | bytes 3145736 | tf_op jit(solution)/shard_map/ppermute | solution.py:26
  147.0 24.0 %collective-permute-start.35 = (bf16[256,512]{1,0:T(8,128)(2,1)S(1)}, bf16[256,512]{1,0:T(8,128)(2,1)S(1)}, u32[]{:S(2)}, u32[]{:S(2)}) collective-permute-start(bf16[256,512]{1,0:T(8,128)(2,1)S(1)} %get-tuple-element.82), channel_id=1, source_target_pairs={{0,96},{16,112},{32,64},{48,80},{64,32},{80,48},{96,0},{112,16},{1... | collective-permute-start | bytes 786440 | tf_op jit(solution)/shard_map/ppermute | solution.py:26
  148.6 22.3 %collective-permute-start.34 = (bf16[256,512]{1,0:T(8,128)(2,1)S(1)}, bf16[256,512]{1,0:T(8,128)(2,1)S(1)}, u32[]{:S(2)}, u32[]{:S(2)}) collective-permute-start(bf16[256,512]{1,0:T(8,128)(2,1)S(1)} %get-tuple-element.81), channel_id=1, source_target_pairs={{0,112},{16,64},{32,80},{48,96},{64,48},{80,0},{96,16},{112,32},{1... | collective-permute-start | bytes 786440 | tf_op jit(solution)/shard_map/ppermute | solution.py:26
  151.9 15.6 %collective-permute-start.42 = (bf16[72,512]{1,0:T(8,128)(2,1)S(1)}, bf16[72,512]{1,0:T(8,128)(2,1)S(1)}, u32[]{:S(2)}, u32[]{:S(2)}) collective-permute-start(bf16[72,512]{1,0:T(8,128)(2,1)S(1)} %convert.12), channel_id=1, source_target_pairs={{0,4},{4,0},{1,5},{5,1},{2,6},{6,2},{3,7},{7,3},{8,12},{12,8},{9,1... | collective-permute-start | bytes 221192 | tf_op jit(solution)/shard_map/ppermute | solution.py:30
  170.9 15.2 %collective-permute-start.32 = (bf16[256,512]{1,0:T(8,128)(2,1)S(1)}, bf16[256,512]{1,0:T(8,128)(2,1)S(1)}, u32[]{:S(2)}, u32[]{:S(2)}) collective-permute-start(bf16[256,512]{1,0:T(8,128)(2,1)S(1)} %get-tuple-element.79), channel_id=1, source_target_pairs={{0,32},{16,48},{32,0},{48,16},{64,96},{80,112},{96,64},{112,80},{1... | collective-permute-start | bytes 786440 | tf_op jit(solution)/shard_map/ppermute | solution.py:26
  177.4 14.2 %collective-permute-start.39 = (bf16[256,512]{1,0:T(8,128)(2,1)S(1)}, bf16[256,512]{1,0:T(8,128)(2,1)S(1)}, u32[]{:S(2)}, u32[]{:S(2)}) collective-permute-start(bf16[256,512]{1,0:T(8,128)(2,1)S(1)} %get-tuple-element.88), channel_id=1, source_target_pairs={{0,16},{16,32},{32,48},{48,0},{64,80},{80,96},{96,112},{112,64},{1... | collective-permute-start | bytes 786440 | tf_op jit(solution)/shard_map/ppermute | solution.py:26
  (28 other events, 376.1 us)

commit v7 on v6

--- a/solution.py
+++ b/solution.py
@@ -330,6 +330,7 @@
     )(index, *pieces)
 
 
+PARTS = ((0, 0), (0, 1), (0, 3), (1, 0), (1, 2), (0, 2), (1, 1), (1, 3))
 CHIP_HALVES = (((0, 0), (0, 1), (0, 3), (1, 0)), ((0, 2), (1, 1), (1, 3), (1, 2)))
 
 
@@ -352,7 +353,9 @@
             "to": [number(REP, o, 1) for o in parts],
             "cross": [c + 1 - core for c in go],
             "stay": [c + core for c in go],
-            "turn": [(at["xh"] - o[0]) % SIZES["xh"] * SIZES["y"] + (at["y"] - o[1]) % SIZES["y"] for o in parts],
+            "turn": [
+                parts.index(((at["xh"] - h) % SIZES["xh"], (at["y"] - y) % SIZES["y"])) for h, y in all_offsets(REP)
+            ],
             "piece": [number(REP, (k, o), -1) for o in range(SIZES["y"]) for k in range(SIZES["xh"])],
         }
         row = []
@@ -371,7 +374,7 @@
     tile = values.shape[-1]
     slot_total = values.shape[1]
     assert local_rows == 2 * tile and slot_total == VARIANTS[-1]
-    parts = all_offsets(REP)
+    parts = list(PARTS)
     halves = CHIP_HALVES[::-1]
     chips = CHIP_HALVES[0] + CHIP_HALVES[1]
     y = SIZES["y"]
@@ -392,9 +395,10 @@
     share_sum = add_shares(messages, share)
     each = len(halves[0])
     across, merged = [], []
-    for i, step in enumerate((("xl", 1), ("z", 1), ("z", 2), ("xh", 1))):
-        index, share_sum = lax.optimization_barrier((index, share_sum))
-        arriving = exchange(share_sum, *step)
+    for i, step in enumerate((("xl", 1), ("z", 1), ("z", 2), None)):
+        if step:
+            index, share_sum = lax.optimization_barrier((index, share_sum))
+            arriving = exchange(share_sum, *step)
         k = i % 2
         if i < 2:
             found = spread(each, begin["cross"] + each * k, begin["turn"], index, targets, counts, messages, values)
@@ -404,14 +408,17 @@
                 each, begin["stay"] + each * k, begin["turn"], index, targets, counts, messages, values, across[k : k + 1]
             )
             merged += found
-        _, share_sum, arriving = lax.optimization_barrier((found, share_sum, arriving))
-        if i < 3:
+        if step:
+            _, share_sum, arriving = lax.optimization_barrier((found, share_sum, arriving))
             share_sum = share_sum + arriving
-        if i == 2:
-            share_sum = share_sum + exchange(share_sum, "core", 1)
+    last = [send_by(piece, CHIP, o) if any(o) else piece for piece, o in zip(merged, halves[0] + halves[1])]
+    _, share_sum = lax.optimization_barrier((found, share_sum))
+    share_sum = share_sum + exchange(share_sum, "core", 1)
+    arriving = exchange(share_sum, "xh", 1)
+    arriving, last[5] = lax.optimization_barrier((arriving, last[5]))
     total = None
-    for piece, o in zip(merged, halves[0] + halves[1]):
-        piece = (send_by(piece, CHIP, o) if any(o) else piece).astype(jnp.float32)
+    for piece in last:
+        piece = piece.astype(jnp.float32)
         total = piece if total is None else total + piece
     grad_features = total.astype(jnp.bfloat16)
 

time: 196 us -> 187 us (0.954)
  waiting for transfers between devices: 83.4 us -> 56.7 us
  starting transfers between devices: 77.1 us -> 88.3 us
  Pallas kernels: 28.8 us -> 35.4 us
    ppermute x5, waiting for transfers between devices: 18.7 us -> 2.56 us  [exchange(): lax.ppermute(value, axis, [(i, i ^ mask) for i in range(SIZES[axis])])]
    ppermute x41, waiting for transfers between devices: 64.7 us -> 54.1 us  [send_by(): return lax.ppermute(value, axes, pairs)]
    ppermute x41, starting transfers between devices: 74.6 us -> 82.2 us  [send_by(): return lax.ppermute(value, axes, pairs)]
    pallas_call x1, Pallas kernels: 9.27 us -> 13.5 us  [aggregate(): pl.pallas_call(lambda *refs: forward_kernel(shards, at_source, at_place,...]
    ppermute x5, starting transfers between devices: 2.5 us -> 6.13 us  [exchange(): lax.ppermute(value, axis, [(i, i ^ mask) for i in range(SIZES[axis])])]
    pallas_call x4, Pallas kernels: 11.4 us -> 13.8 us  [spread(): pl.pallas_call(lambda *refs: backward_kernel(shards, parts, at_source, at...]
  transfers between devices with their start and end apart: 46 -> 46, of which waited for: 21 -> 19; matrix products, arithmetic and copies ran while one was open for 1% -> 1% of each run, Pallas kernels for 9% -> 8%
where the time goes in v7:
time: 187 us; the launch traced here: 184 us
  starting transfers between devices  88.3 us (47%)
  waiting for transfers between devices  56.7 us (30%)
  Pallas kernels  35.4 us (19%)
    ppermute x41, starting transfers between devices, send_by(): return lax.ppermute(value, axes, pairs)  82.2 us
    ppermute x41, waiting for transfers between devices, send_by(): return lax.ppermute(value, axes, pairs)  54.1 us
    pallas_call x4, Pallas kernels, spread(): pl.pallas_call(lambda *refs: backward_kernel(shards, parts, at_source, at...  13.8 us
    pallas_call x1, Pallas kernels, aggregate(): pl.pallas_call(lambda *refs: forward_kernel(shards, at_source, at_place,...  13.5 us
    ppermute x5, starting transfers between devices, exchange(): lax.ppermute(value, axis, [(i, i ^ mask) for i in range(SIZES[axis])])  6.13 us
    pallas_call x1, Pallas kernels, fetch(): pl.pallas_call(fetch_kernel, out_shape=(pltpu.VMEM(values.shape, values.d...  4.61 us
  transfers between devices with their start and end apart: 46, of which 19 were waited for; matrix products, arithmetic and copies ran while one was open for 1% of the time, Pallas kernels for 8%

profile of v7, /device:TPU:0, one launch (start us, length us, event | category | flops | bytes accessed | tf_op | source)
XLA Modules:
  0.0 183.7 jit_solution(3364659172757009553)
XLA Ops:
  4.2 3.6 %collective-permute-start.3 = (bf16[256,512]{1,0:T(8,128)(2,1)}, bf16[256,512]{1,0:T(8,128)(2,1)S(1)}, u32[]{:S(2)}, u32[]{:S(2)}) collective-permute-start(bf16[256,512]{1,0:T(8,128)(2,1)} %refs_4_.1), channel_id=1, source_target_pairs={{0,32},{16,48},{32,0},{48,16},{64,96},{80,112},{96,64},{112,80},{1... | collective-permute-start | bytes 786440 | tf_op jit(solution)/shard_map/ppermute | solution.py:26
  7.8 4.1 %collective-permute-start.5 = (bf16[256,512]{1,0:T(8,128)(2,1)}, bf16[256,512]{1,0:T(8,128)(2,1)S(1)}, u32[]{:S(2)}, u32[]{:S(2)}) collective-permute-start(bf16[256,512]{1,0:T(8,128)(2,1)} %refs_4_.1), channel_id=1, source_target_pairs={{0,112},{16,64},{32,80},{48,96},{64,48},{80,0},{96,16},{112,32},{1... | collective-permute-start | bytes 786440 | tf_op jit(solution)/shard_map/ppermute | solution.py:26
  12.6 4.6 %fetch.1 = (bf16[32,8,128,128]{3,2,1,0:T(8,128)(2,1)S(1)}, s32[56]{0:T(128)S(1)}) custom-call(s32[56]{0:T(128)S(1)} %dynamic-slice_bitcast_fusion.index_ref, bf16[32,8,128,128]{3,2,1,0:T(8,128)(2,1)} %bitcast.20), custom_call_target="tpu_custom_call" | custom-call | bytes 16777216 | tf_op jit(solution)/shard_map/fetch/pallas_call | solution.py:80
  17.3 8.5 %collective-permute-start.6 = (bf16[256,512]{1,0:T(8,128)(2,1)S(1)}, bf16[256,512]{1,0:T(8,128)(2,1)S(1)}, u32[]{:S(2)}, u32[]{:S(2)}) collective-permute-start(bf16[256,512]{1,0:T(8,128)(2,1)S(1)} %copy-done.1), channel_id=1, source_target_pairs={{0,96},{16,112},{32,64},{48,80},{64,32},{80,48},{96,0},{112,16},{1... | collective-permute-start | bytes 786440 | tf_op jit(solution)/shard_map/ppermute | solution.py:26
  26.5 4.2 %collective-permute-done.6.refs_11_ = bf16[256,512]{1,0:T(8,128)(2,1)S(1)} collective-permute-done((bf16[256,512]{1,0:T(8,128)(2,1)S(1)}, bf16[256,512]{1,0:T(8,128)(2,1)S(1)}, u32[]{:S(2)}, u32[]{:S(2)}) %collective-permute-start.6) | collective-permute-done | bytes 262176 | tf_op jit(solution)/shard_map/ppermute | solution.py:26
  30.7 3.5 %collective-permute-done.1.refs_6_ = bf16[256,512]{1,0:T(8,128)(2,1)S(1)} collective-permute-done((bf16[256,512]{1,0:T(8,128)(2,1)S(1)}, bf16[256,512]{1,0:T(8,128)(2,1)S(1)}, u32[]{:S(2)}, u32[]{:S(2)}) %collective-permute-start.1) | collective-permute-done | bytes 262176 | tf_op jit(solution)/shard_map/ppermute | solution.py:26
  36.9 13.5 %aggregate.1 = (bf16[256,512]{1,0:T(8,128)(2,1)S(1)}, bf16[256,512]{1,0:T(8,128)(2,1)S(1)}, bf16[256,512]{1,0:T(8,128)(2,1)S(1)}, bf16[256,512]{1,0:T(8,128)(2,1...) custom-call(s32[56]{0:T(128)S(1)} %get-tuple-element.77.refs_0_, ...), custom_call_target="tpu_custom_call" | custom-call | flops 8589934592 | bytes 16777216 | tf_op jit(solution)/shard_map/aggregate/pallas_call | solution.py:129
  56.8 3.4 %collective-permute-start.19 = (bf16[256,512]{1,0:T(8,128)(2,1)S(1)}, bf16[256,512]{1,0:T(8,128)(2,1)S(1)}, u32[]{:S(2)}, u32[]{:S(2)}) collective-permute-start(bf16[256,512]{1,0:T(8,128)(2,1)S(1)} %get-tuple-element.57), channel_id=1, source_target_pairs={{0,2},{1,3},{2,0},{3,1},{4,6},{5,7},{6,4},{7,5},{8,10},{9,11},{10,... | collective-permute-start | bytes 786440 | tf_op jit(solution)/shard_map/ppermute | solution.py:26
  61.2 14.3 %collective-permute-start.21 = (bf16[256,512]{1,0:T(8,128)(2,1)S(1)}, bf16[256,512]{1,0:T(8,128)(2,1)S(1)}, u32[]{:S(2)}, u32[]{:S(2)}) collective-permute-start(bf16[256,512]{1,0:T(8,128)(2,1)S(1)} %get-tuple-element.59), channel_id=1, source_target_pairs={{0,7},{1,4},{2,5},{3,6},{4,3},{5,0},{6,1},{7,2},{8,15},{9,12},{10,... | collective-permute-start | bytes 786440 | tf_op jit(solution)/shard_map/ppermute | solution.py:26
  82.4 3.2 %collective-permute-start.23 = (bf16[336,512]{1,0:T(8,128)(2,1)S(1)}, bf16[336,512]{1,0:T(8,128)(2,1)S(1)}, u32[]{:S(2)}, u32[]{:S(2)}) collective-permute-start(bf16[336,512]{1,0:T(8,128)(2,1)S(1)} %get-tuple-element.63), channel_id=1, source_target_pairs={{0,3},{1,0},{2,1},{3,2},{4,7},{5,4},{6,5},{7,6},{8,11},{9,8},{10,9... | collective-permute-start | bytes 1032200 | tf_op jit(solution)/shard_map/ppermute | solution.py:26
  88.8 3.3 %collective-permute-start.26 = (bf16[336,512]{1,0:T(8,128)(2,1)S(1)}, bf16[336,512]{1,0:T(8,128)(2,1)S(1)}, u32[]{:S(2)}, u32[]{:S(2)}) collective-permute-start(bf16[336,512]{1,0:T(8,128)(2,1)S(1)} %get-tuple-element.66), channel_id=1, source_target_pairs={{0,2},{1,3},{2,0},{3,1},{4,6},{5,7},{6,4},{7,5},{8,10},{9,11},{10,... | collective-permute-start | bytes 1032200 | tf_op jit(solution)/shard_map/ppermute | solution.py:26
  92.2 10.2 %collective-permute-done.22.refs_1_.refs_5_ = bf16[336,512]{1,0:T(8,128)(2,1)S(1)} collective-permute-done((bf16[336,512]{1,0:T(8,128)(2,1)S(1)}, bf16[336,512]{1,0:T(8,128)(2,1)S(1)}, u32[]{:S(2)}, u32[]{:S(2)}) %collective-permute-start.22) | collective-permute-done | bytes 344096 | tf_op jit(solution)/shard_map/ppermute | solution.py:26
  102.3 4.8 %collective-permute-done.23.refs_2_.refs_6_ = bf16[336,512]{1,0:T(8,128)(2,1)S(1)} collective-permute-done((bf16[336,512]{1,0:T(8,128)(2,1)S(1)}, bf16[336,512]{1,0:T(8,128)(2,1)S(1)}, u32[]{:S(2)}, u32[]{:S(2)}) %collective-permute-start.23) | collective-permute-done | bytes 344096 | tf_op jit(solution)/shard_map/ppermute | solution.py:26
  107.2 3.4 %collective-permute-start.28 = (bf16[336,512]{1,0:T(8,128)(2,1)S(1)}, bf16[336,512]{1,0:T(8,128)(2,1)S(1)}, u32[]{:S(2)}, u32[]{:S(2)}) collective-permute-start(bf16[336,512]{1,0:T(8,128)(2,1)S(1)} %get-tuple-element.68), channel_id=1, source_target_pairs={{0,7},{1,4},{2,5},{3,6},{4,3},{5,0},{6,1},{7,2},{8,15},{9,12},{10,... | collective-permute-start | bytes 1032200 | tf_op jit(solution)/shard_map/ppermute | solution.py:26
  110.6 4.9 %collective-permute-done.26.refs_5_.refs_9_ = bf16[336,512]{1,0:T(8,128)(2,1)S(1)} collective-permute-done((bf16[336,512]{1,0:T(8,128)(2,1)S(1)}, bf16[336,512]{1,0:T(8,128)(2,1)S(1)}, u32[]{:S(2)}, u32[]{:S(2)}) %collective-permute-start.26) | collective-permute-done | bytes 344096 | tf_op jit(solution)/shard_map/ppermute | solution.py:26
  119.6 3.4 %spread.4 = bf16[4,256,512]{2,1,0:T(8,128)(2,1)S(1)} custom-call(s32[56]{0:T(128)S(1)} %get-tuple-element.77.refs_0_, s32[8,32]{1,0:T(8,128)S(1)} %bitcast.10, s32[32]{0:T(128)S(1)} %bitcast.16, bf16[32,8,128,128]{3,2,1,0:T(8,128)(2,1)S(1)} %get-tuple-element.50.refs_3_, bf16[336,512]{1,0:T(8,128)(2,1)S(1)} %get-tuple-element.61.refs_0_.refs_4_, ...), custom_call_target="tpu_custom_call" | custom-call | flops 17179869184 | bytes 4194304 | tf_op jit(solution)/shard_map/spread/pallas_call | solution.py:243
  126.0 3.5 %spread.5 = bf16[4,256,512]{2,1,0:T(8,128)(2,1)S(1)} custom-call(s32[56]{0:T(128)S(1)} %get-tuple-element.77.refs_0_, s32[8,32]{1,0:T(8,128)S(1)} %bitcast.11, s32[32]{0:T(128)S(1)} %bitcast.17, bf16[32,8,128,128]{3,2,1,0:T(8,128)(2,1)S(1)} %get-tuple-element.50.refs_3_, bf16[336,512]{1,0:T(8,128)(2,1)S(1)} %get-tuple-element.61.refs_0_.refs_4_, ...), custom_call_target="tpu_custom_call" | custom-call | flops 17179869184 | bytes 4194304 | tf_op jit(solution)/shard_map/spread/pallas_call | solution.py:243
  130.3 4.1 %collective-permute-start.37 = (f32[72,512]{1,0:T(8,128)S(1)}, f32[72,512]{1,0:T(8,128)S(1)}, u32[]{:S(2)}, u32[]{:S(2)}) collective-permute-start(f32[72,512]{1,0:T(8,128)S(1)} %add.54), channel_id=1, source_target_pairs={{0,32},{16,48},{32,0},{48,16},{1,33},{17,49},{33,1},{49,17},{2,34}... | collective-permute-start | bytes 442376 | tf_op jit(solution)/shard_map/ppermute | solution.py:30
  134.4 3.5 %spread.6 = (bf16[256,512]{1,0:T(8,128)(2,1)S(1)}, bf16[256,512]{1,0:T(8,128)(2,1)S(1)}, bf16[256,512]{1,0:T(8,128)(2,1)S(1)}, bf16[256,512]{1,0:T(8,128)(2,1)S(1)}) custom-call(s32[56]{0:T(128)S(1)} %get-tuple-element.77.refs_0_, s32[8,32]{1,0:T(8,128)S(1)} %bitcast.12, s32[32]{0:T(128)S(1)} %bitcast.18, ...), custom_call_target="tpu_custom_call" | custom-call | flops 17179869184 | bytes 4194304 | tf_op jit(solution)/shard_map/spread/pallas_call | solution.py:243
  138.2 3.4 %spread.7 = (bf16[256,512]{1,0:T(8,128)(2,1)S(1)}, bf16[256,512]{1,0:T(8,128)(2,1)S(1)}, bf16[256,512]{1,0:T(8,128)(2,1)S(1)}, bf16[256,512]{1,0:T(8,128)(2,1)S(1)}) custom-call(s32[56]{0:T(128)S(1)} %get-tuple-element.77.refs_0_, s32[8,32]{1,0:T(8,128)S(1)} %bitcast.13, s32[32]{0:T(128)S(1)} %bitcast.19, ...), custom_call_target="tpu_custom_call" | custom-call | flops 17179869184 | bytes 4194304 | tf_op jit(solution)/shard_map/spread/pallas_call | solution.py:243
  150.2 7.9 %collective-permute-done.32 = bf16[256,512]{1,0:T(8,128)(2,1)S(1)} collective-permute-done((bf16[256,512]{1,0:T(8,128)(2,1)S(1)}, bf16[256,512]{1,0:T(8,128)(2,1)S(1)}, u32[]{:S(2)}, u32[]{:S(2)}) %collective-permute-start.32) | collective-permute-done | bytes 262176 | tf_op jit(solution)/shard_map/ppermute | solution.py:26
  158.1 3.9 %collective-permute-start.35 = (bf16[256,512]{1,0:T(8,128)(2,1)S(1)}, bf16[256,512]{1,0:T(8,128)(2,1)S(1)}, u32[]{:S(2)}, u32[]{:S(2)}) collective-permute-start(bf16[256,512]{1,0:T(8,128)(2,1)S(1)} %get-tuple-element.81), channel_id=1, source_target_pairs={{0,96},{16,112},{32,64},{48,80},{64,32},{80,48},{96,0},{112,16},{1... | collective-permute-start | bytes 786440 | tf_op jit(solution)/shard_map/ppermute | solution.py:26
  162.0 5.8 %collective-permute-done.40 = bf16[256,512]{1,0:T(8,128)(2,1)S(1)} collective-permute-done((bf16[256,512]{1,0:T(8,128)(2,1)S(1)}, bf16[256,512]{1,0:T(8,128)(2,1)S(1)}, u32[]{:S(2)}, u32[]{:S(2)}) %collective-permute-start.40) | collective-permute-done | bytes 262176 | tf_op jit(solution)/shard_map/ppermute | solution.py:26
  171.3 5.2 %collective-permute-start.44 = (bf16[128,512]{1,0:T(8,128)(2,1)S(1)}, bf16[128,512]{1,0:T(8,128)(2,1)S(1)}, u32[]{:S(2)}, u32[]{:S(2)}) collective-permute-start(bf16[128,512]{1,0:T(8,128)(2,1)S(1)} %pad_maximum_fusion.refs_1_), channel_id=1, source_target_pairs={{0,2},{1,3},{2,0},{3,1},{4,6},{5,7},{6,4},{7,5},{8,10},{9,11},{10,... | collective-permute-start | bytes 393224 | tf_op jit(solution)/shard_map/ppermute | solution.py:26
  (99 shorter events, 52.5 us)
Async XLA Ops:
  0.7 16.6 %collective-permute-start = (bf16[256,512]{1,0:T(8,128)(2,1)}, bf16[256,512]{1,0:T(8,128)(2,1)S(1)}, u32[]{:S(2)}, u32[]{:S(2)}) collective-permute-start(bf16[256,512]{1,0:T(8,128)(2,1)} %refs_4_.1), channel_id=1, source_target_pairs={{0,16},{16,32},{32,48},{48,0},{64,80},{80,96},{96,112},{112,64},{1... | collective-permute-start | bytes 786440 | tf_op jit(solution)/shard_map/ppermute | solution.py:26
  2.7 23.0 %collective-permute-start.2 = (bf16[256,512]{1,0:T(8,128)(2,1)}, bf16[256,512]{1,0:T(8,128)(2,1)S(1)}, u32[]{:S(2)}, u32[]{:S(2)}) collective-permute-start(bf16[256,512]{1,0:T(8,128)(2,1)} %refs_4_.1), channel_id=1, source_target_pairs={{0,64},{16,80},{32,96},{48,112},{64,0},{80,16},{96,32},{112,48},{1... | collective-permute-start | bytes 786440 | tf_op jit(solution)/shard_map/ppermute | solution.py:26
  4.2 21.5 %collective-permute-start.3 = (bf16[256,512]{1,0:T(8,128)(2,1)}, bf16[256,512]{1,0:T(8,128)(2,1)S(1)}, u32[]{:S(2)}, u32[]{:S(2)}) collective-permute-start(bf16[256,512]{1,0:T(8,128)(2,1)} %refs_4_.1), channel_id=1, source_target_pairs={{0,32},{16,48},{32,0},{48,16},{64,96},{80,112},{96,64},{112,80},{1... | collective-permute-start | bytes 786440 | tf_op jit(solution)/shard_map/ppermute | solution.py:26
  7.8 18.1 %collective-permute-start.4 = (bf16[256,512]{1,0:T(8,128)(2,1)}, bf16[256,512]{1,0:T(8,128)(2,1)S(1)}, u32[]{:S(2)}, u32[]{:S(2)}) collective-permute-start(bf16[256,512]{1,0:T(8,128)(2,1)} %refs_4_.1), channel_id=1, source_target_pairs={{0,80},{16,96},{32,112},{48,64},{64,16},{80,32},{96,48},{112,0},{1... | collective-permute-start | bytes 786440 | tf_op jit(solution)/shard_map/ppermute | solution.py:26
  7.8 18.6 %collective-permute-start.5 = (bf16[256,512]{1,0:T(8,128)(2,1)}, bf16[256,512]{1,0:T(8,128)(2,1)S(1)}, u32[]{:S(2)}, u32[]{:S(2)}) collective-permute-start(bf16[256,512]{1,0:T(8,128)(2,1)} %refs_4_.1), channel_id=1, source_target_pairs={{0,112},{16,64},{32,80},{48,96},{64,48},{80,0},{96,16},{112,32},{1... | collective-permute-start | bytes 786440 | tf_op jit(solution)/shard_map/ppermute | solution.py:26
  17.3 13.4 %collective-permute-start.6 = (bf16[256,512]{1,0:T(8,128)(2,1)S(1)}, bf16[256,512]{1,0:T(8,128)(2,1)S(1)}, u32[]{:S(2)}, u32[]{:S(2)}) collective-permute-start(bf16[256,512]{1,0:T(8,128)(2,1)S(1)} %copy-done.1), channel_id=1, source_target_pairs={{0,96},{16,112},{32,64},{48,80},{64,32},{80,48},{96,0},{112,16},{1... | collective-permute-start | bytes 786440 | tf_op jit(solution)/shard_map/ppermute | solution.py:26
  53.7 21.8 %collective-permute-start.17 = (bf16[256,512]{1,0:T(8,128)(2,1)S(1)}, bf16[256,512]{1,0:T(8,128)(2,1)S(1)}, u32[]{:S(2)}, u32[]{:S(2)}) collective-permute-start(bf16[256,512]{1,0:T(8,128)(2,1)S(1)} %get-tuple-element.55), channel_id=1, source_target_pairs={{0,4},{1,5},{2,6},{3,7},{4,0},{5,1},{6,2},{7,3},{8,12},{9,13},{10,... | collective-permute-start | bytes 786440 | tf_op jit(solution)/shard_map/ppermute | solution.py:26
  56.0 19.6 %collective-permute-start.18 = (bf16[256,512]{1,0:T(8,128)(2,1)S(1)}, bf16[256,512]{1,0:T(8,128)(2,1)S(1)}, u32[]{:S(2)}, u32[]{:S(2)}) collective-permute-start(bf16[256,512]{1,0:T(8,128)(2,1)S(1)} %get-tuple-element.56), channel_id=1, source_target_pairs={{0,6},{1,7},{2,4},{3,5},{4,2},{5,3},{6,0},{7,1},{8,14},{9,15},{10,... | collective-permute-start | bytes 786440 | tf_op jit(solution)/shard_map/ppermute | solution.py:26
  56.8 21.0 %collective-permute-start.19 = (bf16[256,512]{1,0:T(8,128)(2,1)S(1)}, bf16[256,512]{1,0:T(8,128)(2,1)S(1)}, u32[]{:S(2)}, u32[]{:S(2)}) collective-permute-start(bf16[256,512]{1,0:T(8,128)(2,1)S(1)} %get-tuple-element.57), channel_id=1, source_target_pairs={{0,2},{1,3},{2,0},{3,1},{4,6},{5,7},{6,4},{7,5},{8,10},{9,11},{10,... | collective-permute-start | bytes 786440 | tf_op jit(solution)/shard_map/ppermute | solution.py:26
  60.2 17.6 %collective-permute-start.20 = (bf16[256,512]{1,0:T(8,128)(2,1)S(1)}, bf16[256,512]{1,0:T(8,128)(2,1)S(1)}, u32[]{:S(2)}, u32[]{:S(2)}) collective-permute-start(bf16[256,512]{1,0:T(8,128)(2,1)S(1)} %get-tuple-element.58), channel_id=1, source_target_pairs={{0,5},{1,6},{2,7},{3,4},{4,1},{5,2},{6,3},{7,0},{8,13},{9,14},{10,... | collective-permute-start | bytes 786440 | tf_op jit(solution)/shard_map/ppermute | solution.py:26
  61.2 19.4 %collective-permute-start.21 = (bf16[256,512]{1,0:T(8,128)(2,1)S(1)}, bf16[256,512]{1,0:T(8,128)(2,1)S(1)}, u32[]{:S(2)}, u32[]{:S(2)}) collective-permute-start(bf16[256,512]{1,0:T(8,128)(2,1)S(1)} %get-tuple-element.59), channel_id=1, source_target_pairs={{0,7},{1,4},{2,5},{3,6},{4,3},{5,0},{6,1},{7,2},{8,15},{9,12},{10,... | collective-permute-start | bytes 786440 | tf_op jit(solution)/shard_map/ppermute | solution.py:26
  82.4 19.9 %collective-permute-start.22 = (bf16[336,512]{1,0:T(8,128)(2,1)S(1)}, bf16[336,512]{1,0:T(8,128)(2,1)S(1)}, u32[]{:S(2)}, u32[]{:S(2)}) collective-permute-start(bf16[336,512]{1,0:T(8,128)(2,1)S(1)} %get-tuple-element.62), channel_id=1, source_target_pairs={{0,1},{1,2},{2,3},{3,0},{4,5},{5,6},{6,7},{7,4},{8,9},{9,10},{10,1... | collective-permute-start | bytes 1032200 | tf_op jit(solution)/shard_map/ppermute | solution.py:26
  82.4 24.7 %collective-permute-start.23 = (bf16[336,512]{1,0:T(8,128)(2,1)S(1)}, bf16[336,512]{1,0:T(8,128)(2,1)S(1)}, u32[]{:S(2)}, u32[]{:S(2)}) collective-permute-start(bf16[336,512]{1,0:T(8,128)(2,1)S(1)} %get-tuple-element.63), channel_id=1, source_target_pairs={{0,3},{1,0},{2,1},{3,2},{4,7},{5,4},{6,5},{7,6},{8,11},{9,8},{10,9... | collective-permute-start | bytes 1032200 | tf_op jit(solution)/shard_map/ppermute | solution.py:26
  85.7 24.9 %collective-permute-start.24 = (bf16[336,512]{1,0:T(8,128)(2,1)S(1)}, bf16[336,512]{1,0:T(8,128)(2,1)S(1)}, u32[]{:S(2)}, u32[]{:S(2)}) collective-permute-start(bf16[336,512]{1,0:T(8,128)(2,1)S(1)} %get-tuple-element.64), channel_id=1, source_target_pairs={{0,4},{1,5},{2,6},{3,7},{4,0},{5,1},{6,2},{7,3},{8,12},{9,13},{10,... | collective-permute-start | bytes 1032200 | tf_op jit(solution)/shard_map/ppermute | solution.py:26
  87.9 22.6 %collective-permute-start.25 = (bf16[336,512]{1,0:T(8,128)(2,1)S(1)}, bf16[336,512]{1,0:T(8,128)(2,1)S(1)}, u32[]{:S(2)}, u32[]{:S(2)}) collective-permute-start(bf16[336,512]{1,0:T(8,128)(2,1)S(1)} %get-tuple-element.65), channel_id=1, source_target_pairs={{0,6},{1,7},{2,4},{3,5},{4,2},{5,3},{6,0},{7,1},{8,14},{9,15},{10,... | collective-permute-start | bytes 1032200 | tf_op jit(solution)/shard_map/ppermute | solution.py:26
  88.8 26.6 %collective-permute-start.26 = (bf16[336,512]{1,0:T(8,128)(2,1)S(1)}, bf16[336,512]{1,0:T(8,128)(2,1)S(1)}, u32[]{:S(2)}, u32[]{:S(2)}) collective-permute-start(bf16[336,512]{1,0:T(8,128)(2,1)S(1)} %get-tuple-element.66), channel_id=1, source_target_pairs={{0,2},{1,3},{2,0},{3,1},{4,6},{5,7},{6,4},{7,5},{8,10},{9,11},{10,... | collective-permute-start | bytes 1032200 | tf_op jit(solution)/shard_map/ppermute | solution.py:26
  102.3 15.6 %collective-permute-start.27 = (bf16[336,512]{1,0:T(8,128)(2,1)S(1)}, bf16[336,512]{1,0:T(8,128)(2,1)S(1)}, u32[]{:S(2)}, u32[]{:S(2)}) collective-permute-start(bf16[336,512]{1,0:T(8,128)(2,1)S(1)} %get-tuple-element.67), channel_id=1, source_target_pairs={{0,5},{1,6},{2,7},{3,4},{4,1},{5,2},{6,3},{7,0},{8,13},{9,14},{10,... | collective-permute-start | bytes 1032200 | tf_op jit(solution)/shard_map/ppermute | solution.py:26
  141.7 16.4 %collective-permute-start.32 = (bf16[256,512]{1,0:T(8,128)(2,1)S(1)}, bf16[256,512]{1,0:T(8,128)(2,1)S(1)}, u32[]{:S(2)}, u32[]{:S(2)}) collective-permute-start(bf16[256,512]{1,0:T(8,128)(2,1)S(1)} %get-tuple-element.78), channel_id=1, source_target_pairs={{0,32},{16,48},{32,0},{48,16},{64,96},{80,112},{96,64},{112,80},{1... | collective-permute-start | bytes 786440 | tf_op jit(solution)/shard_map/ppermute | solution.py:26
  144.6 23.2 %collective-permute-start.40 = (bf16[256,512]{1,0:T(8,128)(2,1)S(1)}, bf16[256,512]{1,0:T(8,128)(2,1)S(1)}, u32[]{:S(2)}, u32[]{:S(2)}) collective-permute-start(bf16[256,512]{1,0:T(8,128)(2,1)S(1)} %get-tuple-element.83), channel_id=1, source_target_pairs={{0,16},{16,32},{32,48},{48,0},{64,80},{80,96},{96,112},{112,64},{1... | collective-permute-start | bytes 786440 | tf_op jit(solution)/shard_map/ppermute | solution.py:26
  145.3 16.6 %collective-permute-start.39 = (bf16[72,512]{1,0:T(8,128)(2,1)S(1)}, bf16[72,512]{1,0:T(8,128)(2,1)S(1)}, u32[]{:S(2)}, u32[]{:S(2)}) collective-permute-start(bf16[72,512]{1,0:T(8,128)(2,1)S(1)} %get-tuple-element.92), channel_id=1, source_target_pairs={{0,4},{4,0},{1,5},{5,1},{2,6},{6,2},{3,7},{7,3},{8,12},{12,8},{9,1... | collective-permute-start | bytes 221192 | tf_op jit(solution)/shard_map/ppermute | solution.py:30
  146.0 23.9 %collective-permute-start.33 = (bf16[256,512]{1,0:T(8,128)(2,1)S(1)}, bf16[256,512]{1,0:T(8,128)(2,1)S(1)}, u32[]{:S(2)}, u32[]{:S(2)}) collective-permute-start(bf16[256,512]{1,0:T(8,128)(2,1)S(1)} %get-tuple-element.79), channel_id=1, source_target_pairs={{0,80},{16,96},{32,112},{48,64},{64,16},{80,32},{96,48},{112,0},{1... | collective-permute-start | bytes 786440 | tf_op jit(solution)/shard_map/ppermute | solution.py:26
  147.7 23.7 %collective-permute-start.34 = (bf16[256,512]{1,0:T(8,128)(2,1)S(1)}, bf16[256,512]{1,0:T(8,128)(2,1)S(1)}, u32[]{:S(2)}, u32[]{:S(2)}) collective-permute-start(bf16[256,512]{1,0:T(8,128)(2,1)S(1)} %get-tuple-element.80), channel_id=1, source_target_pairs={{0,112},{16,64},{32,80},{48,96},{64,48},{80,0},{96,16},{112,32},{1... | collective-permute-start | bytes 786440 | tf_op jit(solution)/shard_map/ppermute | solution.py:26
  158.1 18.4 %collective-permute-start.35 = (bf16[256,512]{1,0:T(8,128)(2,1)S(1)}, bf16[256,512]{1,0:T(8,128)(2,1)S(1)}, u32[]{:S(2)}, u32[]{:S(2)}) collective-permute-start(bf16[256,512]{1,0:T(8,128)(2,1)S(1)} %get-tuple-element.81), channel_id=1, source_target_pairs={{0,96},{16,112},{32,64},{48,80},{64,32},{80,48},{96,0},{112,16},{1... | collective-permute-start | bytes 786440 | tf_op jit(solution)/shard_map/ppermute | solution.py:26
  162.0 17.1 %collective-permute-start.41 = (bf16[256,512]{1,0:T(8,128)(2,1)S(1)}, bf16[256,512]{1,0:T(8,128)(2,1)S(1)}, u32[]{:S(2)}, u32[]{:S(2)}) collective-permute-start(bf16[256,512]{1,0:T(8,128)(2,1)S(1)} %get-tuple-element.84), channel_id=1, source_target_pairs={{0,48},{16,0},{32,16},{48,32},{64,112},{80,64},{96,80},{112,96},{1... | collective-permute-start | bytes 786440 | tf_op jit(solution)/shard_map/ppermute | solution.py:26
  (28 other events, 379.1 us)

commit v8 on v7

--- a/solution.py
+++ b/solution.py
@@ -34,7 +34,7 @@
     return list(itertools.product(*[range(SIZES[a]) for a in axes]))
 
 
-EXTRA = 16
+EXTRA = 8
 VARIANTS = (1, 2, 3, 4, 6, 8)
 
 
@@ -331,7 +331,7 @@
 
 
 PARTS = ((0, 0), (0, 1), (0, 3), (1, 0), (1, 2), (0, 2), (1, 1), (1, 3))
-CHIP_HALVES = (((0, 0), (0, 1), (0, 3), (1, 0)), ((0, 2), (1, 1), (1, 3), (1, 2)))
+CHIP_HALVES = (((0, 0), (0, 1), (0, 3), (1, 0)), ((1, 2), (0, 2), (1, 1), (1, 3)))
 
 
 def lists_of_numbers(halves, chips, parts):
@@ -395,7 +395,7 @@
     share_sum = add_shares(messages, share)
     each = len(halves[0])
     across, merged = [], []
-    for i, step in enumerate((("xl", 1), ("z", 1), ("z", 2), None)):
+    for i, step in enumerate((None, ("xl", 1), ("z", 1), ("z", 2))):
         if step:
             index, share_sum = lax.optimization_barrier((index, share_sum))
             arriving = exchange(share_sum, *step)

time: 187 us -> 183 us (0.979)
  Pallas kernels: 35.4 us -> 30.9 us
  waiting for transfers between devices: 56.7 us -> 61 us
  starting transfers between devices: 88.3 us -> 85.8 us
    ppermute x41, starting transfers between devices: 82.2 us -> 77.5 us  [send_by(): return lax.ppermute(value, axes, pairs)]
    pallas_call x1, Pallas kernels: 13.5 us -> 10.6 us  [aggregate(): pl.pallas_call(lambda *refs: forward_kernel(shards, at_source, at_place,...]
    ppermute x41, waiting for transfers between devices: 54.1 us -> 56.9 us  [send_by(): return lax.ppermute(value, axes, pairs)]
    ppermute x5, starting transfers between devices: 6.13 us -> 8.33 us  [exchange(): lax.ppermute(value, axis, [(i, i ^ mask) for i in range(SIZES[axis])])]
  transfers between devices with their start and end apart: 46 -> 46, of which waited for: 19 -> 21; matrix products, arithmetic and copies ran while one was open for 1% -> 1% of each run, Pallas kernels for 8% -> 9%
where the time goes in v8:
time: 183 us; the launch traced here: 181 us
  starting transfers between devices  85.8 us (47%)
  waiting for transfers between devices  61 us (33%)
  Pallas kernels  30.9 us (17%)
    ppermute x41, starting transfers between devices, send_by(): return lax.ppermute(value, axes, pairs)  77.5 us
    ppermute x41, waiting for transfers between devices, send_by(): return lax.ppermute(value, axes, pairs)  56.9 us
    pallas_call x4, Pallas kernels, spread(): pl.pallas_call(lambda *refs: backward_kernel(shards, parts, at_source, at...  12.2 us
    pallas_call x1, Pallas kernels, aggregate(): pl.pallas_call(lambda *refs: forward_kernel(shards, at_source, at_place,...  10.6 us
    ppermute x5, starting transfers between devices, exchange(): lax.ppermute(value, axis, [(i, i ^ mask) for i in range(SIZES[axis])])  8.33 us
    pallas_call x1, Pallas kernels, fetch(): pl.pallas_call(fetch_kernel, out_shape=(pltpu.VMEM(values.shape, values.d...  4.61 us
    ppermute x5, waiting for transfers between devices, exchange(): lax.ppermute(value, axis, [(i, i ^ mask) for i in range(SIZES[axis])])  4 us
  transfers between devices with their start and end apart: 46, of which 21 were waited for; matrix products, arithmetic and copies ran while one was open for 1% of the time, Pallas kernels for 9%

profile of v8, /device:TPU:0, one launch (start us, length us, event | category | flops | bytes accessed | tf_op | source)
XLA Modules:
  0.0 180.9 jit_solution(10436162433554687757)
XLA Ops:
  10.6 4.6 %fetch.1 = (bf16[32,8,128,128]{3,2,1,0:T(8,128)(2,1)S(1)}, s32[56]{0:T(128)S(1)}) custom-call(s32[56]{0:T(128)S(1)} %dynamic-slice_bitcast_fusion.index_ref, bf16[32,8,128,128]{3,2,1,0:T(8,128)(2,1)} %bitcast.20), custom_call_target="tpu_custom_call" | custom-call | bytes 16777216 | tf_op jit(solution)/shard_map/fetch/pallas_call | solution.py:80
  16.1 6.1 %collective-permute-done.1.refs_6_ = bf16[256,512]{1,0:T(8,128)(2,1)S(1)} collective-permute-done((bf16[256,512]{1,0:T(8,128)(2,1)}, bf16[256,512]{1,0:T(8,128)(2,1)S(1)}, u32[]{:S(2)}, u32[]{:S(2)}) %collective-permute-start.1) | collective-permute-done | bytes 262176 | tf_op jit(solution)/shard_map/ppermute | solution.py:26
  22.1 4.7 %collective-permute-start.6 = (bf16[256,512]{1,0:T(8,128)(2,1)S(1)}, bf16[256,512]{1,0:T(8,128)(2,1)S(1)}, u32[]{:S(2)}, u32[]{:S(2)}) collective-permute-start(bf16[256,512]{1,0:T(8,128)(2,1)S(1)} %copy-done.1), channel_id=1, source_target_pairs={{0,112},{16,64},{32,80},{48,96},{64,48},{80,0},{96,16},{112,32},{1... | collective-permute-start | bytes 786440 | tf_op jit(solution)/shard_map/ppermute | solution.py:26
  33.4 10.6 %aggregate.1 = (bf16[256,512]{1,0:T(8,128)(2,1)S(1)}, bf16[256,512]{1,0:T(8,128)(2,1)S(1)}, bf16[256,512]{1,0:T(8,128)(2,1)S(1)}, bf16[256,512]{1,0:T(8,128)(2,1...) custom-call(s32[56]{0:T(128)S(1)} %get-tuple-element.81.refs_0_, ...), custom_call_target="tpu_custom_call" | custom-call | flops 8589934592 | bytes 16777216 | tf_op jit(solution)/shard_map/aggregate/pallas_call | solution.py:129
  44.1 3.2 %collective-permute-start.16 = (bf16[256,512]{1,0:T(8,128)(2,1)S(1)}, bf16[256,512]{1,0:T(8,128)(2,1)S(1)}, u32[]{:S(2)}, u32[]{:S(2)}) collective-permute-start(bf16[256,512]{1,0:T(8,128)(2,1)S(1)} %get-tuple-element.54), channel_id=1, source_target_pairs={{0,3},{1,0},{2,1},{3,2},{4,7},{5,4},{6,5},{7,6},{8,11},{9,8},{10,9... | collective-permute-start | bytes 786440 | tf_op jit(solution)/shard_map/ppermute | solution.py:26
  47.3 2.4 %collective-permute-start.17 = (bf16[256,512]{1,0:T(8,128)(2,1)S(1)}, bf16[256,512]{1,0:T(8,128)(2,1)S(1)}, u32[]{:S(2)}, u32[]{:S(2)}) collective-permute-start(bf16[256,512]{1,0:T(8,128)(2,1)S(1)} %get-tuple-element.55), channel_id=1, source_target_pairs={{0,4},{1,5},{2,6},{3,7},{4,0},{5,1},{6,2},{7,3},{8,12},{9,13},{10,... | collective-permute-start | bytes 786440 | tf_op jit(solution)/shard_map/ppermute | solution.py:26
  49.8 4.4 %collective-permute-start.18 = (bf16[256,512]{1,0:T(8,128)(2,1)S(1)}, bf16[256,512]{1,0:T(8,128)(2,1)S(1)}, u32[]{:S(2)}, u32[]{:S(2)}) collective-permute-start(bf16[256,512]{1,0:T(8,128)(2,1)S(1)} %get-tuple-element.56), channel_id=1, source_target_pairs={{0,6},{1,7},{2,4},{3,5},{4,2},{5,3},{6,0},{7,1},{8,14},{9,15},{10,... | collective-permute-start | bytes 786440 | tf_op jit(solution)/shard_map/ppermute | solution.py:26
  56.1 3.7 %collective-permute-start.21 = (bf16[256,512]{1,0:T(8,128)(2,1)S(1)}, bf16[256,512]{1,0:T(8,128)(2,1)S(1)}, u32[]{:S(2)}, u32[]{:S(2)}) collective-permute-start(bf16[256,512]{1,0:T(8,128)(2,1)S(1)} %get-tuple-element.59), channel_id=1, source_target_pairs={{0,7},{1,4},{2,5},{3,6},{4,3},{5,0},{6,1},{7,2},{8,15},{9,12},{10,... | collective-permute-start | bytes 786440 | tf_op jit(solution)/shard_map/ppermute | solution.py:26
  59.8 7.4 %collective-permute-done.18.refs_5_ = bf16[256,512]{1,0:T(8,128)(2,1)S(1)} collective-permute-done((bf16[256,512]{1,0:T(8,128)(2,1)S(1)}, bf16[256,512]{1,0:T(8,128)(2,1)S(1)}, u32[]{:S(2)}, u32[]{:S(2)}) %collective-permute-start.18) | collective-permute-done | bytes 262176 | tf_op jit(solution)/shard_map/ppermute | solution.py:26
  67.1 7.4 %collective-permute-done.19.refs_6_ = bf16[256,512]{1,0:T(8,128)(2,1)S(1)} collective-permute-done((bf16[256,512]{1,0:T(8,128)(2,1)S(1)}, bf16[256,512]{1,0:T(8,128)(2,1)S(1)}, u32[]{:S(2)}, u32[]{:S(2)}) %collective-permute-start.19) | collective-permute-done | bytes 262176 | tf_op jit(solution)/shard_map/ppermute | solution.py:26
  82.5 2.7 %collective-permute-start.25 = (bf16[328,512]{1,0:T(8,128)(2,1)S(1)}, bf16[328,512]{1,0:T(8,128)(2,1)S(1)}, u32[]{:S(2)}, u32[]{:S(2)}) collective-permute-start(bf16[328,512]{1,0:T(8,128)(2,1)S(1)} %get-tuple-element.65), channel_id=1, source_target_pairs={{0,6},{1,7},{2,4},{3,5},{4,2},{5,3},{6,0},{7,1},{8,14},{9,15},{10,... | collective-permute-start | bytes 1007624 | tf_op jit(solution)/shard_map/ppermute | solution.py:26
  89.4 12.9 %collective-permute-done.23.refs_2_.refs_6_ = bf16[328,512]{1,0:T(8,128)(2,1)S(1)} collective-permute-done((bf16[328,512]{1,0:T(8,128)(2,1)S(1)}, bf16[328,512]{1,0:T(8,128)(2,1)S(1)}, u32[]{:S(2)}, u32[]{:S(2)}) %collective-permute-start.23) | collective-permute-done | bytes 335904 | tf_op jit(solution)/shard_map/ppermute | solution.py:26
  102.2 5.4 %collective-permute-start.28 = (bf16[328,512]{1,0:T(8,128)(2,1)S(1)}, bf16[328,512]{1,0:T(8,128)(2,1)S(1)}, u32[]{:S(2)}, u32[]{:S(2)}) collective-permute-start(bf16[328,512]{1,0:T(8,128)(2,1)S(1)} %get-tuple-element.68), channel_id=1, source_target_pairs={{0,7},{1,4},{2,5},{3,6},{4,3},{5,0},{6,1},{7,2},{8,15},{9,12},{10,... | collective-permute-start | bytes 1007624 | tf_op jit(solution)/shard_map/ppermute | solution.py:26
  107.7 2.5 %collective-permute-done.26.refs_5_.refs_9_ = bf16[328,512]{1,0:T(8,128)(2,1)S(1)} collective-permute-done((bf16[328,512]{1,0:T(8,128)(2,1)S(1)}, bf16[328,512]{1,0:T(8,128)(2,1)S(1)}, u32[]{:S(2)}, u32[]{:S(2)}) %collective-permute-start.26) | collective-permute-done | bytes 335904 | tf_op jit(solution)/shard_map/ppermute | solution.py:26
  110.1 5.0 %collective-permute-done.28.refs_7_.refs_11_ = bf16[328,512]{1,0:T(8,128)(2,1)S(1)} collective-permute-done((bf16[328,512]{1,0:T(8,128)(2,1)S(1)}, bf16[328,512]{1,0:T(8,128)(2,1)S(1)}, u32[]{:S(2)}, u32[]{:S(2)}) %collective-permute-start.28) | collective-permute-done | bytes 335904 | tf_op jit(solution)/shard_map/ppermute | solution.py:26
  116.5 3.0 %spread.5 = bf16[4,256,512]{2,1,0:T(8,128)(2,1)S(1)} custom-call(s32[56]{0:T(128)S(1)} %get-tuple-element.81.refs_0_, s32[8,32]{1,0:T(8,128)S(1)} %bitcast.10, s32[32]{0:T(128)S(1)} %bitcast.16, bf16[32,8,128,128]{3,2,1,0:T(8,128)(2,1)S(1)} %get-tuple-element.50.refs_3_, bf16[328,512]{1,0:T(8,128)(2,1)S(1)} %get-tuple-element.61.refs_0_.refs_4_, ...), custom_call_target="tpu_custom_call" | custom-call | flops 17179869184 | bytes 4194304 | tf_op jit(solution)/shard_map/spread/pallas_call | solution.py:243
  119.6 3.0 %spread.4 = bf16[4,256,512]{2,1,0:T(8,128)(2,1)S(1)} custom-call(s32[56]{0:T(128)S(1)} %get-tuple-element.81.refs_0_, s32[8,32]{1,0:T(8,128)S(1)} %bitcast.11, s32[32]{0:T(128)S(1)} %bitcast.17, bf16[32,8,128,128]{3,2,1,0:T(8,128)(2,1)S(1)} %get-tuple-element.50.refs_3_, bf16[328,512]{1,0:T(8,128)(2,1)S(1)} %get-tuple-element.61.refs_0_.refs_4_, ...), custom_call_target="tpu_custom_call" | custom-call | flops 17179869184 | bytes 4194304 | tf_op jit(solution)/shard_map/spread/pallas_call | solution.py:243
  124.1 3.0 %spread.6 = (bf16[256,512]{1,0:T(8,128)(2,1)S(1)}, bf16[256,512]{1,0:T(8,128)(2,1)S(1)}, bf16[256,512]{1,0:T(8,128)(2,1)S(1)}, bf16[256,512]{1,0:T(8,128)(2,1)S(1)}) custom-call(s32[56]{0:T(128)S(1)} %get-tuple-element.81.refs_0_, s32[8,32]{1,0:T(8,128)S(1)} %bitcast.12, s32[32]{0:T(128)S(1)} %bitcast.18, ...), custom_call_target="tpu_custom_call" | custom-call | flops 17179869184 | bytes 4194304 | tf_op jit(solution)/shard_map/spread/pallas_call | solution.py:243
  131.7 3.2 %spread.7 = (bf16[256,512]{1,0:T(8,128)(2,1)S(1)}, bf16[256,512]{1,0:T(8,128)(2,1)S(1)}, bf16[256,512]{1,0:T(8,128)(2,1)S(1)}, bf16[256,512]{1,0:T(8,128)(2,1)S(1)}) custom-call(s32[56]{0:T(128)S(1)} %get-tuple-element.81.refs_0_, s32[8,32]{1,0:T(8,128)S(1)} %bitcast.13, s32[32]{0:T(128)S(1)} %bitcast.19, ...), custom_call_target="tpu_custom_call" | custom-call | flops 17179869184 | bytes 4194304 | tf_op jit(solution)/shard_map/spread/pallas_call | solution.py:243
  138.3 4.1 %collective-permute-start.39 = (bf16[72,512]{1,0:T(8,128)(2,1)S(1)}, bf16[72,512]{1,0:T(8,128)(2,1)S(1)}, u32[]{:S(2)}, u32[]{:S(2)}) collective-permute-start(bf16[72,512]{1,0:T(8,128)(2,1)S(1)} %get-tuple-element.92), channel_id=1, source_target_pairs={{0,4},{4,0},{1,5},{5,1},{2,6},{6,2},{3,7},{7,3},{8,12},{12,8},{9,1... | collective-permute-start | bytes 221192 | tf_op jit(solution)/shard_map/ppermute | solution.py:30
  151.9 5.8 %collective-permute-done.41 = bf16[256,512]{1,0:T(8,128)(2,1)S(1)} collective-permute-done((bf16[256,512]{1,0:T(8,128)(2,1)S(1)}, bf16[256,512]{1,0:T(8,128)(2,1)S(1)}, u32[]{:S(2)}, u32[]{:S(2)}) %collective-permute-start.41) | collective-permute-done | bytes 262176 | tf_op jit(solution)/shard_map/ppermute | solution.py:26
  157.7 4.0 %collective-permute-start.43 = (bf16[128,512]{1,0:T(8,128)(2,1)S(1)}, bf16[128,512]{1,0:T(8,128)(2,1)S(1)}, u32[]{:S(2)}, u32[]{:S(2)}) collective-permute-start(bf16[128,512]{1,0:T(8,128)(2,1)S(1)} %pad_maximum_fusion.refs_1_), channel_id=1, source_target_pairs={{0,1},{1,2},{2,3},{3,0},{4,5},{5,6},{6,7},{7,4},{8,9},{9,10},{10,1... | collective-permute-start | bytes 393224 | tf_op jit(solution)/shard_map/ppermute | solution.py:26
  161.7 12.5 %collective-permute-start.44 = (bf16[128,512]{1,0:T(8,128)(2,1)S(1)}, bf16[128,512]{1,0:T(8,128)(2,1)S(1)}, u32[]{:S(2)}, u32[]{:S(2)}) collective-permute-start(bf16[128,512]{1,0:T(8,128)(2,1)S(1)} %pad_maximum_fusion.refs_1_), channel_id=1, source_target_pairs={{0,2},{1,3},{2,0},{3,1},{4,6},{5,7},{6,4},{7,5},{8,10},{9,11},{10,... | collective-permute-start | bytes 393224 | tf_op jit(solution)/shard_map/ppermute | solution.py:26
  174.2 2.6 %collective-permute-start.45 = (bf16[128,512]{1,0:T(8,128)(2,1)S(1)}, bf16[128,512]{1,0:T(8,128)(2,1)S(1)}, u32[]{:S(2)}, u32[]{:S(2)}) collective-permute-start(bf16[128,512]{1,0:T(8,128)(2,1)S(1)} %pad_maximum_fusion.refs_1_), channel_id=1, source_target_pairs={{0,3},{1,0},{2,1},{3,2},{4,7},{5,4},{6,5},{7,6},{8,11},{9,8},{10,9... | collective-permute-start | bytes 393224 | tf_op jit(solution)/shard_map/ppermute | solution.py:26
  (99 shorter events, 56.2 us)
Async XLA Ops:
  0.7 14.6 %collective-permute-start = (bf16[256,512]{1,0:T(8,128)(2,1)}, bf16[256,512]{1,0:T(8,128)(2,1)S(1)}, u32[]{:S(2)}, u32[]{:S(2)}) collective-permute-start(bf16[256,512]{1,0:T(8,128)(2,1)} %refs_4_.1), channel_id=1, source_target_pairs={{0,16},{16,32},{32,48},{48,0},{64,80},{80,96},{96,112},{112,64},{1... | collective-permute-start | bytes 786440 | tf_op jit(solution)/shard_map/ppermute | solution.py:26
  2.7 19.4 %collective-permute-start.1 = (bf16[256,512]{1,0:T(8,128)(2,1)}, bf16[256,512]{1,0:T(8,128)(2,1)S(1)}, u32[]{:S(2)}, u32[]{:S(2)}) collective-permute-start(bf16[256,512]{1,0:T(8,128)(2,1)} %refs_4_.1), channel_id=1, source_target_pairs={{0,48},{16,0},{32,16},{48,32},{64,112},{80,64},{96,80},{112,96},{1... | collective-permute-start | bytes 786440 | tf_op jit(solution)/shard_map/ppermute | solution.py:26
  4.9 21.9 %collective-permute-start.2 = (bf16[256,512]{1,0:T(8,128)(2,1)}, bf16[256,512]{1,0:T(8,128)(2,1)S(1)}, u32[]{:S(2)}, u32[]{:S(2)}) collective-permute-start(bf16[256,512]{1,0:T(8,128)(2,1)} %refs_4_.1), channel_id=1, source_target_pairs={{0,64},{16,80},{32,96},{48,112},{64,0},{80,16},{96,32},{112,48},{1... | collective-permute-start | bytes 786440 | tf_op jit(solution)/shard_map/ppermute | solution.py:26
  6.4 20.4 %collective-permute-start.3 = (bf16[256,512]{1,0:T(8,128)(2,1)}, bf16[256,512]{1,0:T(8,128)(2,1)S(1)}, u32[]{:S(2)}, u32[]{:S(2)}) collective-permute-start(bf16[256,512]{1,0:T(8,128)(2,1)} %refs_4_.1), channel_id=1, source_target_pairs={{0,96},{16,112},{32,64},{48,80},{64,32},{80,48},{96,0},{112,16},{1... | collective-permute-start | bytes 786440 | tf_op jit(solution)/shard_map/ppermute | solution.py:26
  8.2 21.3 %collective-permute-start.4 = (bf16[256,512]{1,0:T(8,128)(2,1)}, bf16[256,512]{1,0:T(8,128)(2,1)S(1)}, u32[]{:S(2)}, u32[]{:S(2)}) collective-permute-start(bf16[256,512]{1,0:T(8,128)(2,1)} %refs_4_.1), channel_id=1, source_target_pairs={{0,32},{16,48},{32,0},{48,16},{64,96},{80,112},{96,64},{112,80},{1... | collective-permute-start | bytes 786440 | tf_op jit(solution)/shard_map/ppermute | solution.py:26
  15.3 14.3 %collective-permute-start.5 = (bf16[256,512]{1,0:T(8,128)(2,1)S(1)}, bf16[256,512]{1,0:T(8,128)(2,1)S(1)}, u32[]{:S(2)}, u32[]{:S(2)}) collective-permute-start(bf16[256,512]{1,0:T(8,128)(2,1)S(1)} %copy-done.1), channel_id=1, source_target_pairs={{0,80},{16,96},{32,112},{48,64},{64,16},{80,32},{96,48},{112,0},{1... | collective-permute-start | bytes 786440 | tf_op jit(solution)/shard_map/ppermute | solution.py:26
  47.3 12.4 %collective-permute-start.17 = (bf16[256,512]{1,0:T(8,128)(2,1)S(1)}, bf16[256,512]{1,0:T(8,128)(2,1)S(1)}, u32[]{:S(2)}, u32[]{:S(2)}) collective-permute-start(bf16[256,512]{1,0:T(8,128)(2,1)S(1)} %get-tuple-element.55), channel_id=1, source_target_pairs={{0,4},{1,5},{2,6},{3,7},{4,0},{5,1},{6,2},{7,3},{8,12},{9,13},{10,... | collective-permute-start | bytes 786440 | tf_op jit(solution)/shard_map/ppermute | solution.py:26
  49.8 17.4 %collective-permute-start.18 = (bf16[256,512]{1,0:T(8,128)(2,1)S(1)}, bf16[256,512]{1,0:T(8,128)(2,1)S(1)}, u32[]{:S(2)}, u32[]{:S(2)}) collective-permute-start(bf16[256,512]{1,0:T(8,128)(2,1)S(1)} %get-tuple-element.56), channel_id=1, source_target_pairs={{0,6},{1,7},{2,4},{3,5},{4,2},{5,3},{6,0},{7,1},{8,14},{9,15},{10,... | collective-permute-start | bytes 786440 | tf_op jit(solution)/shard_map/ppermute | solution.py:26
  54.1 20.4 %collective-permute-start.19 = (bf16[256,512]{1,0:T(8,128)(2,1)S(1)}, bf16[256,512]{1,0:T(8,128)(2,1)S(1)}, u32[]{:S(2)}, u32[]{:S(2)}) collective-permute-start(bf16[256,512]{1,0:T(8,128)(2,1)S(1)} %get-tuple-element.57), channel_id=1, source_target_pairs={{0,2},{1,3},{2,0},{3,1},{4,6},{5,7},{6,4},{7,5},{8,10},{9,11},{10,... | collective-permute-start | bytes 786440 | tf_op jit(solution)/shard_map/ppermute | solution.py:26
  54.1 20.4 %collective-permute-start.20 = (bf16[256,512]{1,0:T(8,128)(2,1)S(1)}, bf16[256,512]{1,0:T(8,128)(2,1)S(1)}, u32[]{:S(2)}, u32[]{:S(2)}) collective-permute-start(bf16[256,512]{1,0:T(8,128)(2,1)S(1)} %get-tuple-element.58), channel_id=1, source_target_pairs={{0,5},{1,6},{2,7},{3,4},{4,1},{5,2},{6,3},{7,0},{8,13},{9,14},{10,... | collective-permute-start | bytes 786440 | tf_op jit(solution)/shard_map/ppermute | solution.py:26
  56.1 19.6 %collective-permute-start.21 = (bf16[256,512]{1,0:T(8,128)(2,1)S(1)}, bf16[256,512]{1,0:T(8,128)(2,1)S(1)}, u32[]{:S(2)}, u32[]{:S(2)}) collective-permute-start(bf16[256,512]{1,0:T(8,128)(2,1)S(1)} %get-tuple-element.59), channel_id=1, source_target_pairs={{0,7},{1,4},{2,5},{3,6},{4,3},{5,0},{6,1},{7,2},{8,15},{9,12},{10,... | collective-permute-start | bytes 786440 | tf_op jit(solution)/shard_map/ppermute | solution.py:26
  78.7 23.6 %collective-permute-start.23 = (bf16[328,512]{1,0:T(8,128)(2,1)S(1)}, bf16[328,512]{1,0:T(8,128)(2,1)S(1)}, u32[]{:S(2)}, u32[]{:S(2)}) collective-permute-start(bf16[328,512]{1,0:T(8,128)(2,1)S(1)} %get-tuple-element.63), channel_id=1, source_target_pairs={{0,3},{1,0},{2,1},{3,2},{4,7},{5,4},{6,5},{7,6},{8,11},{9,8},{10,9... | collective-permute-start | bytes 1007624 | tf_op jit(solution)/shard_map/ppermute | solution.py:26
  80.7 26.9 %collective-permute-start.24 = (bf16[328,512]{1,0:T(8,128)(2,1)S(1)}, bf16[328,512]{1,0:T(8,128)(2,1)S(1)}, u32[]{:S(2)}, u32[]{:S(2)}) collective-permute-start(bf16[328,512]{1,0:T(8,128)(2,1)S(1)} %get-tuple-element.64), channel_id=1, source_target_pairs={{0,4},{1,5},{2,6},{3,7},{4,0},{5,1},{6,2},{7,3},{8,12},{9,13},{10,... | collective-permute-start | bytes 1007624 | tf_op jit(solution)/shard_map/ppermute | solution.py:26
  82.5 25.2 %collective-permute-start.25 = (bf16[328,512]{1,0:T(8,128)(2,1)S(1)}, bf16[328,512]{1,0:T(8,128)(2,1)S(1)}, u32[]{:S(2)}, u32[]{:S(2)}) collective-permute-start(bf16[328,512]{1,0:T(8,128)(2,1)S(1)} %get-tuple-element.65), channel_id=1, source_target_pairs={{0,6},{1,7},{2,4},{3,5},{4,2},{5,3},{6,0},{7,1},{8,14},{9,15},{10,... | collective-permute-start | bytes 1007624 | tf_op jit(solution)/shard_map/ppermute | solution.py:26
  85.1 25.0 %collective-permute-start.26 = (bf16[328,512]{1,0:T(8,128)(2,1)S(1)}, bf16[328,512]{1,0:T(8,128)(2,1)S(1)}, u32[]{:S(2)}, u32[]{:S(2)}) collective-permute-start(bf16[328,512]{1,0:T(8,128)(2,1)S(1)} %get-tuple-element.66), channel_id=1, source_target_pairs={{0,2},{1,3},{2,0},{3,1},{4,6},{5,7},{6,4},{7,5},{8,10},{9,11},{10,... | collective-permute-start | bytes 1007624 | tf_op jit(solution)/shard_map/ppermute | solution.py:26
  88.7 21.4 %collective-permute-start.27 = (bf16[328,512]{1,0:T(8,128)(2,1)S(1)}, bf16[328,512]{1,0:T(8,128)(2,1)S(1)}, u32[]{:S(2)}, u32[]{:S(2)}) collective-permute-start(bf16[328,512]{1,0:T(8,128)(2,1)S(1)} %get-tuple-element.67), channel_id=1, source_target_pairs={{0,5},{1,6},{2,7},{3,4},{4,1},{5,2},{6,3},{7,0},{8,13},{9,14},{10,... | collective-permute-start | bytes 1007624 | tf_op jit(solution)/shard_map/ppermute | solution.py:26
  102.2 12.9 %collective-permute-start.28 = (bf16[328,512]{1,0:T(8,128)(2,1)S(1)}, bf16[328,512]{1,0:T(8,128)(2,1)S(1)}, u32[]{:S(2)}, u32[]{:S(2)}) collective-permute-start(bf16[328,512]{1,0:T(8,128)(2,1)S(1)} %get-tuple-element.68), channel_id=1, source_target_pairs={{0,7},{1,4},{2,5},{3,6},{4,3},{5,0},{6,1},{7,2},{8,15},{9,12},{10,... | collective-permute-start | bytes 1007624 | tf_op jit(solution)/shard_map/ppermute | solution.py:26
  142.5 15.2 %collective-permute-start.41 = (bf16[256,512]{1,0:T(8,128)(2,1)S(1)}, bf16[256,512]{1,0:T(8,128)(2,1)S(1)}, u32[]{:S(2)}, u32[]{:S(2)}) collective-permute-start(bf16[256,512]{1,0:T(8,128)(2,1)S(1)} %get-tuple-element.84), channel_id=1, source_target_pairs={{0,48},{16,0},{32,16},{48,32},{64,112},{80,64},{96,80},{112,96},{1... | collective-permute-start | bytes 786440 | tf_op jit(solution)/shard_map/ppermute | solution.py:26
  144.1 17.6 %collective-permute-start.34 = (bf16[256,512]{1,0:T(8,128)(2,1)S(1)}, bf16[256,512]{1,0:T(8,128)(2,1)S(1)}, u32[]{:S(2)}, u32[]{:S(2)}) collective-permute-start(bf16[256,512]{1,0:T(8,128)(2,1)S(1)} %get-tuple-element.77), channel_id=1, source_target_pairs={{0,112},{16,64},{32,80},{48,96},{64,48},{80,0},{96,16},{112,32},{1... | collective-permute-start | bytes 786440 | tf_op jit(solution)/shard_map/ppermute | solution.py:26
  145.5 28.7 %collective-permute-start.33 = (bf16[256,512]{1,0:T(8,128)(2,1)S(1)}, bf16[256,512]{1,0:T(8,128)(2,1)S(1)}, u32[]{:S(2)}, u32[]{:S(2)}) collective-permute-start(bf16[256,512]{1,0:T(8,128)(2,1)S(1)} %get-tuple-element.76), channel_id=1, source_target_pairs={{0,80},{16,96},{32,112},{48,64},{64,16},{80,32},{96,48},{112,0},{1... | collective-permute-start | bytes 786440 | tf_op jit(solution)/shard_map/ppermute | solution.py:26
  147.1 29.7 %collective-permute-start.32 = (bf16[256,512]{1,0:T(8,128)(2,1)S(1)}, bf16[256,512]{1,0:T(8,128)(2,1)S(1)}, u32[]{:S(2)}, u32[]{:S(2)}) collective-permute-start(bf16[256,512]{1,0:T(8,128)(2,1)S(1)} %get-tuple-element.75), channel_id=1, source_target_pairs={{0,32},{16,48},{32,0},{48,16},{64,96},{80,112},{96,64},{112,80},{1... | collective-permute-start | bytes 786440 | tf_op jit(solution)/shard_map/ppermute | solution.py:26
  149.4 27.4 %collective-permute-start.31 = (bf16[256,512]{1,0:T(8,128)(2,1)S(1)}, bf16[256,512]{1,0:T(8,128)(2,1)S(1)}, u32[]{:S(2)}, u32[]{:S(2)}) collective-permute-start(bf16[256,512]{1,0:T(8,128)(2,1)S(1)} %get-tuple-element.74), channel_id=1, source_target_pairs={{0,96},{16,112},{32,64},{48,80},{64,32},{80,48},{96,0},{112,16},{1... | collective-permute-start | bytes 786440 | tf_op jit(solution)/shard_map/ppermute | solution.py:26
  157.7 20.1 %collective-permute-start.43 = (bf16[128,512]{1,0:T(8,128)(2,1)S(1)}, bf16[128,512]{1,0:T(8,128)(2,1)S(1)}, u32[]{:S(2)}, u32[]{:S(2)}) collective-permute-start(bf16[128,512]{1,0:T(8,128)(2,1)S(1)} %pad_maximum_fusion.refs_1_), channel_id=1, source_target_pairs={{0,1},{1,2},{2,3},{3,0},{4,5},{5,6},{6,7},{7,4},{8,9},{9,10},{10,1... | collective-permute-start | bytes 393224 | tf_op jit(solution)/shard_map/ppermute | solution.py:26
  161.7 16.8 %collective-permute-start.44 = (bf16[128,512]{1,0:T(8,128)(2,1)S(1)}, bf16[128,512]{1,0:T(8,128)(2,1)S(1)}, u32[]{:S(2)}, u32[]{:S(2)}) collective-permute-start(bf16[128,512]{1,0:T(8,128)(2,1)S(1)} %pad_maximum_fusion.refs_1_), channel_id=1, source_target_pairs={{0,2},{1,3},{2,0},{3,1},{4,6},{5,7},{6,4},{7,5},{8,10},{9,11},{10,... | collective-permute-start | bytes 393224 | tf_op jit(solution)/shard_map/ppermute | solution.py:26
  (28 other events, 341.2 us)

commit v9 on v8

--- a/solution.py
+++ b/solution.py
@@ -383,7 +383,7 @@
 
     own = [send_by(features, CHIP, o) if any(o) else features for o in chips]
     values, index = fetch(values, index)
-    index, own[1] = lax.optimization_barrier((index, own[1]))
+    index, own[3] = lax.optimization_barrier((index, own[3]))
     crossed = [send_by(x, ("core",), (1,)) for x in own]
     partial = aggregate(begin["come"], begin["to"], len(parts), index, targets, counts, own + crossed, values)
 

time: 183 us -> 188 us (1.027)
  waiting for transfers between devices: 61 us -> 74.1 us
  starting transfers between devices: 85.8 us -> 79.4 us
    ppermute x41, waiting for transfers between devices: 56.9 us -> 70.4 us  [send_by(): return lax.ppermute(value, axes, pairs)]
    ppermute x41, starting transfers between devices: 77.5 us -> 70.7 us  [send_by(): return lax.ppermute(value, axes, pairs)]
where the time goes in v9:
time: 188 us; the launch traced here: 187 us
  starting transfers between devices  79.4 us (42%)
  waiting for transfers between devices  74.1 us (39%)
  Pallas kernels  30.4 us (16%)
    ppermute x41, starting transfers between devices, send_by(): return lax.ppermute(value, axes, pairs)  70.7 us
    ppermute x41, waiting for transfers between devices, send_by(): return lax.ppermute(value, axes, pairs)  70.4 us
    pallas_call x4, Pallas kernels, spread(): pl.pallas_call(lambda *refs: backward_kernel(shards, parts, at_source, at...  12 us
    pallas_call x1, Pallas kernels, aggregate(): pl.pallas_call(lambda *refs: forward_kernel(shards, at_source, at_place,...  10.3 us
    ppermute x5, starting transfers between devices, exchange(): lax.ppermute(value, axis, [(i, i ^ mask) for i in range(SIZES[axis])])  8.61 us
    pallas_call x1, Pallas kernels, fetch(): pl.pallas_call(fetch_kernel, out_shape=(pltpu.VMEM(values.shape, values.d...  4.61 us
  transfers between devices with their start and end apart: 46, of which 21 were waited for; matrix products, arithmetic and copies ran while one was open for 1% of the time, Pallas kernels for 9%

profile of v9, /device:TPU:0, one launch (start us, length us, event | category | flops | bytes accessed | tf_op | source)
XLA Modules:
  0.0 187.1 jit_solution(17045884274724733234)
XLA Ops:
  9.9 3.2 %collective-permute-start.5 = (bf16[256,512]{1,0:T(8,128)(2,1)}, bf16[256,512]{1,0:T(8,128)(2,1)S(1)}, u32[]{:S(2)}, u32[]{:S(2)}) collective-permute-start(bf16[256,512]{1,0:T(8,128)(2,1)} %refs_4_.1), channel_id=1, source_target_pairs={{0,80},{16,96},{32,112},{48,64},{64,16},{80,32},{96,48},{112,0},{1... | collective-permute-start | bytes 786440 | tf_op jit(solution)/shard_map/ppermute | solution.py:26
  13.1 10.1 %collective-permute-done.1.refs_5_ = bf16[256,512]{1,0:T(8,128)(2,1)S(1)} collective-permute-done((bf16[256,512]{1,0:T(8,128)(2,1)}, bf16[256,512]{1,0:T(8,128)(2,1)S(1)}, u32[]{:S(2)}, u32[]{:S(2)}) %collective-permute-start.1) | collective-permute-done | bytes 262176 | tf_op jit(solution)/shard_map/ppermute | solution.py:26
  23.2 3.8 %collective-permute-start.6 = (bf16[256,512]{1,0:T(8,128)(2,1)}, bf16[256,512]{1,0:T(8,128)(2,1)S(1)}, u32[]{:S(2)}, u32[]{:S(2)}) collective-permute-start(bf16[256,512]{1,0:T(8,128)(2,1)} %refs_4_.1), channel_id=1, source_target_pairs={{0,112},{16,64},{32,80},{48,96},{64,48},{80,0},{96,16},{112,32},{1... | collective-permute-start | bytes 786440 | tf_op jit(solution)/shard_map/ppermute | solution.py:26
  27.5 3.1 %collective-permute-done.4.refs_9_ = bf16[256,512]{1,0:T(8,128)(2,1)S(1)} collective-permute-done((bf16[256,512]{1,0:T(8,128)(2,1)}, bf16[256,512]{1,0:T(8,128)(2,1)S(1)}, u32[]{:S(2)}, u32[]{:S(2)}) %collective-permute-start.4) | collective-permute-done | bytes 262176 | tf_op jit(solution)/shard_map/ppermute | solution.py:26
  31.3 4.6 %fetch.1 = (bf16[32,8,128,128]{3,2,1,0:T(8,128)(2,1)S(1)}, s32[56]{0:T(128)S(1)}) custom-call(s32[56]{0:T(128)S(1)} %dynamic-slice_bitcast_fusion.index_ref, bf16[32,8,128,128]{3,2,1,0:T(8,128)(2,1)} %bitcast.20), custom_call_target="tpu_custom_call" | custom-call | bytes 16777216 | tf_op jit(solution)/shard_map/fetch/pallas_call | solution.py:80
  39.2 10.3 %aggregate.1 = (bf16[256,512]{1,0:T(8,128)(2,1)S(1)}, bf16[256,512]{1,0:T(8,128)(2,1)S(1)}, bf16[256,512]{1,0:T(8,128)(2,1)S(1)}, bf16[256,512]{1,0:T(8,128)(2,1...) custom-call(s32[56]{0:T(128)S(1)} %get-tuple-element.81.refs_0_, ...), custom_call_target="tpu_custom_call" | custom-call | flops 8589934592 | bytes 16777216 | tf_op jit(solution)/shard_map/aggregate/pallas_call | solution.py:129
  52.9 5.8 %collective-permute-start.17 = (bf16[256,512]{1,0:T(8,128)(2,1)S(1)}, bf16[256,512]{1,0:T(8,128)(2,1)S(1)}, u32[]{:S(2)}, u32[]{:S(2)}) collective-permute-start(bf16[256,512]{1,0:T(8,128)(2,1)S(1)} %get-tuple-element.55), channel_id=1, source_target_pairs={{0,4},{1,5},{2,6},{3,7},{4,0},{5,1},{6,2},{7,3},{8,12},{9,13},{10,... | collective-permute-start | bytes 786440 | tf_op jit(solution)/shard_map/ppermute | solution.py:26
  58.7 3.0 %collective-permute-start.19 = (bf16[256,512]{1,0:T(8,128)(2,1)S(1)}, bf16[256,512]{1,0:T(8,128)(2,1)S(1)}, u32[]{:S(2)}, u32[]{:S(2)}) collective-permute-start(bf16[256,512]{1,0:T(8,128)(2,1)S(1)} %get-tuple-element.57), channel_id=1, source_target_pairs={{0,2},{1,3},{2,0},{3,1},{4,6},{5,7},{6,4},{7,5},{8,10},{9,11},{10,... | collective-permute-start | bytes 786440 | tf_op jit(solution)/shard_map/ppermute | solution.py:26
  63.8 3.5 %collective-permute-start.21 = (bf16[256,512]{1,0:T(8,128)(2,1)S(1)}, bf16[256,512]{1,0:T(8,128)(2,1)S(1)}, u32[]{:S(2)}, u32[]{:S(2)}) collective-permute-start(bf16[256,512]{1,0:T(8,128)(2,1)S(1)} %get-tuple-element.59), channel_id=1, source_target_pairs={{0,7},{1,4},{2,5},{3,6},{4,3},{5,0},{6,1},{7,2},{8,15},{9,12},{10,... | collective-permute-start | bytes 786440 | tf_op jit(solution)/shard_map/ppermute | solution.py:26
  67.3 5.1 %collective-permute-done.18.refs_5_ = bf16[256,512]{1,0:T(8,128)(2,1)S(1)} collective-permute-done((bf16[256,512]{1,0:T(8,128)(2,1)S(1)}, bf16[256,512]{1,0:T(8,128)(2,1)S(1)}, u32[]{:S(2)}, u32[]{:S(2)}) %collective-permute-start.18) | collective-permute-done | bytes 262176 | tf_op jit(solution)/shard_map/ppermute | solution.py:26
  72.4 8.4 %collective-permute-done.19.refs_6_ = bf16[256,512]{1,0:T(8,128)(2,1)S(1)} collective-permute-done((bf16[256,512]{1,0:T(8,128)(2,1)S(1)}, bf16[256,512]{1,0:T(8,128)(2,1)S(1)}, u32[]{:S(2)}, u32[]{:S(2)}) %collective-permute-start.19) | collective-permute-done | bytes 262176 | tf_op jit(solution)/shard_map/ppermute | solution.py:26
  83.8 3.2 %collective-permute-start.23 = (bf16[328,512]{1,0:T(8,128)(2,1)S(1)}, bf16[328,512]{1,0:T(8,128)(2,1)S(1)}, u32[]{:S(2)}, u32[]{:S(2)}) collective-permute-start(bf16[328,512]{1,0:T(8,128)(2,1)S(1)} %get-tuple-element.63), channel_id=1, source_target_pairs={{0,3},{1,0},{2,1},{3,2},{4,7},{5,4},{6,5},{7,6},{8,11},{9,8},{10,9... | collective-permute-start | bytes 1007624 | tf_op jit(solution)/shard_map/ppermute | solution.py:26
  87.1 3.5 %collective-permute-start.24 = (bf16[328,512]{1,0:T(8,128)(2,1)S(1)}, bf16[328,512]{1,0:T(8,128)(2,1)S(1)}, u32[]{:S(2)}, u32[]{:S(2)}) collective-permute-start(bf16[328,512]{1,0:T(8,128)(2,1)S(1)} %get-tuple-element.64), channel_id=1, source_target_pairs={{0,4},{1,5},{2,6},{3,7},{4,0},{5,1},{6,2},{7,3},{8,12},{9,13},{10,... | collective-permute-start | bytes 1007624 | tf_op jit(solution)/shard_map/ppermute | solution.py:26
  93.6 15.6 %collective-permute-done.22.refs_1_.refs_5_ = bf16[328,512]{1,0:T(8,128)(2,1)S(1)} collective-permute-done((bf16[328,512]{1,0:T(8,128)(2,1)S(1)}, bf16[328,512]{1,0:T(8,128)(2,1)S(1)}, u32[]{:S(2)}, u32[]{:S(2)}) %collective-permute-start.22) | collective-permute-done | bytes 335904 | tf_op jit(solution)/shard_map/ppermute | solution.py:26
  111.4 6.0 %collective-permute-start.28 = (bf16[328,512]{1,0:T(8,128)(2,1)S(1)}, bf16[328,512]{1,0:T(8,128)(2,1)S(1)}, u32[]{:S(2)}, u32[]{:S(2)}) collective-permute-start(bf16[328,512]{1,0:T(8,128)(2,1)S(1)} %get-tuple-element.68), channel_id=1, source_target_pairs={{0,7},{1,4},{2,5},{3,6},{4,3},{5,0},{6,1},{7,2},{8,15},{9,12},{10,... | collective-permute-start | bytes 1007624 | tf_op jit(solution)/shard_map/ppermute | solution.py:26
  119.9 3.1 %collective-permute-done.28.refs_7_.refs_11_ = bf16[328,512]{1,0:T(8,128)(2,1)S(1)} collective-permute-done((bf16[328,512]{1,0:T(8,128)(2,1)S(1)}, bf16[328,512]{1,0:T(8,128)(2,1)S(1)}, u32[]{:S(2)}, u32[]{:S(2)}) %collective-permute-start.28) | collective-permute-done | bytes 335904 | tf_op jit(solution)/shard_map/ppermute | solution.py:26
  123.2 3.0 %spread.5 = bf16[4,256,512]{2,1,0:T(8,128)(2,1)S(1)} custom-call(s32[56]{0:T(128)S(1)} %get-tuple-element.81.refs_0_, s32[8,32]{1,0:T(8,128)S(1)} %bitcast.10, s32[32]{0:T(128)S(1)} %bitcast.16, bf16[32,8,128,128]{3,2,1,0:T(8,128)(2,1)S(1)} %get-tuple-element.50.refs_3_, bf16[328,512]{1,0:T(8,128)(2,1)S(1)} %get-tuple-element.61.refs_0_.refs_4_, ...), custom_call_target="tpu_custom_call" | custom-call | flops 17179869184 | bytes 4194304 | tf_op jit(solution)/shard_map/spread/pallas_call | solution.py:243
  129.9 3.1 %spread.6 = (bf16[256,512]{1,0:T(8,128)(2,1)S(1)}, bf16[256,512]{1,0:T(8,128)(2,1)S(1)}, bf16[256,512]{1,0:T(8,128)(2,1)S(1)}, bf16[256,512]{1,0:T(8,128)(2,1)S(1)}) custom-call(s32[56]{0:T(128)S(1)} %get-tuple-element.81.refs_0_, s32[8,32]{1,0:T(8,128)S(1)} %bitcast.12, s32[32]{0:T(128)S(1)} %bitcast.18, ...), custom_call_target="tpu_custom_call" | custom-call | flops 17179869184 | bytes 4194304 | tf_op jit(solution)/shard_map/spread/pallas_call | solution.py:243
  135.7 5.3 %collective-permute-start.37 = (f32[72,512]{1,0:T(8,128)S(1)}, f32[72,512]{1,0:T(8,128)S(1)}, u32[]{:S(2)}, u32[]{:S(2)}) collective-permute-start(f32[72,512]{1,0:T(8,128)S(1)} %add.57), channel_id=1, source_target_pairs={{0,32},{16,48},{32,0},{48,16},{1,33},{17,49},{33,1},{49,17},{2,34}... | collective-permute-start | bytes 442376 | tf_op jit(solution)/shard_map/ppermute | solution.py:30
  141.0 3.1 %spread.7 = (bf16[256,512]{1,0:T(8,128)(2,1)S(1)}, bf16[256,512]{1,0:T(8,128)(2,1)S(1)}, bf16[256,512]{1,0:T(8,128)(2,1)S(1)}, bf16[256,512]{1,0:T(8,128)(2,1)S(1)}) custom-call(s32[56]{0:T(128)S(1)} %get-tuple-element.81.refs_0_, s32[8,32]{1,0:T(8,128)S(1)} %bitcast.13, s32[32]{0:T(128)S(1)} %bitcast.19, ...), custom_call_target="tpu_custom_call" | custom-call | flops 17179869184 | bytes 4194304 | tf_op jit(solution)/shard_map/spread/pallas_call | solution.py:243
  146.4 3.0 %collective-permute-start.39 = (bf16[72,512]{1,0:T(8,128)(2,1)S(1)}, bf16[72,512]{1,0:T(8,128)(2,1)S(1)}, u32[]{:S(2)}, u32[]{:S(2)}) collective-permute-start(bf16[72,512]{1,0:T(8,128)(2,1)S(1)} %get-tuple-element.92), channel_id=1, source_target_pairs={{0,4},{4,0},{1,5},{5,1},{2,6},{6,2},{3,7},{7,3},{8,12},{12,8},{9,1... | collective-permute-start | bytes 221192 | tf_op jit(solution)/shard_map/ppermute | solution.py:30
  155.4 3.2 %collective-permute-start.32 = (bf16[256,512]{1,0:T(8,128)(2,1)S(1)}, bf16[256,512]{1,0:T(8,128)(2,1)S(1)}, u32[]{:S(2)}, u32[]{:S(2)}) collective-permute-start(bf16[256,512]{1,0:T(8,128)(2,1)S(1)} %get-tuple-element.75), channel_id=1, source_target_pairs={{0,32},{16,48},{32,0},{48,16},{64,96},{80,112},{96,64},{112,80},{1... | collective-permute-start | bytes 786440 | tf_op jit(solution)/shard_map/ppermute | solution.py:26
  160.7 13.8 %collective-permute-done.41 = bf16[256,512]{1,0:T(8,128)(2,1)S(1)} collective-permute-done((bf16[256,512]{1,0:T(8,128)(2,1)S(1)}, bf16[256,512]{1,0:T(8,128)(2,1)S(1)}, u32[]{:S(2)}, u32[]{:S(2)}) %collective-permute-start.41) | collective-permute-done | bytes 262176 | tf_op jit(solution)/shard_map/ppermute | solution.py:26
  176.1 4.3 %collective-permute-start.44 = (bf16[128,512]{1,0:T(8,128)(2,1)S(1)}, bf16[128,512]{1,0:T(8,128)(2,1)S(1)}, u32[]{:S(2)}, u32[]{:S(2)}) collective-permute-start(bf16[128,512]{1,0:T(8,128)(2,1)S(1)} %pad_maximum_fusion.refs_1_), channel_id=1, source_target_pairs={{0,2},{1,3},{2,0},{3,1},{4,6},{5,7},{6,4},{7,5},{8,10},{9,11},{10,... | collective-permute-start | bytes 393224 | tf_op jit(solution)/shard_map/ppermute | solution.py:26
  (99 shorter events, 55.2 us)
Async XLA Ops:
  2.3 20.9 %collective-permute-start.1 = (bf16[256,512]{1,0:T(8,128)(2,1)}, bf16[256,512]{1,0:T(8,128)(2,1)S(1)}, u32[]{:S(2)}, u32[]{:S(2)}) collective-permute-start(bf16[256,512]{1,0:T(8,128)(2,1)} %refs_4_.1), channel_id=1, source_target_pairs={{0,16},{16,32},{32,48},{48,0},{64,80},{80,96},{96,112},{112,64},{1... | collective-permute-start | bytes 786440 | tf_op jit(solution)/shard_map/ppermute | solution.py:26
  4.2 22.8 %collective-permute-start.2 = (bf16[256,512]{1,0:T(8,128)(2,1)}, bf16[256,512]{1,0:T(8,128)(2,1)S(1)}, u32[]{:S(2)}, u32[]{:S(2)}) collective-permute-start(bf16[256,512]{1,0:T(8,128)(2,1)} %refs_4_.1), channel_id=1, source_target_pairs={{0,48},{16,0},{32,16},{48,32},{64,112},{80,64},{96,80},{112,96},{1... | collective-permute-start | bytes 786440 | tf_op jit(solution)/shard_map/ppermute | solution.py:26
  6.4 20.7 %collective-permute-start.3 = (bf16[256,512]{1,0:T(8,128)(2,1)}, bf16[256,512]{1,0:T(8,128)(2,1)S(1)}, u32[]{:S(2)}, u32[]{:S(2)}) collective-permute-start(bf16[256,512]{1,0:T(8,128)(2,1)} %refs_4_.1), channel_id=1, source_target_pairs={{0,96},{16,112},{32,64},{48,80},{64,32},{80,48},{96,0},{112,16},{1... | collective-permute-start | bytes 786440 | tf_op jit(solution)/shard_map/ppermute | solution.py:26
  8.2 22.4 %collective-permute-start.4 = (bf16[256,512]{1,0:T(8,128)(2,1)}, bf16[256,512]{1,0:T(8,128)(2,1)S(1)}, u32[]{:S(2)}, u32[]{:S(2)}) collective-permute-start(bf16[256,512]{1,0:T(8,128)(2,1)} %refs_4_.1), channel_id=1, source_target_pairs={{0,32},{16,48},{32,0},{48,16},{64,96},{80,112},{96,64},{112,80},{1... | collective-permute-start | bytes 786440 | tf_op jit(solution)/shard_map/ppermute | solution.py:26
  9.9 26.1 %collective-permute-start.5 = (bf16[256,512]{1,0:T(8,128)(2,1)}, bf16[256,512]{1,0:T(8,128)(2,1)S(1)}, u32[]{:S(2)}, u32[]{:S(2)}) collective-permute-start(bf16[256,512]{1,0:T(8,128)(2,1)} %refs_4_.1), channel_id=1, source_target_pairs={{0,80},{16,96},{32,112},{48,64},{64,16},{80,32},{96,48},{112,0},{1... | collective-permute-start | bytes 786440 | tf_op jit(solution)/shard_map/ppermute | solution.py:26
  23.2 13.3 %collective-permute-start.6 = (bf16[256,512]{1,0:T(8,128)(2,1)}, bf16[256,512]{1,0:T(8,128)(2,1)S(1)}, u32[]{:S(2)}, u32[]{:S(2)}) collective-permute-start(bf16[256,512]{1,0:T(8,128)(2,1)} %refs_4_.1), channel_id=1, source_target_pairs={{0,112},{16,64},{32,80},{48,96},{64,48},{80,0},{96,16},{112,32},{1... | collective-permute-start | bytes 786440 | tf_op jit(solution)/shard_map/ppermute | solution.py:26
  49.6 12.1 %collective-permute-start.15 = (bf16[256,512]{1,0:T(8,128)(2,1)S(1)}, bf16[256,512]{1,0:T(8,128)(2,1)S(1)}, u32[]{:S(2)}, u32[]{:S(2)}) collective-permute-start(bf16[256,512]{1,0:T(8,128)(2,1)S(1)} %get-tuple-element.53), channel_id=1, source_target_pairs={{0,1},{1,2},{2,3},{3,0},{4,5},{5,6},{6,7},{7,4},{8,9},{9,10},{10,1... | collective-permute-start | bytes 786440 | tf_op jit(solution)/shard_map/ppermute | solution.py:26
  51.1 12.7 %collective-permute-start.16 = (bf16[256,512]{1,0:T(8,128)(2,1)S(1)}, bf16[256,512]{1,0:T(8,128)(2,1)S(1)}, u32[]{:S(2)}, u32[]{:S(2)}) collective-permute-start(bf16[256,512]{1,0:T(8,128)(2,1)S(1)} %get-tuple-element.54), channel_id=1, source_target_pairs={{0,3},{1,0},{2,1},{3,2},{4,7},{5,4},{6,5},{7,6},{8,11},{9,8},{10,9... | collective-permute-start | bytes 786440 | tf_op jit(solution)/shard_map/ppermute | solution.py:26
  52.9 14.4 %collective-permute-start.17 = (bf16[256,512]{1,0:T(8,128)(2,1)S(1)}, bf16[256,512]{1,0:T(8,128)(2,1)S(1)}, u32[]{:S(2)}, u32[]{:S(2)}) collective-permute-start(bf16[256,512]{1,0:T(8,128)(2,1)S(1)} %get-tuple-element.55), channel_id=1, source_target_pairs={{0,4},{1,5},{2,6},{3,7},{4,0},{5,1},{6,2},{7,3},{8,12},{9,13},{10,... | collective-permute-start | bytes 786440 | tf_op jit(solution)/shard_map/ppermute | solution.py:26
  58.7 13.7 %collective-permute-start.18 = (bf16[256,512]{1,0:T(8,128)(2,1)S(1)}, bf16[256,512]{1,0:T(8,128)(2,1)S(1)}, u32[]{:S(2)}, u32[]{:S(2)}) collective-permute-start(bf16[256,512]{1,0:T(8,128)(2,1)S(1)} %get-tuple-element.56), channel_id=1, source_target_pairs={{0,6},{1,7},{2,4},{3,5},{4,2},{5,3},{6,0},{7,1},{8,14},{9,15},{10,... | collective-permute-start | bytes 786440 | tf_op jit(solution)/shard_map/ppermute | solution.py:26
  58.7 22.1 %collective-permute-start.19 = (bf16[256,512]{1,0:T(8,128)(2,1)S(1)}, bf16[256,512]{1,0:T(8,128)(2,1)S(1)}, u32[]{:S(2)}, u32[]{:S(2)}) collective-permute-start(bf16[256,512]{1,0:T(8,128)(2,1)S(1)} %get-tuple-element.57), channel_id=1, source_target_pairs={{0,2},{1,3},{2,0},{3,1},{4,6},{5,7},{6,4},{7,5},{8,10},{9,11},{10,... | collective-permute-start | bytes 786440 | tf_op jit(solution)/shard_map/ppermute | solution.py:26
  61.7 19.1 %collective-permute-start.20 = (bf16[256,512]{1,0:T(8,128)(2,1)S(1)}, bf16[256,512]{1,0:T(8,128)(2,1)S(1)}, u32[]{:S(2)}, u32[]{:S(2)}) collective-permute-start(bf16[256,512]{1,0:T(8,128)(2,1)S(1)} %get-tuple-element.58), channel_id=1, source_target_pairs={{0,5},{1,6},{2,7},{3,4},{4,1},{5,2},{6,3},{7,0},{8,13},{9,14},{10,... | collective-permute-start | bytes 786440 | tf_op jit(solution)/shard_map/ppermute | solution.py:26
  63.8 18.2 %collective-permute-start.21 = (bf16[256,512]{1,0:T(8,128)(2,1)S(1)}, bf16[256,512]{1,0:T(8,128)(2,1)S(1)}, u32[]{:S(2)}, u32[]{:S(2)}) collective-permute-start(bf16[256,512]{1,0:T(8,128)(2,1)S(1)} %get-tuple-element.59), channel_id=1, source_target_pairs={{0,7},{1,4},{2,5},{3,6},{4,3},{5,0},{6,1},{7,2},{8,15},{9,12},{10,... | collective-permute-start | bytes 786440 | tf_op jit(solution)/shard_map/ppermute | solution.py:26
  83.8 25.3 %collective-permute-start.22 = (bf16[328,512]{1,0:T(8,128)(2,1)S(1)}, bf16[328,512]{1,0:T(8,128)(2,1)S(1)}, u32[]{:S(2)}, u32[]{:S(2)}) collective-permute-start(bf16[328,512]{1,0:T(8,128)(2,1)S(1)} %get-tuple-element.62), channel_id=1, source_target_pairs={{0,1},{1,2},{2,3},{3,0},{4,5},{5,6},{6,7},{7,4},{8,9},{9,10},{10,1... | collective-permute-start | bytes 1007624 | tf_op jit(solution)/shard_map/ppermute | solution.py:26
  83.8 27.6 %collective-permute-start.23 = (bf16[328,512]{1,0:T(8,128)(2,1)S(1)}, bf16[328,512]{1,0:T(8,128)(2,1)S(1)}, u32[]{:S(2)}, u32[]{:S(2)}) collective-permute-start(bf16[328,512]{1,0:T(8,128)(2,1)S(1)} %get-tuple-element.63), channel_id=1, source_target_pairs={{0,3},{1,0},{2,1},{3,2},{4,7},{5,4},{6,5},{7,6},{8,11},{9,8},{10,9... | collective-permute-start | bytes 1007624 | tf_op jit(solution)/shard_map/ppermute | solution.py:26
  87.1 30.3 %collective-permute-start.24 = (bf16[328,512]{1,0:T(8,128)(2,1)S(1)}, bf16[328,512]{1,0:T(8,128)(2,1)S(1)}, u32[]{:S(2)}, u32[]{:S(2)}) collective-permute-start(bf16[328,512]{1,0:T(8,128)(2,1)S(1)} %get-tuple-element.64), channel_id=1, source_target_pairs={{0,4},{1,5},{2,6},{3,7},{4,0},{5,1},{6,2},{7,3},{8,12},{9,13},{10,... | collective-permute-start | bytes 1007624 | tf_op jit(solution)/shard_map/ppermute | solution.py:26
  90.5 26.9 %collective-permute-start.25 = (bf16[328,512]{1,0:T(8,128)(2,1)S(1)}, bf16[328,512]{1,0:T(8,128)(2,1)S(1)}, u32[]{:S(2)}, u32[]{:S(2)}) collective-permute-start(bf16[328,512]{1,0:T(8,128)(2,1)S(1)} %get-tuple-element.65), channel_id=1, source_target_pairs={{0,6},{1,7},{2,4},{3,5},{4,2},{5,3},{6,0},{7,1},{8,14},{9,15},{10,... | collective-permute-start | bytes 1007624 | tf_op jit(solution)/shard_map/ppermute | solution.py:26
  90.8 26.6 %collective-permute-start.26 = (bf16[328,512]{1,0:T(8,128)(2,1)S(1)}, bf16[328,512]{1,0:T(8,128)(2,1)S(1)}, u32[]{:S(2)}, u32[]{:S(2)}) collective-permute-start(bf16[328,512]{1,0:T(8,128)(2,1)S(1)} %get-tuple-element.66), channel_id=1, source_target_pairs={{0,2},{1,3},{2,0},{3,1},{4,6},{5,7},{6,4},{7,5},{8,10},{9,11},{10,... | collective-permute-start | bytes 1007624 | tf_op jit(solution)/shard_map/ppermute | solution.py:26
  146.4 12.1 %collective-permute-start.39 = (bf16[72,512]{1,0:T(8,128)(2,1)S(1)}, bf16[72,512]{1,0:T(8,128)(2,1)S(1)}, u32[]{:S(2)}, u32[]{:S(2)}) collective-permute-start(bf16[72,512]{1,0:T(8,128)(2,1)S(1)} %get-tuple-element.92), channel_id=1, source_target_pairs={{0,4},{4,0},{1,5},{5,1},{2,6},{6,2},{3,7},{7,3},{8,12},{12,8},{9,1... | collective-permute-start | bytes 221192 | tf_op jit(solution)/shard_map/ppermute | solution.py:30
  149.5 25.0 %collective-permute-start.41 = (bf16[256,512]{1,0:T(8,128)(2,1)S(1)}, bf16[256,512]{1,0:T(8,128)(2,1)S(1)}, u32[]{:S(2)}, u32[]{:S(2)}) collective-permute-start(bf16[256,512]{1,0:T(8,128)(2,1)S(1)} %get-tuple-element.84), channel_id=1, source_target_pairs={{0,48},{16,0},{32,16},{48,32},{64,112},{80,64},{96,80},{112,96},{1... | collective-permute-start | bytes 786440 | tf_op jit(solution)/shard_map/ppermute | solution.py:26
  152.3 23.8 %collective-permute-start.34 = (bf16[256,512]{1,0:T(8,128)(2,1)S(1)}, bf16[256,512]{1,0:T(8,128)(2,1)S(1)}, u32[]{:S(2)}, u32[]{:S(2)}) collective-permute-start(bf16[256,512]{1,0:T(8,128)(2,1)S(1)} %get-tuple-element.77), channel_id=1, source_target_pairs={{0,112},{16,64},{32,80},{48,96},{64,48},{80,0},{96,16},{112,32},{1... | collective-permute-start | bytes 786440 | tf_op jit(solution)/shard_map/ppermute | solution.py:26
  154.3 26.1 %collective-permute-start.33 = (bf16[256,512]{1,0:T(8,128)(2,1)S(1)}, bf16[256,512]{1,0:T(8,128)(2,1)S(1)}, u32[]{:S(2)}, u32[]{:S(2)}) collective-permute-start(bf16[256,512]{1,0:T(8,128)(2,1)S(1)} %get-tuple-element.76), channel_id=1, source_target_pairs={{0,80},{16,96},{32,112},{48,64},{64,16},{80,32},{96,48},{112,0},{1... | collective-permute-start | bytes 786440 | tf_op jit(solution)/shard_map/ppermute | solution.py:26
  155.4 27.7 %collective-permute-start.32 = (bf16[256,512]{1,0:T(8,128)(2,1)S(1)}, bf16[256,512]{1,0:T(8,128)(2,1)S(1)}, u32[]{:S(2)}, u32[]{:S(2)}) collective-permute-start(bf16[256,512]{1,0:T(8,128)(2,1)S(1)} %get-tuple-element.75), channel_id=1, source_target_pairs={{0,32},{16,48},{32,0},{48,16},{64,96},{80,112},{96,64},{112,80},{1... | collective-permute-start | bytes 786440 | tf_op jit(solution)/shard_map/ppermute | solution.py:26
  158.6 24.5 %collective-permute-start.31 = (bf16[256,512]{1,0:T(8,128)(2,1)S(1)}, bf16[256,512]{1,0:T(8,128)(2,1)S(1)}, u32[]{:S(2)}, u32[]{:S(2)}) collective-permute-start(bf16[256,512]{1,0:T(8,128)(2,1)S(1)} %get-tuple-element.74), channel_id=1, source_target_pairs={{0,96},{16,112},{32,64},{48,80},{64,32},{80,48},{96,0},{112,16},{1... | collective-permute-start | bytes 786440 | tf_op jit(solution)/shard_map/ppermute | solution.py:26
  (28 other events, 392.4 us)

commit v10 on v8

--- a/solution.py
+++ b/solution.py
@@ -330,8 +330,8 @@
     )(index, *pieces)
 
 
-PARTS = ((0, 0), (0, 1), (0, 3), (1, 0), (1, 2), (0, 2), (1, 1), (1, 3))
-CHIP_HALVES = (((0, 0), (0, 1), (0, 3), (1, 0)), ((1, 2), (0, 2), (1, 1), (1, 3)))
+PARTS = ((0, 0), (0, 1), (1, 0), (0, 3), (1, 2), (0, 2), (1, 1), (1, 3))
+CHIP_HALVES = (((0, 0), (0, 1), (1, 0), (0, 3)), ((1, 2), (0, 2), (1, 1), (1, 3)))
 
 
 def lists_of_numbers(halves, chips, parts):

time: 183 us -> 176 us (0.962)
  waiting for transfers between devices: 61 us -> 49.2 us
  starting transfers between devices: 85.8 us -> 91.8 us
  Pallas kernels: 30.9 us -> 28.1 us
    ppermute x41, waiting for transfers between devices: 56.9 us -> 45.7 us  [send_by(): return lax.ppermute(value, axes, pairs)]
    ppermute x41, starting transfers between devices: 77.5 us -> 82.7 us  [send_by(): return lax.ppermute(value, axes, pairs)]
    pallas_call x1, Pallas kernels: 10.6 us -> 8.65 us  [aggregate(): pl.pallas_call(lambda *refs: forward_kernel(shards, at_source, at_place,...]
  transfers between devices with their start and end apart: 46 -> 46, of which waited for: 21 -> 24; matrix products, arithmetic and copies ran while one was open for 1% -> 1% of each run, Pallas kernels for 9% -> 9%
where the time goes in v10:
time: 176 us; the launch traced here: 172 us
  starting transfers between devices  91.8 us (52%)
  waiting for transfers between devices  49.2 us (28%)
  Pallas kernels  28.1 us (16%)
    ppermute x41, starting transfers between devices, send_by(): return lax.ppermute(value, axes, pairs)  82.7 us
    ppermute x41, waiting for transfers between devices, send_by(): return lax.ppermute(value, axes, pairs)  45.7 us
    pallas_call x4, Pallas kernels, spread(): pl.pallas_call(lambda *refs: backward_kernel(shards, parts, at_source, at...  11.4 us
    ppermute x5, starting transfers between devices, exchange(): lax.ppermute(value, axis, [(i, i ^ mask) for i in range(SIZES[axis])])  9.12 us
    pallas_call x1, Pallas kernels, aggregate(): pl.pallas_call(lambda *refs: forward_kernel(shards, at_source, at_place,...  8.65 us
    pallas_call x1, Pallas kernels, fetch(): pl.pallas_call(fetch_kernel, out_shape=(pltpu.VMEM(values.shape, values.d...  4.61 us
  transfers between devices with their start and end apart: 46, of which 24 were waited for; matrix products, arithmetic and copies ran while one was open for 1% of the time, Pallas kernels for 9%

profile of v10, /device:TPU:0, one launch (start us, length us, event | category | flops | bytes accessed | tf_op | source)
XLA Modules:
  0.0 172.4 jit_solution(17568091853692788543)
XLA Ops:
  10.6 4.6 %fetch.1 = (bf16[32,8,128,128]{3,2,1,0:T(8,128)(2,1)S(1)}, s32[56]{0:T(128)S(1)}) custom-call(s32[56]{0:T(128)S(1)} %dynamic-slice_bitcast_fusion.index_ref, bf16[32,8,128,128]{3,2,1,0:T(8,128)(2,1)} %bitcast.20), custom_call_target="tpu_custom_call" | custom-call | bytes 16777216 | tf_op jit(solution)/shard_map/fetch/pallas_call | solution.py:80
  16.1 3.4 %collective-permute-start.6 = (bf16[256,512]{1,0:T(8,128)(2,1)S(1)}, bf16[256,512]{1,0:T(8,128)(2,1)S(1)}, u32[]{:S(2)}, u32[]{:S(2)}) collective-permute-start(bf16[256,512]{1,0:T(8,128)(2,1)S(1)} %copy-done.1), channel_id=1, source_target_pairs={{0,112},{16,64},{32,80},{48,96},{64,48},{80,0},{96,16},{112,32},{1... | collective-permute-start | bytes 786440 | tf_op jit(solution)/shard_map/ppermute | solution.py:26
  19.5 9.4 %collective-permute-done.2.refs_7_ = bf16[256,512]{1,0:T(8,128)(2,1)S(1)} collective-permute-done((bf16[256,512]{1,0:T(8,128)(2,1)}, bf16[256,512]{1,0:T(8,128)(2,1)S(1)}, u32[]{:S(2)}, u32[]{:S(2)}) %collective-permute-start.2) | collective-permute-done | bytes 262176 | tf_op jit(solution)/shard_map/ppermute | solution.py:26
  33.1 8.6 %aggregate.1 = (bf16[256,512]{1,0:T(8,128)(2,1)S(1)}, bf16[256,512]{1,0:T(8,128)(2,1)S(1)}, bf16[256,512]{1,0:T(8,128)(2,1)S(1)}, bf16[256,512]{1,0:T(8,128)(2,1...) custom-call(s32[56]{0:T(128)S(1)} %get-tuple-element.81.refs_0_, ...), custom_call_target="tpu_custom_call" | custom-call | flops 8589934592 | bytes 16777216 | tf_op jit(solution)/shard_map/aggregate/pallas_call | solution.py:129
  41.8 6.6 %collective-permute-start.15 = (bf16[256,512]{1,0:T(8,128)(2,1)S(1)}, bf16[256,512]{1,0:T(8,128)(2,1)S(1)}, u32[]{:S(2)}, u32[]{:S(2)}) collective-permute-start(bf16[256,512]{1,0:T(8,128)(2,1)S(1)} %get-tuple-element.53), channel_id=1, source_target_pairs={{0,1},{1,2},{2,3},{3,0},{4,5},{5,6},{6,7},{7,4},{8,9},{9,10},{10,1... | collective-permute-start | bytes 786440 | tf_op jit(solution)/shard_map/ppermute | solution.py:26
  48.4 3.1 %collective-permute-start.17 = (bf16[256,512]{1,0:T(8,128)(2,1)S(1)}, bf16[256,512]{1,0:T(8,128)(2,1)S(1)}, u32[]{:S(2)}, u32[]{:S(2)}) collective-permute-start(bf16[256,512]{1,0:T(8,128)(2,1)S(1)} %get-tuple-element.55), channel_id=1, source_target_pairs={{0,3},{1,0},{2,1},{3,2},{4,7},{5,4},{6,5},{7,6},{8,11},{9,8},{10,9... | collective-permute-start | bytes 786440 | tf_op jit(solution)/shard_map/ppermute | solution.py:26
  58.0 3.5 %collective-permute-start.21 = (bf16[256,512]{1,0:T(8,128)(2,1)S(1)}, bf16[256,512]{1,0:T(8,128)(2,1)S(1)}, u32[]{:S(2)}, u32[]{:S(2)}) collective-permute-start(bf16[256,512]{1,0:T(8,128)(2,1)S(1)} %get-tuple-element.59), channel_id=1, source_target_pairs={{0,7},{1,4},{2,5},{3,6},{4,3},{5,0},{6,1},{7,2},{8,15},{9,12},{10,... | collective-permute-start | bytes 786440 | tf_op jit(solution)/shard_map/ppermute | solution.py:26
  61.5 6.8 %collective-permute-done.17.refs_4_ = bf16[256,512]{1,0:T(8,128)(2,1)S(1)} collective-permute-done((bf16[256,512]{1,0:T(8,128)(2,1)S(1)}, bf16[256,512]{1,0:T(8,128)(2,1)S(1)}, u32[]{:S(2)}, u32[]{:S(2)}) %collective-permute-start.17) | collective-permute-done | bytes 262176 | tf_op jit(solution)/shard_map/ppermute | solution.py:26
  68.3 5.2 %collective-permute-done.19.refs_6_ = bf16[256,512]{1,0:T(8,128)(2,1)S(1)} collective-permute-done((bf16[256,512]{1,0:T(8,128)(2,1)S(1)}, bf16[256,512]{1,0:T(8,128)(2,1)S(1)}, u32[]{:S(2)}, u32[]{:S(2)}) %collective-permute-start.19) | collective-permute-done | bytes 262176 | tf_op jit(solution)/shard_map/ppermute | solution.py:26
  75.5 3.0 %collective-permute-start.22 = (bf16[328,512]{1,0:T(8,128)(2,1)S(1)}, bf16[328,512]{1,0:T(8,128)(2,1)S(1)}, u32[]{:S(2)}, u32[]{:S(2)}) collective-permute-start(bf16[328,512]{1,0:T(8,128)(2,1)S(1)} %get-tuple-element.62), channel_id=1, source_target_pairs={{0,1},{1,2},{2,3},{3,0},{4,5},{5,6},{6,7},{7,4},{8,9},{9,10},{10,1... | collective-permute-start | bytes 1007624 | tf_op jit(solution)/shard_map/ppermute | solution.py:26
  79.8 3.2 %collective-permute-start.24 = (bf16[328,512]{1,0:T(8,128)(2,1)S(1)}, bf16[328,512]{1,0:T(8,128)(2,1)S(1)}, u32[]{:S(2)}, u32[]{:S(2)}) collective-permute-start(bf16[328,512]{1,0:T(8,128)(2,1)S(1)} %get-tuple-element.64), channel_id=1, source_target_pairs={{0,3},{1,0},{2,1},{3,2},{4,7},{5,4},{6,5},{7,6},{8,11},{9,8},{10,9... | collective-permute-start | bytes 1007624 | tf_op jit(solution)/shard_map/ppermute | solution.py:26
  86.1 3.3 %collective-permute-start.27 = (bf16[328,512]{1,0:T(8,128)(2,1)S(1)}, bf16[328,512]{1,0:T(8,128)(2,1)S(1)}, u32[]{:S(2)}, u32[]{:S(2)}) collective-permute-start(bf16[328,512]{1,0:T(8,128)(2,1)S(1)} %get-tuple-element.67), channel_id=1, source_target_pairs={{0,5},{1,6},{2,7},{3,4},{4,1},{5,2},{6,3},{7,0},{8,13},{9,14},{10,... | collective-permute-start | bytes 1007624 | tf_op jit(solution)/shard_map/ppermute | solution.py:26
  90.8 13.5 %collective-permute-start.28 = (bf16[328,512]{1,0:T(8,128)(2,1)S(1)}, bf16[328,512]{1,0:T(8,128)(2,1)S(1)}, u32[]{:S(2)}, u32[]{:S(2)}) collective-permute-start(bf16[328,512]{1,0:T(8,128)(2,1)S(1)} %get-tuple-element.68), channel_id=1, source_target_pairs={{0,7},{1,4},{2,5},{3,6},{4,3},{5,0},{6,1},{7,2},{8,15},{9,12},{10,... | collective-permute-start | bytes 1007624 | tf_op jit(solution)/shard_map/ppermute | solution.py:26
  104.3 9.0 %collective-permute-done.26.refs_5_.refs_9_ = bf16[328,512]{1,0:T(8,128)(2,1)S(1)} collective-permute-done((bf16[328,512]{1,0:T(8,128)(2,1)S(1)}, bf16[328,512]{1,0:T(8,128)(2,1)S(1)}, u32[]{:S(2)}, u32[]{:S(2)}) %collective-permute-start.26) | collective-permute-done | bytes 335904 | tf_op jit(solution)/shard_map/ppermute | solution.py:26
  115.3 2.8 %spread.5 = bf16[4,256,512]{2,1,0:T(8,128)(2,1)S(1)} custom-call(s32[56]{0:T(128)S(1)} %get-tuple-element.81.refs_0_, s32[8,32]{1,0:T(8,128)S(1)} %bitcast.10, s32[32]{0:T(128)S(1)} %bitcast.16, bf16[32,8,128,128]{3,2,1,0:T(8,128)(2,1)S(1)} %get-tuple-element.50.refs_3_, bf16[328,512]{1,0:T(8,128)(2,1)S(1)} %get-tuple-element.61.refs_0_.refs_4_, ...), custom_call_target="tpu_custom_call" | custom-call | flops 17179869184 | bytes 4194304 | tf_op jit(solution)/shard_map/spread/pallas_call | solution.py:243
  118.2 2.9 %spread.4 = bf16[4,256,512]{2,1,0:T(8,128)(2,1)S(1)} custom-call(s32[56]{0:T(128)S(1)} %get-tuple-element.81.refs_0_, s32[8,32]{1,0:T(8,128)S(1)} %bitcast.11, s32[32]{0:T(128)S(1)} %bitcast.17, bf16[32,8,128,128]{3,2,1,0:T(8,128)(2,1)S(1)} %get-tuple-element.50.refs_3_, bf16[328,512]{1,0:T(8,128)(2,1)S(1)} %get-tuple-element.61.refs_0_.refs_4_, ...), custom_call_target="tpu_custom_call" | custom-call | flops 17179869184 | bytes 4194304 | tf_op jit(solution)/shard_map/spread/pallas_call | solution.py:243
  122.0 2.9 %spread.6 = (bf16[256,512]{1,0:T(8,128)(2,1)S(1)}, bf16[256,512]{1,0:T(8,128)(2,1)S(1)}, bf16[256,512]{1,0:T(8,128)(2,1)S(1)}, bf16[256,512]{1,0:T(8,128)(2,1)S(1)}) custom-call(s32[56]{0:T(128)S(1)} %get-tuple-element.81.refs_0_, s32[8,32]{1,0:T(8,128)S(1)} %bitcast.12, s32[32]{0:T(128)S(1)} %bitcast.18, ...), custom_call_target="tpu_custom_call" | custom-call | flops 17179869184 | bytes 4194304 | tf_op jit(solution)/shard_map/spread/pallas_call | solution.py:243
  124.9 2.9 %collective-permute-done.35 = f32[72,512]{1,0:T(8,128)S(1)} collective-permute-done((f32[72,512]{1,0:T(8,128)S(1)}, f32[72,512]{1,0:T(8,128)S(1)}, u32[]{:S(2)}, u32[]{:S(2)}) %collective-permute-start.35) | collective-permute-done | bytes 147488 | tf_op jit(solution)/shard_map/ppermute | solution.py:30
  127.8 5.7 %collective-permute-start.37 = (f32[72,512]{1,0:T(8,128)S(1)}, f32[72,512]{1,0:T(8,128)S(1)}, u32[]{:S(2)}, u32[]{:S(2)}) collective-permute-start(f32[72,512]{1,0:T(8,128)S(1)} %add.57), channel_id=1, source_target_pairs={{0,32},{16,48},{32,0},{48,16},{1,33},{17,49},{33,1},{49,17},{2,34}... | collective-permute-start | bytes 442376 | tf_op jit(solution)/shard_map/ppermute | solution.py:30
  133.5 2.9 %spread.7 = (bf16[256,512]{1,0:T(8,128)(2,1)S(1)}, bf16[256,512]{1,0:T(8,128)(2,1)S(1)}, bf16[256,512]{1,0:T(8,128)(2,1)S(1)}, bf16[256,512]{1,0:T(8,128)(2,1)S(1)}) custom-call(s32[56]{0:T(128)S(1)} %get-tuple-element.81.refs_0_, s32[8,32]{1,0:T(8,128)S(1)} %bitcast.13, s32[32]{0:T(128)S(1)} %bitcast.19, ...), custom_call_target="tpu_custom_call" | custom-call | flops 17179869184 | bytes 4194304 | tf_op jit(solution)/shard_map/spread/pallas_call | solution.py:243
  139.6 3.2 %collective-permute-start.39 = (bf16[72,512]{1,0:T(8,128)(2,1)S(1)}, bf16[72,512]{1,0:T(8,128)(2,1)S(1)}, u32[]{:S(2)}, u32[]{:S(2)}) collective-permute-start(bf16[72,512]{1,0:T(8,128)(2,1)S(1)} %get-tuple-element.92), channel_id=1, source_target_pairs={{0,4},{4,0},{1,5},{5,1},{2,6},{6,2},{3,7},{7,3},{8,12},{12,8},{9,1... | collective-permute-start | bytes 221192 | tf_op jit(solution)/shard_map/ppermute | solution.py:30
  146.4 2.7 %collective-permute-done.40 = bf16[256,512]{1,0:T(8,128)(2,1)S(1)} collective-permute-done((bf16[256,512]{1,0:T(8,128)(2,1)S(1)}, bf16[256,512]{1,0:T(8,128)(2,1)S(1)}, u32[]{:S(2)}, u32[]{:S(2)}) %collective-permute-start.40) | collective-permute-done | bytes 262176 | tf_op jit(solution)/shard_map/ppermute | solution.py:26
  157.6 6.2 %collective-permute-start.44 = (bf16[128,512]{1,0:T(8,128)(2,1)S(1)}, bf16[128,512]{1,0:T(8,128)(2,1)S(1)}, u32[]{:S(2)}, u32[]{:S(2)}) collective-permute-start(bf16[128,512]{1,0:T(8,128)(2,1)S(1)} %pad_maximum_fusion.refs_1_), channel_id=1, source_target_pairs={{0,2},{1,3},{2,0},{3,1},{4,6},{5,7},{6,4},{7,5},{8,10},{9,11},{10,... | collective-permute-start | bytes 393224 | tf_op jit(solution)/shard_map/ppermute | solution.py:26
  164.2 4.0 %collective-permute-start.45 = (bf16[128,512]{1,0:T(8,128)(2,1)S(1)}, bf16[128,512]{1,0:T(8,128)(2,1)S(1)}, u32[]{:S(2)}, u32[]{:S(2)}) collective-permute-start(bf16[128,512]{1,0:T(8,128)(2,1)S(1)} %pad_maximum_fusion.refs_1_), channel_id=1, source_target_pairs={{0,3},{1,0},{2,1},{3,2},{4,7},{5,4},{6,5},{7,6},{8,11},{9,8},{10,9... | collective-permute-start | bytes 393224 | tf_op jit(solution)/shard_map/ppermute | solution.py:26
  (99 shorter events, 52.0 us)
Async XLA Ops:
  0.7 14.6 %collective-permute-start = (bf16[256,512]{1,0:T(8,128)(2,1)}, bf16[256,512]{1,0:T(8,128)(2,1)S(1)}, u32[]{:S(2)}, u32[]{:S(2)}) collective-permute-start(bf16[256,512]{1,0:T(8,128)(2,1)} %refs_4_.1), channel_id=1, source_target_pairs={{0,16},{16,32},{32,48},{48,0},{64,80},{80,96},{96,112},{112,64},{1... | collective-permute-start | bytes 786440 | tf_op jit(solution)/shard_map/ppermute | solution.py:26
  2.7 13.3 %collective-permute-start.1 = (bf16[256,512]{1,0:T(8,128)(2,1)}, bf16[256,512]{1,0:T(8,128)(2,1)S(1)}, u32[]{:S(2)}, u32[]{:S(2)}) collective-permute-start(bf16[256,512]{1,0:T(8,128)(2,1)} %refs_4_.1), channel_id=1, source_target_pairs={{0,64},{16,80},{32,96},{48,112},{64,0},{80,16},{96,32},{112,48},{1... | collective-permute-start | bytes 786440 | tf_op jit(solution)/shard_map/ppermute | solution.py:26
  4.2 24.7 %collective-permute-start.2 = (bf16[256,512]{1,0:T(8,128)(2,1)}, bf16[256,512]{1,0:T(8,128)(2,1)S(1)}, u32[]{:S(2)}, u32[]{:S(2)}) collective-permute-start(bf16[256,512]{1,0:T(8,128)(2,1)} %refs_4_.1), channel_id=1, source_target_pairs={{0,48},{16,0},{32,16},{48,32},{64,112},{80,64},{96,80},{112,96},{1... | collective-permute-start | bytes 786440 | tf_op jit(solution)/shard_map/ppermute | solution.py:26
  6.4 22.5 %collective-permute-start.3 = (bf16[256,512]{1,0:T(8,128)(2,1)}, bf16[256,512]{1,0:T(8,128)(2,1)S(1)}, u32[]{:S(2)}, u32[]{:S(2)}) collective-permute-start(bf16[256,512]{1,0:T(8,128)(2,1)} %refs_4_.1), channel_id=1, source_target_pairs={{0,96},{16,112},{32,64},{48,80},{64,32},{80,48},{96,0},{112,16},{1... | collective-permute-start | bytes 786440 | tf_op jit(solution)/shard_map/ppermute | solution.py:26
  8.2 21.3 %collective-permute-start.4 = (bf16[256,512]{1,0:T(8,128)(2,1)}, bf16[256,512]{1,0:T(8,128)(2,1)S(1)}, u32[]{:S(2)}, u32[]{:S(2)}) collective-permute-start(bf16[256,512]{1,0:T(8,128)(2,1)} %refs_4_.1), channel_id=1, source_target_pairs={{0,32},{16,48},{32,0},{48,16},{64,96},{80,112},{96,64},{112,80},{1... | collective-permute-start | bytes 786440 | tf_op jit(solution)/shard_map/ppermute | solution.py:26
  15.3 14.3 %collective-permute-start.5 = (bf16[256,512]{1,0:T(8,128)(2,1)S(1)}, bf16[256,512]{1,0:T(8,128)(2,1)S(1)}, u32[]{:S(2)}, u32[]{:S(2)}) collective-permute-start(bf16[256,512]{1,0:T(8,128)(2,1)S(1)} %copy-done.1), channel_id=1, source_target_pairs={{0,80},{16,96},{32,112},{48,64},{64,16},{80,32},{96,48},{112,0},{1... | collective-permute-start | bytes 786440 | tf_op jit(solution)/shard_map/ppermute | solution.py:26
  16.1 13.9 %collective-permute-start.6 = (bf16[256,512]{1,0:T(8,128)(2,1)S(1)}, bf16[256,512]{1,0:T(8,128)(2,1)S(1)}, u32[]{:S(2)}, u32[]{:S(2)}) collective-permute-start(bf16[256,512]{1,0:T(8,128)(2,1)S(1)} %copy-done.1), channel_id=1, source_target_pairs={{0,112},{16,64},{32,80},{48,96},{64,48},{80,0},{96,16},{112,32},{1... | collective-permute-start | bytes 786440 | tf_op jit(solution)/shard_map/ppermute | solution.py:26
  41.8 13.1 %collective-permute-start.15 = (bf16[256,512]{1,0:T(8,128)(2,1)S(1)}, bf16[256,512]{1,0:T(8,128)(2,1)S(1)}, u32[]{:S(2)}, u32[]{:S(2)}) collective-permute-start(bf16[256,512]{1,0:T(8,128)(2,1)S(1)} %get-tuple-element.53), channel_id=1, source_target_pairs={{0,1},{1,2},{2,3},{3,0},{4,5},{5,6},{6,7},{7,4},{8,9},{9,10},{10,1... | collective-permute-start | bytes 786440 | tf_op jit(solution)/shard_map/ppermute | solution.py:26
  48.4 19.9 %collective-permute-start.17 = (bf16[256,512]{1,0:T(8,128)(2,1)S(1)}, bf16[256,512]{1,0:T(8,128)(2,1)S(1)}, u32[]{:S(2)}, u32[]{:S(2)}) collective-permute-start(bf16[256,512]{1,0:T(8,128)(2,1)S(1)} %get-tuple-element.55), channel_id=1, source_target_pairs={{0,3},{1,0},{2,1},{3,2},{4,7},{5,4},{6,5},{7,6},{8,11},{9,8},{10,9... | collective-permute-start | bytes 786440 | tf_op jit(solution)/shard_map/ppermute | solution.py:26
  51.5 16.8 %collective-permute-start.18 = (bf16[256,512]{1,0:T(8,128)(2,1)S(1)}, bf16[256,512]{1,0:T(8,128)(2,1)S(1)}, u32[]{:S(2)}, u32[]{:S(2)}) collective-permute-start(bf16[256,512]{1,0:T(8,128)(2,1)S(1)} %get-tuple-element.56), channel_id=1, source_target_pairs={{0,6},{1,7},{2,4},{3,5},{4,2},{5,3},{6,0},{7,1},{8,14},{9,15},{10,... | collective-permute-start | bytes 786440 | tf_op jit(solution)/shard_map/ppermute | solution.py:26
  53.5 20.0 %collective-permute-start.19 = (bf16[256,512]{1,0:T(8,128)(2,1)S(1)}, bf16[256,512]{1,0:T(8,128)(2,1)S(1)}, u32[]{:S(2)}, u32[]{:S(2)}) collective-permute-start(bf16[256,512]{1,0:T(8,128)(2,1)S(1)} %get-tuple-element.57), channel_id=1, source_target_pairs={{0,2},{1,3},{2,0},{3,1},{4,6},{5,7},{6,4},{7,5},{8,10},{9,11},{10,... | collective-permute-start | bytes 786440 | tf_op jit(solution)/shard_map/ppermute | solution.py:26
  54.9 18.6 %collective-permute-start.20 = (bf16[256,512]{1,0:T(8,128)(2,1)S(1)}, bf16[256,512]{1,0:T(8,128)(2,1)S(1)}, u32[]{:S(2)}, u32[]{:S(2)}) collective-permute-start(bf16[256,512]{1,0:T(8,128)(2,1)S(1)} %get-tuple-element.58), channel_id=1, source_target_pairs={{0,5},{1,6},{2,7},{3,4},{4,1},{5,2},{6,3},{7,0},{8,13},{9,14},{10,... | collective-permute-start | bytes 786440 | tf_op jit(solution)/shard_map/ppermute | solution.py:26
  58.0 15.7 %collective-permute-start.21 = (bf16[256,512]{1,0:T(8,128)(2,1)S(1)}, bf16[256,512]{1,0:T(8,128)(2,1)S(1)}, u32[]{:S(2)}, u32[]{:S(2)}) collective-permute-start(bf16[256,512]{1,0:T(8,128)(2,1)S(1)} %get-tuple-element.59), channel_id=1, source_target_pairs={{0,7},{1,4},{2,5},{3,6},{4,3},{5,0},{6,1},{7,2},{8,15},{9,12},{10,... | collective-permute-start | bytes 786440 | tf_op jit(solution)/shard_map/ppermute | solution.py:26
  79.8 24.5 %collective-permute-start.24 = (bf16[328,512]{1,0:T(8,128)(2,1)S(1)}, bf16[328,512]{1,0:T(8,128)(2,1)S(1)}, u32[]{:S(2)}, u32[]{:S(2)}) collective-permute-start(bf16[328,512]{1,0:T(8,128)(2,1)S(1)} %get-tuple-element.64), channel_id=1, source_target_pairs={{0,3},{1,0},{2,1},{3,2},{4,7},{5,4},{6,5},{7,6},{8,11},{9,8},{10,9... | collective-permute-start | bytes 1007624 | tf_op jit(solution)/shard_map/ppermute | solution.py:26
  83.1 21.2 %collective-permute-start.25 = (bf16[328,512]{1,0:T(8,128)(2,1)S(1)}, bf16[328,512]{1,0:T(8,128)(2,1)S(1)}, u32[]{:S(2)}, u32[]{:S(2)}) collective-permute-start(bf16[328,512]{1,0:T(8,128)(2,1)S(1)} %get-tuple-element.65), channel_id=1, source_target_pairs={{0,6},{1,7},{2,4},{3,5},{4,2},{5,3},{6,0},{7,1},{8,14},{9,15},{10,... | collective-permute-start | bytes 1007624 | tf_op jit(solution)/shard_map/ppermute | solution.py:26
  83.9 29.4 %collective-permute-start.26 = (bf16[328,512]{1,0:T(8,128)(2,1)S(1)}, bf16[328,512]{1,0:T(8,128)(2,1)S(1)}, u32[]{:S(2)}, u32[]{:S(2)}) collective-permute-start(bf16[328,512]{1,0:T(8,128)(2,1)S(1)} %get-tuple-element.66), channel_id=1, source_target_pairs={{0,2},{1,3},{2,0},{3,1},{4,6},{5,7},{6,4},{7,5},{8,10},{9,11},{10,... | collective-permute-start | bytes 1007624 | tf_op jit(solution)/shard_map/ppermute | solution.py:26
  86.1 29.1 %collective-permute-start.27 = (bf16[328,512]{1,0:T(8,128)(2,1)S(1)}, bf16[328,512]{1,0:T(8,128)(2,1)S(1)}, u32[]{:S(2)}, u32[]{:S(2)}) collective-permute-start(bf16[328,512]{1,0:T(8,128)(2,1)S(1)} %get-tuple-element.67), channel_id=1, source_target_pairs={{0,5},{1,6},{2,7},{3,4},{4,1},{5,2},{6,3},{7,0},{8,13},{9,14},{10,... | collective-permute-start | bytes 1007624 | tf_op jit(solution)/shard_map/ppermute | solution.py:26
  90.8 24.4 %collective-permute-start.28 = (bf16[328,512]{1,0:T(8,128)(2,1)S(1)}, bf16[328,512]{1,0:T(8,128)(2,1)S(1)}, u32[]{:S(2)}, u32[]{:S(2)}) collective-permute-start(bf16[328,512]{1,0:T(8,128)(2,1)S(1)} %get-tuple-element.68), channel_id=1, source_target_pairs={{0,7},{1,4},{2,5},{3,6},{4,3},{5,0},{6,1},{7,2},{8,15},{9,12},{10,... | collective-permute-start | bytes 1007624 | tf_op jit(solution)/shard_map/ppermute | solution.py:26
  143.4 14.2 %collective-permute-start.34 = (bf16[256,512]{1,0:T(8,128)(2,1)S(1)}, bf16[256,512]{1,0:T(8,128)(2,1)S(1)}, u32[]{:S(2)}, u32[]{:S(2)}) collective-permute-start(bf16[256,512]{1,0:T(8,128)(2,1)S(1)} %get-tuple-element.77), channel_id=1, source_target_pairs={{0,112},{16,64},{32,80},{48,96},{64,48},{80,0},{96,16},{112,32},{1... | collective-permute-start | bytes 786440 | tf_op jit(solution)/shard_map/ppermute | solution.py:26
  145.8 18.4 %collective-permute-start.33 = (bf16[256,512]{1,0:T(8,128)(2,1)S(1)}, bf16[256,512]{1,0:T(8,128)(2,1)S(1)}, u32[]{:S(2)}, u32[]{:S(2)}) collective-permute-start(bf16[256,512]{1,0:T(8,128)(2,1)S(1)} %get-tuple-element.76), channel_id=1, source_target_pairs={{0,80},{16,96},{32,112},{48,64},{64,16},{80,32},{96,48},{112,0},{1... | collective-permute-start | bytes 786440 | tf_op jit(solution)/shard_map/ppermute | solution.py:26
  149.1 20.3 %collective-permute-start.32 = (bf16[256,512]{1,0:T(8,128)(2,1)S(1)}, bf16[256,512]{1,0:T(8,128)(2,1)S(1)}, u32[]{:S(2)}, u32[]{:S(2)}) collective-permute-start(bf16[256,512]{1,0:T(8,128)(2,1)S(1)} %get-tuple-element.75), channel_id=1, source_target_pairs={{0,32},{16,48},{32,0},{48,16},{64,96},{80,112},{96,64},{112,80},{1... | collective-permute-start | bytes 786440 | tf_op jit(solution)/shard_map/ppermute | solution.py:26
  149.2 20.2 %collective-permute-start.31 = (bf16[256,512]{1,0:T(8,128)(2,1)S(1)}, bf16[256,512]{1,0:T(8,128)(2,1)S(1)}, u32[]{:S(2)}, u32[]{:S(2)}) collective-permute-start(bf16[256,512]{1,0:T(8,128)(2,1)S(1)} %get-tuple-element.74), channel_id=1, source_target_pairs={{0,96},{16,112},{32,64},{48,80},{64,32},{80,48},{96,0},{112,16},{1... | collective-permute-start | bytes 786440 | tf_op jit(solution)/shard_map/ppermute | solution.py:26
  152.5 17.9 %collective-permute-start.43 = (bf16[128,512]{1,0:T(8,128)(2,1)S(1)}, bf16[128,512]{1,0:T(8,128)(2,1)S(1)}, u32[]{:S(2)}, u32[]{:S(2)}) collective-permute-start(bf16[128,512]{1,0:T(8,128)(2,1)S(1)} %pad_maximum_fusion.refs_1_), channel_id=1, source_target_pairs={{0,1},{1,2},{2,3},{3,0},{4,5},{5,6},{6,7},{7,4},{8,9},{9,10},{10,1... | collective-permute-start | bytes 393224 | tf_op jit(solution)/shard_map/ppermute | solution.py:26
  157.6 12.8 %collective-permute-start.44 = (bf16[128,512]{1,0:T(8,128)(2,1)S(1)}, bf16[128,512]{1,0:T(8,128)(2,1)S(1)}, u32[]{:S(2)}, u32[]{:S(2)}) collective-permute-start(bf16[128,512]{1,0:T(8,128)(2,1)S(1)} %pad_maximum_fusion.refs_1_), channel_id=1, source_target_pairs={{0,2},{1,3},{2,0},{3,1},{4,6},{5,7},{6,4},{7,5},{8,10},{9,11},{10,... | collective-permute-start | bytes 393224 | tf_op jit(solution)/shard_map/ppermute | solution.py:26
  (28 other events, 333.4 us)

commit v11 on v10

--- a/solution.py
+++ b/solution.py
@@ -330,7 +330,7 @@
     )(index, *pieces)
 
 
-PARTS = ((0, 0), (0, 1), (1, 0), (0, 3), (1, 2), (0, 2), (1, 1), (1, 3))
+PARTS = ((0, 0), (1, 0), (0, 1), (0, 3), (1, 2), (0, 2), (1, 1), (1, 3))
 CHIP_HALVES = (((0, 0), (0, 1), (1, 0), (0, 3)), ((1, 2), (0, 2), (1, 1), (1, 3)))
 
 

time: 176 us -> 185 us (1.051); the launches traced: 172 us -> 184 us
  waiting for transfers between devices: 49.2 us -> 72.6 us
  starting transfers between devices: 91.8 us -> 79.6 us
    ppermute x41, waiting for transfers between devices: 45.7 us -> 67.7 us  [send_by(): return lax.ppermute(value, axes, pairs)]
    ppermute x41, starting transfers between devices: 82.7 us -> 61 us  [send_by(): return lax.ppermute(value, axes, pairs)]
    ppermute x5, starting transfers between devices: 9.12 us -> 18.6 us  [exchange(): lax.ppermute(value, axis, [(i, i ^ mask) for i in range(SIZES[axis])])]
  transfers between devices with their start and end apart: 46 -> 46, of which waited for: 24 -> 22; matrix products, arithmetic and copies ran while one was open for 1% -> 1% of each run, Pallas kernels for 9% -> 9%
where the time goes in v11:
time: 185 us; the launch traced here: 184 us
  starting transfers between devices  79.6 us (43%)
  waiting for transfers between devices  72.6 us (39%)
  Pallas kernels  28.7 us (16%)
    ppermute x41, waiting for transfers between devices, send_by(): return lax.ppermute(value, axes, pairs)  67.7 us
    ppermute x41, starting transfers between devices, send_by(): return lax.ppermute(value, axes, pairs)  61 us
    ppermute x5, starting transfers between devices, exchange(): lax.ppermute(value, axis, [(i, i ^ mask) for i in range(SIZES[axis])])  18.6 us
    pallas_call x4, Pallas kernels, spread(): pl.pallas_call(lambda *refs: backward_kernel(shards, parts, at_source, at...  11.4 us
    pallas_call x1, Pallas kernels, aggregate(): pl.pallas_call(lambda *refs: forward_kernel(shards, at_source, at_place,...  9.18 us
    ppermute x5, waiting for transfers between devices, exchange(): lax.ppermute(value, axis, [(i, i ^ mask) for i in range(SIZES[axis])])  4.89 us
    pallas_call x1, Pallas kernels, fetch(): pl.pallas_call(fetch_kernel, out_shape=(pltpu.VMEM(values.shape, values.d...  4.61 us
  transfers between devices with their start and end apart: 46, of which 22 were waited for; matrix products, arithmetic and copies ran while one was open for 1% of the time, Pallas kernels for 9%

profile of v11, /device:TPU:0, one launch (start us, length us, event | category | flops | bytes accessed | tf_op | source)
XLA Modules:
  0.0 184.1 jit_solution(12474971197973522230)
XLA Ops:
  10.6 4.6 %fetch.1 = (bf16[32,8,128,128]{3,2,1,0:T(8,128)(2,1)S(1)}, s32[56]{0:T(128)S(1)}) custom-call(s32[56]{0:T(128)S(1)} %dynamic-slice_bitcast_fusion.index_ref, bf16[32,8,128,128]{3,2,1,0:T(8,128)(2,1)} %bitcast.20), custom_call_target="tpu_custom_call" | custom-call | bytes 16777216 | tf_op jit(solution)/shard_map/fetch/pallas_call | solution.py:80
  16.1 3.4 %collective-permute-start.6 = (bf16[256,512]{1,0:T(8,128)(2,1)S(1)}, bf16[256,512]{1,0:T(8,128)(2,1)S(1)}, u32[]{:S(2)}, u32[]{:S(2)}) collective-permute-start(bf16[256,512]{1,0:T(8,128)(2,1)S(1)} %copy-done.1), channel_id=1, source_target_pairs={{0,112},{16,64},{32,80},{48,96},{64,48},{80,0},{96,16},{112,32},{1... | collective-permute-start | bytes 786440 | tf_op jit(solution)/shard_map/ppermute | solution.py:26
  19.5 9.4 %collective-permute-done.2.refs_7_ = bf16[256,512]{1,0:T(8,128)(2,1)S(1)} collective-permute-done((bf16[256,512]{1,0:T(8,128)(2,1)}, bf16[256,512]{1,0:T(8,128)(2,1)S(1)}, u32[]{:S(2)}, u32[]{:S(2)}) %collective-permute-start.2) | collective-permute-done | bytes 262176 | tf_op jit(solution)/shard_map/ppermute | solution.py:26
  33.1 9.2 %aggregate.1 = (bf16[256,512]{1,0:T(8,128)(2,1)S(1)}, bf16[256,512]{1,0:T(8,128)(2,1)S(1)}, bf16[256,512]{1,0:T(8,128)(2,1)S(1)}, bf16[256,512]{1,0:T(8,128)(2,1...) custom-call(s32[56]{0:T(128)S(1)} %get-tuple-element.81.refs_0_, ...), custom_call_target="tpu_custom_call" | custom-call | flops 8589934592 | bytes 16777216 | tf_op jit(solution)/shard_map/aggregate/pallas_call | solution.py:129
  44.6 5.9 %collective-permute-start.16 = (bf16[256,512]{1,0:T(8,128)(2,1)S(1)}, bf16[256,512]{1,0:T(8,128)(2,1)S(1)}, u32[]{:S(2)}, u32[]{:S(2)}) collective-permute-start(bf16[256,512]{1,0:T(8,128)(2,1)S(1)} %get-tuple-element.54), channel_id=1, source_target_pairs={{0,1},{1,2},{2,3},{3,0},{4,5},{5,6},{6,7},{7,4},{8,9},{9,10},{10,1... | collective-permute-start | bytes 786440 | tf_op jit(solution)/shard_map/ppermute | solution.py:26
  53.5 7.1 %collective-permute-start.20 = (bf16[256,512]{1,0:T(8,128)(2,1)S(1)}, bf16[256,512]{1,0:T(8,128)(2,1)S(1)}, u32[]{:S(2)}, u32[]{:S(2)}) collective-permute-start(bf16[256,512]{1,0:T(8,128)(2,1)S(1)} %get-tuple-element.58), channel_id=1, source_target_pairs={{0,5},{1,6},{2,7},{3,4},{4,1},{5,2},{6,3},{7,0},{8,13},{9,14},{10,... | collective-permute-start | bytes 786440 | tf_op jit(solution)/shard_map/ppermute | solution.py:26
  60.6 7.4 %collective-permute-done.16.refs_3_ = bf16[256,512]{1,0:T(8,128)(2,1)S(1)} collective-permute-done((bf16[256,512]{1,0:T(8,128)(2,1)S(1)}, bf16[256,512]{1,0:T(8,128)(2,1)S(1)}, u32[]{:S(2)}, u32[]{:S(2)}) %collective-permute-start.16) | collective-permute-done | bytes 262176 | tf_op jit(solution)/shard_map/ppermute | solution.py:26
  68.0 5.8 %collective-permute-done.19.refs_6_ = bf16[256,512]{1,0:T(8,128)(2,1)S(1)} collective-permute-done((bf16[256,512]{1,0:T(8,128)(2,1)S(1)}, bf16[256,512]{1,0:T(8,128)(2,1)S(1)}, u32[]{:S(2)}, u32[]{:S(2)}) %collective-permute-start.19) | collective-permute-done | bytes 262176 | tf_op jit(solution)/shard_map/ppermute | solution.py:26
  73.9 2.9 %collective-permute-done.21.refs_8_ = bf16[256,512]{1,0:T(8,128)(2,1)S(1)} collective-permute-done((bf16[256,512]{1,0:T(8,128)(2,1)S(1)}, bf16[256,512]{1,0:T(8,128)(2,1)S(1)}, u32[]{:S(2)}, u32[]{:S(2)}) %collective-permute-start.21) | collective-permute-done | bytes 262176 | tf_op jit(solution)/shard_map/ppermute | solution.py:26
  82.9 3.3 %collective-permute-start.25 = (bf16[328,512]{1,0:T(8,128)(2,1)S(1)}, bf16[328,512]{1,0:T(8,128)(2,1)S(1)}, u32[]{:S(2)}, u32[]{:S(2)}) collective-permute-start(bf16[328,512]{1,0:T(8,128)(2,1)S(1)} %get-tuple-element.65), channel_id=1, source_target_pairs={{0,6},{1,7},{2,4},{3,5},{4,2},{5,3},{6,0},{7,1},{8,14},{9,15},{10,... | collective-permute-start | bytes 1007624 | tf_op jit(solution)/shard_map/ppermute | solution.py:26
  92.4 7.5 %collective-permute-done.23.refs_2_.refs_6_ = bf16[328,512]{1,0:T(8,128)(2,1)S(1)} collective-permute-done((bf16[328,512]{1,0:T(8,128)(2,1)S(1)}, bf16[328,512]{1,0:T(8,128)(2,1)S(1)}, u32[]{:S(2)}, u32[]{:S(2)}) %collective-permute-start.23) | collective-permute-done | bytes 335904 | tf_op jit(solution)/shard_map/ppermute | solution.py:26
  99.9 4.0 %collective-permute-start.28 = (bf16[328,512]{1,0:T(8,128)(2,1)S(1)}, bf16[328,512]{1,0:T(8,128)(2,1)S(1)}, u32[]{:S(2)}, u32[]{:S(2)}) collective-permute-start(bf16[328,512]{1,0:T(8,128)(2,1)S(1)} %get-tuple-element.68), channel_id=1, source_target_pairs={{0,7},{1,4},{2,5},{3,6},{4,3},{5,0},{6,1},{7,2},{8,15},{9,12},{10,... | collective-permute-start | bytes 1007624 | tf_op jit(solution)/shard_map/ppermute | solution.py:26
  103.8 6.2 %collective-permute-done.26.refs_5_.refs_9_ = bf16[328,512]{1,0:T(8,128)(2,1)S(1)} collective-permute-done((bf16[328,512]{1,0:T(8,128)(2,1)S(1)}, bf16[328,512]{1,0:T(8,128)(2,1)S(1)}, u32[]{:S(2)}, u32[]{:S(2)}) %collective-permute-start.26) | collective-permute-done | bytes 335904 | tf_op jit(solution)/shard_map/ppermute | solution.py:26
  110.1 5.6 %collective-permute-done.28.refs_7_.refs_11_ = bf16[328,512]{1,0:T(8,128)(2,1)S(1)} collective-permute-done((bf16[328,512]{1,0:T(8,128)(2,1)S(1)}, bf16[328,512]{1,0:T(8,128)(2,1)S(1)}, u32[]{:S(2)}, u32[]{:S(2)}) %collective-permute-start.28) | collective-permute-done | bytes 335904 | tf_op jit(solution)/shard_map/ppermute | solution.py:26
  115.8 4.1 %collective-permute-start.29 = (f32[72,512]{1,0:T(8,128)S(1)}, f32[72,512]{1,0:T(8,128)S(1)}, u32[]{:S(2)}, u32[]{:S(2)}) collective-permute-start(f32[72,512]{1,0:T(8,128)S(1)} %add_shares.1), channel_id=1, source_target_pairs={{0,64},{64,0},{1,65},{65,1},{2,66},{66,2},{3,67},{67,3},{4,68},{68... | collective-permute-start | bytes 442376 | tf_op jit(solution)/shard_map/ppermute | solution.py:30
  126.3 7.2 %collective-permute-start.35 = (f32[72,512]{1,0:T(8,128)S(1)}, f32[72,512]{1,0:T(8,128)S(1)}, u32[]{:S(2)}, u32[]{:S(2)}) collective-permute-start(f32[72,512]{1,0:T(8,128)S(1)} %add.53), channel_id=1, source_target_pairs={{0,16},{16,0},{32,48},{48,32},{1,17},{17,1},{33,49},{49,33},{2,18}... | collective-permute-start | bytes 442376 | tf_op jit(solution)/shard_map/ppermute | solution.py:30
  133.5 2.9 %spread.6 = (bf16[256,512]{1,0:T(8,128)(2,1)S(1)}, bf16[256,512]{1,0:T(8,128)(2,1)S(1)}, bf16[256,512]{1,0:T(8,128)(2,1)S(1)}, bf16[256,512]{1,0:T(8,128)(2,1)S(1)}) custom-call(s32[56]{0:T(128)S(1)} %get-tuple-element.81.refs_0_, s32[8,32]{1,0:T(8,128)S(1)} %bitcast.12, s32[32]{0:T(128)S(1)} %bitcast.18, ...), custom_call_target="tpu_custom_call" | custom-call | flops 17179869184 | bytes 4194304 | tf_op jit(solution)/shard_map/spread/pallas_call | solution.py:243
  137.7 3.0 %spread.7 = (bf16[256,512]{1,0:T(8,128)(2,1)S(1)}, bf16[256,512]{1,0:T(8,128)(2,1)S(1)}, bf16[256,512]{1,0:T(8,128)(2,1)S(1)}, bf16[256,512]{1,0:T(8,128)(2,1)S(1)}) custom-call(s32[56]{0:T(128)S(1)} %get-tuple-element.81.refs_0_, s32[8,32]{1,0:T(8,128)S(1)} %bitcast.13, s32[32]{0:T(128)S(1)} %bitcast.19, ...), custom_call_target="tpu_custom_call" | custom-call | flops 17179869184 | bytes 4194304 | tf_op jit(solution)/shard_map/spread/pallas_call | solution.py:243
  140.7 3.7 %collective-permute-done.37 = f32[72,512]{1,0:T(8,128)S(1)} collective-permute-done((f32[72,512]{1,0:T(8,128)S(1)}, f32[72,512]{1,0:T(8,128)S(1)}, u32[]{:S(2)}, u32[]{:S(2)}) %collective-permute-start.37) | collective-permute-done | bytes 147488 | tf_op jit(solution)/shard_map/ppermute | solution.py:30
  146.7 7.1 %collective-permute-start.39 = (bf16[72,512]{1,0:T(8,128)(2,1)S(1)}, bf16[72,512]{1,0:T(8,128)(2,1)S(1)}, u32[]{:S(2)}, u32[]{:S(2)}) collective-permute-start(bf16[72,512]{1,0:T(8,128)(2,1)S(1)} %get-tuple-element.92), channel_id=1, source_target_pairs={{0,4},{4,0},{1,5},{5,1},{2,6},{6,2},{3,7},{7,3},{8,12},{12,8},{9,1... | collective-permute-start | bytes 221192 | tf_op jit(solution)/shard_map/ppermute | solution.py:30
  154.4 2.9 %collective-permute-start.34 = (bf16[256,512]{1,0:T(8,128)(2,1)S(1)}, bf16[256,512]{1,0:T(8,128)(2,1)S(1)}, u32[]{:S(2)}, u32[]{:S(2)}) collective-permute-start(bf16[256,512]{1,0:T(8,128)(2,1)S(1)} %get-tuple-element.77), channel_id=1, source_target_pairs={{0,112},{16,64},{32,80},{48,96},{64,48},{80,0},{96,16},{112,32},{1... | collective-permute-start | bytes 786440 | tf_op jit(solution)/shard_map/ppermute | solution.py:26
  163.7 6.0 %collective-permute-done.34 = bf16[256,512]{1,0:T(8,128)(2,1)S(1)} collective-permute-done((bf16[256,512]{1,0:T(8,128)(2,1)S(1)}, bf16[256,512]{1,0:T(8,128)(2,1)S(1)}, u32[]{:S(2)}, u32[]{:S(2)}) %collective-permute-start.34) | collective-permute-done | bytes 262176 | tf_op jit(solution)/shard_map/ppermute | solution.py:26
  169.7 6.2 %collective-permute-done.33 = bf16[256,512]{1,0:T(8,128)(2,1)S(1)} collective-permute-done((bf16[256,512]{1,0:T(8,128)(2,1)S(1)}, bf16[256,512]{1,0:T(8,128)(2,1)S(1)}, u32[]{:S(2)}, u32[]{:S(2)}) %collective-permute-start.33) | collective-permute-done | bytes 262176 | tf_op jit(solution)/shard_map/ppermute | solution.py:26
  176.6 5.0 %collective-permute-done.31 = bf16[256,512]{1,0:T(8,128)(2,1)S(1)} collective-permute-done((bf16[256,512]{1,0:T(8,128)(2,1)S(1)}, bf16[256,512]{1,0:T(8,128)(2,1)S(1)}, u32[]{:S(2)}, u32[]{:S(2)}) %collective-permute-start.31) | collective-permute-done | bytes 262176 | tf_op jit(solution)/shard_map/ppermute | solution.py:26
  (99 shorter events, 52.8 us)
Async XLA Ops:
  0.7 14.6 %collective-permute-start = (bf16[256,512]{1,0:T(8,128)(2,1)}, bf16[256,512]{1,0:T(8,128)(2,1)S(1)}, u32[]{:S(2)}, u32[]{:S(2)}) collective-permute-start(bf16[256,512]{1,0:T(8,128)(2,1)} %refs_4_.1), channel_id=1, source_target_pairs={{0,16},{16,32},{32,48},{48,0},{64,80},{80,96},{96,112},{112,64},{1... | collective-permute-start | bytes 786440 | tf_op jit(solution)/shard_map/ppermute | solution.py:26
  2.7 13.3 %collective-permute-start.1 = (bf16[256,512]{1,0:T(8,128)(2,1)}, bf16[256,512]{1,0:T(8,128)(2,1)S(1)}, u32[]{:S(2)}, u32[]{:S(2)}) collective-permute-start(bf16[256,512]{1,0:T(8,128)(2,1)} %refs_4_.1), channel_id=1, source_target_pairs={{0,64},{16,80},{32,96},{48,112},{64,0},{80,16},{96,32},{112,48},{1... | collective-permute-start | bytes 786440 | tf_op jit(solution)/shard_map/ppermute | solution.py:26
  4.2 24.7 %collective-permute-start.2 = (bf16[256,512]{1,0:T(8,128)(2,1)}, bf16[256,512]{1,0:T(8,128)(2,1)S(1)}, u32[]{:S(2)}, u32[]{:S(2)}) collective-permute-start(bf16[256,512]{1,0:T(8,128)(2,1)} %refs_4_.1), channel_id=1, source_target_pairs={{0,48},{16,0},{32,16},{48,32},{64,112},{80,64},{96,80},{112,96},{1... | collective-permute-start | bytes 786440 | tf_op jit(solution)/shard_map/ppermute | solution.py:26
  6.4 22.5 %collective-permute-start.3 = (bf16[256,512]{1,0:T(8,128)(2,1)}, bf16[256,512]{1,0:T(8,128)(2,1)S(1)}, u32[]{:S(2)}, u32[]{:S(2)}) collective-permute-start(bf16[256,512]{1,0:T(8,128)(2,1)} %refs_4_.1), channel_id=1, source_target_pairs={{0,96},{16,112},{32,64},{48,80},{64,32},{80,48},{96,0},{112,16},{1... | collective-permute-start | bytes 786440 | tf_op jit(solution)/shard_map/ppermute | solution.py:26
  8.2 21.3 %collective-permute-start.4 = (bf16[256,512]{1,0:T(8,128)(2,1)}, bf16[256,512]{1,0:T(8,128)(2,1)S(1)}, u32[]{:S(2)}, u32[]{:S(2)}) collective-permute-start(bf16[256,512]{1,0:T(8,128)(2,1)} %refs_4_.1), channel_id=1, source_target_pairs={{0,32},{16,48},{32,0},{48,16},{64,96},{80,112},{96,64},{112,80},{1... | collective-permute-start | bytes 786440 | tf_op jit(solution)/shard_map/ppermute | solution.py:26
  15.3 14.3 %collective-permute-start.5 = (bf16[256,512]{1,0:T(8,128)(2,1)S(1)}, bf16[256,512]{1,0:T(8,128)(2,1)S(1)}, u32[]{:S(2)}, u32[]{:S(2)}) collective-permute-start(bf16[256,512]{1,0:T(8,128)(2,1)S(1)} %copy-done.1), channel_id=1, source_target_pairs={{0,80},{16,96},{32,112},{48,64},{64,16},{80,32},{96,48},{112,0},{1... | collective-permute-start | bytes 786440 | tf_op jit(solution)/shard_map/ppermute | solution.py:26
  16.1 13.9 %collective-permute-start.6 = (bf16[256,512]{1,0:T(8,128)(2,1)S(1)}, bf16[256,512]{1,0:T(8,128)(2,1)S(1)}, u32[]{:S(2)}, u32[]{:S(2)}) collective-permute-start(bf16[256,512]{1,0:T(8,128)(2,1)S(1)} %copy-done.1), channel_id=1, source_target_pairs={{0,112},{16,64},{32,80},{48,96},{64,48},{80,0},{96,16},{112,32},{1... | collective-permute-start | bytes 786440 | tf_op jit(solution)/shard_map/ppermute | solution.py:26
  44.6 23.4 %collective-permute-start.16 = (bf16[256,512]{1,0:T(8,128)(2,1)S(1)}, bf16[256,512]{1,0:T(8,128)(2,1)S(1)}, u32[]{:S(2)}, u32[]{:S(2)}) collective-permute-start(bf16[256,512]{1,0:T(8,128)(2,1)S(1)} %get-tuple-element.54), channel_id=1, source_target_pairs={{0,1},{1,2},{2,3},{3,0},{4,5},{5,6},{6,7},{7,4},{8,9},{9,10},{10,1... | collective-permute-start | bytes 786440 | tf_op jit(solution)/shard_map/ppermute | solution.py:26
  50.5 17.6 %collective-permute-start.17 = (bf16[256,512]{1,0:T(8,128)(2,1)S(1)}, bf16[256,512]{1,0:T(8,128)(2,1)S(1)}, u32[]{:S(2)}, u32[]{:S(2)}) collective-permute-start(bf16[256,512]{1,0:T(8,128)(2,1)S(1)} %get-tuple-element.55), channel_id=1, source_target_pairs={{0,3},{1,0},{2,1},{3,2},{4,7},{5,4},{6,5},{7,6},{8,11},{9,8},{10,9... | collective-permute-start | bytes 786440 | tf_op jit(solution)/shard_map/ppermute | solution.py:26
  50.5 17.6 %collective-permute-start.18 = (bf16[256,512]{1,0:T(8,128)(2,1)S(1)}, bf16[256,512]{1,0:T(8,128)(2,1)S(1)}, u32[]{:S(2)}, u32[]{:S(2)}) collective-permute-start(bf16[256,512]{1,0:T(8,128)(2,1)S(1)} %get-tuple-element.56), channel_id=1, source_target_pairs={{0,6},{1,7},{2,4},{3,5},{4,2},{5,3},{6,0},{7,1},{8,14},{9,15},{10,... | collective-permute-start | bytes 786440 | tf_op jit(solution)/shard_map/ppermute | solution.py:26
  52.1 21.8 %collective-permute-start.19 = (bf16[256,512]{1,0:T(8,128)(2,1)S(1)}, bf16[256,512]{1,0:T(8,128)(2,1)S(1)}, u32[]{:S(2)}, u32[]{:S(2)}) collective-permute-start(bf16[256,512]{1,0:T(8,128)(2,1)S(1)} %get-tuple-element.57), channel_id=1, source_target_pairs={{0,2},{1,3},{2,0},{3,1},{4,6},{5,7},{6,4},{7,5},{8,10},{9,11},{10,... | collective-permute-start | bytes 786440 | tf_op jit(solution)/shard_map/ppermute | solution.py:26
  53.5 20.4 %collective-permute-start.20 = (bf16[256,512]{1,0:T(8,128)(2,1)S(1)}, bf16[256,512]{1,0:T(8,128)(2,1)S(1)}, u32[]{:S(2)}, u32[]{:S(2)}) collective-permute-start(bf16[256,512]{1,0:T(8,128)(2,1)S(1)} %get-tuple-element.58), channel_id=1, source_target_pairs={{0,5},{1,6},{2,7},{3,4},{4,1},{5,2},{6,3},{7,0},{8,13},{9,14},{10,... | collective-permute-start | bytes 786440 | tf_op jit(solution)/shard_map/ppermute | solution.py:26
  79.6 20.2 %collective-permute-start.23 = (bf16[328,512]{1,0:T(8,128)(2,1)S(1)}, bf16[328,512]{1,0:T(8,128)(2,1)S(1)}, u32[]{:S(2)}, u32[]{:S(2)}) collective-permute-start(bf16[328,512]{1,0:T(8,128)(2,1)S(1)} %get-tuple-element.63), channel_id=1, source_target_pairs={{0,1},{1,2},{2,3},{3,0},{4,5},{5,6},{6,7},{7,4},{8,9},{9,10},{10,1... | collective-permute-start | bytes 1007624 | tf_op jit(solution)/shard_map/ppermute | solution.py:26
  81.1 22.7 %collective-permute-start.24 = (bf16[328,512]{1,0:T(8,128)(2,1)S(1)}, bf16[328,512]{1,0:T(8,128)(2,1)S(1)}, u32[]{:S(2)}, u32[]{:S(2)}) collective-permute-start(bf16[328,512]{1,0:T(8,128)(2,1)S(1)} %get-tuple-element.64), channel_id=1, source_target_pairs={{0,3},{1,0},{2,1},{3,2},{4,7},{5,4},{6,5},{7,6},{8,11},{9,8},{10,9... | collective-permute-start | bytes 1007624 | tf_op jit(solution)/shard_map/ppermute | solution.py:26
  82.9 21.0 %collective-permute-start.25 = (bf16[328,512]{1,0:T(8,128)(2,1)S(1)}, bf16[328,512]{1,0:T(8,128)(2,1)S(1)}, u32[]{:S(2)}, u32[]{:S(2)}) collective-permute-start(bf16[328,512]{1,0:T(8,128)(2,1)S(1)} %get-tuple-element.65), channel_id=1, source_target_pairs={{0,6},{1,7},{2,4},{3,5},{4,2},{5,3},{6,0},{7,1},{8,14},{9,15},{10,... | collective-permute-start | bytes 1007624 | tf_op jit(solution)/shard_map/ppermute | solution.py:26
  86.1 23.9 %collective-permute-start.26 = (bf16[328,512]{1,0:T(8,128)(2,1)S(1)}, bf16[328,512]{1,0:T(8,128)(2,1)S(1)}, u32[]{:S(2)}, u32[]{:S(2)}) collective-permute-start(bf16[328,512]{1,0:T(8,128)(2,1)S(1)} %get-tuple-element.66), channel_id=1, source_target_pairs={{0,2},{1,3},{2,0},{3,1},{4,6},{5,7},{6,4},{7,5},{8,10},{9,11},{10,... | collective-permute-start | bytes 1007624 | tf_op jit(solution)/shard_map/ppermute | solution.py:26
  90.4 19.7 %collective-permute-start.27 = (bf16[328,512]{1,0:T(8,128)(2,1)S(1)}, bf16[328,512]{1,0:T(8,128)(2,1)S(1)}, u32[]{:S(2)}, u32[]{:S(2)}) collective-permute-start(bf16[328,512]{1,0:T(8,128)(2,1)S(1)} %get-tuple-element.67), channel_id=1, source_target_pairs={{0,5},{1,6},{2,7},{3,4},{4,1},{5,2},{6,3},{7,0},{8,13},{9,14},{10,... | collective-permute-start | bytes 1007624 | tf_op jit(solution)/shard_map/ppermute | solution.py:26
  99.9 15.9 %collective-permute-start.28 = (bf16[328,512]{1,0:T(8,128)(2,1)S(1)}, bf16[328,512]{1,0:T(8,128)(2,1)S(1)}, u32[]{:S(2)}, u32[]{:S(2)}) collective-permute-start(bf16[328,512]{1,0:T(8,128)(2,1)S(1)} %get-tuple-element.68), channel_id=1, source_target_pairs={{0,7},{1,4},{2,5},{3,6},{4,3},{5,0},{6,1},{7,2},{8,15},{9,12},{10,... | collective-permute-start | bytes 1007624 | tf_op jit(solution)/shard_map/ppermute | solution.py:26
  154.4 15.3 %collective-permute-start.34 = (bf16[256,512]{1,0:T(8,128)(2,1)S(1)}, bf16[256,512]{1,0:T(8,128)(2,1)S(1)}, u32[]{:S(2)}, u32[]{:S(2)}) collective-permute-start(bf16[256,512]{1,0:T(8,128)(2,1)S(1)} %get-tuple-element.77), channel_id=1, source_target_pairs={{0,112},{16,64},{32,80},{48,96},{64,48},{80,0},{96,16},{112,32},{1... | collective-permute-start | bytes 786440 | tf_op jit(solution)/shard_map/ppermute | solution.py:26
  157.3 18.6 %collective-permute-start.33 = (bf16[256,512]{1,0:T(8,128)(2,1)S(1)}, bf16[256,512]{1,0:T(8,128)(2,1)S(1)}, u32[]{:S(2)}, u32[]{:S(2)}) collective-permute-start(bf16[256,512]{1,0:T(8,128)(2,1)S(1)} %get-tuple-element.76), channel_id=1, source_target_pairs={{0,80},{16,96},{32,112},{48,64},{64,16},{80,32},{96,48},{112,0},{1... | collective-permute-start | bytes 786440 | tf_op jit(solution)/shard_map/ppermute | solution.py:26
  157.5 19.1 %collective-permute-start.32 = (bf16[256,512]{1,0:T(8,128)(2,1)S(1)}, bf16[256,512]{1,0:T(8,128)(2,1)S(1)}, u32[]{:S(2)}, u32[]{:S(2)}) collective-permute-start(bf16[256,512]{1,0:T(8,128)(2,1)S(1)} %get-tuple-element.75), channel_id=1, source_target_pairs={{0,32},{16,48},{32,0},{48,16},{64,96},{80,112},{96,64},{112,80},{1... | collective-permute-start | bytes 786440 | tf_op jit(solution)/shard_map/ppermute | solution.py:26
  159.1 22.4 %collective-permute-start.31 = (bf16[256,512]{1,0:T(8,128)(2,1)S(1)}, bf16[256,512]{1,0:T(8,128)(2,1)S(1)}, u32[]{:S(2)}, u32[]{:S(2)}) collective-permute-start(bf16[256,512]{1,0:T(8,128)(2,1)S(1)} %get-tuple-element.74), channel_id=1, source_target_pairs={{0,96},{16,112},{32,64},{48,80},{64,32},{80,48},{96,0},{112,16},{1... | collective-permute-start | bytes 786440 | tf_op jit(solution)/shard_map/ppermute | solution.py:26
  163.2 19.4 %collective-permute-start.43 = (bf16[128,512]{1,0:T(8,128)(2,1)S(1)}, bf16[128,512]{1,0:T(8,128)(2,1)S(1)}, u32[]{:S(2)}, u32[]{:S(2)}) collective-permute-start(bf16[128,512]{1,0:T(8,128)(2,1)S(1)} %pad_maximum_fusion.refs_1_), channel_id=1, source_target_pairs={{0,1},{1,2},{2,3},{3,0},{4,5},{5,6},{6,7},{7,4},{8,9},{9,10},{10,1... | collective-permute-start | bytes 393224 | tf_op jit(solution)/shard_map/ppermute | solution.py:26
  169.7 12.8 %collective-permute-start.44 = (bf16[128,512]{1,0:T(8,128)(2,1)S(1)}, bf16[128,512]{1,0:T(8,128)(2,1)S(1)}, u32[]{:S(2)}, u32[]{:S(2)}) collective-permute-start(bf16[128,512]{1,0:T(8,128)(2,1)S(1)} %pad_maximum_fusion.refs_1_), channel_id=1, source_target_pairs={{0,2},{1,3},{2,0},{3,1},{4,6},{5,7},{6,4},{7,5},{8,10},{9,11},{10,... | collective-permute-start | bytes 393224 | tf_op jit(solution)/shard_map/ppermute | solution.py:26
  (28 other events, 364.2 us)
